TPU v7x, 256 devices: a whole 4x4x8 slice. The times are simulated.
256 devices in a mesh: row: 8 (over z), col: 32 (over y, x, core).
Axes of the slice: x: 4, y: 4, z: 8, core: 2. Of those that a mesh axis runs over, the one named last changes fastest.
Arguments:
- factor: bfloat16 [32, 8, 8, 32, 128, 128], P(None, 'row', None, 'col'), may hold values from -0.046875 to 0.046875
- pattern: int32 [32, 8, 8, 32], P(None, 'row', None, 'col'), may hold values 0 or 1
- loads: float32 [8, 32, 128, 256], P(None, 'col'), may hold values from -6 to 6
- block_inverse: float32 [8, 32, 128, 128], P(None, 'col'), may hold values from -1 to 2, as said below
Outputs:
- solution: float32 [8, 32, 128, 256], P(None, 'col')
Inputs may be any that keep to these rules, and one draw needn't show every extreme that they name: `block_inverse`: each block is lower triangular with diagonal entries between 0.5 and 1.5.
All inputs are finite; a program needn't handle non-finite values. No bound on the sum of `pattern` on one device may be relied on, other than what follows from the above.
Results may differ from a plain program's by a relative error of at most 0.0045.
Values may be sent and summed in bfloat16 or wider, within the bound.
No kernel may reach another device: no remote copies, remote signals or barrier semaphores. Data moves between devices by JAX's collectives and lax.ppermute only.
A program may use at most 128 MiB of HBM per device.

v0:
```python
import jax
import jax.numpy as jnp
from jax import lax
from jax.sharding import PartitionSpec as P

LEVELS = 8


def spread(value, axis, source):
    kept = jnp.where(lax.axis_index(axis) == source, value, 0).astype(value.dtype)
    return lax.psum(kept, axis)


def per_device(factor, pattern, loads, block_inverse):
    row_count = lax.axis_size("row")
    col_count = lax.axis_size("col")
    groups = col_count // row_count
    my_row = lax.axis_index("row")
    my_col = lax.axis_index("col")
    masked = factor[:, 0, :, 0] * pattern[:, 0, :, 0].astype(jnp.bfloat16)[:, :, None, None]
    per_row = factor.shape[0] // LEVELS
    per_col = factor.shape[2] // LEVELS
    rhs_local = loads[:, 0]
    inverse_local = block_inverse[:, 0]
    forward_vals = []
    forward_low = []
    for level_id in range(LEVELS):
        rhs_level = rhs_local[level_id * per_col : (level_id + 1) * per_col]
        inverse_level = inverse_local[level_id * per_col : (level_id + 1) * per_col]
        if level_id > 0:
            panel = masked[level_id * per_row : (level_id + 1) * per_row, : level_id * per_col]
            earlier = jnp.concatenate(forward_low, axis=0)
            partial_sum = jnp.einsum(
                "abpq,bqs->aps", panel, earlier, preferred_element_type=jnp.float32
            )
            row_total = lax.psum(partial_sum, "col")
            row_total = row_total.reshape((per_col, groups) + row_total.shape[1:])
            own_total = lax.dynamic_index_in_dim(
                row_total, my_col // row_count, axis=1, keepdims=False
            )
            solved = jnp.einsum(
                "mpq,mqs->mps",
                inverse_level,
                rhs_level - own_total,
                precision=lax.Precision.HIGHEST,
            )
            solved = spread(solved, "row", my_col % row_count)
        else:
            solved = jnp.einsum(
                "mpq,mqs->mps", inverse_level, rhs_level, precision=lax.Precision.HIGHEST
            )
        forward_vals.append(solved)
        forward_low.append(solved.astype(jnp.bfloat16))
    solution_parts = [None] * LEVELS
    later = []
    for level_id in reversed(range(LEVELS)):
        inverse_level = inverse_local[level_id * per_col : (level_id + 1) * per_col]
        resid = forward_vals[level_id]
        if level_id < LEVELS - 1:
            panel = masked[
                (level_id + 1) * per_row :, level_id * per_col : (level_id + 1) * per_col
            ]
            after = jnp.concatenate(later, axis=0)
            partial_sum = jnp.einsum(
                "abpq,aps->bqs", panel, after, preferred_element_type=jnp.float32
            )
            resid = resid - lax.psum(partial_sum, "row")
        solved = jnp.einsum("mqp,mqs->mps", inverse_level, resid, precision=lax.Precision.HIGHEST)
        solution_parts[level_id] = solved
        if level_id > 0:
            low_solved = solved.astype(jnp.bfloat16)
            pieces = lax.all_gather(low_solved[None], "col", axis=0, tiled=True)
            pieces = pieces.reshape((groups, row_count) + low_solved.shape)
            picked = lax.dynamic_index_in_dim(pieces, my_row, axis=1, keepdims=False)
            arranged = jnp.swapaxes(picked, 0, 1).reshape((per_row,) + low_solved.shape[1:])
            later = [arranged] + later
    solution = jnp.concatenate(solution_parts, axis=0)
    return solution[:, None]


def solution(mesh):
    in_specs = (
        P(None, "row", None, "col", None, None),
        P(None, "row", None, "col"),
        P(None, "col", None, None),
        P(None, "col", None, None),
    )
    out_specs = P(None, "col", None, None)
    return jax.shard_map(
        per_device, mesh=mesh, in_specs=in_specs, out_specs=out_specs, check_vma=False
    )
```

profile of v0, /device:TPU:2, one launch (start us, length us, event | category | flops | bytes accessed | tf_op | source)
XLA Modules:
  0.0 2246.1 jit_solution(3896068341786399089)
XLA Ops:
  8.5 7.4 bitcast_multiply_fusion
  15.9 1.9 fusion.36
  17.9 116.1 %all-reduce.22.cloned.1.call-done = f32[4,128,256]{2,1,0:T(8,128)} async-done(((f32[4,128,256]{2,1,0:T(8,128)}), f32[4,128,256]{2,1,0:T(8,128)}) %all-reduce.22.cloned.1.call-update) | async-done | bytes 524304 | tf_op jit(solution)/shard_map/psum | solution.py:36
  134.0 1.8 fusion.7
  135.9 72.4 %all-reduce.24.cloned.1.call-done = f32[1,128,256]{2,1,0:T(8,128)} async-done(((f32[1,128,256]{2,1,0:T(8,128)}), f32[1,128,256]{2,1,0:T(8,128)}) %all-reduce.24.cloned.1.call-update) | async-done | bytes 131088 | tf_op jit(solution)/shard_map/psum | solution.py:11
  209.3 2.0 convolution_bitcast_fusion.5
  211.3 111.8 %all-reduce.26.cloned.1.call-done = f32[4,128,256]{2,1,0:T(8,128)} async-done(((f32[4,128,256]{2,1,0:T(8,128)}), f32[4,128,256]{2,1,0:T(8,128)}) %all-reduce.26.cloned.1.call-update) | async-done | bytes 524304 | tf_op jit(solution)/shard_map/psum | solution.py:36
  323.1 1.8 fusion.6
  325.1 72.3 %all-reduce.28.cloned.1.call-done = f32[1,128,256]{2,1,0:T(8,128)} async-done(((f32[1,128,256]{2,1,0:T(8,128)}), f32[1,128,256]{2,1,0:T(8,128)}) %all-reduce.28.cloned.1.call-update) | async-done | bytes 131088 | tf_op jit(solution)/shard_map/psum | solution.py:11
  398.3 2.1 convolution_bitcast_fusion.4
  400.5 111.6 %all-reduce.30.cloned.1.call-done = f32[4,128,256]{2,1,0:T(8,128)} async-done(((f32[4,128,256]{2,1,0:T(8,128)}), f32[4,128,256]{2,1,0:T(8,128)}) %all-reduce.30.cloned.1.call-update) | async-done | bytes 524304 | tf_op jit(solution)/shard_map/psum | solution.py:36
  512.1 1.8 fusion.5
  514.0 72.3 %all-reduce.32.cloned.1.call-done = f32[1,128,256]{2,1,0:T(8,128)} async-done(((f32[1,128,256]{2,1,0:T(8,128)}), f32[1,128,256]{2,1,0:T(8,128)}) %all-reduce.32.cloned.1.call-update) | async-done | bytes 131088 | tf_op jit(solution)/shard_map/psum | solution.py:11
  587.3 2.1 convolution_bitcast_fusion.3
  589.5 111.6 %all-reduce.34.cloned.1.call-done = f32[4,128,256]{2,1,0:T(8,128)} async-done(((f32[4,128,256]{2,1,0:T(8,128)}), f32[4,128,256]{2,1,0:T(8,128)}) %all-reduce.34.cloned.1.call-update) | async-done | bytes 524304 | tf_op jit(solution)/shard_map/psum | solution.py:36
  701.1 1.8 fusion.4
  703.1 72.4 %all-reduce.36.cloned.1.call-done = f32[1,128,256]{2,1,0:T(8,128)} async-done(((f32[1,128,256]{2,1,0:T(8,128)}), f32[1,128,256]{2,1,0:T(8,128)}) %all-reduce.36.cloned.1.call-update) | async-done | bytes 131088 | tf_op jit(solution)/shard_map/psum | solution.py:11
  776.4 2.3 convolution_bitcast_fusion.2
  778.8 111.6 %all-reduce.38.cloned.1.call-done = f32[4,128,256]{2,1,0:T(8,128)} async-done(((f32[4,128,256]{2,1,0:T(8,128)}), f32[4,128,256]{2,1,0:T(8,128)}) %all-reduce.38.cloned.1.call-update) | async-done | bytes 524304 | tf_op jit(solution)/shard_map/psum | solution.py:36
  890.4 1.8 fusion.3
  892.3 72.3 %all-reduce.40.cloned.1.call-done = f32[1,128,256]{2,1,0:T(8,128)} async-done(((f32[1,128,256]{2,1,0:T(8,128)}), f32[1,128,256]{2,1,0:T(8,128)}) %all-reduce.40.cloned.1.call-update) | async-done | bytes 131088 | tf_op jit(solution)/shard_map/psum | solution.py:11
  965.6 2.3 convolution_bitcast_fusion.1
  967.9 111.7 %all-reduce.42.cloned.1.call-done = f32[4,128,256]{2,1,0:T(8,128)} async-done(((f32[4,128,256]{2,1,0:T(8,128)}), f32[4,128,256]{2,1,0:T(8,128)}) %all-reduce.42.cloned.1.call-update) | async-done | bytes 524304 | tf_op jit(solution)/shard_map/psum | solution.py:36
  1079.6 1.8 fusion.2
  1081.5 72.3 %all-reduce.44.cloned.1.call-done = f32[1,128,256]{2,1,0:T(8,128)} async-done(((f32[1,128,256]{2,1,0:T(8,128)}), f32[1,128,256]{2,1,0:T(8,128)}) %all-reduce.44.cloned.1.call-update) | async-done | bytes 131088 | tf_op jit(solution)/shard_map/psum | solution.py:11
  1154.8 2.4 convolution_bitcast_fusion
  1157.2 111.7 %all-reduce.46.cloned.1.call-done = f32[4,128,256]{2,1,0:T(8,128)} async-done(((f32[4,128,256]{2,1,0:T(8,128)}), f32[4,128,256]{2,1,0:T(8,128)}) %all-reduce.46.cloned.1.call-update) | async-done | bytes 524304 | tf_op jit(solution)/shard_map/psum | solution.py:36
  1268.9 1.8 fusion.1
  1270.8 72.3 %all-reduce.48.cloned.1.call-done = f32[128,256]{1,0:T(8,128)} async-done(((f32[128,256]{1,0:T(8,128)}), f32[128,256]{1,0:T(8,128)}) %all-reduce.48.cloned.1.call-update) | async-done | bytes 131088 | tf_op jit(solution)/shard_map/psum | solution.py:11
  1343.2 1.9 bitcast_convert_fusion.6
  1345.2 48.3 %all-gather.15.cloned.1.call-done = bf16[4096,256]{0,1:T(8,128)(2,1)} async-done(((bf16[128,256]{0,1:T(8,128)(2,1)}), bf16[4096,256]{0,1:T(8,128)(2,1)}) %all-gather.15.cloned.1.call-update) | async-done | bytes 2097168 | tf_op jit(solution)/shard_map/all_gather | solution.py:72
  1393.4 2.1 copy.59
  1396.6 1.8 convolution_bitcast_fusion.9
  1398.4 71.8 %all-reduce.50.cloned.1.call-done = f32[1,128,256]{2,1,0:T(8,128)} async-done(((f32[1,128,256]{2,1,0:T(8,128)}), f32[1,128,256]{2,1,0:T(8,128)}) %all-reduce.50.cloned.1.call-update) | async-done | bytes 131088 | tf_op jit(solution)/shard_map/psum | solution.py:67
  1470.2 1.9 bitcast_convert_fusion.5
  1472.2 48.6 %all-gather.17.cloned.1.call-done = bf16[4096,256]{0,1:T(8,128)(2,1)} async-done(((bf16[128,256]{0,1:T(8,128)(2,1)}), bf16[4096,256]{0,1:T(8,128)(2,1)}) %all-gather.17.cloned.1.call-update) | async-done | bytes 2097168 | tf_op jit(solution)/shard_map/all_gather | solution.py:72
  1520.8 2.1 copy.60
  1523.9 1.9 convolution_bitcast_fusion.8
  1525.9 71.8 %all-reduce.52.cloned.1.call-done = f32[1,128,256]{2,1,0:T(8,128)} async-done(((f32[1,128,256]{2,1,0:T(8,128)}), f32[1,128,256]{2,1,0:T(8,128)}) %all-reduce.52.cloned.1.call-update) | async-done | bytes 131088 | tf_op jit(solution)/shard_map/psum | solution.py:67
  1597.6 1.9 bitcast_convert_fusion.4
  1599.6 48.4 %all-gather.19.cloned.1.call-done = bf16[4096,256]{0,1:T(8,128)(2,1)} async-done(((bf16[128,256]{0,1:T(8,128)(2,1)}), bf16[4096,256]{0,1:T(8,128)(2,1)}) %all-gather.19.cloned.1.call-update) | async-done | bytes 2097168 | tf_op jit(solution)/shard_map/all_gather | solution.py:72
  1648.1 2.1 copy.61
  1651.2 2.0 convolution_bitcast_fusion.11
  1653.2 71.8 %all-reduce.54.cloned.1.call-done = f32[1,128,256]{2,1,0:T(8,128)} async-done(((f32[1,128,256]{2,1,0:T(8,128)}), f32[1,128,256]{2,1,0:T(8,128)}) %all-reduce.54.cloned.1.call-update) | async-done | bytes 131088 | tf_op jit(solution)/shard_map/psum | solution.py:67
  1725.0 1.9 bitcast_convert_fusion.3
  1727.2 48.6 %all-gather.21.cloned.1.call-done = bf16[4096,256]{0,1:T(8,128)(2,1)} async-done(((bf16[128,256]{0,1:T(8,128)(2,1)}), bf16[4096,256]{0,1:T(8,128)(2,1)}) %all-gather.21.cloned.1.call-update) | async-done | bytes 2097168 | tf_op jit(solution)/shard_map/all_gather | solution.py:72
  1775.8 2.1 copy.62
  1778.9 2.1 convolution_bitcast_fusion.13
  1781.1 71.8 %all-reduce.56.cloned.1.call-done = f32[1,128,256]{2,1,0:T(8,128)} async-done(((f32[1,128,256]{2,1,0:T(8,128)}), f32[1,128,256]{2,1,0:T(8,128)}) %all-reduce.56.cloned.1.call-update) | async-done | bytes 131088 | tf_op jit(solution)/shard_map/psum | solution.py:67
  1852.8 2.0 bitcast_convert_fusion.2
  1854.9 48.4 %all-gather.23.cloned.1.call-done = bf16[4096,256]{0,1:T(8,128)(2,1)} async-done(((bf16[128,256]{0,1:T(8,128)(2,1)}), bf16[4096,256]{0,1:T(8,128)(2,1)}) %all-gather.23.cloned.1.call-update) | async-done | bytes 2097168 | tf_op jit(solution)/shard_map/all_gather | solution.py:72
  1903.3 2.1 copy.63
  1906.5 2.1 convolution_bitcast_fusion.12
  1908.8 71.8 %all-reduce.58.cloned.1.call-done = f32[1,128,256]{2,1,0:T(8,128)} async-done(((f32[1,128,256]{2,1,0:T(8,128)}), f32[1,128,256]{2,1,0:T(8,128)}) %all-reduce.58.cloned.1.call-update) | async-done | bytes 131088 | tf_op jit(solution)/shard_map/psum | solution.py:67
  1980.5 2.0 bitcast_convert_fusion.1
  1982.6 48.7 %all-gather.25.cloned.1.call-done = bf16[4096,256]{0,1:T(8,128)(2,1)} async-done(((bf16[128,256]{0,1:T(8,128)(2,1)}), bf16[4096,256]{0,1:T(8,128)(2,1)}) %all-gather.25.cloned.1.call-update) | async-done | bytes 2097168 | tf_op jit(solution)/shard_map/all_gather | solution.py:72
  2031.3 2.1 copy.64
  2034.5 2.2 convolution_bitcast_fusion.7
  2036.8 71.8 %all-reduce.60.cloned.1.call-done = f32[1,128,256]{2,1,0:T(8,128)} async-done(((f32[1,128,256]{2,1,0:T(8,128)}), f32[1,128,256]{2,1,0:T(8,128)}) %all-reduce.60.cloned.1.call-update) | async-done | bytes 131088 | tf_op jit(solution)/shard_map/psum | solution.py:67
  2108.6 2.0 bitcast_convert_fusion
  2110.7 48.2 %all-gather.27.cloned.1.call-done = bf16[4096,256]{0,1:T(8,128)(2,1)} async-done(((bf16[128,256]{0,1:T(8,128)(2,1)}), bf16[4096,256]{0,1:T(8,128)(2,1)}) %all-gather.27.cloned.1.call-update) | async-done | bytes 2097168 | tf_op jit(solution)/shard_map/all_gather | solution.py:72
  2158.9 2.1 copy.65
  2162.2 2.4 convolution_bitcast_fusion.6
  2164.6 71.8 %all-reduce.62.cloned.1.call-done = f32[1,128,256]{2,1,0:T(8,128)} async-done(((f32[1,128,256]{2,1,0:T(8,128)}), f32[1,128,256]{2,1,0:T(8,128)}) %all-reduce.62.cloned.1.call-update) | async-done | bytes 131088 | tf_op jit(solution)/shard_map/psum | solution.py:67
  (133 shorter events, 19.5 us)
Async XLA Ops:
  6.5 127.4 %all-reduce.22.cloned.1.call-start = ((), (), s32[]{:S(2)}) async-start(), calls=%async_computation | async-start | bytes 1048576 | tf_op jit(solution)/shard_map/psum | solution.py:36
  8.4 125.5 %copy-start = (f32[8,1,128,128]{3,2,1,0:T(8,128)S(1)}, f32[8,1,128,128]{3,2,1,0:T(8,128)}, u32[]{:S(2)}) copy-start(f32[8,1,128,128]{3,2,1,0:T(8,128)} %param.7) | copy-start | bytes 1572868
  8.5 125.5 %copy-start.1 = (f32[8,1,128,256]{3,2,1,0:T(8,128)S(1)}, f32[8,1,128,256]{3,2,1,0:T(8,128)}, u32[]{:S(2)}) copy-start(f32[8,1,128,256]{3,2,1,0:T(8,128)} %param.6) | copy-start | bytes 3145732
  17.8 190.6 %all-reduce.24.cloned.1.call-start = ((), (), s32[]{:S(2)}) async-start(), calls=%async_computation.1 | async-start | bytes 262144 | tf_op jit(solution)/shard_map/psum | solution.py:11
  135.8 187.3 %all-reduce.26.cloned.1.call-start = ((), (), s32[]{:S(2)}) async-start(), calls=%async_computation.2 | async-start | bytes 1048576 | tf_op jit(solution)/shard_map/psum | solution.py:36
  211.3 186.1 %all-reduce.28.cloned.1.call-start = ((), (), s32[]{:S(2)}) async-start(), calls=%async_computation.3 | async-start | bytes 262144 | tf_op jit(solution)/shard_map/psum | solution.py:11
  325.0 187.1 %all-reduce.30.cloned.1.call-start = ((), (), s32[]{:S(2)}) async-start(), calls=%async_computation.4 | async-start | bytes 1048576 | tf_op jit(solution)/shard_map/psum | solution.py:36
  400.4 185.9 %all-reduce.32.cloned.1.call-start = ((), (), s32[]{:S(2)}) async-start(), calls=%async_computation.5 | async-start | bytes 262144 | tf_op jit(solution)/shard_map/psum | solution.py:11
  514.0 187.1 %all-reduce.34.cloned.1.call-start = ((), (), s32[]{:S(2)}) async-start(), calls=%async_computation.6 | async-start | bytes 1048576 | tf_op jit(solution)/shard_map/psum | solution.py:36
  589.4 186.1 %all-reduce.36.cloned.1.call-start = ((), (), s32[]{:S(2)}) async-start(), calls=%async_computation.7 | async-start | bytes 262144 | tf_op jit(solution)/shard_map/psum | solution.py:11
  703.0 187.4 %all-reduce.38.cloned.1.call-start = ((), (), s32[]{:S(2)}) async-start(), calls=%async_computation.8 | async-start | bytes 1048576 | tf_op jit(solution)/shard_map/psum | solution.py:36
  778.7 185.9 %all-reduce.40.cloned.1.call-start = ((), (), s32[]{:S(2)}) async-start(), calls=%async_computation.9 | async-start | bytes 262144 | tf_op jit(solution)/shard_map/psum | solution.py:11
  892.3 187.3 %all-reduce.42.cloned.1.call-start = ((), (), s32[]{:S(2)}) async-start(), calls=%async_computation.10 | async-start | bytes 1048576 | tf_op jit(solution)/shard_map/psum | solution.py:36
  967.9 186.0 %all-reduce.44.cloned.1.call-start = ((), (), s32[]{:S(2)}) async-start(), calls=%async_computation.11 | async-start | bytes 262144 | tf_op jit(solution)/shard_map/psum | solution.py:11
  1081.5 187.4 %all-reduce.46.cloned.1.call-start = ((), (), s32[]{:S(2)}) async-start(), calls=%async_computation.12 | async-start | bytes 1048576 | tf_op jit(solution)/shard_map/psum | solution.py:36
  1157.2 186.0 %all-reduce.48.cloned.1.call-start = ((), (), s32[]{:S(2)}) async-start(), calls=%async_computation.13 | async-start | bytes 262144 | tf_op jit(solution)/shard_map/psum | solution.py:11
  1270.8 122.7 %all-gather.15.cloned.1.call-start = ((), (), s32[]{:S(2)}) async-start(), calls=%async_computation.21 | async-start | bytes 2162688 | tf_op jit(solution)/shard_map/all_gather | solution.py:72
  1345.1 125.1 %all-reduce.50.cloned.1.call-start = ((), (), s32[]{:S(2)}) async-start(), calls=%async_computation.14 | async-start | bytes 262144 | tf_op jit(solution)/shard_map/psum | solution.py:67
  1395.5 74.7 %copy-start.9 = (f32[1,128,256]{2,1,0:T(8,128)S(1)}, f32[1,128,256]{2,1,0:T(8,128)}, u32[]{:S(2)}) copy-start(f32[1,128,256]{2,1,0:T(8,128)} %all-reduce.44.cloned.1.call-done) | copy-start | bytes 393220
  1398.4 122.4 %all-gather.17.cloned.1.call-start = ((), (), s32[]{:S(2)}) async-start(), calls=%async_computation.22 | async-start | bytes 2162688 | tf_op jit(solution)/shard_map/all_gather | solution.py:72
  1472.1 125.5 %all-reduce.52.cloned.1.call-start = ((), (), s32[]{:S(2)}) async-start(), calls=%async_computation.15 | async-start | bytes 262144 | tf_op jit(solution)/shard_map/psum | solution.py:67
  1522.9 74.8 %copy-start.6 = (f32[1,128,256]{2,1,0:T(8,128)S(1)}, f32[1,128,256]{2,1,0:T(8,128)}, u32[]{:S(2)}) copy-start(f32[1,128,256]{2,1,0:T(8,128)} %all-reduce.40.cloned.1.call-done) | copy-start | bytes 393220
  1525.8 122.3 %all-gather.19.cloned.1.call-start = ((), (), s32[]{:S(2)}) async-start(), calls=%async_computation.23 | async-start | bytes 2162688 | tf_op jit(solution)/shard_map/all_gather | solution.py:72
  1599.6 125.4 %all-reduce.54.cloned.1.call-start = ((), (), s32[]{:S(2)}) async-start(), calls=%async_computation.16 | async-start | bytes 262144 | tf_op jit(solution)/shard_map/psum | solution.py:67
  1650.7 74.3 %copy-start.5 = (f32[1,128,256]{2,1,0:T(8,128)S(1)}, f32[1,128,256]{2,1,0:T(8,128)}, u32[]{:S(2)}) copy-start(f32[1,128,256]{2,1,0:T(8,128)} %all-reduce.36.cloned.1.call-done) | copy-start | bytes 393220
  1653.2 122.6 %all-gather.21.cloned.1.call-start = ((), (), s32[]{:S(2)}) async-start(), calls=%async_computation.24 | async-start | bytes 2162688 | tf_op jit(solution)/shard_map/all_gather | solution.py:72
  1727.0 125.9 %all-reduce.56.cloned.1.call-start = ((), (), s32[]{:S(2)}) async-start(), calls=%async_computation.17 | async-start | bytes 262144 | tf_op jit(solution)/shard_map/psum | solution.py:67
  1778.9 74.0 %copy-start.4 = (f32[1,128,256]{2,1,0:T(8,128)S(1)}, f32[1,128,256]{2,1,0:T(8,128)}, u32[]{:S(2)}) copy-start(f32[1,128,256]{2,1,0:T(8,128)} %all-reduce.32.cloned.1.call-done) | copy-start | bytes 393220
  1781.0 122.3 %all-gather.23.cloned.1.call-start = ((), (), s32[]{:S(2)}) async-start(), calls=%async_computation.25 | async-start | bytes 2162688 | tf_op jit(solution)/shard_map/all_gather | solution.py:72
  1854.8 125.7 %all-reduce.58.cloned.1.call-start = ((), (), s32[]{:S(2)}) async-start(), calls=%async_computation.18 | async-start | bytes 262144 | tf_op jit(solution)/shard_map/psum | solution.py:67
  1906.5 74.1 %copy-start.3 = (f32[1,128,256]{2,1,0:T(8,128)S(1)}, f32[1,128,256]{2,1,0:T(8,128)}, u32[]{:S(2)}) copy-start(f32[1,128,256]{2,1,0:T(8,128)} %all-reduce.28.cloned.1.call-done) | copy-start | bytes 393220
  1908.7 122.6 %all-gather.25.cloned.1.call-start = ((), (), s32[]{:S(2)}) async-start(), calls=%async_computation.26 | async-start | bytes 2162688 | tf_op jit(solution)/shard_map/all_gather | solution.py:72
  1982.5 126.1 %all-reduce.60.cloned.1.call-start = ((), (), s32[]{:S(2)}) async-start(), calls=%async_computation.19 | async-start | bytes 262144 | tf_op jit(solution)/shard_map/psum | solution.py:67
  2034.5 74.1 %copy-start.2 = (f32[1,128,256]{2,1,0:T(8,128)S(1)}, f32[1,128,256]{2,1,0:T(8,128)}, u32[]{:S(2)}) copy-start(f32[1,128,256]{2,1,0:T(8,128)} %all-reduce.24.cloned.1.call-done) | copy-start | bytes 393220
  2036.8 122.1 %all-gather.27.cloned.1.call-start = ((), (), s32[]{:S(2)}) async-start(), calls=%async_computation.27 | async-start | bytes 2162688 | tf_op jit(solution)/shard_map/all_gather | solution.py:72
  2110.6 125.8 %all-reduce.62.cloned.1.call-start = ((), (), s32[]{:S(2)}) async-start(), calls=%async_computation.20 | async-start | bytes 262144 | tf_op jit(solution)/shard_map/psum | solution.py:67
  2162.2 75.5 %copy-start.10 = (f32[256,128]{1,0:T(8,128)S(1)}, f32[256,128]{1,0:T(8,128)}, u32[]{:S(2)}) copy-start(f32[256,128]{1,0:T(8,128)} %get-tuple-element.39) | copy-start | bytes 393220
  2162.2 75.6 %copy-start.8 = (f32[256,128]{1,0:T(8,128)S(1)}, f32[256,128]{1,0:T(8,128)}, u32[]{:S(2)}) copy-start(f32[256,128]{1,0:T(8,128)} %get-tuple-element.37) | copy-start | bytes 393220
  2162.2 75.6 %copy-start.7 = (f32[256,128]{1,0:T(8,128)S(1)}, f32[256,128]{1,0:T(8,128)}, u32[]{:S(2)}) copy-start(f32[256,128]{1,0:T(8,128)} %get-tuple-element.35) | copy-start | bytes 393220
Sparse Core Ops, SparseCore 0:
  17.9 116.0 all-reduce.21
  136.4 71.9 all-reduce.23
  211.6 111.5 all-reduce.25
  325.4 71.9 all-reduce.27
  400.5 111.5 all-reduce.29
  514.4 71.9 all-reduce.31
  589.5 111.5 all-reduce.33
  703.5 71.9 all-reduce.35
  778.8 111.5 all-reduce.37
  892.7 71.9 all-reduce.39
  968.0 111.5 all-reduce.41
  1081.9 71.9 all-reduce.43
  1157.3 111.5 all-reduce.45
  1271.2 71.9 all-reduce.47
  1345.5 47.9 all-gather.14
  1398.5 71.6 all-reduce.49
  1472.8 47.9 all-gather.16
  1525.9 71.6 all-reduce.51
  1600.1 47.9 all-gather.18
  1653.3 71.6 all-reduce.53
  1727.8 47.9 all-gather.20
  1781.1 71.6 all-reduce.55
  1855.3 47.9 all-gather.22
  1908.8 71.6 all-reduce.57
  1983.3 47.9 all-gather.24
  2036.9 71.6 all-reduce.59
  2110.9 47.9 all-gather.26
  2164.7 71.6 all-reduce.61
where the time goes:
time: 2250 us
  waiting for transfers between devices  2130 us (95%)
  matrix products  58.4 us (3%)
  local copies, waits for them, and re-layouts  23.5 us (1%)
    psum x7, waiting for transfers between devices, per_device(): row_total = lax.psum(partial_sum, 'col')  786 us
    psum x7, waiting for transfers between devices, spread(): return lax.psum(kept, axis)  507 us
    psum x7, waiting for transfers between devices, per_device(): resid = resid - lax.psum(partial_sum, 'row')  502 us
    all_gather x7, waiting for transfers between devices, per_device(): pieces = lax.all_gather(low_solved[None], 'col', axis=0, tiled=True)  339 us
  transfers between devices with their start and end apart: 28, of which 28 were waited for; matrix products, arithmetic and copies ran while one was open for 0% of the time, Pallas kernels for 0%

commit v1 on v0

v1 whole, which is shorter than its diff:
```python
import jax
import jax.numpy as jnp
from jax import lax
from jax.sharding import Mesh
from jax.sharding import PartitionSpec as P

LEVELS = 8
NATIVE = 4
PER_ROW = 4
SUB = 8
BF16 = jnp.bfloat16
F32 = jnp.float32
HIGHEST = lax.Precision.HIGHEST
COL = ("grp", "sub")


def exchange(pieces, axis):
    return lax.all_to_all(pieces, axis, 0, 0, tiled=True)


def spread(piece, axis, count):
    return exchange(jnp.broadcast_to(piece[None], (count,) + piece.shape), axis)


def per_device(factor, pattern, loads, block_inverse):
    my_row = lax.axis_index("row")
    n_row = lax.axis_size("row")
    n_col = lax.axis_size("grp") * lax.axis_size("sub")
    scen = loads.shape[3]
    part = scen // n_row
    inverse = block_inverse[:, 0]
    loads_t = jnp.swapaxes(loads[:, 0], 1, 2)
    panels = [None]
    for t in range(1, LEVELS):
        rows = slice(t * PER_ROW, (t + 1) * PER_ROW)
        mask = pattern[rows, 0, :t, 0].astype(BF16)[:, :, None, None]
        panels.append(factor[rows, 0, :t, 0] * mask)
    full = [None] * LEVELS
    for t in range(NATIVE + 1, LEVELS):
        full[t] = lax.all_gather(panels[t], "row", axis=0)
    early = lax.all_gather(jnp.concatenate(panels[1 : NATIVE + 1], axis=1), "row", axis=0)
    at = 0
    for t in range(1, NATIVE + 1):
        full[t] = early[:, :, at : at + t]
        at += t

    def forward_solve(level, resid):
        return lax.dot_general(
            resid, inverse[level], (((1,), (1,)), ((), ())), precision=HIGHEST
        )

    def backward_solve(level, resid):
        return lax.dot_general(
            resid, inverse[level], (((1,), (0,)), ((), ())), precision=HIGHEST
        )

    solved = [forward_solve(0, loads_t[0])]
    low = [solved[0].astype(BF16)]
    for t in range(1, NATIVE + 1):
        sums = sum(
            jnp.einsum("sq,apq->asp", low[m], panels[t][:, m], preferred_element_type=F32)
            for m in range(t)
        )
        pieces = sums.astype(BF16).reshape(n_col, part, -1)
        total = jnp.sum(exchange(pieces, COL).astype(F32), axis=0).astype(BF16)
        total = exchange(spread(total, "row", n_row), "sub")
        total = total.reshape(scen, -1).astype(F32)
        solved.append(forward_solve(t, loads_t[t] - total))
        low.append(solved[t].astype(BF16))

    def own(value):
        return lax.dynamic_slice_in_dim(value, my_row * part, part, axis=0)

    solved = [own(v) for v in solved]
    low = [own(v) for v in low]
    for t in range(NATIVE + 1, LEVELS):
        sums = sum(
            jnp.einsum("sq,rapq->arsp", low[m], full[t][:, :, m], preferred_element_type=F32)
            for m in range(t)
        )
        pieces = sums.astype(BF16).reshape(n_col, part, -1)
        total = jnp.sum(exchange(pieces, COL).astype(F32), axis=0)
        solved.append(forward_solve(t, own(loads_t[t]) - total))
        low.append(solved[t].astype(BF16))

    out = [None] * LEVELS
    after = [None] * LEVELS
    out[LEVELS - 1] = backward_solve(LEVELS - 1, solved[LEVELS - 1])
    for j in reversed(range(LEVELS - 1)):
        spread_low = spread(out[j + 1].astype(BF16), COL, n_col)
        after[j + 1] = spread_low.reshape(PER_ROW, n_row, part, -1)
        total = sum(
            jnp.einsum(
                "arsp,rapq->sq", after[t], full[t][:, :, j], preferred_element_type=F32
            )
            for t in range(j + 1, LEVELS)
        )
        out[j] = backward_solve(j, solved[j] - total)
    both = spread(jnp.stack(out), "row", n_row)
    both = jnp.transpose(both, (1, 3, 0, 2)).reshape(LEVELS, 1, -1, scen)
    return both


def solution(mesh):
    n_col = mesh.shape["col"]
    n_row = mesh.shape["row"]
    split = Mesh(
        mesh.devices.reshape(n_row, n_col // SUB, SUB), ("row", "grp", "sub")
    )
    in_specs = (
        P(None, "row", None, COL, None, None),
        P(None, "row", None, COL),
        P(None, COL, None, None),
        P(None, COL, None, None),
    )
    return jax.shard_map(
        per_device, mesh=split, in_specs=in_specs, out_specs=P(None, COL, None, None), check_vma=False
    )
```

time: 2250 us -> 466 us (0.21)
  waiting for transfers between devices: 2130 us -> 101 us
  blocking collectives: 0 us -> 169 us
  starting transfers between devices: 1.32 us -> 58.2 us
    psum x21 -> x0, waiting for transfers between devices: 1800 us -> none  [the longest x7 786 us: per_device(): row_total = lax.psum(partial_sum, 'col')]
    all_gather x7 -> x4, waiting for transfers between devices: 339 us -> 48.2 us  [the longest x1 29.3 us: per_device(): lax.all_gather(jnp.concatenate(panels[1:NATIVE + 1], axis=1), 'row', axis=0)]
    all_to_all x0 -> x11, blocking collectives: none -> 169 us  [exchange(): return lax.all_to_all(pieces, axis, 0, 0, tiled=True)]
    all_to_all x0 -> x12, starting transfers between devices: none -> 58.1 us  [exchange(): return lax.all_to_all(pieces, axis, 0, 0, tiled=True)]
    all_to_all x0 -> x12, waiting for transfers between devices: none -> 52.8 us  [exchange(): return lax.all_to_all(pieces, axis, 0, 0, tiled=True)]
    dot_general x30 -> x72, matrix products: 58.4 us -> 68.6 us  [the longest x18 30.5 us: per_device(): jnp.einsum('sq,rapq->arsp', low[m], full[t][:, :, m], preferred_element_t...]
  transfers between devices with their start and end apart: 28 -> 16, of which waited for: 28 -> 13; matrix products, arithmetic and copies ran while one was open for 0% -> 21% of each run, Pallas kernels for 0% -> 0%
where the time goes in v1:
time: 466 us; the launch traced here: 462 us
  blocking collectives  169 us (36%)
  waiting for transfers between devices  101 us (22%)
  matrix products  68.6 us (15%)
  starting transfers between devices  58.2 us (12%)
  local copies, waits for them, and re-layouts  37.1 us (8%)
  between operations  14.1 us (3%)
  other arithmetic  13.4 us (3%)
    all_to_all x11, blocking collectives, exchange(): return lax.all_to_all(pieces, axis, 0, 0, tiled=True)  169 us
    all_to_all x12, starting transfers between devices, exchange(): return lax.all_to_all(pieces, axis, 0, 0, tiled=True)  58.1 us
    all_to_all x12, waiting for transfers between devices, exchange(): return lax.all_to_all(pieces, axis, 0, 0, tiled=True)  52.8 us
    dot_general x18, matrix products, per_device(): jnp.einsum('sq,rapq->arsp', low[m], full[t][:, :, m], preferred_element_t...  30.5 us
    all_gather x1, waiting for transfers between devices, per_device(): lax.all_gather(jnp.concatenate(panels[1:NATIVE + 1], axis=1), 'row', axis=0)  29.3 us
    dot_general x28, matrix products, per_device(): jnp.einsum('arsp,rapq->sq', after[t], full[t][:, :, j], preferred_element...  23 us
    all_gather x3, waiting for transfers between devices, per_device(): full[t] = lax.all_gather(panels[t], 'row', axis=0)  19 us
    squeeze x3, local copies, waits for them, and re-layouts, per_device(): full[t][:, :, m]  17.5 us
  transfers between devices with their start and end apart: 16, of which 13 were waited for; matrix products, arithmetic and copies ran while one was open for 21% of the time, Pallas kernels for 0%

profile of v1, /device:TPU:2, one launch (start us, length us, event | category | flops | bytes accessed | tf_op | source)
XLA Modules:
  0.0 461.9 jit_solution(6783858555946395817)
XLA Ops:
  7.5 2.1 fusion.62
  10.0 2.2 fusion.61
  12.7 2.3 fusion.60
  24.9 15.1 %all_to_all.115 = bf16[32,32,128]{2,1,0:T(8,128)(2,1)S(1)} all-to-all(bf16[32,32,128]{2,1,0:T(8,128)(2,1)S(1)} %bitcast.647), channel_id=1, replica_groups=mesh['row'=8,'grp'=4,'sub'=8] {'grp','sub'}, dimensions={0} | all-to-all | bytes 524288 | tf_op jit(solution)/shard_map/all_to_all | solution.py:18
  40.1 17.7 %all_to_all.116 = bf16[8,32,128]{2,1,0:T(8,128)(2,1)} all-to-all(bf16[8,32,128]{2,1,0:T(8,128)(2,1)S(1)} %broadcast_in_dim.24), channel_id=1, replica_groups=mesh['row'=8,'grp'=4,'sub'=8] {'row'}, dimensions={0} | all-to-all | bytes 131072 | tf_op jit(solution)/shard_map/all_to_all | solution.py:18
  57.8 4.6 %all-to-all-start.2 = ((bf16[8,32,128]{2,1,0:T(8,128)(2,1)}), bf16[8,32,128]{2,1,0:T(8,128)(2,1)S(1)}, u32[]{:S(2)}, u32[]{:S(2)}) async-start(bf16[8,32,128]{2,1,0:T(8,128)(2,1)} %all_to_all.116), calls=%async_computation.2 | async-start | bytes 131072 | tf_op jit(solution)/shard_map/all_to_all | solution.py:18
  62.6 4.0 all-to-all-done.2
  69.6 12.2 %all_to_all.117 = bf16[32,32,128]{2,1,0:T(8,128)(2,1)S(1)} all-to-all(bf16[32,32,128]{2,1,0:T(8,128)(2,1)S(1)} %bitcast.648), channel_id=1, replica_groups=mesh['row'=8,'grp'=4,'sub'=8] {'grp','sub'}, dimensions={0} | all-to-all | bytes 524288 | tf_op jit(solution)/shard_map/all_to_all | solution.py:18
  82.4 4.0 all-to-all-start.4
  87.4 7.6 %all-to-all-done.4 = bf16[8,32,128]{2,1,0:T(8,128)(2,1)} async-done(((bf16[8,32,128]{2,1,0:T(8,128)(2,1)}), bf16[8,32,128]{2,1,0:T(8,128)(2,1)}, u32[]{:S(2)}, u32[]{:S(2)}) %all-to-all-start.4) | async-done | bytes 65568 | tf_op jit(solution)/shard_map/all_to_all | solution.py:18
  95.1 4.5 all-to-all-start.5
  100.9 2.9 all-to-all-done.5
  105.8 5.0 %all-to-all-start.6 = ((bf16[32,32,128]{2,1,0:T(8,128)(2,1)}), bf16[32,32,128]{2,1,0:T(8,128)(2,1)S(1)}, u32[]{:S(2)}, u32[]{:S(2)}) async-start(bf16[32,32,128]{2,1,0:T(8,128)(2,1)} %bitcast.30), calls=%async_computation.6 | async-start | bytes 524288 | tf_op jit(solution)/shard_map/all_to_all | solution.py:18
  111.0 7.6 %all-to-all-done.6 = bf16[32,32,128]{2,1,0:T(8,128)(2,1)S(1)} async-done(((bf16[32,32,128]{2,1,0:T(8,128)(2,1)}), bf16[32,32,128]{2,1,0:T(8,128)(2,1)S(1)}, u32[]{:S(2)}, u32[]{:S(2)}) %all-to-all-start.6) | async-done | bytes 262176 | tf_op jit(solution)/shard_map/all_to_all | solution.py:18
  119.2 4.0 all-to-all-start.7
  123.5 9.2 %all-to-all-done.7 = bf16[8,32,128]{2,1,0:T(8,128)(2,1)} async-done(((bf16[8,32,128]{2,1,0:T(8,128)(2,1)}), bf16[8,32,128]{2,1,0:T(8,128)(2,1)}, u32[]{:S(2)}, u32[]{:S(2)}) %all-to-all-start.7) | async-done | bytes 65568 | tf_op jit(solution)/shard_map/all_to_all | solution.py:18
  132.7 4.6 all-to-all-start.8
  137.5 4.0 all-to-all-done.8
  142.8 12.2 %all_to_all.118 = bf16[32,32,128]{2,1,0:T(8,128)(2,1)S(1)} all-to-all(bf16[32,32,128]{2,1,0:T(8,128)(2,1)S(1)} %bitcast.649), channel_id=1, replica_groups=mesh['row'=8,'grp'=4,'sub'=8] {'grp','sub'}, dimensions={0} | all-to-all | bytes 524288 | tf_op jit(solution)/shard_map/all_to_all | solution.py:18
  155.0 11.6 %all_to_all.119 = bf16[8,32,128]{2,1,0:T(8,128)(2,1)} all-to-all(bf16[8,32,128]{2,1,0:T(8,128)(2,1)S(1)} %broadcast_in_dim.27), channel_id=1, replica_groups=mesh['row'=8,'grp'=4,'sub'=8] {'row'}, dimensions={0} | all-to-all | bytes 131072 | tf_op jit(solution)/shard_map/all_to_all | solution.py:18
  166.7 4.6 all-to-all-start.11
  171.3 4.2 all-to-all-done.11
  175.8 1.7 fusion.163
  177.5 1.7 convolution_add_fusion.14
  179.2 1.7 convolution_add_fusion.13
  180.9 1.7 convolution_add_fusion.12
  182.6 1.7 fusion.12
  185.0 5.0 %all-to-all-start.12 = ((bf16[32,32,128]{2,1,0:T(8,128)(2,1)}), bf16[32,32,128]{2,1,0:T(8,128)(2,1)S(1)}, u32[]{:S(2)}, u32[]{:S(2)}) async-start(bf16[32,32,128]{2,1,0:T(8,128)(2,1)} %bitcast.65), calls=%async_computation.12 | async-start | bytes 524288 | tf_op jit(solution)/shard_map/all_to_all | solution.py:18
  190.1 7.8 %all-to-all-done.12 = bf16[32,32,128]{2,1,0:T(8,128)(2,1)S(1)} async-done(((bf16[32,32,128]{2,1,0:T(8,128)(2,1)}), bf16[32,32,128]{2,1,0:T(8,128)(2,1)S(1)}, u32[]{:S(2)}, u32[]{:S(2)}) %all-to-all-start.12) | async-done | bytes 262176 | tf_op jit(solution)/shard_map/all_to_all | solution.py:18
  198.1 1.7 fusion.161
  199.8 1.7 convolution_add_fusion.10
  201.5 1.7 convolution_add_fusion.9
  203.2 1.7 convolution_add_fusion.8
  204.9 1.7 convolution_add_fusion.7
  206.6 1.7 fusion.11
  208.3 12.4 %all_to_all.120 = bf16[32,32,128]{2,1,0:T(8,128)(2,1)S(1)} all-to-all(bf16[32,32,128]{2,1,0:T(8,128)(2,1)S(1)} %bitcast.650), channel_id=1, replica_groups=mesh['row'=8,'grp'=4,'sub'=8] {'grp','sub'}, dimensions={0} | all-to-all | bytes 524288 | tf_op jit(solution)/shard_map/all_to_all | solution.py:18
  221.0 18.9 %all-gather.10.cloned.1.call-done = bf16[8,4,7,128,128]{4,3,1,0,2:T(8,128)(2,1)} async-done(((bf16[1,4,7,128,128]{4,3,1,0,2:T(8,128)(2,1)}), bf16[8,4,7,128,128]{4,3,1,0,2:T(8,128)(2,1)}) %all-gather.10.cloned.1.call-update) | async-done | bytes 7340048 | tf_op jit(solution)/shard_map/all_gather | solution.py:40
  239.9 1.7 fusion.159
  241.6 1.7 convolution_add_fusion.5
  243.3 1.7 convolution_add_fusion.4
  245.0 1.7 convolution_add_fusion.3
  246.7 1.7 convolution_add_fusion.2
  248.4 1.7 convolution_add_fusion.1
  250.0 1.7 fusion.10
  251.8 14.9 %all_to_all.121 = bf16[32,32,128]{2,1,0:T(8,128)(2,1)S(1)} all-to-all(bf16[32,32,128]{2,1,0:T(8,128)(2,1)S(1)} %bitcast.651), channel_id=1, replica_groups=mesh['row'=8,'grp'=4,'sub'=8] {'grp','sub'}, dimensions={0} | all-to-all | bytes 524288 | tf_op jit(solution)/shard_map/all_to_all | solution.py:18
  267.8 5.0 %all-to-all-start.15 = ((bf16[32,32,128]{2,1,0:T(8,128)(2,1)}), bf16[32,32,128]{2,1,0:T(8,128)(2,1)S(1)}, u32[]{:S(2)}, u32[]{:S(2)}) async-start(bf16[32,32,128]{2,1,0:T(8,128)(2,1)} %broadcast_in_dim.28), calls=%async_computation.15 | async-start | bytes 524288 | tf_op jit(solution)/shard_map/all_to_all | solution.py:18
  272.8 6.8 %slice_bitcast_fusion.6 = (bf16[8,4,128,128]{3,2,1,0:T(8,128)(2,1)S(1)}, bf16[8,4,128,128]{3,2,1,0:T(8,128)(2,1)}, bf16[8,4,128,128]{3,2,1,0:T(8,128)(2,1)}, bf1...) fusion(bf16[8,4,7,128,128]{4,3,1,0,2:T(8,128)(2,1)} %all-gather, ...), kind=kLoop, calls=%fused_computation.100 | loop fusion | bytes 14680064 | tf_op jit(solution)/shard_map/squeeze | solution.py:78
  283.1 6.5 %all-to-all-start.16 = ((bf16[32,32,128]{2,1,0:T(8,128)(2,1)}), bf16[32,32,128]{2,1,0:T(8,128)(2,1)S(1)}, u32[]{:S(2)}, u32[]{:S(2)}) async-start(bf16[32,32,128]{2,1,0:T(8,128)(2,1)} %broadcast_in_dim.29), calls=%async_computation.16 | async-start | bytes 524288 | tf_op jit(solution)/shard_map/all_to_all | solution.py:18
  289.6 5.6 %slice_bitcast_fusion.12 = (bf16[8,4,128,128]{3,2,1,0:T(8,128)(2,1)}, bf16[8,4,128,128]{3,2,1,0:T(8,128)(2,1)}, bf16[8,4,128,128]{3,2,1,0:T(8,128)(2,1)}, bf16[8...) fusion(bf16[8,4,6,128,128]{4,3,1,0,2:T(8,128)(2,1)} %all-gather.8.cloned.1.call-done), kind=kLoop, calls=%fused_computation.106 | loop fusion | bytes 12582912 | tf_op jit(solution)/shard_map/squeeze | solution.py:78
  295.2 2.0 all-to-all-done.16
  301.2 5.3 %all-to-all-start.17 = ((bf16[32,32,128]{2,1,0:T(8,128)(2,1)}), bf16[32,32,128]{2,1,0:T(8,128)(2,1)S(1)}, u32[]{:S(2)}, u32[]{:S(2)}) async-start(bf16[32,32,128]{2,1,0:T(8,128)(2,1)} %broadcast_in_dim.30), calls=%async_computation.17 | async-start | bytes 524288 | tf_op jit(solution)/shard_map/all_to_all | solution.py:18
  306.6 5.0 %slice_bitcast_fusion.17 = (bf16[8,4,128,128]{3,2,1,0:T(8,128)(2,1)}, bf16[8,4,128,128]{3,2,1,0:T(8,128)(2,1)}, bf16[8,4,128,128]{3,2,1,0:T(8,128)(2,1)}, bf16[8...) fusion(bf16[8,4,5,128,128]{4,3,1,0,2:T(8,128)(2,1)} %all-gather.6.cloned.1.call-done), kind=kLoop, calls=%fused_computation.111 | loop fusion | bytes 10485760 | tf_op jit(solution)/shard_map/squeeze | solution.py:78
  311.6 2.6 all-to-all-done.17
  319.8 5.0 %all-to-all-start.18 = ((bf16[32,32,128]{2,1,0:T(8,128)(2,1)}), bf16[32,32,128]{2,1,0:T(8,128)(2,1)S(1)}, u32[]{:S(2)}, u32[]{:S(2)}) async-start(bf16[32,32,128]{2,1,0:T(8,128)(2,1)} %broadcast_in_dim.31), calls=%async_computation.18 | async-start | bytes 524288 | tf_op jit(solution)/shard_map/all_to_all | solution.py:18
  324.7 29.3 %all-gather.12.cloned.1.call-done = bf16[32,10,128,128]{3,2,0,1:T(8,128)(2,1)} async-done(((bf16[4,10,128,128]{3,2,0,1:T(8,128)(2,1)}), bf16[32,10,128,128]{3,2,0,1:T(8,128)(2,1)}) %all-gather.12.cloned.1.call-update) | async-done | bytes 10485776 | tf_op jit(solution)/shard_map/all_gather | solution.py:41
  354.0 7.7 %fusion.195 = (bf16[8,4,1,128,128]{4,3,1,0,2:T(8,128)(2,1)}, bf16[8,4,1,128,128]{4,3,1,0,2:T(8,128)(2,1)}, bf16[8,4,1,128,128]{4,3,1,0,2:T(8,128)(2,1)}, bf16[8,...) fusion(bf16[8,4,10,128,128]{4,3,1,0,2:T(8,128)(2,1)} %bitcast.625), kind=kLoop, calls=%fused_computation.311 | loop fusion | bytes 20971520 | tf_op jit(solution)/shard_map/slice | solution.py:94
  361.8 1.7 convolution_bitcast_fusion.22
  363.5 1.7 fusion.31
  365.2 1.6 fusion.30
  366.8 1.6 fusion.38
  369.5 14.9 %all_to_all.122 = bf16[32,32,128]{2,1,0:T(8,128)(2,1)S(1)} all-to-all(bf16[32,32,128]{2,1,0:T(8,128)(2,1)S(1)} %broadcast_in_dim.32), channel_id=1, replica_groups=mesh['row'=8,'grp'=4,'sub'=8] {'grp','sub'}, dimensions={0} | all-to-all | bytes 524288 | tf_op jit(solution)/shard_map/all_to_all | solution.py:18
  387.9 12.5 %all_to_all.123 = bf16[32,32,128]{2,1,0:T(8,128)(2,1)S(1)} all-to-all(bf16[32,32,128]{2,1,0:T(8,128)(2,1)S(1)} %broadcast_in_dim.33), channel_id=1, replica_groups=mesh['row'=8,'grp'=4,'sub'=8] {'grp','sub'}, dimensions={0} | all-to-all | bytes 524288 | tf_op jit(solution)/shard_map/all_to_all | solution.py:18
  404.0 12.5 %all_to_all.124 = bf16[32,32,128]{2,1,0:T(8,128)(2,1)S(1)} all-to-all(bf16[32,32,128]{2,1,0:T(8,128)(2,1)S(1)} %broadcast_in_dim.34), channel_id=1, replica_groups=mesh['row'=8,'grp'=4,'sub'=8] {'grp','sub'}, dimensions={0} | all-to-all | bytes 524288 | tf_op jit(solution)/shard_map/all_to_all | solution.py:18
  420.5 33.5 %all_to_all.125 = f32[8,8,32,128]{3,2,1,0:T(8,128)S(1)} all-to-all(f32[8,8,32,128]{3,2,1,0:T(8,128)S(1)} %broadcast_in_dim.35), channel_id=1, replica_groups=mesh['row'=8,'grp'=4,'sub'=8] {'row'}, dimensions={0} | all-to-all | bytes 2097152 | tf_op jit(solution)/shard_map/all_to_all | solution.py:18
  (157 shorter events, 51.4 us)
Async XLA Ops:
  6.5 169.2 %all-gather.6.cloned.1.call-start = ((), (), s32[]{:S(2)}) async-start(), calls=%async_computation.23 | async-start | bytes 5898240 | tf_op jit(solution)/shard_map/all_gather | solution.py:40
  9.7 188.4 %all-gather.8.cloned.1.call-start = ((), (), s32[]{:S(2)}) async-start(), calls=%async_computation.24 | async-start | bytes 7077888 | tf_op jit(solution)/shard_map/all_gather | solution.py:40
  12.3 10.3 %copy-start.16 = (f32[8,1,128,128]{3,2,1,0:T(8,128)S(1)}, f32[8,1,128,128]{3,2,1,0:T(8,128)}, u32[]{:S(2)}) copy-start(f32[8,1,128,128]{3,2,1,0:T(8,128)} %param.7) | copy-start | bytes 1572868
  12.3 227.6 %all-gather.10.cloned.1.call-start = ((), (), s32[]{:S(2)}) async-start(), calls=%async_computation.25 | async-start | bytes 8257536 | tf_op jit(solution)/shard_map/all_gather | solution.py:40
  15.0 339.0 %all-gather.12.cloned.1.call-start = ((), (), s32[]{:S(2)}) async-start(), calls=%async_computation.26 | async-start | bytes 11796480 | tf_op jit(solution)/shard_map/all_gather | solution.py:41
  57.8 8.8 %all-to-all-start.2 = ((bf16[8,32,128]{2,1,0:T(8,128)(2,1)}), bf16[8,32,128]{2,1,0:T(8,128)(2,1)S(1)}, u32[]{:S(2)}, u32[]{:S(2)}) async-start(bf16[8,32,128]{2,1,0:T(8,128)(2,1)} %all_to_all.116), calls=%async_computation.2 | async-start | bytes 131072 | tf_op jit(solution)/shard_map/all_to_all | solution.py:18
  82.4 12.6 %all-to-all-start.4 = ((bf16[8,32,128]{2,1,0:T(8,128)(2,1)}), bf16[8,32,128]{2,1,0:T(8,128)(2,1)}, u32[]{:S(2)}, u32[]{:S(2)}) async-start(bf16[8,32,128]{2,1,0:T(8,128)(2,1)} %broadcast_in_dim.25), calls=%async_computation.4 | async-start | bytes 131072 | tf_op jit(solution)/shard_map/all_to_all | solution.py:18
  95.1 8.7 %all-to-all-start.5 = ((bf16[8,32,128]{2,1,0:T(8,128)(2,1)}), bf16[8,32,128]{2,1,0:T(8,128)(2,1)S(1)}, u32[]{:S(2)}, u32[]{:S(2)}) async-start(bf16[8,32,128]{2,1,0:T(8,128)(2,1)} %all-to-all-done.4), calls=%async_computation.5 | async-start | bytes 131072 | tf_op jit(solution)/shard_map/all_to_all | solution.py:18
  105.8 12.8 %all-to-all-start.6 = ((bf16[32,32,128]{2,1,0:T(8,128)(2,1)}), bf16[32,32,128]{2,1,0:T(8,128)(2,1)S(1)}, u32[]{:S(2)}, u32[]{:S(2)}) async-start(bf16[32,32,128]{2,1,0:T(8,128)(2,1)} %bitcast.30), calls=%async_computation.6 | async-start | bytes 524288 | tf_op jit(solution)/shard_map/all_to_all | solution.py:18
  119.2 13.4 %all-to-all-start.7 = ((bf16[8,32,128]{2,1,0:T(8,128)(2,1)}), bf16[8,32,128]{2,1,0:T(8,128)(2,1)}, u32[]{:S(2)}, u32[]{:S(2)}) async-start(bf16[8,32,128]{2,1,0:T(8,128)(2,1)} %broadcast_in_dim.26), calls=%async_computation.7 | async-start | bytes 131072 | tf_op jit(solution)/shard_map/all_to_all | solution.py:18
  132.7 8.8 %all-to-all-start.8 = ((bf16[8,32,128]{2,1,0:T(8,128)(2,1)}), bf16[8,32,128]{2,1,0:T(8,128)(2,1)S(1)}, u32[]{:S(2)}, u32[]{:S(2)}) async-start(bf16[8,32,128]{2,1,0:T(8,128)(2,1)} %all-to-all-done.7), calls=%async_computation.8 | async-start | bytes 131072 | tf_op jit(solution)/shard_map/all_to_all | solution.py:18
  166.7 8.8 %all-to-all-start.11 = ((bf16[8,32,128]{2,1,0:T(8,128)(2,1)}), bf16[8,32,128]{2,1,0:T(8,128)(2,1)S(1)}, u32[]{:S(2)}, u32[]{:S(2)}) async-start(bf16[8,32,128]{2,1,0:T(8,128)(2,1)} %all_to_all.119), calls=%async_computation.11 | async-start | bytes 131072 | tf_op jit(solution)/shard_map/all_to_all | solution.py:18
  175.7 70.9 %copy-start.17 = (f32[256,128]{1,0:T(8,128)}, f32[256,128]{1,0:T(8,128)S(1)}, u32[]{:S(2)}) copy-start(f32[256,128]{1,0:T(8,128)S(1)} %fusion.68) | copy-start | bytes 393220
  185.0 12.8 %all-to-all-start.12 = ((bf16[32,32,128]{2,1,0:T(8,128)(2,1)}), bf16[32,32,128]{2,1,0:T(8,128)(2,1)S(1)}, u32[]{:S(2)}, u32[]{:S(2)}) async-start(bf16[32,32,128]{2,1,0:T(8,128)(2,1)} %bitcast.65), calls=%async_computation.12 | async-start | bytes 524288 | tf_op jit(solution)/shard_map/all_to_all | solution.py:18
  267.8 12.8 %all-to-all-start.15 = ((bf16[32,32,128]{2,1,0:T(8,128)(2,1)}), bf16[32,32,128]{2,1,0:T(8,128)(2,1)S(1)}, u32[]{:S(2)}, u32[]{:S(2)}) async-start(bf16[32,32,128]{2,1,0:T(8,128)(2,1)} %broadcast_in_dim.28), calls=%async_computation.15 | async-start | bytes 524288 | tf_op jit(solution)/shard_map/all_to_all | solution.py:18
  283.1 14.2 %all-to-all-start.16 = ((bf16[32,32,128]{2,1,0:T(8,128)(2,1)}), bf16[32,32,128]{2,1,0:T(8,128)(2,1)S(1)}, u32[]{:S(2)}, u32[]{:S(2)}) async-start(bf16[32,32,128]{2,1,0:T(8,128)(2,1)} %broadcast_in_dim.29), calls=%async_computation.16 | async-start | bytes 524288 | tf_op jit(solution)/shard_map/all_to_all | solution.py:18
  301.2 13.0 %all-to-all-start.17 = ((bf16[32,32,128]{2,1,0:T(8,128)(2,1)}), bf16[32,32,128]{2,1,0:T(8,128)(2,1)S(1)}, u32[]{:S(2)}, u32[]{:S(2)}) async-start(bf16[32,32,128]{2,1,0:T(8,128)(2,1)} %broadcast_in_dim.30), calls=%async_computation.17 | async-start | bytes 524288 | tf_op jit(solution)/shard_map/all_to_all | solution.py:18
  319.8 42.0 %all-to-all-start.18 = ((bf16[32,32,128]{2,1,0:T(8,128)(2,1)}), bf16[32,32,128]{2,1,0:T(8,128)(2,1)S(1)}, u32[]{:S(2)}, u32[]{:S(2)}) async-start(bf16[32,32,128]{2,1,0:T(8,128)(2,1)} %broadcast_in_dim.31), calls=%async_computation.18 | async-start | bytes 524288 | tf_op jit(solution)/shard_map/all_to_all | solution.py:18
  361.7 22.7 %copy-start.15 = (bf16[8,4,1,128,128]{4,3,1,0,2:T(8,128)(2,1)S(1)}, bf16[8,4,1,128,128]{4,3,1,0,2:T(8,128)(2,1)}, u32[]{:S(2)}) copy-start(bf16[8,4,1,128,128]{4,3,1,0,2:T(8,128)(2,1)} %get-tuple-element.13) | copy-start | bytes 3145732
  361.7 23.0 %copy-start.14 = (bf16[8,4,1,128,128]{4,3,1,0,2:T(8,128)(2,1)S(1)}, bf16[8,4,1,128,128]{4,3,1,0,2:T(8,128)(2,1)}, u32[]{:S(2)}) copy-start(bf16[8,4,1,128,128]{4,3,1,0,2:T(8,128)(2,1)} %get-tuple-element.12) | copy-start | bytes 3145732
  361.8 23.3 %copy-start.10 = (bf16[8,4,128,128]{3,2,1,0:T(8,128)(2,1)S(1)}, bf16[8,4,128,128]{3,2,1,0:T(8,128)(2,1)}, u32[]{:S(2)}) copy-start(bf16[8,4,128,128]{3,2,1,0:T(8,128)(2,1)} %get-tuple-element.31) | copy-start | bytes 3145732
  361.8 23.6 %copy-start.4 = (bf16[8,4,128,128]{3,2,1,0:T(8,128)(2,1)S(1)}, bf16[8,4,128,128]{3,2,1,0:T(8,128)(2,1)}, u32[]{:S(2)}) copy-start(bf16[8,4,128,128]{3,2,1,0:T(8,128)(2,1)} %get-tuple-element.26) | copy-start | bytes 3145732
  361.8 23.9 %copy-start = (bf16[8,4,128,128]{3,2,1,0:T(8,128)(2,1)S(1)}, bf16[8,4,128,128]{3,2,1,0:T(8,128)(2,1)}, u32[]{:S(2)}) copy-start(bf16[8,4,128,128]{3,2,1,0:T(8,128)(2,1)} %get-tuple-element.20) | copy-start | bytes 3145732
  363.4 37.0 %copy-start.13 = (bf16[8,4,1,128,128]{4,3,1,0,2:T(8,128)(2,1)S(1)}, bf16[8,4,1,128,128]{4,3,1,0,2:T(8,128)(2,1)}, u32[]{:S(2)}) copy-start(bf16[8,4,1,128,128]{4,3,1,0,2:T(8,128)(2,1)} %get-tuple-element.11) | copy-start | bytes 3145732
  365.1 35.5 %copy-start.12 = (bf16[8,4,1,128,128]{4,3,1,0,2:T(8,128)(2,1)S(1)}, bf16[8,4,1,128,128]{4,3,1,0,2:T(8,128)(2,1)}, u32[]{:S(2)}) copy-start(bf16[8,4,1,128,128]{4,3,1,0,2:T(8,128)(2,1)} %get-tuple-element.10) | copy-start | bytes 3145732
  366.8 34.2 %copy-start.11 = (bf16[8,4,1,128,128]{4,3,1,0,2:T(8,128)(2,1)S(1)}, bf16[8,4,1,128,128]{4,3,1,0,2:T(8,128)(2,1)}, u32[]{:S(2)}) copy-start(bf16[8,4,1,128,128]{4,3,1,0,2:T(8,128)(2,1)} %get-tuple-element.9) | copy-start | bytes 3145732
  368.4 32.9 %copy-start.5 = (bf16[8,4,128,128]{3,2,1,0:T(8,128)(2,1)S(1)}, bf16[8,4,128,128]{3,2,1,0:T(8,128)(2,1)}, u32[]{:S(2)}) copy-start(bf16[8,4,128,128]{3,2,1,0:T(8,128)(2,1)} %get-tuple-element.32) | copy-start | bytes 3145732
  384.4 17.2 %copy-start.3 = (bf16[8,4,128,128]{3,2,1,0:T(8,128)(2,1)S(1)}, bf16[8,4,128,128]{3,2,1,0:T(8,128)(2,1)}, u32[]{:S(2)}) copy-start(bf16[8,4,128,128]{3,2,1,0:T(8,128)(2,1)} %get-tuple-element.27) | copy-start | bytes 3145732
  385.3 31.1 %copy-start.9 = (bf16[8,4,1,128,128]{4,3,1,0,2:T(8,128)(2,1)S(1)}, bf16[8,4,1,128,128]{4,3,1,0,2:T(8,128)(2,1)}, u32[]{:S(2)}) copy-start(bf16[8,4,1,128,128]{4,3,1,0,2:T(8,128)(2,1)} %get-tuple-element.8) | copy-start | bytes 3145732
  385.6 31.1 %copy-start.8 = (bf16[8,4,1,128,128]{4,3,1,0,2:T(8,128)(2,1)S(1)}, bf16[8,4,1,128,128]{4,3,1,0,2:T(8,128)(2,1)}, u32[]{:S(2)}) copy-start(bf16[8,4,1,128,128]{4,3,1,0,2:T(8,128)(2,1)} %get-tuple-element.7) | copy-start | bytes 3145732
  386.8 30.3 %copy-start.7 = (bf16[8,4,1,128,128]{4,3,1,0,2:T(8,128)(2,1)S(1)}, bf16[8,4,1,128,128]{4,3,1,0,2:T(8,128)(2,1)}, u32[]{:S(2)}) copy-start(bf16[8,4,1,128,128]{4,3,1,0,2:T(8,128)(2,1)} %get-tuple-element.6) | copy-start | bytes 3145732
  400.4 16.9 %copy-start.6 = (bf16[8,4,1,128,128]{4,3,1,0,2:T(8,128)(2,1)S(1)}, bf16[8,4,1,128,128]{4,3,1,0,2:T(8,128)(2,1)}, u32[]{:S(2)}) copy-start(bf16[8,4,1,128,128]{4,3,1,0,2:T(8,128)(2,1)} %get-tuple-element.5) | copy-start | bytes 3145732
  400.7 17.0 %copy-start.2 = (bf16[8,4,128,128]{3,2,1,0:T(8,128)(2,1)S(1)}, bf16[8,4,128,128]{3,2,1,0:T(8,128)(2,1)}, u32[]{:S(2)}) copy-start(bf16[8,4,128,128]{3,2,1,0:T(8,128)(2,1)} %get-tuple-element.28) | copy-start | bytes 3145732
  401.0 17.0 %copy-start.1 = (bf16[8,4,128,128]{3,2,1,0:T(8,128)(2,1)S(1)}, bf16[8,4,128,128]{3,2,1,0:T(8,128)(2,1)}, u32[]{:S(2)}) copy-start(bf16[8,4,128,128]{3,2,1,0:T(8,128)(2,1)} %get-tuple-element.22) | copy-start | bytes 3145732
Sparse Core Ops, SparseCore 0:
  9.8 68.9 all-gather.5
  80.6 74.5 all-gather.7
  157.1 82.7 all-gather.9
  241.6 112.3 all-gather.11

commit v2 on v1

v2 whole, which is shorter than its diff:
```python
import functools

import jax
import jax.numpy as jnp
from jax import lax
from jax.experimental import pallas as pl
from jax.experimental.pallas import tpu as pltpu
from jax.sharding import Mesh
from jax.sharding import PartitionSpec as P

LEVELS = 8
NATIVE = 3
PER_ROW = 4
SUB = 8
BF16 = jnp.bfloat16
F32 = jnp.float32
HIGHEST = lax.Precision.HIGHEST
COL = ("grp", "sub")
ALL = ("row", "grp", "sub")
CHUNKS = ((6, 5, 4, 3, 2), (1, 0))


def exchange(pieces, axis):
    return lax.all_to_all(pieces, axis, 0, 0, tiled=True)


def spread(piece, axis, count):
    return exchange(jnp.broadcast_to(piece[None], (count,) + piece.shape), axis)


def times_column(x_ref, g_ref, row):
    x = jnp.concatenate([x_ref[a, row] for a in range(PER_ROW)], axis=1)
    g = g_ref[0].reshape(-1, g_ref.shape[-1])
    return jnp.dot(x, g, preferred_element_type=F32)


def far_kernel(count, *refs):
    x_refs, g_refs, out_ref = refs[:count], refs[count : 2 * count], refs[2 * count]
    row = pl.program_id(0)

    @pl.when(row == 0)
    def _():
        out_ref[...] = jnp.zeros_like(out_ref)

    out_ref[...] += sum(times_column(x, g, row) for x, g in zip(x_refs, g_refs))


def near_kernel(x_ref, g_ref, rest_ref, inverse_ref, out_ref, low_ref, acc_ref):
    row = pl.program_id(0)

    @pl.when(row == 0)
    def _():
        acc_ref[...] = rest_ref[...]

    acc_ref[...] -= times_column(x_ref, g_ref, row)

    @pl.when(row == pl.num_programs(0) - 1)
    def _():
        solved = jnp.dot(
            acc_ref[...], inverse_ref[...], precision=HIGHEST, preferred_element_type=F32
        )
        out_ref[...] = solved
        low_ref[...] = jnp.broadcast_to(solved.astype(BF16)[None], low_ref.shape)


def whole(shape):
    return pl.BlockSpec(shape, lambda r: (0,) * len(shape))


def column_spec(first, block):
    return pl.BlockSpec((1, PER_ROW, block, block), lambda r: (r, first, 0, 0))


def far_sums(xs, packed, firsts):
    n_row, part, block = xs[0].shape[1:]
    return pl.pallas_call(
        functools.partial(far_kernel, len(xs)),
        grid=(n_row,),
        in_specs=[whole(x.shape) for x in xs] + [column_spec(f, block) for f in firsts],
        out_specs=whole((part, block)),
        out_shape=jax.ShapeDtypeStruct((part, block), F32),
        cost_estimate=pl.CostEstimate(
            flops=2 * len(xs) * n_row * PER_ROW * part * block * block,
            bytes_accessed=2 * len(xs) * n_row * PER_ROW * block * block,
            transcendentals=0,
        ),
        name="far_sums",
    )(*xs, *([packed] * len(xs)))


def near_solve(x, packed, first, rest, inverse, n_col):
    n_row, part, block = x.shape[1:]
    return pl.pallas_call(
        near_kernel,
        grid=(n_row,),
        in_specs=[
            whole(x.shape),
            column_spec(first, block),
            whole(rest.shape),
            whole(inverse.shape),
        ],
        out_specs=[whole((part, block)), whole((n_col, part, block))],
        out_shape=[
            jax.ShapeDtypeStruct((part, block), F32),
            jax.ShapeDtypeStruct((n_col, part, block), BF16),
        ],
        scratch_shapes=[pltpu.VMEM((part, block), F32)],
        cost_estimate=pl.CostEstimate(
            flops=2 * n_row * PER_ROW * part * block * block,
            bytes_accessed=2 * n_row * PER_ROW * block * block,
            transcendentals=0,
        ),
        name="near_solve",
    )(x, packed, rest, inverse)


def per_device(factor, pattern, loads, block_inverse):
    my_row = lax.axis_index("row")
    n_row = lax.axis_size("row")
    n_grp = lax.axis_size("grp")
    n_sub = lax.axis_size("sub")
    n_col = n_grp * n_sub
    scen = loads.shape[3]
    block = loads.shape[2]
    part = scen // n_row
    inverse = block_inverse[:, 0]
    loads_t = jnp.swapaxes(loads[:, 0], 1, 2)

    columns = []
    for j in range(LEVELS - 1):
        rows = slice((j + 1) * PER_ROW, LEVELS * PER_ROW)
        mask = pattern[rows, 0, j, 0].astype(BF16)[:, None, None]
        columns.append(factor[rows, 0, j, 0] * mask)
    gathered, where = [None] * LEVELS, [None] * LEVELS
    for chunk in CHUNKS:
        packed = jnp.concatenate([columns[j] for j in chunk], axis=0)
        packed = lax.all_gather(packed, "row", axis=0)
        at = 0
        for j in chunk:
            size = columns[j].shape[0]
            gathered[j], where[j] = packed, at // PER_ROW
            at += size

    def local(t, m):
        return columns[m][(t - m - 1) * PER_ROW : (t - m) * PER_ROW]

    def split(t, m):
        at = (where[m] + t - m - 1) * PER_ROW
        return gathered[m][:, at : at + PER_ROW]

    def forward_solve(level, resid):
        return lax.dot_general(
            resid, inverse[level], (((1,), (1,)), ((), ())), precision=HIGHEST
        )

    def backward_solve(level, resid):
        return lax.dot_general(
            resid, inverse[level], (((1,), (0,)), ((), ())), precision=HIGHEST
        )

    def local_sums(t, count):
        return sum(
            jnp.einsum("sq,apq->asp", low[m], local(t, m), preferred_element_type=F32)
            for m in range(count)
        ).astype(BF16)

    solved = [forward_solve(0, loads_t[0])]
    low = [solved[0].astype(BF16)]
    for t in range(1, NATIVE + 1):
        pieces = local_sums(t, t).reshape(n_col, part, block)
        total = jnp.sum(exchange(pieces, COL).astype(F32), axis=0).astype(BF16)
        total = exchange(spread(total, "row", n_row), "sub")
        total = total.reshape(scen, block).astype(F32)
        solved.append(forward_solve(t, loads_t[t] - total))
        low.append(solved[t].astype(BF16))

    pieces = jnp.stack(
        [local_sums(t, NATIVE + 1).reshape(n_col, part, block) for t in range(NATIVE + 1, LEVELS)],
        axis=1,
    )
    total = jnp.sum(exchange(pieces, COL).astype(F32), axis=0).astype(BF16)
    turn = [
        ((r * n_grp + g) * n_sub + k, (k * n_grp + g) * n_sub + r)
        for r in range(n_row)
        for g in range(n_grp)
        for k in range(n_sub)
    ]
    early = lax.ppermute(total, ALL, turn).astype(F32)

    def own(value):
        return lax.dynamic_slice_in_dim(value, my_row * part, part, axis=0)

    solved = [own(v) for v in solved]
    low = low + [None] * (LEVELS - NATIVE - 1)
    for t in range(NATIVE + 1, LEVELS):
        total = early[t - NATIVE - 1]
        if t > NATIVE + 1:
            sums = sum(
                jnp.einsum("sq,rapq->arsp", low[m], split(t, m), preferred_element_type=F32)
                for m in range(NATIVE + 1, t)
            )
            pieces = sums.astype(BF16).reshape(n_col, part, block)
            total = total + jnp.sum(exchange(pieces, COL).astype(F32), axis=0)
        solved.append(forward_solve(t, own(loads_t[t]) - total))
        low[t] = solved[t].astype(BF16)

    out = [None] * LEVELS
    out[LEVELS - 1] = backward_solve(LEVELS - 1, solved[LEVELS - 1])
    wide = jnp.broadcast_to(out[LEVELS - 1].astype(BF16)[None], (n_col, part, block))
    later = []
    for j in reversed(range(LEVELS - 1)):
        rest = solved[j]
        if later:
            rest = rest - far_sums(
                [x for _, x in later],
                gathered[j],
                [where[j] + t - j - 1 for t, _ in later],
            )
        near = exchange(wide, COL).reshape(PER_ROW, n_row, part, block)
        out[j], wide = near_solve(near, gathered[j], where[j], rest, inverse[j], n_col)
        later.append((j + 1, near))

    both = spread(jnp.stack(out).astype(BF16), "row", n_row)
    return jnp.transpose(both, (1, 3, 0, 2)).reshape(LEVELS, 1, block, scen).astype(F32)


def solution(mesh):
    n_col = mesh.shape["col"]
    n_row = mesh.shape["row"]
    devices = mesh.devices.reshape(n_row, n_col // SUB, SUB)
    in_specs = (
        P(None, "row", None, COL, None, None),
        P(None, "row", None, COL),
        P(None, COL, None, None),
        P(None, COL, None, None),
    )
    return jax.shard_map(
        per_device,
        mesh=Mesh(devices, ALL),
        in_specs=in_specs,
        out_specs=P(None, COL, None, None),
        check_vma=False,
    )
```

time: 466 us -> 415 us (0.89)
  blocking collectives: 169 us -> 57 us
  Pallas kernels: 0 us -> 75.5 us
  starting transfers between devices: 58.2 us -> 108 us
  waiting for transfers between devices: 101 us -> 70.5 us
  matrix products: 68.6 us -> 44.3 us
  local copies, waits for them, and re-layouts: 37.1 us -> 18.9 us
  other arithmetic: 13.4 us -> 22 us
    all_to_all x11 -> x3, blocking collectives: 169 us -> 57 us  [exchange(): return lax.all_to_all(pieces, axis, 0, 0, tiled=True)]
    pallas_call x0 -> x13, Pallas kernels: none -> 75.5 us  [the longest x7 37.9 us: near_solve(): pl.pallas_call(near_kernel, grid=(n_row,), in_specs=[whole(x.shape), colu...]
    all_to_all x12 -> x18, starting transfers between devices: 58.1 us -> 105 us  [exchange(): return lax.all_to_all(pieces, axis, 0, 0, tiled=True)]
    all_gather x4 -> x2, waiting for transfers between devices: 48.2 us -> 2.27 us  [per_device(): packed = lax.all_gather(packed, 'row', axis=0)]
    dot_general x56 -> x28, matrix products: 59.2 us -> 39.6 us  [the longest x22 29.5 us: local_sums(): jnp.einsum('sq,apq->asp', low[m], local(t, m), preferred_element_type=F32)]
    squeeze x3 -> x1, local copies, waits for them, and re-layouts: 17.5 us -> 0.78 us  [forward_solve(): inverse[level]]
    all_to_all x12 -> x18, waiting for transfers between devices: 52.8 us -> 62.8 us  [exchange(): return lax.all_to_all(pieces, axis, 0, 0, tiled=True)]
    mul x7 -> x2, other arithmetic: 11.2 us -> 2.57 us  [per_device(): columns.append(factor[rows, 0, j, 0] * mask)]
  transfers between devices with their start and end apart: 16 -> 21, of which waited for: 13 -> 17; matrix products, arithmetic and copies ran while one was open for 21% -> 17% of each run, Pallas kernels for 0% -> 16%
where the time goes in v2:
time: 415 us; the launch traced here: 410 us
  starting transfers between devices  108 us (26%)
  Pallas kernels  75.5 us (18%)
  waiting for transfers between devices  70.5 us (17%)
  blocking collectives  57 us (14%)
  matrix products  44.3 us (11%)
  other arithmetic  22 us (5%)
  local copies, waits for them, and re-layouts  18.9 us (5%)
  between operations  13.9 us (3%)
    all_to_all x18, starting transfers between devices, exchange(): return lax.all_to_all(pieces, axis, 0, 0, tiled=True)  105 us
    all_to_all x18, waiting for transfers between devices, exchange(): return lax.all_to_all(pieces, axis, 0, 0, tiled=True)  62.8 us
    all_to_all x3, blocking collectives, exchange(): return lax.all_to_all(pieces, axis, 0, 0, tiled=True)  57 us
    pallas_call x7, Pallas kernels, near_solve(): pl.pallas_call(near_kernel, grid=(n_row,), in_specs=[whole(x.shape), colu...  37.9 us
    pallas_call x6, Pallas kernels, far_sums(): pl.pallas_call(functools.partial(far_kernel, len(xs)), grid=(n_row,), in_...  37.6 us
    dot_general x22, matrix products, local_sums(): jnp.einsum('sq,apq->asp', low[m], local(t, m), preferred_element_type=F32)  29.5 us
    dot_general x6, matrix products, per_device(): jnp.einsum('sq,rapq->arsp', low[m], split(t, m), preferred_element_type=F32)  10.2 us
  transfers between devices with their start and end apart: 21, of which 17 were waited for; matrix products, arithmetic and copies ran while one was open for 17% of the time, Pallas kernels for 16%

profile of v2, /device:TPU:2, one launch (start us, length us, event | category | flops | bytes accessed | tf_op | source)
XLA Modules:
  0.0 410.3 jit_solution(15143052908522553677)
XLA Ops:
  19.0 1.6 copy.32
  22.4 1.8 copy.35
  24.2 7.7 %all-to-all-start = ((bf16[32,32,128]{2,1,0:T(8,128)(2,1)}), bf16[32,32,128]{2,1,0:T(8,128)(2,1)}, u32[]{:S(2)}, u32[]{:S(2)}) async-start(bf16[32,32,128]{2,1,0:T(8,128)(2,1)} %bitcast.366), calls=%async_computation | async-start | bytes 524288 | tf_op jit(solution)/shard_map/all_to_all | solution.py:24
  36.0 3.6 all-to-all-done
  41.3 8.5 %all-to-all-start.1 = ((bf16[8,32,128]{2,1,0:T(8,128)(2,1)}), bf16[8,32,128]{2,1,0:T(8,128)(2,1)}, u32[]{:S(2)}, u32[]{:S(2)}) async-start(bf16[8,32,128]{2,1,0:T(8,128)(2,1)} %broadcast_in_dim.10), calls=%async_computation.1 | async-start | bytes 131072 | tf_op jit(solution)/shard_map/all_to_all | solution.py:24
  50.7 8.4 %all-to-all-done.1 = bf16[8,32,128]{2,1,0:T(8,128)(2,1)} async-done(((bf16[8,32,128]{2,1,0:T(8,128)(2,1)}), bf16[8,32,128]{2,1,0:T(8,128)(2,1)}, u32[]{:S(2)}, u32[]{:S(2)}) %all-to-all-start.1) | async-done | bytes 65568 | tf_op jit(solution)/shard_map/all_to_all | solution.py:24
  59.2 4.6 %all-to-all-start.2 = ((bf16[8,32,128]{2,1,0:T(8,128)(2,1)}), bf16[8,32,128]{2,1,0:T(8,128)(2,1)S(1)}, u32[]{:S(2)}, u32[]{:S(2)}) async-start(bf16[8,32,128]{2,1,0:T(8,128)(2,1)} %all-to-all-done.1), calls=%async_computation.2 | async-start | bytes 131072 | tf_op jit(solution)/shard_map/all_to_all | solution.py:24
  64.8 3.2 all-to-all-done.2
  71.0 5.6 %all-to-all-start.3 = ((bf16[32,32,128]{2,1,0:T(8,128)(2,1)}), bf16[32,32,128]{2,1,0:T(8,128)(2,1)}, u32[]{:S(2)}, u32[]{:S(2)}) async-start(bf16[32,32,128]{2,1,0:T(8,128)(2,1)} %bitcast.19), calls=%async_computation.3 | async-start | bytes 524288 | tf_op jit(solution)/shard_map/all_to_all | solution.py:24
  78.0 2.1 convolution_add_fusion.17
  80.0 2.1 convolution_add_fusion.11
  82.1 2.4 all-to-all-done.3
  86.2 4.0 all-to-all-start.4
  90.1 2.1 convolution_add_fusion.8
  92.2 7.4 %all-to-all-done.4 = bf16[8,32,128]{2,1,0:T(8,128)(2,1)} async-done(((bf16[8,32,128]{2,1,0:T(8,128)(2,1)}), bf16[8,32,128]{2,1,0:T(8,128)(2,1)}, u32[]{:S(2)}, u32[]{:S(2)}) %all-to-all-start.4) | async-done | bytes 65568 | tf_op jit(solution)/shard_map/all_to_all | solution.py:24
  99.6 4.6 %all-to-all-start.5 = ((bf16[8,32,128]{2,1,0:T(8,128)(2,1)}), bf16[8,32,128]{2,1,0:T(8,128)(2,1)S(1)}, u32[]{:S(2)}, u32[]{:S(2)}) async-start(bf16[8,32,128]{2,1,0:T(8,128)(2,1)} %all-to-all-done.4), calls=%async_computation.5 | async-start | bytes 131072 | tf_op jit(solution)/shard_map/all_to_all | solution.py:24
  105.2 3.2 all-to-all-done.5
  111.3 5.0 %all-to-all-start.6 = ((bf16[32,32,128]{2,1,0:T(8,128)(2,1)}), bf16[32,32,128]{2,1,0:T(8,128)(2,1)S(1)}, u32[]{:S(2)}, u32[]{:S(2)}) async-start(bf16[32,32,128]{2,1,0:T(8,128)(2,1)} %bitcast.27), calls=%async_computation.6 | async-start | bytes 524288 | tf_op jit(solution)/shard_map/all_to_all | solution.py:24
  116.3 1.4 convolution_add_fusion.15
  117.7 1.4 convolution_add_fusion.10
  119.2 5.0 %all-to-all-done.6 = bf16[32,32,128]{2,1,0:T(8,128)(2,1)S(1)} async-done(((bf16[32,32,128]{2,1,0:T(8,128)(2,1)}), bf16[32,32,128]{2,1,0:T(8,128)(2,1)S(1)}, u32[]{:S(2)}, u32[]{:S(2)}) %all-to-all-start.6) | async-done | bytes 262176 | tf_op jit(solution)/shard_map/all_to_all | solution.py:24
  124.8 4.0 all-to-all-start.7
  128.8 1.4 convolution_add_fusion.7
  130.2 8.0 %all-to-all-done.7 = bf16[8,32,128]{2,1,0:T(8,128)(2,1)} async-done(((bf16[8,32,128]{2,1,0:T(8,128)(2,1)}), bf16[8,32,128]{2,1,0:T(8,128)(2,1)}, u32[]{:S(2)}, u32[]{:S(2)}) %all-to-all-start.7) | async-done | bytes 65568 | tf_op jit(solution)/shard_map/all_to_all | solution.py:24
  138.2 4.6 %all-to-all-start.8 = ((bf16[8,32,128]{2,1,0:T(8,128)(2,1)}), bf16[8,32,128]{2,1,0:T(8,128)(2,1)S(1)}, u32[]{:S(2)}, u32[]{:S(2)}) async-start(bf16[8,32,128]{2,1,0:T(8,128)(2,1)} %all-to-all-done.7), calls=%async_computation.8 | async-start | bytes 131072 | tf_op jit(solution)/shard_map/all_to_all | solution.py:24
  142.8 2.2 convolution_add_fusion.4
  145.0 2.0 all-to-all-done.8
  153.9 20.6 %all_to_all.105 = bf16[32,4,32,128]{3,2,1,0:T(8,128)(2,1)S(1)} all-to-all(bf16[32,4,32,128]{3,2,1,0:T(8,128)(2,1)S(1)} %copy.44), channel_id=1, replica_groups=mesh['row'=8,'grp'=4,'sub'=8] {'grp','sub'}, dimensions={0} | all-to-all | bytes 2097152 | tf_op jit(solution)/shard_map/all_to_all | solution.py:24
  174.7 3.2 collective-permute-start
  178.0 5.4 %collective-permute-done = bf16[4,32,128]{2,1,0:T(8,128)(2,1)S(1)} collective-permute-done((bf16[4,32,128]{2,1,0:T(8,128)(2,1)S(1)}, bf16[4,32,128]{2,1,0:T(8,128)(2,1)S(1)}, u32[]{:S(2)}, u32[]{:S(2)}) %collective-permute-start) | collective-permute-done | bytes 32800 | tf_op jit(solution)/shard_map/ppermute | solution.py:188
  183.5 2.2 all-gather.5.cloned.1.call-done
  185.8 1.7 fusion.15
  188.2 6.7 %all-to-all-start.10 = ((bf16[32,32,128]{2,1,0:T(8,128)(2,1)}), bf16[32,32,128]{2,1,0:T(8,128)(2,1)S(1)}, u32[]{:S(2)}, u32[]{:S(2)}) async-start(bf16[32,32,128]{2,1,0:T(8,128)(2,1)} %bitcast.53), calls=%async_computation.10 | async-start | bytes 524288 | tf_op jit(solution)/shard_map/all_to_all | solution.py:24
  194.9 1.7 fusion.91
  196.6 1.7 fusion.94
  198.3 4.3 %all-to-all-done.10 = bf16[32,32,128]{2,1,0:T(8,128)(2,1)S(1)} async-done(((bf16[32,32,128]{2,1,0:T(8,128)(2,1)}), bf16[32,32,128]{2,1,0:T(8,128)(2,1)S(1)}, u32[]{:S(2)}, u32[]{:S(2)}) %all-to-all-start.10) | async-done | bytes 262176 | tf_op jit(solution)/shard_map/all_to_all | solution.py:24
  202.9 1.7 fusion.17
  205.3 5.0 %all-to-all-start.11 = ((bf16[32,32,128]{2,1,0:T(8,128)(2,1)}), bf16[32,32,128]{2,1,0:T(8,128)(2,1)S(1)}, u32[]{:S(2)}, u32[]{:S(2)}) async-start(bf16[32,32,128]{2,1,0:T(8,128)(2,1)} %bitcast.61), calls=%async_computation.11 | async-start | bytes 524288 | tf_op jit(solution)/shard_map/all_to_all | solution.py:24
  210.3 1.7 convolution_add_fusion.2
  212.0 6.1 %all-to-all-done.11 = bf16[32,32,128]{2,1,0:T(8,128)(2,1)S(1)} async-done(((bf16[32,32,128]{2,1,0:T(8,128)(2,1)}), bf16[32,32,128]{2,1,0:T(8,128)(2,1)S(1)}, u32[]{:S(2)}, u32[]{:S(2)}) %all-to-all-start.11) | async-done | bytes 262176 | tf_op jit(solution)/shard_map/all_to_all | solution.py:24
  218.4 1.7 fusion.16
  220.1 12.4 %all_to_all.106 = bf16[32,32,128]{2,1,0:T(8,128)(2,1)S(1)} all-to-all(bf16[32,32,128]{2,1,0:T(8,128)(2,1)S(1)} %bitcast.367), channel_id=1, replica_groups=mesh['row'=8,'grp'=4,'sub'=8] {'grp','sub'}, dimensions={0} | all-to-all | bytes 524288 | tf_op jit(solution)/shard_map/all_to_all | solution.py:24
  233.7 5.0 %all-to-all-start.13 = ((bf16[32,32,128]{2,1,0:T(8,128)(2,1)}), bf16[32,32,128]{2,1,0:T(8,128)(2,1)S(1)}, u32[]{:S(2)}, u32[]{:S(2)}) async-start(bf16[32,32,128]{2,1,0:T(8,128)(2,1)} %broadcast_in_dim.13), calls=%async_computation.13 | async-start | bytes 524288 | tf_op jit(solution)/shard_map/all_to_all | solution.py:24
  239.5 7.0 %all-to-all-done.13 = bf16[32,32,128]{2,1,0:T(8,128)(2,1)S(1)} async-done(((bf16[32,32,128]{2,1,0:T(8,128)(2,1)}), bf16[32,32,128]{2,1,0:T(8,128)(2,1)S(1)}, u32[]{:S(2)}, u32[]{:S(2)}) %all-to-all-start.13) | async-done | bytes 262176 | tf_op jit(solution)/shard_map/all_to_all | solution.py:24
  247.2 5.4 %near_solve.7 = (f32[32,128]{1,0:T(8,128)}, bf16[32,32,128]{2,1,0:T(8,128)(2,1)}) custom-call(bf16[4,8,32,128]{3,2,1,0:T(8,128)(2,1)} %bitcast.332, bf16[8,60,128,128]{3,2,1,0:T(8,128)(2,1)} %bitcast.304, f32[32,128]{1,0:T(8,128)} %copy-done.10, f32[128,128]{1,0:T(8,128)} %get-tuple-element.41.inverse_ref), custom_call_target="tpu_custom_call" | custom-call | flops 33554432 | bytes 1048576 | tf_op jit(solution)/shard_map/near_solve/pallas_call | solution.py:93
  252.7 5.0 %all-to-all-start.14 = ((bf16[32,32,128]{2,1,0:T(8,128)(2,1)}), bf16[32,32,128]{2,1,0:T(8,128)(2,1)S(1)}, u32[]{:S(2)}, u32[]{:S(2)}) async-start(bf16[32,32,128]{2,1,0:T(8,128)(2,1)} %get-tuple-element.18), calls=%async_computation.14 | async-start | bytes 524288 | tf_op jit(solution)/shard_map/all_to_all | solution.py:24
  257.6 5.1 %far_sums.6 = f32[32,128]{1,0:T(8,128)} custom-call(bf16[4,8,32,128]{3,2,1,0:T(8,128)(2,1)} %bitcast.333, bf16[8,60,128,128]{3,2,1,0:T(8,128)(2,1)} %bitcast.305), custom_call_target="tpu_custom_call" | custom-call | flops 33554432 | bytes 1048576 | tf_op jit(solution)/shard_map/far_sums/pallas_call | solution.py:76
  266.2 5.4 %near_solve.8 = (f32[32,128]{1,0:T(8,128)}, bf16[32,32,128]{2,1,0:T(8,128)(2,1)}) custom-call(bf16[4,8,32,128]{3,2,1,0:T(8,128)(2,1)} %bitcast.339, bf16[8,60,128,128]{3,2,1,0:T(8,128)(2,1)} %bitcast.306, f32[32,128]{1,0:T(8,128)} %sub.74.rest_ref, f32[128,128]{1,0:T(8,128)} %get-tuple-element.36.inverse_ref), custom_call_target="tpu_custom_call" | custom-call | flops 33554432 | bytes 1048576 | tf_op jit(solution)/shard_map/near_solve/pallas_call | solution.py:93
  271.6 6.1 %all-to-all-start.15 = ((bf16[32,32,128]{2,1,0:T(8,128)(2,1)}), bf16[32,32,128]{2,1,0:T(8,128)(2,1)S(1)}, u32[]{:S(2)}, u32[]{:S(2)}) async-start(bf16[32,32,128]{2,1,0:T(8,128)(2,1)} %get-tuple-element.19), calls=%async_computation.15 | async-start | bytes 524288 | tf_op jit(solution)/shard_map/all_to_all | solution.py:24
  277.7 5.7 %far_sums.7 = f32[32,128]{1,0:T(8,128)} custom-call(bf16[4,8,32,128]{3,2,1,0:T(8,128)(2,1)} %bitcast.334, bf16[4,8,32,128]{3,2,1,0:T(8,128)(2,1)} %bitcast.340, bf16[8,60,128,128]{3,2,1,0:T(8,128)(2,1)} %bitcast.307, bf16[8,60,128,128]{3,2,1,0:T(8,128)(2,1)} %bitcast.308), custom_call_target="tpu_custom_call" | custom-call | flops 67108864 | bytes 2097152 | tf_op jit(solution)/shard_map/far_sums/pallas_call | solution.py:76
  286.1 5.4 %near_solve.9 = (f32[32,128]{1,0:T(8,128)}, bf16[32,32,128]{2,1,0:T(8,128)(2,1)}) custom-call(bf16[4,8,32,128]{3,2,1,0:T(8,128)(2,1)} %bitcast.345, bf16[8,60,128,128]{3,2,1,0:T(8,128)(2,1)} %bitcast.309, f32[32,128]{1,0:T(8,128)} %sub.75.rest_ref, f32[128,128]{1,0:T(8,128)} %get-tuple-element.37.inverse_ref), custom_call_target="tpu_custom_call" | custom-call | flops 33554432 | bytes 1048576 | tf_op jit(solution)/shard_map/near_solve/pallas_call | solution.py:93
  291.5 6.7 %all-to-all-start.16 = ((bf16[32,32,128]{2,1,0:T(8,128)(2,1)}), bf16[32,32,128]{2,1,0:T(8,128)(2,1)S(1)}, u32[]{:S(2)}, u32[]{:S(2)}) async-start(bf16[32,32,128]{2,1,0:T(8,128)(2,1)} %get-tuple-element.20), calls=%async_computation.16 | async-start | bytes 524288 | tf_op jit(solution)/shard_map/all_to_all | solution.py:24
  298.2 6.1 %far_sums.8 = f32[32,128]{1,0:T(8,128)} custom-call(bf16[4,8,32,128]{3,2,1,0:T(8,128)(2,1)} %bitcast.335, bf16[4,8,32,128]{3,2,1,0:T(8,128)(2,1)} %bitcast.341, bf16[4,8,32,128]{3,2,1,0:T(8,128)(2,1)} %bitcast.346, bf16[8,60,128,128]{3,2,1,0:T(8,128)(2,1)} %bitcast.310, bf16[8,60,128,128]{3,2,1,0:T(8,128)(2,1)} %bitcast.311, bf16[8,60,128,128]{3,2,1,0:T(8,128)(2,1)} %bitcast.312), custom_call_target="tpu_custom_call" | custom-call | flops 100663296 | bytes 3145728 | tf_op jit(solution)/shard_map/far_sums/pallas_call | solution.py:76
  306.6 5.4 %near_solve.10 = (f32[32,128]{1,0:T(8,128)}, bf16[32,32,128]{2,1,0:T(8,128)(2,1)}) custom-call(bf16[4,8,32,128]{3,2,1,0:T(8,128)(2,1)} %bitcast.350, bf16[8,60,128,128]{3,2,1,0:T(8,128)(2,1)} %bitcast.313, f32[32,128]{1,0:T(8,128)} %dynamic-slice_subtract_fusion.3.rest_ref, f32[128,128]{1,0:T(8,128)} %get-tuple-element.38.inverse_ref), custom_call_target="tpu_custom_call" | custom-call | flops 33554432 | bytes 1048576 | tf_op jit(solution)/shard_map/near_solve/pallas_call | solution.py:93
  312.0 7.2 %all-to-all-start.17 = ((bf16[32,32,128]{2,1,0:T(8,128)(2,1)}), bf16[32,32,128]{2,1,0:T(8,128)(2,1)S(1)}, u32[]{:S(2)}, u32[]{:S(2)}) async-start(bf16[32,32,128]{2,1,0:T(8,128)(2,1)} %get-tuple-element.21), calls=%async_computation.17 | async-start | bytes 524288 | tf_op jit(solution)/shard_map/all_to_all | solution.py:24
  319.2 6.5 %far_sums.9 = f32[32,128]{1,0:T(8,128)} custom-call(bf16[4,8,32,128]{3,2,1,0:T(8,128)(2,1)} %bitcast.336, bf16[4,8,32,128]{3,2,1,0:T(8,128)(2,1)} %bitcast.342, bf16[4,8,32,128]{3,2,1,0:T(8,128)(2,1)} %bitcast.347, bf16[4,8,32,128]{3,2,1,0:T(8,128)(2,1)} %bitcast.351, bf16[8,60,128,128]{3,2,1,0:T(8,128)(2,1)} %bitcast.314, ...), custom_call_target="tpu_custom_call" | custom-call | flops 134217728 | bytes 4194304 | tf_op jit(solution)/shard_map/far_sums/pallas_call | solution.py:76
  327.7 5.4 %near_solve.11 = (f32[32,128]{1,0:T(8,128)}, bf16[32,32,128]{2,1,0:T(8,128)(2,1)}) custom-call(bf16[4,8,32,128]{3,2,1,0:T(8,128)(2,1)} %bitcast.354, bf16[8,60,128,128]{3,2,1,0:T(8,128)(2,1)} %bitcast.318, f32[32,128]{1,0:T(8,128)} %dynamic-slice_subtract_fusion.2.rest_ref, f32[128,128]{1,0:T(8,128)} %get-tuple-element.39.inverse_ref), custom_call_target="tpu_custom_call" | custom-call | flops 33554432 | bytes 1048576 | tf_op jit(solution)/shard_map/near_solve/pallas_call | solution.py:93
  333.1 7.4 %all-to-all-start.18 = ((bf16[32,32,128]{2,1,0:T(8,128)(2,1)}), bf16[32,32,128]{2,1,0:T(8,128)(2,1)S(1)}, u32[]{:S(2)}, u32[]{:S(2)}) async-start(bf16[32,32,128]{2,1,0:T(8,128)(2,1)} %get-tuple-element.22), calls=%async_computation.18 | async-start | bytes 524288 | tf_op jit(solution)/shard_map/all_to_all | solution.py:24
  340.5 6.9 %far_sums.10 = f32[32,128]{1,0:T(8,128)} custom-call(bf16[4,8,32,128]{3,2,1,0:T(8,128)(2,1)} %bitcast.337, bf16[4,8,32,128]{3,2,1,0:T(8,128)(2,1)} %bitcast.343, bf16[4,8,32,128]{3,2,1,0:T(8,128)(2,1)} %bitcast.348, bf16[4,8,32,128]{3,2,1,0:T(8,128)(2,1)} %bitcast.352, bf16[4,8,32,128]{3,2,1,0:T(8,128)(2,1)} %bitcast.355, ...), custom_call_target="tpu_custom_call" | custom-call | flops 167772160 | bytes 5242880 | tf_op jit(solution)/shard_map/far_sums/pallas_call | solution.py:76
  349.5 5.4 %near_solve.12 = (f32[32,128]{1,0:T(8,128)}, bf16[32,32,128]{2,1,0:T(8,128)(2,1)}) custom-call(bf16[4,8,32,128]{3,2,1,0:T(8,128)(2,1)} %bitcast.363, bf16[8,52,128,128]{3,2,1,0:T(8,128)(2,1)} %bitcast.324, f32[32,128]{1,0:T(8,128)} %dynamic-slice_subtract_fusion.1.rest_ref, f32[128,128]{1,0:T(8,128)} %get-tuple-element.40.inverse_ref), custom_call_target="tpu_custom_call" | custom-call | flops 33554432 | bytes 1048576 | tf_op jit(solution)/shard_map/near_solve/pallas_call | solution.py:93
  354.9 7.4 %all-to-all-start.19 = ((bf16[32,32,128]{2,1,0:T(8,128)(2,1)}), bf16[32,32,128]{2,1,0:T(8,128)(2,1)S(1)}, u32[]{:S(2)}, u32[]{:S(2)}) async-start(bf16[32,32,128]{2,1,0:T(8,128)(2,1)} %get-tuple-element.23), calls=%async_computation.19 | async-start | bytes 524288 | tf_op jit(solution)/shard_map/all_to_all | solution.py:24
  362.3 7.3 %far_sums.11 = f32[32,128]{1,0:T(8,128)} custom-call(bf16[4,8,32,128]{3,2,1,0:T(8,128)(2,1)} %bitcast.338, bf16[4,8,32,128]{3,2,1,0:T(8,128)(2,1)} %bitcast.344, bf16[4,8,32,128]{3,2,1,0:T(8,128)(2,1)} %bitcast.349, bf16[4,8,32,128]{3,2,1,0:T(8,128)(2,1)} %bitcast.353, bf16[4,8,32,128]{3,2,1,0:T(8,128)(2,1)} %bitcast.356, bf16[4,8,32,128]{3,2,1,0:T(8,128)(2,1)} %bitcast.364, ...), custom_call_target="tpu_custom_call" | custom-call | flops 201326592 | bytes 6291456 | tf_op jit(solution)/shard_map/far_sums/pallas_call | solution.py:76
  371.7 5.4 %near_solve.13 = (f32[32,128]{1,0:T(8,128)}, bf16[32,32,128]{2,1,0:T(8,128)(2,1)}) custom-call(bf16[4,8,32,128]{3,2,1,0:T(8,128)(2,1)} %bitcast.365, bf16[8,52,128,128]{3,2,1,0:T(8,128)(2,1)} %bitcast.331, f32[32,128]{1,0:T(8,128)} %dynamic-slice_subtract_fusion.rest_ref, f32[128,128]{1,0:T(8,128)} %get-tuple-element.35.inverse_ref), custom_call_target="tpu_custom_call" | custom-call | flops 33554432 | bytes 1048576 | tf_op jit(solution)/shard_map/near_solve/pallas_call | solution.py:93
  378.1 24.0 %all_to_all.107 = bf16[8,8,32,128]{3,2,1,0:T(8,128)(2,1)S(1)} all-to-all(bf16[8,8,32,128]{3,2,1,0:T(8,128)(2,1)S(1)} %broadcast_in_dim.14), channel_id=1, replica_groups=mesh['row'=8,'grp'=4,'sub'=8] {'row'}, dimensions={0} | all-to-all | bytes 1048576 | tf_op jit(solution)/shard_map/all_to_all | solution.py:24
  (127 shorter events, 61.4 us)
Async XLA Ops:
  6.5 14.0 %copy-start.7 = (f32[8,1,128,128]{3,2,1,0:T(8,128)S(1)}, f32[8,1,128,128]{3,2,1,0:T(8,128)}, u32[]{:S(2)}) copy-start(f32[8,1,128,128]{3,2,1,0:T(8,128)} %param.7) | copy-start | bytes 1572868
  6.5 179.3 %all-gather.5.cloned.1.call-start = ((), (), s32[]{:S(2)}) async-start(), calls=%async_computation.21 | async-start | bytes 17694720 | tf_op jit(solution)/shard_map/all_gather | solution.py:137
  13.6 1.3 copy-start.6
  14.9 325.7 %all-gather.7.cloned.1.call-start = ((), (), s32[]{:S(2)}) async-start(), calls=%async_computation.22 | async-start | bytes 15335424 | tf_op jit(solution)/shard_map/all_gather | solution.py:137
  24.2 15.4 %all-to-all-start = ((bf16[32,32,128]{2,1,0:T(8,128)(2,1)}), bf16[32,32,128]{2,1,0:T(8,128)(2,1)}, u32[]{:S(2)}, u32[]{:S(2)}) async-start(bf16[32,32,128]{2,1,0:T(8,128)(2,1)} %bitcast.366), calls=%async_computation | async-start | bytes 524288 | tf_op jit(solution)/shard_map/all_to_all | solution.py:24
  41.3 17.9 %all-to-all-start.1 = ((bf16[8,32,128]{2,1,0:T(8,128)(2,1)}), bf16[8,32,128]{2,1,0:T(8,128)(2,1)}, u32[]{:S(2)}, u32[]{:S(2)}) async-start(bf16[8,32,128]{2,1,0:T(8,128)(2,1)} %broadcast_in_dim.10), calls=%async_computation.1 | async-start | bytes 131072 | tf_op jit(solution)/shard_map/all_to_all | solution.py:24
  59.2 8.8 %all-to-all-start.2 = ((bf16[8,32,128]{2,1,0:T(8,128)(2,1)}), bf16[8,32,128]{2,1,0:T(8,128)(2,1)S(1)}, u32[]{:S(2)}, u32[]{:S(2)}) async-start(bf16[8,32,128]{2,1,0:T(8,128)(2,1)} %all-to-all-done.1), calls=%async_computation.2 | async-start | bytes 131072 | tf_op jit(solution)/shard_map/all_to_all | solution.py:24
  64.8 39.4 %copy-start.8 = (f32[4,128,256]{2,1,0:T(8,128)S(1)}, f32[4,128,256]{2,1,0:T(8,128)}, u32[]{:S(2)}) copy-start(f32[4,128,256]{2,1,0:T(8,128)} %fusion.52) | copy-start | bytes 1572868
  71.0 13.5 %all-to-all-start.3 = ((bf16[32,32,128]{2,1,0:T(8,128)(2,1)}), bf16[32,32,128]{2,1,0:T(8,128)(2,1)}, u32[]{:S(2)}, u32[]{:S(2)}) async-start(bf16[32,32,128]{2,1,0:T(8,128)(2,1)} %bitcast.19), calls=%async_computation.3 | async-start | bytes 524288 | tf_op jit(solution)/shard_map/all_to_all | solution.py:24
  86.2 13.4 %all-to-all-start.4 = ((bf16[8,32,128]{2,1,0:T(8,128)(2,1)}), bf16[8,32,128]{2,1,0:T(8,128)(2,1)}, u32[]{:S(2)}, u32[]{:S(2)}) async-start(bf16[8,32,128]{2,1,0:T(8,128)(2,1)} %broadcast_in_dim.11), calls=%async_computation.4 | async-start | bytes 131072 | tf_op jit(solution)/shard_map/all_to_all | solution.py:24
  99.6 8.8 %all-to-all-start.5 = ((bf16[8,32,128]{2,1,0:T(8,128)(2,1)}), bf16[8,32,128]{2,1,0:T(8,128)(2,1)S(1)}, u32[]{:S(2)}, u32[]{:S(2)}) async-start(bf16[8,32,128]{2,1,0:T(8,128)(2,1)} %all-to-all-done.4), calls=%async_computation.5 | async-start | bytes 131072 | tf_op jit(solution)/shard_map/all_to_all | solution.py:24
  111.3 12.8 %all-to-all-start.6 = ((bf16[32,32,128]{2,1,0:T(8,128)(2,1)}), bf16[32,32,128]{2,1,0:T(8,128)(2,1)S(1)}, u32[]{:S(2)}, u32[]{:S(2)}) async-start(bf16[32,32,128]{2,1,0:T(8,128)(2,1)} %bitcast.27), calls=%async_computation.6 | async-start | bytes 524288 | tf_op jit(solution)/shard_map/all_to_all | solution.py:24
  124.8 13.4 %all-to-all-start.7 = ((bf16[8,32,128]{2,1,0:T(8,128)(2,1)}), bf16[8,32,128]{2,1,0:T(8,128)(2,1)}, u32[]{:S(2)}, u32[]{:S(2)}) async-start(bf16[8,32,128]{2,1,0:T(8,128)(2,1)} %broadcast_in_dim.12), calls=%async_computation.7 | async-start | bytes 131072 | tf_op jit(solution)/shard_map/all_to_all | solution.py:24
  138.2 8.8 %all-to-all-start.8 = ((bf16[8,32,128]{2,1,0:T(8,128)(2,1)}), bf16[8,32,128]{2,1,0:T(8,128)(2,1)S(1)}, u32[]{:S(2)}, u32[]{:S(2)}) async-start(bf16[8,32,128]{2,1,0:T(8,128)(2,1)} %all-to-all-done.7), calls=%async_computation.8 | async-start | bytes 131072 | tf_op jit(solution)/shard_map/all_to_all | solution.py:24
  174.7 8.6 %collective-permute-start = (bf16[4,32,128]{2,1,0:T(8,128)(2,1)S(1)}, bf16[4,32,128]{2,1,0:T(8,128)(2,1)S(1)}, u32[]{:S(2)}, u32[]{:S(2)}) collective-permute-start(bf16[4,32,128]{2,1,0:T(8,128)(2,1)S(1)} %reduce_sum.84), channel_id=1, source_target_pairs={{0,0},{1,32},{2,64},{3,96},{4,128},{5,160},{6,192},{7,224},{8,8},{... | collective-permute-start | bytes 98312 | tf_op jit(solution)/shard_map/ppermute | solution.py:188
  188.2 14.4 %all-to-all-start.10 = ((bf16[32,32,128]{2,1,0:T(8,128)(2,1)}), bf16[32,32,128]{2,1,0:T(8,128)(2,1)S(1)}, u32[]{:S(2)}, u32[]{:S(2)}) async-start(bf16[32,32,128]{2,1,0:T(8,128)(2,1)} %bitcast.53), calls=%async_computation.10 | async-start | bytes 524288 | tf_op jit(solution)/shard_map/all_to_all | solution.py:24
  205.3 12.8 %all-to-all-start.11 = ((bf16[32,32,128]{2,1,0:T(8,128)(2,1)}), bf16[32,32,128]{2,1,0:T(8,128)(2,1)S(1)}, u32[]{:S(2)}, u32[]{:S(2)}) async-start(bf16[32,32,128]{2,1,0:T(8,128)(2,1)} %bitcast.61), calls=%async_computation.11 | async-start | bytes 524288 | tf_op jit(solution)/shard_map/all_to_all | solution.py:24
  218.3 28.2 %copy-start.10 = (f32[32,128]{1,0:T(8,128)}, f32[32,128]{1,0:T(8,128)S(1)}, u32[]{:S(2)}) copy-start(f32[32,128]{1,0:T(8,128)S(1)} %fusion.69.rest_ref) | copy-start | bytes 49156
  233.7 12.8 %all-to-all-start.13 = ((bf16[32,32,128]{2,1,0:T(8,128)(2,1)}), bf16[32,32,128]{2,1,0:T(8,128)(2,1)S(1)}, u32[]{:S(2)}, u32[]{:S(2)}) async-start(bf16[32,32,128]{2,1,0:T(8,128)(2,1)} %broadcast_in_dim.13), calls=%async_computation.13 | async-start | bytes 524288 | tf_op jit(solution)/shard_map/all_to_all | solution.py:24
  246.5 0.7 copy-start
  252.7 12.8 %all-to-all-start.14 = ((bf16[32,32,128]{2,1,0:T(8,128)(2,1)}), bf16[32,32,128]{2,1,0:T(8,128)(2,1)S(1)}, u32[]{:S(2)}, u32[]{:S(2)}) async-start(bf16[32,32,128]{2,1,0:T(8,128)(2,1)} %get-tuple-element.18), calls=%async_computation.14 | async-start | bytes 524288 | tf_op jit(solution)/shard_map/all_to_all | solution.py:24
  265.4 0.7 copy-start.1
  271.6 13.8 %all-to-all-start.15 = ((bf16[32,32,128]{2,1,0:T(8,128)(2,1)}), bf16[32,32,128]{2,1,0:T(8,128)(2,1)S(1)}, u32[]{:S(2)}, u32[]{:S(2)}) async-start(bf16[32,32,128]{2,1,0:T(8,128)(2,1)} %get-tuple-element.19), calls=%async_computation.15 | async-start | bytes 524288 | tf_op jit(solution)/shard_map/all_to_all | solution.py:24
  285.4 0.7 copy-start.2
  291.5 14.4 %all-to-all-start.16 = ((bf16[32,32,128]{2,1,0:T(8,128)(2,1)}), bf16[32,32,128]{2,1,0:T(8,128)(2,1)S(1)}, u32[]{:S(2)}, u32[]{:S(2)}) async-start(bf16[32,32,128]{2,1,0:T(8,128)(2,1)} %get-tuple-element.20), calls=%async_computation.16 | async-start | bytes 524288 | tf_op jit(solution)/shard_map/all_to_all | solution.py:24
  305.9 0.7 copy-start.3
  312.0 15.0 %all-to-all-start.17 = ((bf16[32,32,128]{2,1,0:T(8,128)(2,1)}), bf16[32,32,128]{2,1,0:T(8,128)(2,1)S(1)}, u32[]{:S(2)}, u32[]{:S(2)}) async-start(bf16[32,32,128]{2,1,0:T(8,128)(2,1)} %get-tuple-element.21), calls=%async_computation.17 | async-start | bytes 524288 | tf_op jit(solution)/shard_map/all_to_all | solution.py:24
  327.0 0.7 copy-start.4
  333.1 15.7 %all-to-all-start.18 = ((bf16[32,32,128]{2,1,0:T(8,128)(2,1)}), bf16[32,32,128]{2,1,0:T(8,128)(2,1)S(1)}, u32[]{:S(2)}, u32[]{:S(2)}) async-start(bf16[32,32,128]{2,1,0:T(8,128)(2,1)} %get-tuple-element.22), calls=%async_computation.18 | async-start | bytes 524288 | tf_op jit(solution)/shard_map/all_to_all | solution.py:24
  348.8 0.7 copy-start.5
  354.9 16.1 %all-to-all-start.19 = ((bf16[32,32,128]{2,1,0:T(8,128)(2,1)}), bf16[32,32,128]{2,1,0:T(8,128)(2,1)S(1)}, u32[]{:S(2)}, u32[]{:S(2)}) async-start(bf16[32,32,128]{2,1,0:T(8,128)(2,1)} %get-tuple-element.23), calls=%async_computation.19 | async-start | bytes 524288 | tf_op jit(solution)/shard_map/all_to_all | solution.py:24
  369.6 8.3 %copy-start.16 = (f32[32,128]{1,0:T(8,128)S(1)}, f32[32,128]{1,0:T(8,128)}, u32[]{:S(2)}) copy-start(f32[32,128]{1,0:T(8,128)} %get-tuple-element.25) | copy-start | bytes 49156
  369.6 8.3 %copy-start.15 = (f32[32,128]{1,0:T(8,128)S(1)}, f32[32,128]{1,0:T(8,128)}, u32[]{:S(2)}) copy-start(f32[32,128]{1,0:T(8,128)} %get-tuple-element.26) | copy-start | bytes 49156
  369.6 8.3 %copy-start.14 = (f32[32,128]{1,0:T(8,128)S(1)}, f32[32,128]{1,0:T(8,128)}, u32[]{:S(2)}) copy-start(f32[32,128]{1,0:T(8,128)} %get-tuple-element.27) | copy-start | bytes 49156
  369.6 8.3 %copy-start.13 = (f32[32,128]{1,0:T(8,128)S(1)}, f32[32,128]{1,0:T(8,128)}, u32[]{:S(2)}) copy-start(f32[32,128]{1,0:T(8,128)} %get-tuple-element.28) | copy-start | bytes 49156
  369.6 8.3 %copy-start.12 = (f32[32,128]{1,0:T(8,128)S(1)}, f32[32,128]{1,0:T(8,128)}, u32[]{:S(2)}) copy-start(f32[32,128]{1,0:T(8,128)} %get-tuple-element.29) | copy-start | bytes 49156
  369.6 8.3 %copy-start.11 = (f32[32,128]{1,0:T(8,128)S(1)}, f32[32,128]{1,0:T(8,128)}, u32[]{:S(2)}) copy-start(f32[32,128]{1,0:T(8,128)} %get-tuple-element.30) | copy-start | bytes 49156
  371.0 0.7 copy-start.9
Sparse Core Ops, SparseCore 0:
  15.0 170.7 all-gather.4
  187.6 143.1 all-gather.6

commit v3 on v2

--- a/solution.py
+++ b/solution.py
@@ -9,7 +9,8 @@
 from jax.sharding import PartitionSpec as P
 
 LEVELS = 8
-NATIVE = 3
+NATIVE = 2
+FAR_STEPS = 2
 PER_ROW = 4
 SUB = 8
 BF16 = jnp.bfloat16
@@ -17,7 +18,7 @@
 HIGHEST = lax.Precision.HIGHEST
 COL = ("grp", "sub")
 ALL = ("row", "grp", "sub")
-CHUNKS = ((6, 5, 4, 3, 2), (1, 0))
+CHUNKS = ((6, 5, 4, 3), (2, 1), (0,))
 
 
 def exchange(pieces, axis):
@@ -28,55 +29,51 @@
     return exchange(jnp.broadcast_to(piece[None], (count,) + piece.shape), axis)
 
 
-def times_column(x_ref, g_ref, row):
-    x = jnp.concatenate([x_ref[a, row] for a in range(PER_ROW)], axis=1)
-    g = g_ref[0].reshape(-1, g_ref.shape[-1])
+def times_column(x_ref, g_ref, rows):
+    x = jnp.concatenate([x_ref[a, r] for r in rows for a in range(PER_ROW)], axis=1)
+    g = g_ref[...].reshape(-1, g_ref.shape[-1])
     return jnp.dot(x, g, preferred_element_type=F32)
 
 
 def far_kernel(count, *refs):
-    x_refs, g_refs, out_ref = refs[:count], refs[count : 2 * count], refs[2 * count]
-    row = pl.program_id(0)
-
-    @pl.when(row == 0)
-    def _():
-        out_ref[...] = jnp.zeros_like(out_ref)
-
-    out_ref[...] += sum(times_column(x, g, row) for x, g in zip(x_refs, g_refs))
-
-
-def near_kernel(x_ref, g_ref, rest_ref, inverse_ref, out_ref, low_ref, acc_ref):
-    row = pl.program_id(0)
-
-    @pl.when(row == 0)
-    def _():
-        acc_ref[...] = rest_ref[...]
-
-    acc_ref[...] -= times_column(x_ref, g_ref, row)
-
-    @pl.when(row == pl.num_programs(0) - 1)
-    def _():
-        solved = jnp.dot(
-            acc_ref[...], inverse_ref[...], precision=HIGHEST, preferred_element_type=F32
-        )
-        out_ref[...] = solved
-        low_ref[...] = jnp.broadcast_to(solved.astype(BF16)[None], low_ref.shape)
+    y_ref, x_refs, g_refs, out_ref = refs[0], refs[1 : count + 1], refs[count + 1 : -1], refs[-1]
+    n_row = x_refs[0].shape[1]
+    step = n_row // FAR_STEPS
+    for s in range(FAR_STEPS):
+
+        @pl.when(pl.program_id(0) == s)
+        def _():
+            rows = range(s * step, (s + 1) * step)
+            got = sum(times_column(x, g, rows) for x, g in zip(x_refs, g_refs))
+            out_ref[...] = (y_ref[...] if s == 0 else out_ref[...]) - got
+
+
+def near_kernel(x_ref, g_ref, rest_ref, inverse_ref, out_ref, low_ref):
+    got = times_column(x_ref, g_ref, range(x_ref.shape[1]))
+    solved = jnp.dot(
+        rest_ref[...] - got, inverse_ref[...], precision=HIGHEST, preferred_element_type=F32
+    )
+    out_ref[...] = solved
+    low_ref[...] = jnp.broadcast_to(solved.astype(BF16)[None], low_ref.shape)
 
 
 def whole(shape):
-    return pl.BlockSpec(shape, lambda r: (0,) * len(shape))
-
-
-def column_spec(first, block):
-    return pl.BlockSpec((1, PER_ROW, block, block), lambda r: (r, first, 0, 0))
-
-
-def far_sums(xs, packed, firsts):
+    return pl.BlockSpec(shape, lambda s: (0,) * len(shape))
+
+
+def column_spec(rows, first, block):
+    return pl.BlockSpec((rows, PER_ROW, block, block), lambda s: (s, first, 0, 0))
+
+
+def far_rest(y, xs, packed, firsts):
     n_row, part, block = xs[0].shape[1:]
+    step = n_row // FAR_STEPS
     return pl.pallas_call(
         functools.partial(far_kernel, len(xs)),
-        grid=(n_row,),
-        in_specs=[whole(x.shape) for x in xs] + [column_spec(f, block) for f in firsts],
+        grid=(FAR_STEPS,),
+        in_specs=[whole(y.shape)]
+        + [whole(x.shape) for x in xs]
+        + [column_spec(step, f, block) for f in firsts],
         out_specs=whole((part, block)),
         out_shape=jax.ShapeDtypeStruct((part, block), F32),
         cost_estimate=pl.CostEstimate(
@@ -84,18 +81,18 @@
             bytes_accessed=2 * len(xs) * n_row * PER_ROW * block * block,
             transcendentals=0,
         ),
-        name="far_sums",
-    )(*xs, *([packed] * len(xs)))
+        name="far_rest",
+    )(y, *xs, *([packed] * len(xs)))
 
 
 def near_solve(x, packed, first, rest, inverse, n_col):
     n_row, part, block = x.shape[1:]
     return pl.pallas_call(
         near_kernel,
-        grid=(n_row,),
+        grid=(1,),
         in_specs=[
             whole(x.shape),
-            column_spec(first, block),
+            column_spec(n_row, first, block),
             whole(rest.shape),
             whole(inverse.shape),
         ],
@@ -104,7 +101,6 @@
             jax.ShapeDtypeStruct((part, block), F32),
             jax.ShapeDtypeStruct((n_col, part, block), BF16),
         ],
-        scratch_shapes=[pltpu.VMEM((part, block), F32)],
         cost_estimate=pl.CostEstimate(
             flops=2 * n_row * PER_ROW * part * block * block,
             bytes_accessed=2 * n_row * PER_ROW * block * block,
@@ -126,14 +122,31 @@
     inverse = block_inverse[:, 0]
     loads_t = jnp.swapaxes(loads[:, 0], 1, 2)
 
-    columns = []
-    for j in range(LEVELS - 1):
+    def forward_solve(level, resid):
+        return lax.dot_general(
+            resid, inverse[level], (((1,), (1,)), ((), ())), precision=HIGHEST
+        )
+
+    def backward_solve(level, resid):
+        return lax.dot_general(
+            resid, inverse[level], (((1,), (0,)), ((), ())), precision=HIGHEST
+        )
+
+    solved = [forward_solve(0, loads_t[0])]
+    low = [solved[0].astype(BF16)]
+
+    flags = pattern[:, 0, :, 0].astype(BF16)
+    flags_after, low[0] = lax.optimization_barrier((flags, low[0]))
+
+    def column(j, flags):
         rows = slice((j + 1) * PER_ROW, LEVELS * PER_ROW)
-        mask = pattern[rows, 0, j, 0].astype(BF16)[:, None, None]
-        columns.append(factor[rows, 0, j, 0] * mask)
+        return factor[rows, 0, j, 0] * flags[rows, j][:, None, None]
+
+    columns = [column(j, flags) for j in range(LEVELS - 1)]
     gathered, where = [None] * LEVELS, [None] * LEVELS
     for chunk in CHUNKS:
-        packed = jnp.concatenate([columns[j] for j in chunk], axis=0)
+        use = flags if chunk is CHUNKS[0] else flags_after
+        packed = jnp.concatenate([column(j, use) for j in chunk], axis=0)
         packed = lax.all_gather(packed, "row", axis=0)
         at = 0
         for j in chunk:
@@ -148,24 +161,12 @@
         at = (where[m] + t - m - 1) * PER_ROW
         return gathered[m][:, at : at + PER_ROW]
 
-    def forward_solve(level, resid):
-        return lax.dot_general(
-            resid, inverse[level], (((1,), (1,)), ((), ())), precision=HIGHEST
-        )
-
-    def backward_solve(level, resid):
-        return lax.dot_general(
-            resid, inverse[level], (((1,), (0,)), ((), ())), precision=HIGHEST
-        )
-
     def local_sums(t, count):
         return sum(
             jnp.einsum("sq,apq->asp", low[m], local(t, m), preferred_element_type=F32)
             for m in range(count)
         ).astype(BF16)
 
-    solved = [forward_solve(0, loads_t[0])]
-    low = [solved[0].astype(BF16)]
     for t in range(1, NATIVE + 1):
         pieces = local_sums(t, t).reshape(n_col, part, block)
         total = jnp.sum(exchange(pieces, COL).astype(F32), axis=0).astype(BF16)
@@ -211,7 +212,8 @@
     for j in reversed(range(LEVELS - 1)):
         rest = solved[j]
         if later:
-            rest = rest - far_sums(
+            rest = far_rest(
+                rest,
                 [x for _, x in later],
                 gathered[j],
                 [where[j] + t - j - 1 for t, _ in later],

time: 415 us -> 383 us (0.923)
  Pallas kernels: 75.5 us -> 37.8 us
  waiting for transfers between devices: 70.5 us -> 98.6 us
  starting transfers between devices: 108 us -> 93.5 us
  other arithmetic: 22 us -> 14.9 us
    pallas_call x13, Pallas kernels: 75.5 us -> 37.8 us  [the longest x6 20.1 us: far_rest(): pl.pallas_call(functools.partial(far_kernel, len(xs)), grid=(FAR_STEPS,),...]
    all_gather x2 -> x3, waiting for transfers between devices: 2.27 us -> 27.3 us  [per_device(): packed = lax.all_gather(packed, 'row', axis=0)]
    all_to_all x18 -> x16, starting transfers between devices: 105 us -> 90.2 us  [exchange(): return lax.all_to_all(pieces, axis, 0, 0, tiled=True)]
    sub x6 -> x0, other arithmetic: 8.02 us -> none  [per_device(): rest - far_sums([x for _, x in later], gathered[j], [where[j] + t - j - 1...]
    mul x2 -> x8, other arithmetic: 2.57 us -> 10.3 us  [column(): return factor[rows, 0, j, 0] * flags[rows, j][:, None, None]]
    dot_general x22 -> x18, matrix products: 29.5 us -> 21.8 us  [local_sums(): jnp.einsum('sq,apq->asp', low[m], local(t, m), preferred_element_type=F32)]
    dot_general x6 -> x10, matrix products: 10.2 us -> 17 us  [per_device(): jnp.einsum('sq,rapq->arsp', low[m], split(t, m), preferred_element_type=F32)]
    unnamed x11 -> x7, other arithmetic: 5.34 us -> 0.78 us
  transfers between devices with their start and end apart: 21 -> 20, of which waited for: 17 -> 16; matrix products, arithmetic and copies ran while one was open for 17% -> 17% of each run, Pallas kernels for 16% -> 9%
where the time goes in v3:
time: 383 us; the launch traced here: 380 us
  waiting for transfers between devices  98.6 us (26%)
  starting transfers between devices  93.5 us (24%)
  blocking collectives  57.5 us (15%)
  matrix products  43.4 us (11%)
  Pallas kernels  37.8 us (10%)
  local copies, waits for them, and re-layouts  20.6 us (5%)
  other arithmetic  14.9 us (4%)
  between operations  13.7 us (4%)
    all_to_all x16, starting transfers between devices, exchange(): return lax.all_to_all(pieces, axis, 0, 0, tiled=True)  90.2 us
    all_to_all x16, waiting for transfers between devices, exchange(): return lax.all_to_all(pieces, axis, 0, 0, tiled=True)  66.8 us
    all_to_all x3, blocking collectives, exchange(): return lax.all_to_all(pieces, axis, 0, 0, tiled=True)  57.5 us
    all_gather x3, waiting for transfers between devices, per_device(): packed = lax.all_gather(packed, 'row', axis=0)  27.3 us
    dot_general x18, matrix products, local_sums(): jnp.einsum('sq,apq->asp', low[m], local(t, m), preferred_element_type=F32)  21.8 us
    pallas_call x6, Pallas kernels, far_rest(): pl.pallas_call(functools.partial(far_kernel, len(xs)), grid=(FAR_STEPS,),...  20.1 us
    pallas_call x7, Pallas kernels, near_solve(): pl.pallas_call(near_kernel, grid=(1,), in_specs=[whole(x.shape), column_s...  17.6 us
    dot_general x10, matrix products, per_device(): jnp.einsum('sq,rapq->arsp', low[m], split(t, m), preferred_element_type=F32)  17 us
  transfers between devices with their start and end apart: 20, of which 16 were waited for; matrix products, arithmetic and copies ran while one was open for 17% of the time, Pallas kernels for 9%

profile of v3, /device:TPU:2, one launch (start us, length us, event | category | flops | bytes accessed | tf_op | source)
XLA Modules:
  0.0 379.9 jit_solution(12558374902928455155)
XLA Ops:
  13.2 1.6 copy.27
  22.0 7.6 %all-to-all-start = ((bf16[32,32,128]{2,1,0:T(8,128)(2,1)}), bf16[32,32,128]{2,1,0:T(8,128)(2,1)S(1)}, u32[]{:S(2)}, u32[]{:S(2)}) async-start(bf16[32,32,128]{2,1,0:T(8,128)(2,1)} %bitcast.11), calls=%async_computation | async-start | bytes 524288 | tf_op jit(solution)/shard_map/all_to_all | solution.py:25
  29.8 2.2 bitcast_multiply_fusion
  38.1 8.5 %all-to-all-start.1 = ((bf16[8,32,128]{2,1,0:T(8,128)(2,1)}), bf16[8,32,128]{2,1,0:T(8,128)(2,1)}, u32[]{:S(2)}, u32[]{:S(2)}) async-start(bf16[8,32,128]{2,1,0:T(8,128)(2,1)} %broadcast_in_dim.8), calls=%async_computation.1 | async-start | bytes 131072 | tf_op jit(solution)/shard_map/all_to_all | solution.py:25
  46.7 9.3 %all-to-all-done.1 = bf16[8,32,128]{2,1,0:T(8,128)(2,1)} async-done(((bf16[8,32,128]{2,1,0:T(8,128)(2,1)}), bf16[8,32,128]{2,1,0:T(8,128)(2,1)}, u32[]{:S(2)}, u32[]{:S(2)}) %all-to-all-start.1) | async-done | bytes 65568 | tf_op jit(solution)/shard_map/all_to_all | solution.py:25
  56.0 4.7 %all-to-all-start.2 = ((bf16[8,32,128]{2,1,0:T(8,128)(2,1)}), bf16[8,32,128]{2,1,0:T(8,128)(2,1)S(1)}, u32[]{:S(2)}, u32[]{:S(2)}) async-start(bf16[8,32,128]{2,1,0:T(8,128)(2,1)} %all-to-all-done.1), calls=%async_computation.2 | async-start | bytes 131072 | tf_op jit(solution)/shard_map/all_to_all | solution.py:25
  60.8 4.1 %all-to-all-done.2 = bf16[8,32,128]{2,1,0:T(8,128)(2,1)S(1)} async-done(((bf16[8,32,128]{2,1,0:T(8,128)(2,1)}), bf16[8,32,128]{2,1,0:T(8,128)(2,1)S(1)}, u32[]{:S(2)}, u32[]{:S(2)}) %all-to-all-start.2) | async-done | bytes 65568 | tf_op jit(solution)/shard_map/all_to_all | solution.py:25
  67.8 6.5 %all-to-all-start.3 = ((bf16[32,32,128]{2,1,0:T(8,128)(2,1)}), bf16[32,32,128]{2,1,0:T(8,128)(2,1)S(1)}, u32[]{:S(2)}, u32[]{:S(2)}) async-start(bf16[32,32,128]{2,1,0:T(8,128)(2,1)} %bitcast.19), calls=%async_computation.3 | async-start | bytes 524288 | tf_op jit(solution)/shard_map/all_to_all | solution.py:25
  78.5 3.5 all-to-all-done.3
  82.7 4.0 %all-to-all-start.4 = ((bf16[8,32,128]{2,1,0:T(8,128)(2,1)}), bf16[8,32,128]{2,1,0:T(8,128)(2,1)}, u32[]{:S(2)}, u32[]{:S(2)}) async-start(bf16[8,32,128]{2,1,0:T(8,128)(2,1)} %broadcast_in_dim.9), calls=%async_computation.4 | async-start | bytes 131072 | tf_op jit(solution)/shard_map/all_to_all | solution.py:25
  86.7 2.2 convolution_add_fusion.9
  88.9 7.2 %all-to-all-done.4 = bf16[8,32,128]{2,1,0:T(8,128)(2,1)} async-done(((bf16[8,32,128]{2,1,0:T(8,128)(2,1)}), bf16[8,32,128]{2,1,0:T(8,128)(2,1)}, u32[]{:S(2)}, u32[]{:S(2)}) %all-to-all-start.4) | async-done | bytes 65568 | tf_op jit(solution)/shard_map/all_to_all | solution.py:25
  96.1 4.6 %all-to-all-start.5 = ((bf16[8,32,128]{2,1,0:T(8,128)(2,1)}), bf16[8,32,128]{2,1,0:T(8,128)(2,1)S(1)}, u32[]{:S(2)}, u32[]{:S(2)}) async-start(bf16[8,32,128]{2,1,0:T(8,128)(2,1)} %all-to-all-done.4), calls=%async_computation.5 | async-start | bytes 131072 | tf_op jit(solution)/shard_map/all_to_all | solution.py:25
  100.7 2.2 convolution_add_fusion.7
  102.9 2.0 all-to-all-done.5
  110.0 1.4 fusion.10
  113.6 23.4 %all_to_all.95 = bf16[32,5,32,128]{3,2,1,0:T(8,128)(2,1)S(1)} all-to-all(bf16[32,5,32,128]{3,2,1,0:T(8,128)(2,1)S(1)} %copy.38), channel_id=1, replica_groups=mesh['row'=8,'grp'=4,'sub'=8] {'grp','sub'}, dimensions={0} | all-to-all | bytes 2621440 | tf_op jit(solution)/shard_map/all_to_all | solution.py:25
  137.2 3.2 collective-permute-start
  140.5 4.5 %collective-permute-done = bf16[5,32,128]{2,1,0:T(8,128)(2,1)S(1)} collective-permute-done((bf16[5,32,128]{2,1,0:T(8,128)(2,1)S(1)}, bf16[5,32,128]{2,1,0:T(8,128)(2,1)S(1)}, u32[]{:S(2)}, u32[]{:S(2)}) %collective-permute-start) | collective-permute-done | bytes 40992 | tf_op jit(solution)/shard_map/ppermute | solution.py:189
  145.7 1.7 fusion.16
  148.2 9.4 %all-to-all-start.7 = ((bf16[32,32,128]{2,1,0:T(8,128)(2,1)}), bf16[32,32,128]{2,1,0:T(8,128)(2,1)S(1)}, u32[]{:S(2)}, u32[]{:S(2)}) async-start(bf16[32,32,128]{2,1,0:T(8,128)(2,1)} %bitcast.49), calls=%async_computation.7 | async-start | bytes 524288 | tf_op jit(solution)/shard_map/all_to_all | solution.py:25
  157.5 1.7 fusion.96
  159.2 1.7 fusion.93
  160.9 1.7 fusion.91
  162.6 2.6 all-to-all-done.7
  165.5 1.7 fusion.19
  168.0 5.0 %all-to-all-start.8 = ((bf16[32,32,128]{2,1,0:T(8,128)(2,1)}), bf16[32,32,128]{2,1,0:T(8,128)(2,1)S(1)}, u32[]{:S(2)}, u32[]{:S(2)}) async-start(bf16[32,32,128]{2,1,0:T(8,128)(2,1)} %bitcast.57), calls=%async_computation.8 | async-start | bytes 524288 | tf_op jit(solution)/shard_map/all_to_all | solution.py:25
  172.9 1.7 convolution_add_fusion.5
  174.6 1.7 convolution_add_fusion.2
  176.3 4.4 %all-to-all-done.8 = bf16[32,32,128]{2,1,0:T(8,128)(2,1)S(1)} async-done(((bf16[32,32,128]{2,1,0:T(8,128)(2,1)}), bf16[32,32,128]{2,1,0:T(8,128)(2,1)S(1)}, u32[]{:S(2)}, u32[]{:S(2)}) %all-to-all-start.8) | async-done | bytes 262176 | tf_op jit(solution)/shard_map/all_to_all | solution.py:25
  181.0 1.7 fusion.18
  183.4 5.0 %all-to-all-start.9 = ((bf16[32,32,128]{2,1,0:T(8,128)(2,1)}), bf16[32,32,128]{2,1,0:T(8,128)(2,1)S(1)}, u32[]{:S(2)}, u32[]{:S(2)}) async-start(bf16[32,32,128]{2,1,0:T(8,128)(2,1)} %bitcast.65), calls=%async_computation.9 | async-start | bytes 524288 | tf_op jit(solution)/shard_map/all_to_all | solution.py:25
  188.4 1.7 convolution_add_fusion.3
  190.1 6.1 %all-to-all-done.9 = bf16[32,32,128]{2,1,0:T(8,128)(2,1)S(1)} async-done(((bf16[32,32,128]{2,1,0:T(8,128)(2,1)}), bf16[32,32,128]{2,1,0:T(8,128)(2,1)S(1)}, u32[]{:S(2)}, u32[]{:S(2)}) %all-to-all-start.9) | async-done | bytes 262176 | tf_op jit(solution)/shard_map/all_to_all | solution.py:25
  196.5 1.7 fusion.17
  198.2 12.4 %all_to_all.96 = bf16[32,32,128]{2,1,0:T(8,128)(2,1)S(1)} all-to-all(bf16[32,32,128]{2,1,0:T(8,128)(2,1)S(1)} %bitcast.378), channel_id=1, replica_groups=mesh['row'=8,'grp'=4,'sub'=8] {'grp','sub'}, dimensions={0} | all-to-all | bytes 524288 | tf_op jit(solution)/shard_map/all_to_all | solution.py:25
  211.8 5.0 %all-to-all-start.11 = ((bf16[32,32,128]{2,1,0:T(8,128)(2,1)}), bf16[32,32,128]{2,1,0:T(8,128)(2,1)S(1)}, u32[]{:S(2)}, u32[]{:S(2)}) async-start(bf16[32,32,128]{2,1,0:T(8,128)(2,1)} %broadcast_in_dim.10), calls=%async_computation.11 | async-start | bytes 524288 | tf_op jit(solution)/shard_map/all_to_all | solution.py:25
  217.6 7.0 %all-to-all-done.11 = bf16[32,32,128]{2,1,0:T(8,128)(2,1)S(1)} async-done(((bf16[32,32,128]{2,1,0:T(8,128)(2,1)}), bf16[32,32,128]{2,1,0:T(8,128)(2,1)S(1)}, u32[]{:S(2)}, u32[]{:S(2)}) %all-to-all-start.11) | async-done | bytes 262176 | tf_op jit(solution)/shard_map/all_to_all | solution.py:25
  225.3 2.5 near_solve.7
  227.8 5.0 %all-to-all-start.12 = ((bf16[32,32,128]{2,1,0:T(8,128)(2,1)}), bf16[32,32,128]{2,1,0:T(8,128)(2,1)S(1)}, u32[]{:S(2)}, u32[]{:S(2)}) async-start(bf16[32,32,128]{2,1,0:T(8,128)(2,1)} %get-tuple-element.21), calls=%async_computation.12 | async-start | bytes 524288 | tf_op jit(solution)/shard_map/all_to_all | solution.py:25
  232.8 2.2 far_rest.6.rest_ref
  235.0 5.6 %all-to-all-done.12 = bf16[32,32,128]{2,1,0:T(8,128)(2,1)S(1)} async-done(((bf16[32,32,128]{2,1,0:T(8,128)(2,1)}), bf16[32,32,128]{2,1,0:T(8,128)(2,1)S(1)}, u32[]{:S(2)}, u32[]{:S(2)}) %all-to-all-start.12) | async-done | bytes 262176 | tf_op jit(solution)/shard_map/all_to_all | solution.py:25
  241.3 2.5 near_solve.8
  243.9 5.0 %all-to-all-start.13 = ((bf16[32,32,128]{2,1,0:T(8,128)(2,1)}), bf16[32,32,128]{2,1,0:T(8,128)(2,1)S(1)}, u32[]{:S(2)}, u32[]{:S(2)}) async-start(bf16[32,32,128]{2,1,0:T(8,128)(2,1)} %get-tuple-element.22), calls=%async_computation.13 | async-start | bytes 524288 | tf_op jit(solution)/shard_map/all_to_all | solution.py:25
  248.9 2.6 far_rest.7.rest_ref
  251.5 5.2 %all-to-all-done.13 = bf16[32,32,128]{2,1,0:T(8,128)(2,1)S(1)} async-done(((bf16[32,32,128]{2,1,0:T(8,128)(2,1)}), bf16[32,32,128]{2,1,0:T(8,128)(2,1)S(1)}, u32[]{:S(2)}, u32[]{:S(2)}) %all-to-all-start.13) | async-done | bytes 262176 | tf_op jit(solution)/shard_map/all_to_all | solution.py:25
  257.4 2.5 near_solve.9
  259.9 5.0 %all-to-all-start.14 = ((bf16[32,32,128]{2,1,0:T(8,128)(2,1)}), bf16[32,32,128]{2,1,0:T(8,128)(2,1)S(1)}, u32[]{:S(2)}, u32[]{:S(2)}) async-start(bf16[32,32,128]{2,1,0:T(8,128)(2,1)} %get-tuple-element.23), calls=%async_computation.14 | async-start | bytes 524288 | tf_op jit(solution)/shard_map/all_to_all | solution.py:25
  264.9 3.1 far_rest.8.rest_ref
  268.0 4.7 %all-to-all-done.14 = bf16[32,32,128]{2,1,0:T(8,128)(2,1)S(1)} async-done(((bf16[32,32,128]{2,1,0:T(8,128)(2,1)}), bf16[32,32,128]{2,1,0:T(8,128)(2,1)S(1)}, u32[]{:S(2)}, u32[]{:S(2)}) %all-to-all-start.14) | async-done | bytes 262176 | tf_op jit(solution)/shard_map/all_to_all | solution.py:25
  273.4 2.5 near_solve.10
  275.9 5.0 %all-to-all-start.15 = ((bf16[32,32,128]{2,1,0:T(8,128)(2,1)}), bf16[32,32,128]{2,1,0:T(8,128)(2,1)S(1)}, u32[]{:S(2)}, u32[]{:S(2)}) async-start(bf16[32,32,128]{2,1,0:T(8,128)(2,1)} %get-tuple-element.24), calls=%async_computation.15 | async-start | bytes 524288 | tf_op jit(solution)/shard_map/all_to_all | solution.py:25
  282.2 3.7 far_rest.9.rest_ref
  285.9 2.8 all-to-all-done.15
  289.4 2.5 near_solve.11
  291.9 5.0 %all-to-all-start.16 = ((bf16[32,32,128]{2,1,0:T(8,128)(2,1)}), bf16[32,32,128]{2,1,0:T(8,128)(2,1)S(1)}, u32[]{:S(2)}, u32[]{:S(2)}) async-start(bf16[32,32,128]{2,1,0:T(8,128)(2,1)} %get-tuple-element.26), calls=%async_computation.16 | async-start | bytes 524288 | tf_op jit(solution)/shard_map/all_to_all | solution.py:25
  298.2 4.1 %far_rest.10.rest_ref = f32[32,128]{1,0:T(8,128)} custom-call(f32[32,128]{1,0:T(8,128)} %constant_dynamic-slice_fusion.1.refs_0_, bf16[4,8,32,128]{3,2,1,0:T(8,128)(2,1)} %bitcast.346, bf16[4,8,32,128]{3,2,1,0:T(8,128)(2,1)} %bitcast.352, bf16[4,8,32,128]{3,2,1,0:T(8,128)(2,1)} %bitcast.357, bf16[4,8,32,128]{3,2,1,0:T(8,128)(2,1)} %bitcast.361, ...), custom_call_target="tpu_custom_call" | custom-call | flops 167772160 | bytes 5242880 | tf_op jit(solution)/shard_map/far_rest/pallas_call | solution.py:71
  302.3 2.4 all-to-all-done.16
  305.4 2.5 near_solve.12
  307.9 5.1 %all-to-all-start.17 = ((bf16[32,32,128]{2,1,0:T(8,128)(2,1)}), bf16[32,32,128]{2,1,0:T(8,128)(2,1)S(1)}, u32[]{:S(2)}, u32[]{:S(2)}) async-start(bf16[32,32,128]{2,1,0:T(8,128)(2,1)} %get-tuple-element.27), calls=%async_computation.17 | async-start | bytes 524288 | tf_op jit(solution)/shard_map/all_to_all | solution.py:25
  314.4 27.3 %all-gather.6.cloned.1.call-done.refs_7_.refs_8_.refs_9_.refs_10_.refs_11_.refs_12_.g_ref = bf16[8,28,128,128]{3,2,1,0:T(8,128)(2,1)} async-done(((bf16[1,28,128,128]{3,2,1,0:T(8,128)(2,1)}), bf16[8,28,128,128]{3,2,1,0:T(8,128)(2,1)}) %all-gather.6.cloned.1.call-update) | async-done | bytes 7340048 | tf_op jit(solution)/shard_map/all_gather | solution.py:150
  341.7 4.5 %far_rest.11.rest_ref = f32[32,128]{1,0:T(8,128)} custom-call(f32[32,128]{1,0:T(8,128)} %constant_dynamic-slice_fusion.refs_0_, bf16[4,8,32,128]{3,2,1,0:T(8,128)(2,1)} %bitcast.347, bf16[4,8,32,128]{3,2,1,0:T(8,128)(2,1)} %bitcast.353, bf16[4,8,32,128]{3,2,1,0:T(8,128)(2,1)} %bitcast.358, bf16[4,8,32,128]{3,2,1,0:T(8,128)(2,1)} %bitcast.362, ...), custom_call_target="tpu_custom_call" | custom-call | flops 201326592 | bytes 6291456 | tf_op jit(solution)/shard_map/far_rest/pallas_call | solution.py:71
  346.9 2.5 near_solve.13
  350.3 21.6 %all_to_all.97 = bf16[8,8,32,128]{3,2,1,0:T(8,128)(2,1)S(1)} all-to-all(bf16[8,8,32,128]{3,2,1,0:T(8,128)(2,1)S(1)} %broadcast_in_dim.11), channel_id=1, replica_groups=mesh['row'=8,'grp'=4,'sub'=8] {'row'}, dimensions={0} | all-to-all | bytes 1048576 | tf_op jit(solution)/shard_map/all_to_all | solution.py:25
  (133 shorter events, 52.4 us)
Async XLA Ops:
  6.5 8.2 %copy-start.6 = (f32[8,1,128,128]{3,2,1,0:T(8,128)S(1)}, f32[8,1,128,128]{3,2,1,0:T(8,128)}, u32[]{:S(2)}) copy-start(f32[8,1,128,128]{3,2,1,0:T(8,128)} %param.7) | copy-start | bytes 1572868
  6.5 139.2 %all-gather.8.cloned.1.call-start = ((), (), s32[]{:S(2)}) async-start(), calls=%async_computation.20 | async-start | bytes 11796480 | tf_op jit(solution)/shard_map/all_gather | solution.py:150
  13.2 269.0 %all-gather.10.cloned.1.call-start = ((), (), s32[]{:S(2)}) async-start(), calls=%async_computation.21 | async-start | bytes 12976128 | tf_op jit(solution)/shard_map/all_gather | solution.py:150
  22.0 15.4 %all-to-all-start = ((bf16[32,32,128]{2,1,0:T(8,128)(2,1)}), bf16[32,32,128]{2,1,0:T(8,128)(2,1)S(1)}, u32[]{:S(2)}, u32[]{:S(2)}) async-start(bf16[32,32,128]{2,1,0:T(8,128)(2,1)} %bitcast.11), calls=%async_computation | async-start | bytes 524288 | tf_op jit(solution)/shard_map/all_to_all | solution.py:25
  29.7 312.0 %all-gather.6.cloned.1.call-start = ((), (), s32[]{:S(2)}) async-start(), calls=%async_computation.19 | async-start | bytes 8257536 | tf_op jit(solution)/shard_map/all_gather | solution.py:150
  38.1 17.9 %all-to-all-start.1 = ((bf16[8,32,128]{2,1,0:T(8,128)(2,1)}), bf16[8,32,128]{2,1,0:T(8,128)(2,1)}, u32[]{:S(2)}, u32[]{:S(2)}) async-start(bf16[8,32,128]{2,1,0:T(8,128)(2,1)} %broadcast_in_dim.8), calls=%async_computation.1 | async-start | bytes 131072 | tf_op jit(solution)/shard_map/all_to_all | solution.py:25
  56.0 8.9 %all-to-all-start.2 = ((bf16[8,32,128]{2,1,0:T(8,128)(2,1)}), bf16[8,32,128]{2,1,0:T(8,128)(2,1)S(1)}, u32[]{:S(2)}, u32[]{:S(2)}) async-start(bf16[8,32,128]{2,1,0:T(8,128)(2,1)} %all-to-all-done.1), calls=%async_computation.2 | async-start | bytes 131072 | tf_op jit(solution)/shard_map/all_to_all | solution.py:25
  67.8 14.2 %all-to-all-start.3 = ((bf16[32,32,128]{2,1,0:T(8,128)(2,1)}), bf16[32,32,128]{2,1,0:T(8,128)(2,1)S(1)}, u32[]{:S(2)}, u32[]{:S(2)}) async-start(bf16[32,32,128]{2,1,0:T(8,128)(2,1)} %bitcast.19), calls=%async_computation.3 | async-start | bytes 524288 | tf_op jit(solution)/shard_map/all_to_all | solution.py:25
  82.7 13.4 %all-to-all-start.4 = ((bf16[8,32,128]{2,1,0:T(8,128)(2,1)}), bf16[8,32,128]{2,1,0:T(8,128)(2,1)}, u32[]{:S(2)}, u32[]{:S(2)}) async-start(bf16[8,32,128]{2,1,0:T(8,128)(2,1)} %broadcast_in_dim.9), calls=%async_computation.4 | async-start | bytes 131072 | tf_op jit(solution)/shard_map/all_to_all | solution.py:25
  96.1 8.8 %all-to-all-start.5 = ((bf16[8,32,128]{2,1,0:T(8,128)(2,1)}), bf16[8,32,128]{2,1,0:T(8,128)(2,1)S(1)}, u32[]{:S(2)}, u32[]{:S(2)}) async-start(bf16[8,32,128]{2,1,0:T(8,128)(2,1)} %all-to-all-done.4), calls=%async_computation.5 | async-start | bytes 131072 | tf_op jit(solution)/shard_map/all_to_all | solution.py:25
  137.2 7.7 %collective-permute-start = (bf16[5,32,128]{2,1,0:T(8,128)(2,1)S(1)}, bf16[5,32,128]{2,1,0:T(8,128)(2,1)S(1)}, u32[]{:S(2)}, u32[]{:S(2)}) collective-permute-start(bf16[5,32,128]{2,1,0:T(8,128)(2,1)S(1)} %reduce_sum.82), channel_id=1, source_target_pairs={{0,0},{1,32},{2,64},{3,96},{4,128},{5,160},{6,192},{7,224},{8,8},{... | collective-permute-start | bytes 122888 | tf_op jit(solution)/shard_map/ppermute | solution.py:189
  148.2 17.1 %all-to-all-start.7 = ((bf16[32,32,128]{2,1,0:T(8,128)(2,1)}), bf16[32,32,128]{2,1,0:T(8,128)(2,1)S(1)}, u32[]{:S(2)}, u32[]{:S(2)}) async-start(bf16[32,32,128]{2,1,0:T(8,128)(2,1)} %bitcast.49), calls=%async_computation.7 | async-start | bytes 524288 | tf_op jit(solution)/shard_map/all_to_all | solution.py:25
  165.5 32.7 %copy-start.8 = (f32[32,128]{1,0:T(8,128)}, f32[32,128]{1,0:T(8,128)S(1)}, u32[]{:S(2)}) copy-start(f32[32,128]{1,0:T(8,128)S(1)} %fusion.68.refs_0_) | copy-start | bytes 49156
  168.0 12.8 %all-to-all-start.8 = ((bf16[32,32,128]{2,1,0:T(8,128)(2,1)}), bf16[32,32,128]{2,1,0:T(8,128)(2,1)S(1)}, u32[]{:S(2)}, u32[]{:S(2)}) async-start(bf16[32,32,128]{2,1,0:T(8,128)(2,1)} %bitcast.57), calls=%async_computation.8 | async-start | bytes 524288 | tf_op jit(solution)/shard_map/all_to_all | solution.py:25
  181.0 46.9 %copy-start.9 = (f32[32,128]{1,0:T(8,128)}, f32[32,128]{1,0:T(8,128)S(1)}, u32[]{:S(2)}) copy-start(f32[32,128]{1,0:T(8,128)S(1)} %fusion.64.refs_0_) | copy-start | bytes 49156
  183.4 12.8 %all-to-all-start.9 = ((bf16[32,32,128]{2,1,0:T(8,128)(2,1)}), bf16[32,32,128]{2,1,0:T(8,128)(2,1)S(1)}, u32[]{:S(2)}, u32[]{:S(2)}) async-start(bf16[32,32,128]{2,1,0:T(8,128)(2,1)} %bitcast.65), calls=%async_computation.9 | async-start | bytes 524288 | tf_op jit(solution)/shard_map/all_to_all | solution.py:25
  196.4 28.2 %copy-start.10 = (f32[32,128]{1,0:T(8,128)}, f32[32,128]{1,0:T(8,128)S(1)}, u32[]{:S(2)}) copy-start(f32[32,128]{1,0:T(8,128)S(1)} %fusion.60.rest_ref) | copy-start | bytes 49156
  211.8 12.8 %all-to-all-start.11 = ((bf16[32,32,128]{2,1,0:T(8,128)(2,1)}), bf16[32,32,128]{2,1,0:T(8,128)(2,1)S(1)}, u32[]{:S(2)}, u32[]{:S(2)}) async-start(bf16[32,32,128]{2,1,0:T(8,128)(2,1)} %broadcast_in_dim.10), calls=%async_computation.11 | async-start | bytes 524288 | tf_op jit(solution)/shard_map/all_to_all | solution.py:25
  224.6 0.7 copy-start
  227.8 12.8 %all-to-all-start.12 = ((bf16[32,32,128]{2,1,0:T(8,128)(2,1)}), bf16[32,32,128]{2,1,0:T(8,128)(2,1)S(1)}, u32[]{:S(2)}, u32[]{:S(2)}) async-start(bf16[32,32,128]{2,1,0:T(8,128)(2,1)} %get-tuple-element.21), calls=%async_computation.12 | async-start | bytes 524288 | tf_op jit(solution)/shard_map/all_to_all | solution.py:25
  240.6 0.7 copy-start.1
  243.9 12.8 %all-to-all-start.13 = ((bf16[32,32,128]{2,1,0:T(8,128)(2,1)}), bf16[32,32,128]{2,1,0:T(8,128)(2,1)S(1)}, u32[]{:S(2)}, u32[]{:S(2)}) async-start(bf16[32,32,128]{2,1,0:T(8,128)(2,1)} %get-tuple-element.22), calls=%async_computation.13 | async-start | bytes 524288 | tf_op jit(solution)/shard_map/all_to_all | solution.py:25
  256.7 0.7 copy-start.2
  259.9 12.8 %all-to-all-start.14 = ((bf16[32,32,128]{2,1,0:T(8,128)(2,1)}), bf16[32,32,128]{2,1,0:T(8,128)(2,1)S(1)}, u32[]{:S(2)}, u32[]{:S(2)}) async-start(bf16[32,32,128]{2,1,0:T(8,128)(2,1)} %get-tuple-element.23), calls=%async_computation.14 | async-start | bytes 524288 | tf_op jit(solution)/shard_map/all_to_all | solution.py:25
  272.7 0.7 copy-start.3
  275.9 12.8 %all-to-all-start.15 = ((bf16[32,32,128]{2,1,0:T(8,128)(2,1)}), bf16[32,32,128]{2,1,0:T(8,128)(2,1)S(1)}, u32[]{:S(2)}, u32[]{:S(2)}) async-start(bf16[32,32,128]{2,1,0:T(8,128)(2,1)} %get-tuple-element.24), calls=%async_computation.15 | async-start | bytes 524288 | tf_op jit(solution)/shard_map/all_to_all | solution.py:25
  288.7 0.7 copy-start.4
  291.9 12.8 %all-to-all-start.16 = ((bf16[32,32,128]{2,1,0:T(8,128)(2,1)}), bf16[32,32,128]{2,1,0:T(8,128)(2,1)S(1)}, u32[]{:S(2)}, u32[]{:S(2)}) async-start(bf16[32,32,128]{2,1,0:T(8,128)(2,1)} %get-tuple-element.26), calls=%async_computation.16 | async-start | bytes 524288 | tf_op jit(solution)/shard_map/all_to_all | solution.py:25
  304.7 0.7 copy-start.5
  307.9 38.2 %all-to-all-start.17 = ((bf16[32,32,128]{2,1,0:T(8,128)(2,1)}), bf16[32,32,128]{2,1,0:T(8,128)(2,1)S(1)}, u32[]{:S(2)}, u32[]{:S(2)}) async-start(bf16[32,32,128]{2,1,0:T(8,128)(2,1)} %get-tuple-element.27), calls=%async_computation.17 | async-start | bytes 524288 | tf_op jit(solution)/shard_map/all_to_all | solution.py:25
  314.4 35.7 %copy-start.16 = (f32[32,128]{1,0:T(8,128)S(1)}, f32[32,128]{1,0:T(8,128)}, u32[]{:S(2)}) copy-start(f32[32,128]{1,0:T(8,128)} %get-tuple-element.29) | copy-start | bytes 49156
  314.4 35.7 %copy-start.15 = (f32[32,128]{1,0:T(8,128)S(1)}, f32[32,128]{1,0:T(8,128)}, u32[]{:S(2)}) copy-start(f32[32,128]{1,0:T(8,128)} %get-tuple-element.30) | copy-start | bytes 49156
  314.4 35.8 %copy-start.14 = (f32[32,128]{1,0:T(8,128)S(1)}, f32[32,128]{1,0:T(8,128)}, u32[]{:S(2)}) copy-start(f32[32,128]{1,0:T(8,128)} %get-tuple-element.31) | copy-start | bytes 49156
  314.4 35.8 %copy-start.13 = (f32[32,128]{1,0:T(8,128)S(1)}, f32[32,128]{1,0:T(8,128)}, u32[]{:S(2)}) copy-start(f32[32,128]{1,0:T(8,128)} %get-tuple-element.32) | copy-start | bytes 49156
  314.4 35.8 %copy-start.12 = (f32[32,128]{1,0:T(8,128)S(1)}, f32[32,128]{1,0:T(8,128)}, u32[]{:S(2)}) copy-start(f32[32,128]{1,0:T(8,128)} %get-tuple-element.33) | copy-start | bytes 49156
  314.4 35.8 %copy-start.11 = (f32[32,128]{1,0:T(8,128)S(1)}, f32[32,128]{1,0:T(8,128)}, u32[]{:S(2)}) copy-start(f32[32,128]{1,0:T(8,128)} %get-tuple-element.34) | copy-start | bytes 49156
  346.2 0.7 copy-start.7
Sparse Core Ops, SparseCore 0:
  13.3 119.5 all-gather.7
  134.7 122.2 all-gather.9
  258.7 82.8 all-gather.5

commit v4 on v3

--- a/solution.py
+++ b/solution.py
@@ -18,7 +18,13 @@
 HIGHEST = lax.Precision.HIGHEST
 COL = ("grp", "sub")
 ALL = ("row", "grp", "sub")
-CHUNKS = ((6, 5, 4, 3), (2, 1), (0,))
+CHUNKS = (
+    ((6, 7, 8), (5, 6, 8), (4, 5, 8), (3, 4, 8)),
+    ((2, 3, 5), (1, 2, 5)),
+    ((0, 1, 5),),
+)
+CROSS_FROM, CROSS_TO = 5, 3
+CROSS_STEPS = 4
 
 
 def exchange(pieces, axis):
@@ -46,6 +52,36 @@
             rows = range(s * step, (s + 1) * step)
             got = sum(times_column(x, g, rows) for x, g in zip(x_refs, g_refs))
             out_ref[...] = (y_ref[...] if s == 0 else out_ref[...]) - got
+
+
+def cross_kernel(x_ref, g_ref, out_ref):
+    x = jnp.concatenate([x_ref[a] for a in range(x_ref.shape[0])], axis=1)
+    for k in range(g_ref.shape[0]):
+        for j in range(g_ref.shape[1]):
+            g = g_ref[k, j].reshape(-1, g_ref.shape[-1])
+            out_ref[k, j] = jnp.dot(x, g, preferred_element_type=F32).astype(BF16)
+
+
+def cross_sums(x, g):
+    n_sub, count, depth, block, _ = g.shape
+    part = x.shape[1]
+    step = n_sub // CROSS_STEPS
+    return pl.pallas_call(
+        cross_kernel,
+        grid=(CROSS_STEPS,),
+        in_specs=[
+            whole(x.shape),
+            pl.BlockSpec((step, count, depth, block, block), lambda s: (s, 0, 0, 0, 0)),
+        ],
+        out_specs=pl.BlockSpec((step, count, part, block), lambda s: (s, 0, 0, 0)),
+        out_shape=jax.ShapeDtypeStruct((n_sub, count, part, block), BF16),
+        cost_estimate=pl.CostEstimate(
+            flops=2 * n_sub * count * depth * part * block * block,
+            bytes_accessed=2 * n_sub * count * depth * block * block,
+            transcendentals=0,
+        ),
+        name="cross_sums",
+    )(x, g)
 
 
 def near_kernel(x_ref, g_ref, rest_ref, inverse_ref, out_ref, low_ref):
@@ -138,28 +174,35 @@
     flags = pattern[:, 0, :, 0].astype(BF16)
     flags_after, low[0] = lax.optimization_barrier((flags, low[0]))
 
-    def column(j, flags):
-        rows = slice((j + 1) * PER_ROW, LEVELS * PER_ROW)
+    def column(j, first, end, flags):
+        rows = slice(first * PER_ROW, end * PER_ROW)
         return factor[rows, 0, j, 0] * flags[rows, j][:, None, None]
 
-    columns = [column(j, flags) for j in range(LEVELS - 1)]
-    gathered, where = [None] * LEVELS, [None] * LEVELS
-    for chunk in CHUNKS:
-        use = flags if chunk is CHUNKS[0] else flags_after
-        packed = jnp.concatenate([column(j, use) for j in chunk], axis=0)
+    columns = [column(j, j + 1, LEVELS, flags) for j in range(LEVELS - 1)]
+
+    def crossing():
+        blocks = [column(j, CROSS_FROM, LEVELS, flags_after) for j in range(CROSS_TO)]
+        return lax.all_gather(jnp.stack(blocks), "sub", axis=0)
+
+    place = {}
+    for at_chunk, chunk in enumerate(CHUNKS):
+        use = flags_after if at_chunk else flags
+        packed = jnp.concatenate([column(j, a, b, use) for j, a, b in chunk], axis=0)
         packed = lax.all_gather(packed, "row", axis=0)
         at = 0
-        for j in chunk:
-            size = columns[j].shape[0]
-            gathered[j], where[j] = packed, at // PER_ROW
-            at += size
+        for j, a, b in chunk:
+            for t in range(a, b):
+                place[t, j] = packed, at
+                at += 1
+        if at_chunk == 0:
+            crossed = crossing()
 
     def local(t, m):
         return columns[m][(t - m - 1) * PER_ROW : (t - m) * PER_ROW]
 
     def split(t, m):
-        at = (where[m] + t - m - 1) * PER_ROW
-        return gathered[m][:, at : at + PER_ROW]
+        packed, at = place[t, m]
+        return packed[:, at * PER_ROW : (at + 1) * PER_ROW]
 
     def local_sums(t, count):
         return sum(
@@ -211,16 +254,26 @@
     later = []
     for j in reversed(range(LEVELS - 1)):
         rest = solved[j]
-        if later:
+        if j < CROSS_TO:
+            rest = rest - cross[j]
+        far = [(t, x) for t, x in later if (t, j) in place]
+        if far:
             rest = far_rest(
-                rest,
-                [x for _, x in later],
-                gathered[j],
-                [where[j] + t - j - 1 for t, _ in later],
+                rest, [x for _, x in far], place[far[0][0], j][0], [place[t, j][1] for t, _ in far]
             )
         near = exchange(wide, COL).reshape(PER_ROW, n_row, part, block)
-        out[j], wide = near_solve(near, gathered[j], where[j], rest, inverse[j], n_col)
+        packed, at = place[j + 1, j]
+        out[j], wide = near_solve(near, packed, at, rest, inverse[j], n_col)
         later.append((j + 1, near))
+        if j + 1 == CROSS_FROM:
+            mine = [
+                lax.dynamic_index_in_dim(x, lax.axis_index("sub"), axis=1, keepdims=False)
+                for _, x in reversed(later)
+            ]
+            mine, wide = lax.optimization_barrier((jnp.concatenate(mine, axis=0), wide))
+            mine = lax.ppermute(mine, ALL, turn)
+            cross = exchange(cross_sums(mine, crossed), "row")
+            cross = lax.ppermute(jnp.sum(cross.astype(F32), axis=0), ALL, turn)
 
     both = spread(jnp.stack(out).astype(BF16), "row", n_row)
     return jnp.transpose(both, (1, 3, 0, 2)).reshape(LEVELS, 1, block, scen).astype(F32)

time: 383 us -> 408 us (1.065)
  starting transfers between devices: 93.5 us -> 104 us
  waiting for transfers between devices: 98.6 us -> 106 us
    all_to_all x16 -> x17, waiting for transfers between devices: 66.8 us -> 97.4 us  [exchange(): return lax.all_to_all(pieces, axis, 0, 0, tiled=True)]
    all_gather x3, waiting for transfers between devices: 27.3 us -> 0.02 us  [per_device(): packed = lax.all_gather(packed, 'row', axis=0)]
    pallas_call x0 -> x1, Pallas kernels: none -> 5.97 us  [cross_sums(): pl.pallas_call(cross_kernel, grid=(CROSS_STEPS,), in_specs=[whole(x.shape...]
    ppermute x0 -> x2, waiting for transfers between devices: none -> 5.22 us  [the longest x1 5.22 us: per_device(): mine = lax.ppermute(mine, ALL, turn)]
    ppermute x0 -> x2, starting transfers between devices: none -> 5.2 us  [the longest x1 3.08 us: per_device(): mine = lax.ppermute(mine, ALL, turn)]
    pallas_call x6, Pallas kernels: 20.1 us -> 15.8 us  [far_rest(): pl.pallas_call(functools.partial(far_kernel, len(xs)), grid=(FAR_STEPS,),...]
    all_to_all x16 -> x17, starting transfers between devices: 90.2 us -> 94.3 us  [exchange(): return lax.all_to_all(pieces, axis, 0, 0, tiled=True)]
    mul x8 -> x7, other arithmetic: 10.3 us -> 9.27 us  [column(): return factor[rows, 0, j, 0] * flags[rows, j][:, None, None]]
  transfers between devices with their start and end apart: 20 -> 24, of which waited for: 16 -> 19; matrix products, arithmetic and copies ran while one was open for 17% -> 16% of each run, Pallas kernels for 9% -> 9%
where the time goes in v4:
time: 408 us; the launch traced here: 403 us
  waiting for transfers between devices  106 us (26%)
  starting transfers between devices  104 us (25%)
  blocking collectives  58.2 us (14%)
  matrix products  44 us (11%)
  Pallas kernels  39.3 us (10%)
  local copies, waits for them, and re-layouts  22 us (5%)
  other arithmetic  16 us (4%)
  between operations  13.8 us (3%)
    all_to_all x17, waiting for transfers between devices, exchange(): return lax.all_to_all(pieces, axis, 0, 0, tiled=True)  97.4 us
    all_to_all x17, starting transfers between devices, exchange(): return lax.all_to_all(pieces, axis, 0, 0, tiled=True)  94.3 us
    all_to_all x3, blocking collectives, exchange(): return lax.all_to_all(pieces, axis, 0, 0, tiled=True)  58.2 us
    dot_general x18, matrix products, local_sums(): jnp.einsum('sq,apq->asp', low[m], local(t, m), preferred_element_type=F32)  21.6 us
    pallas_call x7, Pallas kernels, near_solve(): pl.pallas_call(near_kernel, grid=(1,), in_specs=[whole(x.shape), column_s...  17.6 us
    dot_general x10, matrix products, per_device(): jnp.einsum('sq,rapq->arsp', low[m], split(t, m), preferred_element_type=F32)  17 us
    pallas_call x6, Pallas kernels, far_rest(): pl.pallas_call(functools.partial(far_kernel, len(xs)), grid=(FAR_STEPS,),...  15.8 us
    mul x7, other arithmetic, column(): return factor[rows, 0, j, 0] * flags[rows, j][:, None, None]  9.27 us
  transfers between devices with their start and end apart: 24, of which 19 were waited for; matrix products, arithmetic and copies ran while one was open for 16% of the time, Pallas kernels for 9%

profile of v4, /device:TPU:2, one launch (start us, length us, event | category | flops | bytes accessed | tf_op | source)
XLA Modules:
  0.0 403.4 jit_solution(13922318516794377624)
XLA Ops:
  8.9 1.8 fusion.113
  22.9 7.6 %all-to-all-start = ((bf16[32,32,128]{2,1,0:T(8,128)(2,1)}), bf16[32,32,128]{2,1,0:T(8,128)(2,1)S(1)}, u32[]{:S(2)}, u32[]{:S(2)}) async-start(bf16[32,32,128]{2,1,0:T(8,128)(2,1)} %bitcast.11), calls=%async_computation | async-start | bytes 524288 | tf_op jit(solution)/shard_map/all_to_all | solution.py:31
  35.9 2.3 all-to-all-done
  38.9 8.5 %all-to-all-start.1 = ((bf16[8,32,128]{2,1,0:T(8,128)(2,1)}), bf16[8,32,128]{2,1,0:T(8,128)(2,1)}, u32[]{:S(2)}, u32[]{:S(2)}) async-start(bf16[8,32,128]{2,1,0:T(8,128)(2,1)} %broadcast_in_dim.8), calls=%async_computation.1 | async-start | bytes 131072 | tf_op jit(solution)/shard_map/all_to_all | solution.py:31
  47.5 9.3 %all-to-all-done.1 = bf16[8,32,128]{2,1,0:T(8,128)(2,1)} async-done(((bf16[8,32,128]{2,1,0:T(8,128)(2,1)}), bf16[8,32,128]{2,1,0:T(8,128)(2,1)}, u32[]{:S(2)}, u32[]{:S(2)}) %all-to-all-start.1) | async-done | bytes 65568 | tf_op jit(solution)/shard_map/all_to_all | solution.py:31
  56.8 4.6 %all-to-all-start.2 = ((bf16[8,32,128]{2,1,0:T(8,128)(2,1)}), bf16[8,32,128]{2,1,0:T(8,128)(2,1)S(1)}, u32[]{:S(2)}, u32[]{:S(2)}) async-start(bf16[8,32,128]{2,1,0:T(8,128)(2,1)} %all-to-all-done.1), calls=%async_computation.2 | async-start | bytes 131072 | tf_op jit(solution)/shard_map/all_to_all | solution.py:31
  61.5 4.1 %all-to-all-done.2 = bf16[8,32,128]{2,1,0:T(8,128)(2,1)S(1)} async-done(((bf16[8,32,128]{2,1,0:T(8,128)(2,1)}), bf16[8,32,128]{2,1,0:T(8,128)(2,1)S(1)}, u32[]{:S(2)}, u32[]{:S(2)}) %all-to-all-start.2) | async-done | bytes 65568 | tf_op jit(solution)/shard_map/all_to_all | solution.py:31
  68.6 5.0 %all-to-all-start.3 = ((bf16[32,32,128]{2,1,0:T(8,128)(2,1)}), bf16[32,32,128]{2,1,0:T(8,128)(2,1)S(1)}, u32[]{:S(2)}, u32[]{:S(2)}) async-start(bf16[32,32,128]{2,1,0:T(8,128)(2,1)} %bitcast.19), calls=%async_computation.3 | async-start | bytes 524288 | tf_op jit(solution)/shard_map/all_to_all | solution.py:31
  77.8 3.6 all-to-all-done.3
  82.1 4.0 all-to-all-start.4
  86.1 2.2 convolution_add_fusion.9
  88.3 7.2 %all-to-all-done.4 = bf16[8,32,128]{2,1,0:T(8,128)(2,1)} async-done(((bf16[8,32,128]{2,1,0:T(8,128)(2,1)}), bf16[8,32,128]{2,1,0:T(8,128)(2,1)}, u32[]{:S(2)}, u32[]{:S(2)}) %all-to-all-start.4) | async-done | bytes 65568 | tf_op jit(solution)/shard_map/all_to_all | solution.py:31
  95.5 4.6 %all-to-all-start.5 = ((bf16[8,32,128]{2,1,0:T(8,128)(2,1)}), bf16[8,32,128]{2,1,0:T(8,128)(2,1)S(1)}, u32[]{:S(2)}, u32[]{:S(2)}) async-start(bf16[8,32,128]{2,1,0:T(8,128)(2,1)} %all-to-all-done.4), calls=%async_computation.5 | async-start | bytes 131072 | tf_op jit(solution)/shard_map/all_to_all | solution.py:31
  100.1 2.2 convolution_add_fusion.7
  102.3 2.0 all-to-all-done.5
  115.2 5.0 %all-to-all-start.6 = ((bf16[32,5,32,128]{3,2,1,0:T(8,128)(2,1)}), bf16[32,5,32,128]{3,2,1,0:T(8,128)(2,1)S(1)}, u32[]{:S(2)}, u32[]{:S(2)}) async-start(bf16[32,5,32,128]{3,2,1,0:T(8,128)(2,1)} %copy.50), calls=%async_computation.6 | async-start | bytes 2621440 | tf_op jit(solution)/shard_map/all_to_all | solution.py:31
  120.4 2.0 bitcast_multiply_fusion.3
  122.4 16.9 %all-to-all-done.6 = bf16[32,5,32,128]{3,2,1,0:T(8,128)(2,1)S(1)} async-done(((bf16[32,5,32,128]{3,2,1,0:T(8,128)(2,1)}), bf16[32,5,32,128]{3,2,1,0:T(8,128)(2,1)S(1)}, u32[]{:S(2)}, u32[]{:S(2)}) %all-to-all-start.6) | async-done | bytes 1310752 | tf_op jit(solution)/shard_map/all_to_all | solution.py:31
  139.5 3.9 collective-permute-start
  143.5 3.7 collective-permute-done
  148.0 1.8 fusion.16
  150.5 9.2 %all-to-all-start.7 = ((bf16[32,32,128]{2,1,0:T(8,128)(2,1)}), bf16[32,32,128]{2,1,0:T(8,128)(2,1)S(1)}, u32[]{:S(2)}, u32[]{:S(2)}) async-start(bf16[32,32,128]{2,1,0:T(8,128)(2,1)} %bitcast.49), calls=%async_computation.7 | async-start | bytes 524288 | tf_op jit(solution)/shard_map/all_to_all | solution.py:31
  161.5 1.7 fusion.96
  164.9 5.7 %all-to-all-done.7 = bf16[32,32,128]{2,1,0:T(8,128)(2,1)S(1)} async-done(((bf16[32,32,128]{2,1,0:T(8,128)(2,1)}), bf16[32,32,128]{2,1,0:T(8,128)(2,1)S(1)}, u32[]{:S(2)}, u32[]{:S(2)}) %all-to-all-start.7) | async-done | bytes 262176 | tf_op jit(solution)/shard_map/all_to_all | solution.py:31
  173.3 5.0 %all-to-all-start.8 = ((bf16[32,32,128]{2,1,0:T(8,128)(2,1)}), bf16[32,32,128]{2,1,0:T(8,128)(2,1)S(1)}, u32[]{:S(2)}, u32[]{:S(2)}) async-start(bf16[32,32,128]{2,1,0:T(8,128)(2,1)} %bitcast.57), calls=%async_computation.8 | async-start | bytes 524288 | tf_op jit(solution)/shard_map/all_to_all | solution.py:31
  178.2 1.7 convolution_add_fusion.5
  179.9 1.7 convolution_add_fusion.2
  181.6 7.5 %all-to-all-done.8 = bf16[32,32,128]{2,1,0:T(8,128)(2,1)S(1)} async-done(((bf16[32,32,128]{2,1,0:T(8,128)(2,1)}), bf16[32,32,128]{2,1,0:T(8,128)(2,1)S(1)}, u32[]{:S(2)}, u32[]{:S(2)}) %all-to-all-start.8) | async-done | bytes 262176 | tf_op jit(solution)/shard_map/all_to_all | solution.py:31
  191.8 5.0 %all-to-all-start.9 = ((bf16[32,32,128]{2,1,0:T(8,128)(2,1)}), bf16[32,32,128]{2,1,0:T(8,128)(2,1)S(1)}, u32[]{:S(2)}, u32[]{:S(2)}) async-start(bf16[32,32,128]{2,1,0:T(8,128)(2,1)} %bitcast.65), calls=%async_computation.9 | async-start | bytes 524288 | tf_op jit(solution)/shard_map/all_to_all | solution.py:31
  198.5 6.1 %all-to-all-done.9 = bf16[32,32,128]{2,1,0:T(8,128)(2,1)S(1)} async-done(((bf16[32,32,128]{2,1,0:T(8,128)(2,1)}), bf16[32,32,128]{2,1,0:T(8,128)(2,1)S(1)}, u32[]{:S(2)}, u32[]{:S(2)}) %all-to-all-start.9) | async-done | bytes 262176 | tf_op jit(solution)/shard_map/all_to_all | solution.py:31
  206.6 12.5 %all_to_all.100 = bf16[32,32,128]{2,1,0:T(8,128)(2,1)S(1)} all-to-all(bf16[32,32,128]{2,1,0:T(8,128)(2,1)S(1)} %bitcast.412), channel_id=1, replica_groups=mesh['row'=8,'grp'=4,'sub'=8] {'grp','sub'}, dimensions={0} | all-to-all | bytes 524288 | tf_op jit(solution)/shard_map/all_to_all | solution.py:31
  220.3 5.0 %all-to-all-start.11 = ((bf16[32,32,128]{2,1,0:T(8,128)(2,1)}), bf16[32,32,128]{2,1,0:T(8,128)(2,1)S(1)}, u32[]{:S(2)}, u32[]{:S(2)}) async-start(bf16[32,32,128]{2,1,0:T(8,128)(2,1)} %broadcast_in_dim.10), calls=%async_computation.11 | async-start | bytes 524288 | tf_op jit(solution)/shard_map/all_to_all | solution.py:31
  226.0 7.0 %all-to-all-done.11 = bf16[32,32,128]{2,1,0:T(8,128)(2,1)S(1)} async-done(((bf16[32,32,128]{2,1,0:T(8,128)(2,1)}), bf16[32,32,128]{2,1,0:T(8,128)(2,1)S(1)}, u32[]{:S(2)}, u32[]{:S(2)}) %all-to-all-start.11) | async-done | bytes 262176 | tf_op jit(solution)/shard_map/all_to_all | solution.py:31
  233.7 2.5 near_solve.7
  236.2 5.0 %all-to-all-start.12 = ((bf16[32,32,128]{2,1,0:T(8,128)(2,1)}), bf16[32,32,128]{2,1,0:T(8,128)(2,1)S(1)}, u32[]{:S(2)}, u32[]{:S(2)}) async-start(bf16[32,32,128]{2,1,0:T(8,128)(2,1)} %get-tuple-element.23), calls=%async_computation.12 | async-start | bytes 524288 | tf_op jit(solution)/shard_map/all_to_all | solution.py:31
  241.2 2.2 far_rest.6.rest_ref
  243.4 5.6 %all-to-all-done.12 = bf16[32,32,128]{2,1,0:T(8,128)(2,1)S(1)} async-done(((bf16[32,32,128]{2,1,0:T(8,128)(2,1)}), bf16[32,32,128]{2,1,0:T(8,128)(2,1)S(1)}, u32[]{:S(2)}, u32[]{:S(2)}) %all-to-all-start.12) | async-done | bytes 262176 | tf_op jit(solution)/shard_map/all_to_all | solution.py:31
  249.7 2.5 near_solve.8
  252.2 5.0 %all-to-all-start.13 = ((bf16[32,32,128]{2,1,0:T(8,128)(2,1)}), bf16[32,32,128]{2,1,0:T(8,128)(2,1)S(1)}, u32[]{:S(2)}, u32[]{:S(2)}) async-start(bf16[32,32,128]{2,1,0:T(8,128)(2,1)} %get-tuple-element.24), calls=%async_computation.13 | async-start | bytes 524288 | tf_op jit(solution)/shard_map/all_to_all | solution.py:31
  258.0 2.6 far_rest.7.rest_ref
  261.4 3.7 all-to-all-done.13
  265.7 2.5 near_solve.9
  269.0 3.1 collective-permute-start.1
  272.2 5.2 %collective-permute-done.1.x_ref = bf16[12,32,128]{2,1,0:T(8,128)(2,1)S(1)} collective-permute-done((bf16[12,32,128]{2,1,0:T(8,128)(2,1)S(1)}, bf16[12,32,128]{2,1,0:T(8,128)(2,1)S(1)}, u32[]{:S(2)}, u32[]{:S(2)}) %collective-permute-start.1) | collective-permute-done | bytes 98336 | tf_op jit(solution)/shard_map/ppermute | solution.py:274
  278.0 6.0 %cross_sums.1 = bf16[8,3,32,128]{3,2,1,0:T(8,128)(2,1)} custom-call(bf16[12,32,128]{2,1,0:T(8,128)(2,1)} %copy-done.14, bf16[8,3,12,128,128]{4,3,2,1,0:T(8,128)(2,1)} %bitcast.379), custom_call_target="tpu_custom_call" | custom-call | flops 301989888 | bytes 9437184 | tf_op jit(solution)/shard_map/cross_sums/pallas_call | solution.py:69
  284.0 21.0 %all_to_all.101 = bf16[8,3,32,128]{3,2,1,0:T(8,128)(2,1)S(1)} all-to-all(bf16[8,3,32,128]{3,2,1,0:T(8,128)(2,1)} %cross_sums.1), channel_id=1, replica_groups=mesh['row'=8,'grp'=4,'sub'=8] {'row'}, dimensions={0} | all-to-all | bytes 393216 | tf_op jit(solution)/shard_map/all_to_all | solution.py:31
  305.0 5.7 %all-to-all-start.14 = ((bf16[32,32,128]{2,1,0:T(8,128)(2,1)}), bf16[32,32,128]{2,1,0:T(8,128)(2,1)S(1)}, u32[]{:S(2)}, u32[]{:S(2)}) async-start(bf16[32,32,128]{2,1,0:T(8,128)(2,1)} %get-tuple-element.26), calls=%async_computation.14 | async-start | bytes 524288 | tf_op jit(solution)/shard_map/all_to_all | solution.py:31
  310.7 2.1 collective-permute-start.2
  312.9 3.1 far_rest.8.rest_ref
  316.0 2.5 all-to-all-done.14
  319.2 2.5 near_solve.10
  321.7 5.1 %all-to-all-start.15 = ((bf16[32,32,128]{2,1,0:T(8,128)(2,1)}), bf16[32,32,128]{2,1,0:T(8,128)(2,1)S(1)}, u32[]{:S(2)}, u32[]{:S(2)}) async-start(bf16[32,32,128]{2,1,0:T(8,128)(2,1)} %get-tuple-element.27), calls=%async_computation.15 | async-start | bytes 524288 | tf_op jit(solution)/shard_map/all_to_all | solution.py:31
  328.2 2.2 far_rest.9.rest_ref
  330.4 4.1 %all-to-all-done.15 = bf16[32,32,128]{2,1,0:T(8,128)(2,1)S(1)} async-done(((bf16[32,32,128]{2,1,0:T(8,128)(2,1)}), bf16[32,32,128]{2,1,0:T(8,128)(2,1)S(1)}, u32[]{:S(2)}, u32[]{:S(2)}) %all-to-all-start.15) | async-done | bytes 262176 | tf_op jit(solution)/shard_map/all_to_all | solution.py:31
  335.2 2.5 near_solve.11
  337.7 5.0 %all-to-all-start.17 = ((bf16[32,32,128]{2,1,0:T(8,128)(2,1)}), bf16[32,32,128]{2,1,0:T(8,128)(2,1)S(1)}, u32[]{:S(2)}, u32[]{:S(2)}) async-start(bf16[32,32,128]{2,1,0:T(8,128)(2,1)} %get-tuple-element.30), calls=%async_computation.17 | async-start | bytes 524288 | tf_op jit(solution)/shard_map/all_to_all | solution.py:31
  342.7 2.6 far_rest.10.rest_ref
  345.3 5.2 %all-to-all-done.17 = bf16[32,32,128]{2,1,0:T(8,128)(2,1)S(1)} async-done(((bf16[32,32,128]{2,1,0:T(8,128)(2,1)}), bf16[32,32,128]{2,1,0:T(8,128)(2,1)S(1)}, u32[]{:S(2)}, u32[]{:S(2)}) %all-to-all-start.17) | async-done | bytes 262176 | tf_op jit(solution)/shard_map/all_to_all | solution.py:31
  351.2 2.5 near_solve.12
  353.7 5.0 %all-to-all-start.18 = ((bf16[32,32,128]{2,1,0:T(8,128)(2,1)}), bf16[32,32,128]{2,1,0:T(8,128)(2,1)S(1)}, u32[]{:S(2)}, u32[]{:S(2)}) async-start(bf16[32,32,128]{2,1,0:T(8,128)(2,1)} %get-tuple-element.31), calls=%async_computation.18 | async-start | bytes 524288 | tf_op jit(solution)/shard_map/all_to_all | solution.py:31
  358.7 3.1 far_rest.11.rest_ref
  361.8 4.6 %all-to-all-done.18 = bf16[32,32,128]{2,1,0:T(8,128)(2,1)S(1)} async-done(((bf16[32,32,128]{2,1,0:T(8,128)(2,1)}), bf16[32,32,128]{2,1,0:T(8,128)(2,1)S(1)}, u32[]{:S(2)}, u32[]{:S(2)}) %all-to-all-start.18) | async-done | bytes 262176 | tf_op jit(solution)/shard_map/all_to_all | solution.py:31
  367.2 2.5 near_solve.13
  370.6 24.8 %all_to_all.102 = bf16[8,8,32,128]{3,2,1,0:T(8,128)(2,1)S(1)} all-to-all(bf16[8,8,32,128]{3,2,1,0:T(8,128)(2,1)S(1)} %broadcast_in_dim.11), channel_id=1, replica_groups=mesh['row'=8,'grp'=4,'sub'=8] {'row'}, dimensions={0} | all-to-all | bytes 1048576 | tf_op jit(solution)/shard_map/all_to_all | solution.py:31
  (154 shorter events, 67.2 us)
Async XLA Ops:
  6.5 141.5 %all-gather.10.cloned.1.call-start = ((), (), s32[]{:S(2)}) async-start(), calls=%async_computation.21 | async-start | bytes 11796480 | tf_op jit(solution)/shard_map/all_gather | solution.py:191
  16.8 255.4 %all-gather.14.cloned.1.call-start = ((), (), s32[]{:S(2)}) async-start(), calls=%async_computation.23 | async-start | bytes 10616832 | tf_op jit(solution)/shard_map/all_gather | solution.py:185
  19.4 308.8 %all-gather.12.cloned.1.call-start = ((), (), s32[]{:S(2)}) async-start(), calls=%async_computation.22 | async-start | bytes 5898240 | tf_op jit(solution)/shard_map/all_gather | solution.py:191
  20.5 45.2 %copy-start.6 = (f32[8,1,128,128]{3,2,1,0:T(8,128)S(1)}, f32[8,1,128,128]{3,2,1,0:T(8,128)}, u32[]{:S(2)}) copy-start(f32[8,1,128,128]{3,2,1,0:T(8,128)} %param.7) | copy-start | bytes 1572868
  22.9 15.3 %all-to-all-start = ((bf16[32,32,128]{2,1,0:T(8,128)(2,1)}), bf16[32,32,128]{2,1,0:T(8,128)(2,1)S(1)}, u32[]{:S(2)}, u32[]{:S(2)}) async-start(bf16[32,32,128]{2,1,0:T(8,128)(2,1)} %bitcast.11), calls=%async_computation | async-start | bytes 524288 | tf_op jit(solution)/shard_map/all_to_all | solution.py:31
  38.9 17.9 %all-to-all-start.1 = ((bf16[8,32,128]{2,1,0:T(8,128)(2,1)}), bf16[8,32,128]{2,1,0:T(8,128)(2,1)}, u32[]{:S(2)}, u32[]{:S(2)}) async-start(bf16[8,32,128]{2,1,0:T(8,128)(2,1)} %broadcast_in_dim.8), calls=%async_computation.1 | async-start | bytes 131072 | tf_op jit(solution)/shard_map/all_to_all | solution.py:31
  56.8 8.8 %all-to-all-start.2 = ((bf16[8,32,128]{2,1,0:T(8,128)(2,1)}), bf16[8,32,128]{2,1,0:T(8,128)(2,1)S(1)}, u32[]{:S(2)}, u32[]{:S(2)}) async-start(bf16[8,32,128]{2,1,0:T(8,128)(2,1)} %all-to-all-done.1), calls=%async_computation.2 | async-start | bytes 131072 | tf_op jit(solution)/shard_map/all_to_all | solution.py:31
  68.6 12.8 %all-to-all-start.3 = ((bf16[32,32,128]{2,1,0:T(8,128)(2,1)}), bf16[32,32,128]{2,1,0:T(8,128)(2,1)S(1)}, u32[]{:S(2)}, u32[]{:S(2)}) async-start(bf16[32,32,128]{2,1,0:T(8,128)(2,1)} %bitcast.19), calls=%async_computation.3 | async-start | bytes 524288 | tf_op jit(solution)/shard_map/all_to_all | solution.py:31
  82.1 13.4 %all-to-all-start.4 = ((bf16[8,32,128]{2,1,0:T(8,128)(2,1)}), bf16[8,32,128]{2,1,0:T(8,128)(2,1)}, u32[]{:S(2)}, u32[]{:S(2)}) async-start(bf16[8,32,128]{2,1,0:T(8,128)(2,1)} %broadcast_in_dim.9), calls=%async_computation.4 | async-start | bytes 131072 | tf_op jit(solution)/shard_map/all_to_all | solution.py:31
  95.5 8.8 %all-to-all-start.5 = ((bf16[8,32,128]{2,1,0:T(8,128)(2,1)}), bf16[8,32,128]{2,1,0:T(8,128)(2,1)S(1)}, u32[]{:S(2)}, u32[]{:S(2)}) async-start(bf16[8,32,128]{2,1,0:T(8,128)(2,1)} %all-to-all-done.4), calls=%async_computation.5 | async-start | bytes 131072 | tf_op jit(solution)/shard_map/all_to_all | solution.py:31
  106.4 5.9 %copy-start.7 = (f32[4,128,256]{2,1,0:T(8,128)S(1)}, f32[4,128,256]{2,1,0:T(8,128)}, u32[]{:S(2)}) copy-start(f32[4,128,256]{2,1,0:T(8,128)} %convolution_add_fusion.7) | copy-start | bytes 1572868
  108.5 5.2 %copy-start.9 = (bf16[4,256,128]{2,1,0:T(8,128)(2,1)S(1)}, bf16[4,256,128]{2,1,0:T(8,128)(2,1)}, u32[]{:S(2)}) copy-start(bf16[4,256,128]{2,1,0:T(8,128)(2,1)} %copy.45) | copy-start | bytes 786436
  109.3 4.4 %copy-start.10 = (bf16[4,256,128]{2,1,0:T(8,128)(2,1)S(1)}, bf16[4,256,128]{2,1,0:T(8,128)(2,1)}, u32[]{:S(2)}) copy-start(bf16[4,256,128]{2,1,0:T(8,128)(2,1)} %copy.46) | copy-start | bytes 786436
  115.2 24.1 %all-to-all-start.6 = ((bf16[32,5,32,128]{3,2,1,0:T(8,128)(2,1)}), bf16[32,5,32,128]{3,2,1,0:T(8,128)(2,1)S(1)}, u32[]{:S(2)}, u32[]{:S(2)}) async-start(bf16[32,5,32,128]{3,2,1,0:T(8,128)(2,1)} %copy.50), calls=%async_computation.6 | async-start | bytes 2621440 | tf_op jit(solution)/shard_map/all_to_all | solution.py:31
  120.3 238.4 %all-gather.8.cloned.1.call-start = ((), (), s32[]{:S(2)}) async-start(), calls=%async_computation.20 | async-start | bytes 4718592 | tf_op jit(solution)/shard_map/all_gather | solution.py:191
  139.5 7.7 %collective-permute-start = (bf16[5,32,128]{2,1,0:T(8,128)(2,1)S(1)}, bf16[5,32,128]{2,1,0:T(8,128)(2,1)S(1)}, u32[]{:S(2)}, u32[]{:S(2)}) collective-permute-start(bf16[5,32,128]{2,1,0:T(8,128)(2,1)S(1)} %reduce_sum.91), channel_id=1, source_target_pairs={{0,0},{1,32},{2,64},{3,96},{4,128},{5,160},{6,192},{7,224},{8,8},{... | collective-permute-start | bytes 122888 | tf_op jit(solution)/shard_map/ppermute | solution.py:232
  150.5 20.0 %all-to-all-start.7 = ((bf16[32,32,128]{2,1,0:T(8,128)(2,1)}), bf16[32,32,128]{2,1,0:T(8,128)(2,1)S(1)}, u32[]{:S(2)}, u32[]{:S(2)}) async-start(bf16[32,32,128]{2,1,0:T(8,128)(2,1)} %bitcast.49), calls=%async_computation.7 | async-start | bytes 524288 | tf_op jit(solution)/shard_map/all_to_all | solution.py:31
  170.8 20.3 %copy-start.11 = (f32[32,128]{1,0:T(8,128)}, f32[32,128]{1,0:T(8,128)S(1)}, u32[]{:S(2)}) copy-start(f32[32,128]{1,0:T(8,128)S(1)} %fusion.71.refs_0_) | copy-start | bytes 49156
  173.3 15.8 %all-to-all-start.8 = ((bf16[32,32,128]{2,1,0:T(8,128)(2,1)}), bf16[32,32,128]{2,1,0:T(8,128)(2,1)S(1)}, u32[]{:S(2)}, u32[]{:S(2)}) async-start(bf16[32,32,128]{2,1,0:T(8,128)(2,1)} %bitcast.57), calls=%async_computation.8 | async-start | bytes 524288 | tf_op jit(solution)/shard_map/all_to_all | solution.py:31
  189.4 17.2 %copy-start.12 = (f32[32,128]{1,0:T(8,128)}, f32[32,128]{1,0:T(8,128)S(1)}, u32[]{:S(2)}) copy-start(f32[32,128]{1,0:T(8,128)S(1)} %fusion.67.refs_0_) | copy-start | bytes 49156
  191.8 12.8 %all-to-all-start.9 = ((bf16[32,32,128]{2,1,0:T(8,128)(2,1)}), bf16[32,32,128]{2,1,0:T(8,128)(2,1)S(1)}, u32[]{:S(2)}, u32[]{:S(2)}) async-start(bf16[32,32,128]{2,1,0:T(8,128)(2,1)} %bitcast.65), calls=%async_computation.9 | async-start | bytes 524288 | tf_op jit(solution)/shard_map/all_to_all | solution.py:31
  204.8 28.2 %copy-start.13 = (f32[32,128]{1,0:T(8,128)}, f32[32,128]{1,0:T(8,128)S(1)}, u32[]{:S(2)}) copy-start(f32[32,128]{1,0:T(8,128)S(1)} %fusion.63.rest_ref) | copy-start | bytes 49156
  220.3 12.8 %all-to-all-start.11 = ((bf16[32,32,128]{2,1,0:T(8,128)(2,1)}), bf16[32,32,128]{2,1,0:T(8,128)(2,1)S(1)}, u32[]{:S(2)}, u32[]{:S(2)}) async-start(bf16[32,32,128]{2,1,0:T(8,128)(2,1)} %broadcast_in_dim.10), calls=%async_computation.11 | async-start | bytes 524288 | tf_op jit(solution)/shard_map/all_to_all | solution.py:31
  233.0 0.7 copy-start
  236.2 12.8 %all-to-all-start.12 = ((bf16[32,32,128]{2,1,0:T(8,128)(2,1)}), bf16[32,32,128]{2,1,0:T(8,128)(2,1)S(1)}, u32[]{:S(2)}, u32[]{:S(2)}) async-start(bf16[32,32,128]{2,1,0:T(8,128)(2,1)} %get-tuple-element.23), calls=%async_computation.12 | async-start | bytes 524288 | tf_op jit(solution)/shard_map/all_to_all | solution.py:31
  249.0 0.7 copy-start.2
  252.2 12.8 %all-to-all-start.13 = ((bf16[32,32,128]{2,1,0:T(8,128)(2,1)}), bf16[32,32,128]{2,1,0:T(8,128)(2,1)S(1)}, u32[]{:S(2)}, u32[]{:S(2)}) async-start(bf16[32,32,128]{2,1,0:T(8,128)(2,1)} %get-tuple-element.24), calls=%async_computation.13 | async-start | bytes 524288 | tf_op jit(solution)/shard_map/all_to_all | solution.py:31
  265.0 0.7 copy-start.4
  269.0 8.3 %collective-permute-start.1 = (bf16[12,32,128]{2,1,0:T(8,128)(2,1)S(1)}, bf16[12,32,128]{2,1,0:T(8,128)(2,1)S(1)}, u32[]{:S(2)}, u32[]{:S(2)}) collective-permute-start(bf16[12,32,128]{2,1,0:T(8,128)(2,1)S(1)} %pad_maximum_fusion.3), channel_id=1, source_target_pairs={{0,0},{1,32},{2,64},{3,96},{4,128},{5,160},{6,192},{7,224},{8,8},{... | collective-permute-start | bytes 294920 | tf_op jit(solution)/shard_map/ppermute | solution.py:274
  277.4 0.6 copy-start.14
  305.0 13.5 %all-to-all-start.14 = ((bf16[32,32,128]{2,1,0:T(8,128)(2,1)}), bf16[32,32,128]{2,1,0:T(8,128)(2,1)S(1)}, u32[]{:S(2)}, u32[]{:S(2)}) async-start(bf16[32,32,128]{2,1,0:T(8,128)(2,1)} %get-tuple-element.26), calls=%async_computation.14 | async-start | bytes 524288 | tf_op jit(solution)/shard_map/all_to_all | solution.py:31
  310.7 16.1 %collective-permute-start.2 = (f32[3,32,128]{2,1,0:T(8,128)S(1)}, f32[3,32,128]{2,1,0:T(8,128)S(1)}, u32[]{:S(2)}, u32[]{:S(2)}) collective-permute-start(f32[3,32,128]{2,1,0:T(8,128)S(1)} %convert_reduce_fusion.4), channel_id=1, source_target_pairs={{0,0},{1,32},{2,64},{3,96},{4,128},{5,160},{6,192},{7,224},{8,8},{... | collective-permute-start | bytes 147464 | tf_op jit(solution)/shard_map/ppermute | solution.py:276
  318.5 0.7 copy-start.1
  321.7 12.8 %all-to-all-start.15 = ((bf16[32,32,128]{2,1,0:T(8,128)(2,1)}), bf16[32,32,128]{2,1,0:T(8,128)(2,1)S(1)}, u32[]{:S(2)}, u32[]{:S(2)}) async-start(bf16[32,32,128]{2,1,0:T(8,128)(2,1)} %get-tuple-element.27), calls=%async_computation.15 | async-start | bytes 524288 | tf_op jit(solution)/shard_map/all_to_all | solution.py:31
  334.5 0.7 copy-start.3
  337.7 12.8 %all-to-all-start.17 = ((bf16[32,32,128]{2,1,0:T(8,128)(2,1)}), bf16[32,32,128]{2,1,0:T(8,128)(2,1)S(1)}, u32[]{:S(2)}, u32[]{:S(2)}) async-start(bf16[32,32,128]{2,1,0:T(8,128)(2,1)} %get-tuple-element.30), calls=%async_computation.17 | async-start | bytes 524288 | tf_op jit(solution)/shard_map/all_to_all | solution.py:31
  350.5 0.7 copy-start.5
  353.7 12.8 %all-to-all-start.18 = ((bf16[32,32,128]{2,1,0:T(8,128)(2,1)}), bf16[32,32,128]{2,1,0:T(8,128)(2,1)S(1)}, u32[]{:S(2)}, u32[]{:S(2)}) async-start(bf16[32,32,128]{2,1,0:T(8,128)(2,1)} %get-tuple-element.31), calls=%async_computation.18 | async-start | bytes 524288 | tf_op jit(solution)/shard_map/all_to_all | solution.py:31
  361.8 8.6 %copy-start.20 = (f32[32,128]{1,0:T(8,128)S(1)}, f32[32,128]{1,0:T(8,128)}, u32[]{:S(2)}) copy-start(f32[32,128]{1,0:T(8,128)} %get-tuple-element.33) | copy-start | bytes 49156
  361.8 8.6 %copy-start.19 = (f32[32,128]{1,0:T(8,128)S(1)}, f32[32,128]{1,0:T(8,128)}, u32[]{:S(2)}) copy-start(f32[32,128]{1,0:T(8,128)} %get-tuple-element.34) | copy-start | bytes 49156
  361.8 8.6 %copy-start.18 = (f32[32,128]{1,0:T(8,128)S(1)}, f32[32,128]{1,0:T(8,128)}, u32[]{:S(2)}) copy-start(f32[32,128]{1,0:T(8,128)} %get-tuple-element.35) | copy-start | bytes 49156
  361.8 8.7 %copy-start.17 = (f32[32,128]{1,0:T(8,128)S(1)}, f32[32,128]{1,0:T(8,128)}, u32[]{:S(2)}) copy-start(f32[32,128]{1,0:T(8,128)} %get-tuple-element.36) | copy-start | bytes 49156
  361.8 8.7 %copy-start.16 = (f32[32,128]{1,0:T(8,128)S(1)}, f32[32,128]{1,0:T(8,128)}, u32[]{:S(2)}) copy-start(f32[32,128]{1,0:T(8,128)} %get-tuple-element.37) | copy-start | bytes 49156
  361.8 8.7 %copy-start.15 = (f32[32,128]{1,0:T(8,128)S(1)}, f32[32,128]{1,0:T(8,128)}, u32[]{:S(2)}) copy-start(f32[32,128]{1,0:T(8,128)} %get-tuple-element.38) | copy-start | bytes 49156
  366.5 0.7 copy-start.8
Sparse Core Ops, SparseCore 0:
  16.9 119.5 all-gather.9
  138.3 60.1 all-gather.13
  200.3 67.4 all-gather.11
  269.4 58.6 all-gather.7

commit v5 on v4

--- a/solution.py
+++ b/solution.py
@@ -84,6 +84,93 @@
     )(x, g)
 
 
+def times_row(y, g):
+    g = g.reshape(-1, g.shape[-1])
+    return lax.dot_general(y, g, (((1,), (1,)), ((), ())), preferred_element_type=F32)
+
+
+def ahead_kernel(count, *refs):
+    y_refs, g_refs, out_ref = refs[:count], refs[count:-1], refs[-1]
+    block = out_ref.shape[-1]
+    for r in range(out_ref.shape[0]):
+        got = sum(times_row(y[...], g[r]) for y, g in zip(y_refs, g_refs))
+        for a in range(PER_ROW):
+            out_ref[r, a] = got[:, a * block : (a + 1) * block]
+
+
+def ahead_sums(ys, packed, firsts, n_row):
+    part, block = ys[0].shape
+    step = n_row // FAR_STEPS
+    return pl.pallas_call(
+        functools.partial(ahead_kernel, len(ys)),
+        grid=(FAR_STEPS,),
+        in_specs=[whole(y.shape) for y in ys] + [column_spec(step, f, block) for f in firsts],
+        out_specs=pl.BlockSpec((step, PER_ROW, part, block), lambda s: (s, 0, 0, 0)),
+        out_shape=jax.ShapeDtypeStruct((n_row, PER_ROW, part, block), F32),
+        cost_estimate=pl.CostEstimate(
+            flops=2 * len(ys) * n_row * PER_ROW * part * block * block,
+            bytes_accessed=2 * len(ys) * n_row * PER_ROW * block * block,
+            transcendentals=0,
+        ),
+        name="ahead_sums",
+    )(*ys, *([packed] * len(ys)))
+
+
+def step_kernel(has_got, has_acc, *refs):
+    refs = list(refs)
+    got_ref = refs.pop(0) if has_got else None
+    acc_ref = refs.pop(0) if has_acc else None
+    base_ref, inverse_ref, g_ref, y_ref, low_ref, out_ref = refs
+    resid = base_ref[...]
+    if has_got:
+        resid = resid - jnp.sum(got_ref[...].astype(F32), axis=0)
+    y = lax.dot_general(
+        resid,
+        inverse_ref[...],
+        (((1,), (1,)), ((), ())),
+        precision=HIGHEST,
+        preferred_element_type=F32,
+    )
+    y_ref[...] = y
+    low = y.astype(BF16)
+    low_ref[...] = low
+    n_row, block = g_ref.shape[0], g_ref.shape[-1]
+    for r in range(n_row):
+        new = times_row(low, g_ref[r])
+        for a in range(PER_ROW):
+            piece = new[:, a * block : (a + 1) * block]
+            if has_acc:
+                piece = piece + acc_ref[r, a]
+            out_ref[a * n_row + r] = piece.astype(BF16)
+
+
+def forward_step(got, acc, base, inverse, packed, first):
+    n_row = packed.shape[0]
+    part, block = base.shape
+    whole_in = [x for x in (got, acc) if x is not None] + [base, inverse]
+    return pl.pallas_call(
+        functools.partial(step_kernel, got is not None, acc is not None),
+        grid=(1,),
+        in_specs=[whole(x.shape) for x in whole_in] + [column_spec(n_row, first, block)],
+        out_specs=[
+            whole((part, block)),
+            whole((part, block)),
+            whole((n_row * PER_ROW, part, block)),
+        ],
+        out_shape=[
+            jax.ShapeDtypeStruct((part, block), F32),
+            jax.ShapeDtypeStruct((part, block), BF16),
+            jax.ShapeDtypeStruct((n_row * PER_ROW, part, block), BF16),
+        ],
+        cost_estimate=pl.CostEstimate(
+            flops=2 * n_row * PER_ROW * part * block * block,
+            bytes_accessed=2 * n_row * PER_ROW * block * block,
+            transcendentals=0,
+        ),
+        name="forward_step",
+    )(*whole_in, packed)
+
+
 def near_kernel(x_ref, g_ref, rest_ref, inverse_ref, out_ref, low_ref):
     got = times_column(x_ref, g_ref, range(x_ref.shape[1]))
     solved = jnp.dot(
@@ -200,10 +287,6 @@
     def local(t, m):
         return columns[m][(t - m - 1) * PER_ROW : (t - m) * PER_ROW]
 
-    def split(t, m):
-        packed, at = place[t, m]
-        return packed[:, at * PER_ROW : (at + 1) * PER_ROW]
-
     def local_sums(t, count):
         return sum(
             jnp.einsum("sq,apq->asp", low[m], local(t, m), preferred_element_type=F32)
@@ -236,17 +319,25 @@
 
     solved = [own(v) for v in solved]
     low = low + [None] * (LEVELS - NATIVE - 1)
+    got = None
     for t in range(NATIVE + 1, LEVELS):
-        total = early[t - NATIVE - 1]
-        if t > NATIVE + 1:
-            sums = sum(
-                jnp.einsum("sq,rapq->arsp", low[m], split(t, m), preferred_element_type=F32)
-                for m in range(NATIVE + 1, t)
-            )
-            pieces = sums.astype(BF16).reshape(n_col, part, block)
-            total = total + jnp.sum(exchange(pieces, COL).astype(F32), axis=0)
-        solved.append(forward_solve(t, own(loads_t[t]) - total))
-        low[t] = solved[t].astype(BF16)
+        base = own(loads_t[t]) - early[t - NATIVE - 1]
+        if t < LEVELS - 1:
+            acc = None
+            before = range(NATIVE + 1, t)
+            if before:
+                acc = ahead_sums(
+                    [low[m] for m in before],
+                    place[t + 1, t][0],
+                    [place[t + 1, m][1] for m in before],
+                    n_row,
+                )
+            packed, at = place[t + 1, t]
+            y, low[t], pieces = forward_step(got, acc, base, inverse[t], packed, at)
+            got = exchange(pieces, COL)
+        else:
+            y = forward_solve(t, base - jnp.sum(got.astype(F32), axis=0))
+        solved.append(y)
 
     out = [None] * LEVELS
     out[LEVELS - 1] = backward_solve(LEVELS - 1, solved[LEVELS - 1])
@@ -262,6 +353,10 @@
                 rest, [x for _, x in far], place[far[0][0], j][0], [place[t, j][1] for t, _ in far]
             )
         near = exchange(wide, COL).reshape(PER_ROW, n_row, part, block)
+        if j + 2 == CROSS_FROM:
+            crossing_pieces, near = lax.optimization_barrier((crossing_pieces, near))
+            cross = exchange(crossing_pieces, "row")
+            cross = lax.ppermute(jnp.sum(cross.astype(F32), axis=0), ALL, turn)
         packed, at = place[j + 1, j]
         out[j], wide = near_solve(near, packed, at, rest, inverse[j], n_col)
         later.append((j + 1, near))
@@ -272,8 +367,7 @@
             ]
             mine, wide = lax.optimization_barrier((jnp.concatenate(mine, axis=0), wide))
             mine = lax.ppermute(mine, ALL, turn)
-            cross = exchange(cross_sums(mine, crossed), "row")
-            cross = lax.ppermute(jnp.sum(cross.astype(F32), axis=0), ALL, turn)
+            crossing_pieces = cross_sums(mine, crossed)
 
     both = spread(jnp.stack(out).astype(BF16), "row", n_row)
     return jnp.transpose(both, (1, 3, 0, 2)).reshape(LEVELS, 1, block, scen).astype(F32)

time: 408 us -> 412 us (level)
  Pallas kernels: 39.3 us -> 60 us
  matrix products: 44 us -> 25.1 us
  blocking collectives: 58.2 us -> 65.6 us
    pallas_call x0 -> x7, Pallas kernels: none -> 20.6 us  [the longest x4 12.1 us: forward_step(): pl.pallas_call(functools.partial(step_kernel, got is not None, acc is not...]
    dot_general x10 -> x0, matrix products: 17 us -> none  [per_device(): jnp.einsum('sq,rapq->arsp', low[m], split(t, m), preferred_element_type=F32)]
    all_to_all x3 -> x4, blocking collectives: 58.2 us -> 65.6 us  [exchange(): return lax.all_to_all(pieces, axis, 0, 0, tiled=True)]
    ppermute x1, waiting for transfers between devices: 5.22 us -> 12.4 us  [per_device(): mine = lax.ppermute(mine, ALL, turn)]
    all_to_all x17 -> x16, waiting for transfers between devices: 97.4 us -> 91.4 us  [exchange(): return lax.all_to_all(pieces, axis, 0, 0, tiled=True)]
    all_to_all x17 -> x16, starting transfers between devices: 94.3 us -> 92.1 us  [exchange(): return lax.all_to_all(pieces, axis, 0, 0, tiled=True)]
  transfers between devices with their start and end apart: 24 -> 23, of which waited for: 19 -> 17; matrix products, arithmetic and copies ran while one was open for 16% -> 10% of each run, Pallas kernels for 9% -> 14%
where the time goes in v5:
time: 412 us; the launch traced here: 407 us
  waiting for transfers between devices  107 us (26%)
  starting transfers between devices  101 us (25%)
  blocking collectives  65.6 us (16%)
  Pallas kernels  60 us (15%)
  matrix products  25.1 us (6%)
  local copies, waits for them, and re-layouts  18.3 us (4%)
  other arithmetic  16.5 us (4%)
  between operations  13.7 us (3%)
    all_to_all x16, starting transfers between devices, exchange(): return lax.all_to_all(pieces, axis, 0, 0, tiled=True)  92.1 us
    all_to_all x16, waiting for transfers between devices, exchange(): return lax.all_to_all(pieces, axis, 0, 0, tiled=True)  91.4 us
    all_to_all x4, blocking collectives, exchange(): return lax.all_to_all(pieces, axis, 0, 0, tiled=True)  65.6 us
    dot_general x18, matrix products, local_sums(): jnp.einsum('sq,apq->asp', low[m], local(t, m), preferred_element_type=F32)  19.4 us
    pallas_call x7, Pallas kernels, near_solve(): pl.pallas_call(near_kernel, grid=(1,), in_specs=[whole(x.shape), column_s...  17.7 us
    pallas_call x6, Pallas kernels, far_rest(): pl.pallas_call(functools.partial(far_kernel, len(xs)), grid=(FAR_STEPS,),...  15.8 us
    ppermute x1, waiting for transfers between devices, per_device(): mine = lax.ppermute(mine, ALL, turn)  12.4 us
    pallas_call x4, Pallas kernels, forward_step(): pl.pallas_call(functools.partial(step_kernel, got is not None, acc is not...  12.1 us
  transfers between devices with their start and end apart: 23, of which 17 were waited for; matrix products, arithmetic and copies ran while one was open for 10% of the time, Pallas kernels for 14%

profile of v5, /device:TPU:2, one launch (start us, length us, event | category | flops | bytes accessed | tf_op | source)
XLA Modules:
  0.0 407.2 jit_solution(13833188491566806297)
XLA Ops:
  8.9 1.8 fusion.65
  22.9 7.6 %all-to-all-start = ((bf16[32,32,128]{2,1,0:T(8,128)(2,1)}), bf16[32,32,128]{2,1,0:T(8,128)(2,1)S(1)}, u32[]{:S(2)}, u32[]{:S(2)}) async-start(bf16[32,32,128]{2,1,0:T(8,128)(2,1)} %bitcast.11), calls=%async_computation | async-start | bytes 524288 | tf_op jit(solution)/shard_map/all_to_all | solution.py:31
  30.6 2.0 bitcast_multiply_fusion.3
  38.9 8.5 %all-to-all-start.1 = ((bf16[8,32,128]{2,1,0:T(8,128)(2,1)}), bf16[8,32,128]{2,1,0:T(8,128)(2,1)}, u32[]{:S(2)}, u32[]{:S(2)}) async-start(bf16[8,32,128]{2,1,0:T(8,128)(2,1)} %broadcast_in_dim.8), calls=%async_computation.1 | async-start | bytes 131072 | tf_op jit(solution)/shard_map/all_to_all | solution.py:31
  47.4 9.3 %all-to-all-done.1 = bf16[8,32,128]{2,1,0:T(8,128)(2,1)} async-done(((bf16[8,32,128]{2,1,0:T(8,128)(2,1)}), bf16[8,32,128]{2,1,0:T(8,128)(2,1)}, u32[]{:S(2)}, u32[]{:S(2)}) %all-to-all-start.1) | async-done | bytes 65568 | tf_op jit(solution)/shard_map/all_to_all | solution.py:31
  56.7 4.6 %all-to-all-start.2 = ((bf16[8,32,128]{2,1,0:T(8,128)(2,1)}), bf16[8,32,128]{2,1,0:T(8,128)(2,1)S(1)}, u32[]{:S(2)}, u32[]{:S(2)}) async-start(bf16[8,32,128]{2,1,0:T(8,128)(2,1)} %all-to-all-done.1), calls=%async_computation.2 | async-start | bytes 131072 | tf_op jit(solution)/shard_map/all_to_all | solution.py:31
  61.5 4.1 %all-to-all-done.2 = bf16[8,32,128]{2,1,0:T(8,128)(2,1)S(1)} async-done(((bf16[8,32,128]{2,1,0:T(8,128)(2,1)}), bf16[8,32,128]{2,1,0:T(8,128)(2,1)S(1)}, u32[]{:S(2)}, u32[]{:S(2)}) %all-to-all-start.2) | async-done | bytes 65568 | tf_op jit(solution)/shard_map/all_to_all | solution.py:31
  69.4 5.6 %all-to-all-start.3 = ((bf16[32,32,128]{2,1,0:T(8,128)(2,1)}), bf16[32,32,128]{2,1,0:T(8,128)(2,1)S(1)}, u32[]{:S(2)}, u32[]{:S(2)}) async-start(bf16[32,32,128]{2,1,0:T(8,128)(2,1)} %bitcast.19), calls=%async_computation.3 | async-start | bytes 524288 | tf_op jit(solution)/shard_map/all_to_all | solution.py:31
  78.8 3.9 all-to-all-done.3
  83.4 4.0 all-to-all-start.4
  88.8 8.0 %all-to-all-done.4 = bf16[8,32,128]{2,1,0:T(8,128)(2,1)} async-done(((bf16[8,32,128]{2,1,0:T(8,128)(2,1)}), bf16[8,32,128]{2,1,0:T(8,128)(2,1)}, u32[]{:S(2)}, u32[]{:S(2)}) %all-to-all-start.4) | async-done | bytes 65568 | tf_op jit(solution)/shard_map/all_to_all | solution.py:31
  96.8 4.6 %all-to-all-start.5 = ((bf16[8,32,128]{2,1,0:T(8,128)(2,1)}), bf16[8,32,128]{2,1,0:T(8,128)(2,1)S(1)}, u32[]{:S(2)}, u32[]{:S(2)}) async-start(bf16[8,32,128]{2,1,0:T(8,128)(2,1)} %all-to-all-done.4), calls=%async_computation.5 | async-start | bytes 131072 | tf_op jit(solution)/shard_map/all_to_all | solution.py:31
  101.4 2.2 convolution_add_fusion.1
  103.6 2.0 all-to-all-done.5
  105.6 1.8 fusion.67
  115.8 5.0 %all-to-all-start.6 = ((bf16[32,5,32,128]{3,2,1,0:T(8,128)(2,1)}), bf16[32,5,32,128]{3,2,1,0:T(8,128)(2,1)S(1)}, u32[]{:S(2)}, u32[]{:S(2)}) async-start(bf16[32,5,32,128]{3,2,1,0:T(8,128)(2,1)} %copy.45), calls=%async_computation.6 | async-start | bytes 2621440 | tf_op jit(solution)/shard_map/all_to_all | solution.py:31
  120.9 19.0 %all-to-all-done.6 = bf16[32,5,32,128]{3,2,1,0:T(8,128)(2,1)S(1)} async-done(((bf16[32,5,32,128]{3,2,1,0:T(8,128)(2,1)}), bf16[32,5,32,128]{3,2,1,0:T(8,128)(2,1)S(1)}, u32[]{:S(2)}, u32[]{:S(2)}) %all-to-all-start.6) | async-done | bytes 1310752 | tf_op jit(solution)/shard_map/all_to_all | solution.py:31
  140.1 3.9 collective-permute-start
  144.8 3.0 collective-permute-done
  148.4 2.9 forward_step.4
  151.4 9.2 %all-to-all-start.7 = ((bf16[32,32,128]{2,1,0:T(8,128)(2,1)}), bf16[32,32,128]{2,1,0:T(8,128)(2,1)S(1)}, u32[]{:S(2)}, u32[]{:S(2)}) async-start(bf16[32,32,128]{2,1,0:T(8,128)(2,1)} %get-tuple-element.36), calls=%async_computation.7 | async-start | bytes 524288 | tf_op jit(solution)/shard_map/all_to_all | solution.py:31
  160.6 2.3 ahead_sums.3.refs_1_
  162.9 8.4 %all-to-all-done.7.refs_0_ = bf16[32,32,128]{2,1,0:T(8,128)(2,1)S(1)} async-done(((bf16[32,32,128]{2,1,0:T(8,128)(2,1)}), bf16[32,32,128]{2,1,0:T(8,128)(2,1)S(1)}, u32[]{:S(2)}, u32[]{:S(2)}) %all-to-all-start.7) | async-done | bytes 262176 | tf_op jit(solution)/shard_map/all_to_all | solution.py:31
  172.0 3.1 forward_step.5
  175.1 5.1 %all-to-all-start.8 = ((bf16[32,32,128]{2,1,0:T(8,128)(2,1)}), bf16[32,32,128]{2,1,0:T(8,128)(2,1)S(1)}, u32[]{:S(2)}, u32[]{:S(2)}) async-start(bf16[32,32,128]{2,1,0:T(8,128)(2,1)} %get-tuple-element.38), calls=%async_computation.8 | async-start | bytes 524288 | tf_op jit(solution)/shard_map/all_to_all | solution.py:31
  180.2 2.9 ahead_sums.4.refs_1_
  183.0 8.0 %all-to-all-done.8.refs_0_ = bf16[32,32,128]{2,1,0:T(8,128)(2,1)S(1)} async-done(((bf16[32,32,128]{2,1,0:T(8,128)(2,1)}), bf16[32,32,128]{2,1,0:T(8,128)(2,1)S(1)}, u32[]{:S(2)}, u32[]{:S(2)}) %all-to-all-start.8) | async-done | bytes 262176 | tf_op jit(solution)/shard_map/all_to_all | solution.py:31
  191.7 3.0 forward_step.6
  194.8 5.0 %all-to-all-start.9 = ((bf16[32,32,128]{2,1,0:T(8,128)(2,1)}), bf16[32,32,128]{2,1,0:T(8,128)(2,1)S(1)}, u32[]{:S(2)}, u32[]{:S(2)}) async-start(bf16[32,32,128]{2,1,0:T(8,128)(2,1)} %get-tuple-element.40), calls=%async_computation.9 | async-start | bytes 524288 | tf_op jit(solution)/shard_map/all_to_all | solution.py:31
  199.7 3.3 ahead_sums.5.refs_1_
  203.1 4.4 %all-to-all-done.9.refs_0_ = bf16[32,32,128]{2,1,0:T(8,128)(2,1)S(1)} async-done(((bf16[32,32,128]{2,1,0:T(8,128)(2,1)}), bf16[32,32,128]{2,1,0:T(8,128)(2,1)S(1)}, u32[]{:S(2)}, u32[]{:S(2)}) %all-to-all-start.9) | async-done | bytes 262176 | tf_op jit(solution)/shard_map/all_to_all | solution.py:31
  208.2 3.0 forward_step.7
  211.3 12.8 %all_to_all.100 = bf16[32,32,128]{2,1,0:T(8,128)(2,1)S(1)} all-to-all(bf16[32,32,128]{2,1,0:T(8,128)(2,1)} %get-tuple-element.42), channel_id=1, replica_groups=mesh['row'=8,'grp'=4,'sub'=8] {'grp','sub'}, dimensions={0} | all-to-all | bytes 524288 | tf_op jit(solution)/shard_map/all_to_all | solution.py:31
  224.5 12.6 %all_to_all.101 = bf16[32,32,128]{2,1,0:T(8,128)(2,1)} all-to-all(bf16[32,32,128]{2,1,0:T(8,128)(2,1)S(1)} %broadcast_in_dim.10), channel_id=1, replica_groups=mesh['row'=8,'grp'=4,'sub'=8] {'grp','sub'}, dimensions={0} | all-to-all | bytes 524288 | tf_op jit(solution)/shard_map/all_to_all | solution.py:31
  237.1 2.5 near_solve.7
  239.6 5.0 %all-to-all-start.12 = ((bf16[32,32,128]{2,1,0:T(8,128)(2,1)}), bf16[32,32,128]{2,1,0:T(8,128)(2,1)S(1)}, u32[]{:S(2)}, u32[]{:S(2)}) async-start(bf16[32,32,128]{2,1,0:T(8,128)(2,1)} %get-tuple-element.44), calls=%async_computation.12 | async-start | bytes 524288 | tf_op jit(solution)/shard_map/all_to_all | solution.py:31
  244.6 2.2 far_rest.6.rest_ref
  246.8 5.6 %all-to-all-done.12 = bf16[32,32,128]{2,1,0:T(8,128)(2,1)S(1)} async-done(((bf16[32,32,128]{2,1,0:T(8,128)(2,1)}), bf16[32,32,128]{2,1,0:T(8,128)(2,1)S(1)}, u32[]{:S(2)}, u32[]{:S(2)}) %all-to-all-start.12) | async-done | bytes 262176 | tf_op jit(solution)/shard_map/all_to_all | solution.py:31
  253.1 2.5 near_solve.8
  255.6 5.0 %all-to-all-start.13 = ((bf16[32,32,128]{2,1,0:T(8,128)(2,1)}), bf16[32,32,128]{2,1,0:T(8,128)(2,1)S(1)}, u32[]{:S(2)}, u32[]{:S(2)}) async-start(bf16[32,32,128]{2,1,0:T(8,128)(2,1)} %get-tuple-element.46), calls=%async_computation.13 | async-start | bytes 524288 | tf_op jit(solution)/shard_map/all_to_all | solution.py:31
  261.4 2.6 far_rest.7.rest_ref
  264.8 3.7 all-to-all-done.13
  269.1 2.5 near_solve.9
  272.4 5.0 %all-to-all-start.14 = ((bf16[32,32,128]{2,1,0:T(8,128)(2,1)}), bf16[32,32,128]{2,1,0:T(8,128)(2,1)S(1)}, u32[]{:S(2)}, u32[]{:S(2)}) async-start(bf16[32,32,128]{2,1,0:T(8,128)(2,1)} %get-tuple-element.51), calls=%async_computation.14 | async-start | bytes 524288 | tf_op jit(solution)/shard_map/all_to_all | solution.py:31
  277.4 1.9 collective-permute-start.1
  279.4 12.4 %collective-permute-done.1.x_ref = bf16[12,32,128]{2,1,0:T(8,128)(2,1)S(1)} collective-permute-done((bf16[12,32,128]{2,1,0:T(8,128)(2,1)S(1)}, bf16[12,32,128]{2,1,0:T(8,128)(2,1)S(1)}, u32[]{:S(2)}, u32[]{:S(2)}) %collective-permute-start.1) | collective-permute-done | bytes 98336 | tf_op jit(solution)/shard_map/ppermute | solution.py:369
  292.4 5.9 %cross_sums.1 = bf16[8,3,32,128]{3,2,1,0:T(8,128)(2,1)} custom-call(bf16[12,32,128]{2,1,0:T(8,128)(2,1)} %copy-done.12, bf16[8,3,12,128,128]{4,3,2,1,0:T(8,128)(2,1)} %bitcast.298), custom_call_target="tpu_custom_call" | custom-call | flops 301989888 | bytes 9437184 | tf_op jit(solution)/shard_map/cross_sums/pallas_call | solution.py:69
  298.3 16.2 %all_to_all.102 = bf16[8,3,32,128]{3,2,1,0:T(8,128)(2,1)S(1)} all-to-all(bf16[8,3,32,128]{3,2,1,0:T(8,128)(2,1)} %cross_sums.1), channel_id=1, replica_groups=mesh['row'=8,'grp'=4,'sub'=8] {'row'}, dimensions={0} | all-to-all | bytes 393216 | tf_op jit(solution)/shard_map/all_to_all | solution.py:31
  314.5 3.0 collective-permute-start.2
  317.5 3.1 far_rest.8.rest_ref
  320.7 2.6 near_solve.10
  323.2 8.0 %all-to-all-start.15 = ((bf16[32,32,128]{2,1,0:T(8,128)(2,1)}), bf16[32,32,128]{2,1,0:T(8,128)(2,1)S(1)}, u32[]{:S(2)}, u32[]{:S(2)}) async-start(bf16[32,32,128]{2,1,0:T(8,128)(2,1)} %get-tuple-element.54), calls=%async_computation.15 | async-start | bytes 524288 | tf_op jit(solution)/shard_map/all_to_all | solution.py:31
  332.6 2.2 far_rest.9.rest_ref
  334.8 4.1 %all-to-all-done.15 = bf16[32,32,128]{2,1,0:T(8,128)(2,1)S(1)} async-done(((bf16[32,32,128]{2,1,0:T(8,128)(2,1)}), bf16[32,32,128]{2,1,0:T(8,128)(2,1)S(1)}, u32[]{:S(2)}, u32[]{:S(2)}) %all-to-all-start.15) | async-done | bytes 262176 | tf_op jit(solution)/shard_map/all_to_all | solution.py:31
  339.6 2.5 near_solve.11
  342.2 5.0 %all-to-all-start.17 = ((bf16[32,32,128]{2,1,0:T(8,128)(2,1)}), bf16[32,32,128]{2,1,0:T(8,128)(2,1)S(1)}, u32[]{:S(2)}, u32[]{:S(2)}) async-start(bf16[32,32,128]{2,1,0:T(8,128)(2,1)} %get-tuple-element.56), calls=%async_computation.17 | async-start | bytes 524288 | tf_op jit(solution)/shard_map/all_to_all | solution.py:31
  347.1 2.6 far_rest.10.rest_ref
  349.8 5.2 %all-to-all-done.17 = bf16[32,32,128]{2,1,0:T(8,128)(2,1)S(1)} async-done(((bf16[32,32,128]{2,1,0:T(8,128)(2,1)}), bf16[32,32,128]{2,1,0:T(8,128)(2,1)S(1)}, u32[]{:S(2)}, u32[]{:S(2)}) %all-to-all-start.17) | async-done | bytes 262176 | tf_op jit(solution)/shard_map/all_to_all | solution.py:31
  355.6 2.5 near_solve.12
  358.2 5.0 %all-to-all-start.18 = ((bf16[32,32,128]{2,1,0:T(8,128)(2,1)}), bf16[32,32,128]{2,1,0:T(8,128)(2,1)S(1)}, u32[]{:S(2)}, u32[]{:S(2)}) async-start(bf16[32,32,128]{2,1,0:T(8,128)(2,1)} %get-tuple-element.57), calls=%async_computation.18 | async-start | bytes 524288 | tf_op jit(solution)/shard_map/all_to_all | solution.py:31
  363.2 3.1 far_rest.11.rest_ref
  366.3 4.7 %all-to-all-done.18 = bf16[32,32,128]{2,1,0:T(8,128)(2,1)S(1)} async-done(((bf16[32,32,128]{2,1,0:T(8,128)(2,1)}), bf16[32,32,128]{2,1,0:T(8,128)(2,1)S(1)}, u32[]{:S(2)}, u32[]{:S(2)}) %all-to-all-start.18) | async-done | bytes 262176 | tf_op jit(solution)/shard_map/all_to_all | solution.py:31
  371.7 2.6 near_solve.13
  375.2 24.1 %all_to_all.103 = bf16[8,8,32,128]{3,2,1,0:T(8,128)(2,1)S(1)} all-to-all(bf16[8,8,32,128]{3,2,1,0:T(8,128)(2,1)S(1)} %broadcast_in_dim.11), channel_id=1, replica_groups=mesh['row'=8,'grp'=4,'sub'=8] {'row'}, dimensions={0} | all-to-all | bytes 1048576 | tf_op jit(solution)/shard_map/all_to_all | solution.py:31
  (136 shorter events, 53.4 us)
Async XLA Ops:
  6.5 141.9 %all-gather.10.cloned.1.call-start = ((), (), s32[]{:S(2)}) async-start(), calls=%async_computation.21 | async-start | bytes 11796480 | tf_op jit(solution)/shard_map/all_gather | solution.py:278
  16.8 262.6 %all-gather.12.cloned.1.call-start = ((), (), s32[]{:S(2)}) async-start(), calls=%async_computation.22 | async-start | bytes 10616832 | tf_op jit(solution)/shard_map/all_gather | solution.py:272
  19.4 313.2 %all-gather.14.cloned.1.call-start = ((), (), s32[]{:S(2)}) async-start(), calls=%async_computation.23 | async-start | bytes 5898240 | tf_op jit(solution)/shard_map/all_gather | solution.py:278
  22.9 15.3 %all-to-all-start = ((bf16[32,32,128]{2,1,0:T(8,128)(2,1)}), bf16[32,32,128]{2,1,0:T(8,128)(2,1)S(1)}, u32[]{:S(2)}, u32[]{:S(2)}) async-start(bf16[32,32,128]{2,1,0:T(8,128)(2,1)} %bitcast.11), calls=%async_computation | async-start | bytes 524288 | tf_op jit(solution)/shard_map/all_to_all | solution.py:31
  30.5 332.7 %all-gather.8.cloned.1.call-start = ((), (), s32[]{:S(2)}) async-start(), calls=%async_computation.20 | async-start | bytes 4718592 | tf_op jit(solution)/shard_map/all_gather | solution.py:278
  38.9 17.9 %all-to-all-start.1 = ((bf16[8,32,128]{2,1,0:T(8,128)(2,1)}), bf16[8,32,128]{2,1,0:T(8,128)(2,1)}, u32[]{:S(2)}, u32[]{:S(2)}) async-start(bf16[8,32,128]{2,1,0:T(8,128)(2,1)} %broadcast_in_dim.8), calls=%async_computation.1 | async-start | bytes 131072 | tf_op jit(solution)/shard_map/all_to_all | solution.py:31
  56.7 8.8 %all-to-all-start.2 = ((bf16[8,32,128]{2,1,0:T(8,128)(2,1)}), bf16[8,32,128]{2,1,0:T(8,128)(2,1)S(1)}, u32[]{:S(2)}, u32[]{:S(2)}) async-start(bf16[8,32,128]{2,1,0:T(8,128)(2,1)} %all-to-all-done.1), calls=%async_computation.2 | async-start | bytes 131072 | tf_op jit(solution)/shard_map/all_to_all | solution.py:31
  67.4 9.0 %copy-start.6 = (f32[4,128,256]{2,1,0:T(8,128)S(1)}, f32[4,128,256]{2,1,0:T(8,128)}, u32[]{:S(2)}) copy-start(f32[4,128,256]{2,1,0:T(8,128)} %fusion.47) | copy-start | bytes 1572868
  69.4 13.3 %all-to-all-start.3 = ((bf16[32,32,128]{2,1,0:T(8,128)(2,1)}), bf16[32,32,128]{2,1,0:T(8,128)(2,1)S(1)}, u32[]{:S(2)}, u32[]{:S(2)}) async-start(bf16[32,32,128]{2,1,0:T(8,128)(2,1)} %bitcast.19), calls=%async_computation.3 | async-start | bytes 524288 | tf_op jit(solution)/shard_map/all_to_all | solution.py:31
  83.4 13.4 %all-to-all-start.4 = ((bf16[8,32,128]{2,1,0:T(8,128)(2,1)}), bf16[8,32,128]{2,1,0:T(8,128)(2,1)}, u32[]{:S(2)}, u32[]{:S(2)}) async-start(bf16[8,32,128]{2,1,0:T(8,128)(2,1)} %broadcast_in_dim.9), calls=%async_computation.4 | async-start | bytes 131072 | tf_op jit(solution)/shard_map/all_to_all | solution.py:31
  96.8 8.8 %all-to-all-start.5 = ((bf16[8,32,128]{2,1,0:T(8,128)(2,1)}), bf16[8,32,128]{2,1,0:T(8,128)(2,1)S(1)}, u32[]{:S(2)}, u32[]{:S(2)}) async-start(bf16[8,32,128]{2,1,0:T(8,128)(2,1)} %all-to-all-done.4), calls=%async_computation.5 | async-start | bytes 131072 | tf_op jit(solution)/shard_map/all_to_all | solution.py:31
  110.1 2.8 copy-start.5
  115.8 24.1 %all-to-all-start.6 = ((bf16[32,5,32,128]{3,2,1,0:T(8,128)(2,1)}), bf16[32,5,32,128]{3,2,1,0:T(8,128)(2,1)S(1)}, u32[]{:S(2)}, u32[]{:S(2)}) async-start(bf16[32,5,32,128]{3,2,1,0:T(8,128)(2,1)} %copy.45), calls=%async_computation.6 | async-start | bytes 2621440 | tf_op jit(solution)/shard_map/all_to_all | solution.py:31
  120.9 23.2 %copy-start.7 = (f32[8,1,128,128]{3,2,1,0:T(8,128)S(1)}, f32[8,1,128,128]{3,2,1,0:T(8,128)}, u32[]{:S(2)}) copy-start(f32[8,1,128,128]{3,2,1,0:T(8,128)} %param.7) | copy-start | bytes 1572868
  140.1 7.7 %collective-permute-start = (bf16[5,32,128]{2,1,0:T(8,128)(2,1)S(1)}, bf16[5,32,128]{2,1,0:T(8,128)(2,1)S(1)}, u32[]{:S(2)}, u32[]{:S(2)}) collective-permute-start(bf16[5,32,128]{2,1,0:T(8,128)(2,1)S(1)} %reduce_sum.58), channel_id=1, source_target_pairs={{0,0},{1,32},{2,64},{3,96},{4,128},{5,160},{6,192},{7,224},{8,8},{... | collective-permute-start | bytes 122888 | tf_op jit(solution)/shard_map/ppermute | solution.py:315
  151.4 20.0 %all-to-all-start.7 = ((bf16[32,32,128]{2,1,0:T(8,128)(2,1)}), bf16[32,32,128]{2,1,0:T(8,128)(2,1)S(1)}, u32[]{:S(2)}, u32[]{:S(2)}) async-start(bf16[32,32,128]{2,1,0:T(8,128)(2,1)} %get-tuple-element.36), calls=%async_computation.7 | async-start | bytes 524288 | tf_op jit(solution)/shard_map/all_to_all | solution.py:31
  171.3 0.7 copy-start.10
  175.1 15.9 %all-to-all-start.8 = ((bf16[32,32,128]{2,1,0:T(8,128)(2,1)}), bf16[32,32,128]{2,1,0:T(8,128)(2,1)S(1)}, u32[]{:S(2)}, u32[]{:S(2)}) async-start(bf16[32,32,128]{2,1,0:T(8,128)(2,1)} %get-tuple-element.38), calls=%async_computation.8 | async-start | bytes 524288 | tf_op jit(solution)/shard_map/all_to_all | solution.py:31
  191.0 0.7 copy-start.11
  194.8 12.8 %all-to-all-start.9 = ((bf16[32,32,128]{2,1,0:T(8,128)(2,1)}), bf16[32,32,128]{2,1,0:T(8,128)(2,1)S(1)}, u32[]{:S(2)}, u32[]{:S(2)}) async-start(bf16[32,32,128]{2,1,0:T(8,128)(2,1)} %get-tuple-element.40), calls=%async_computation.9 | async-start | bytes 524288 | tf_op jit(solution)/shard_map/all_to_all | solution.py:31
  207.5 0.7 copy-start.9
  239.6 12.8 %all-to-all-start.12 = ((bf16[32,32,128]{2,1,0:T(8,128)(2,1)}), bf16[32,32,128]{2,1,0:T(8,128)(2,1)S(1)}, u32[]{:S(2)}, u32[]{:S(2)}) async-start(bf16[32,32,128]{2,1,0:T(8,128)(2,1)} %get-tuple-element.44), calls=%async_computation.12 | async-start | bytes 524288 | tf_op jit(solution)/shard_map/all_to_all | solution.py:31
  252.4 0.7 copy-start.1
  255.6 12.8 %all-to-all-start.13 = ((bf16[32,32,128]{2,1,0:T(8,128)(2,1)}), bf16[32,32,128]{2,1,0:T(8,128)(2,1)S(1)}, u32[]{:S(2)}, u32[]{:S(2)}) async-start(bf16[32,32,128]{2,1,0:T(8,128)(2,1)} %get-tuple-element.46), calls=%async_computation.13 | async-start | bytes 524288 | tf_op jit(solution)/shard_map/all_to_all | solution.py:31
  268.4 0.7 copy-start.3
  272.4 25.8 %all-to-all-start.14 = ((bf16[32,32,128]{2,1,0:T(8,128)(2,1)}), bf16[32,32,128]{2,1,0:T(8,128)(2,1)S(1)}, u32[]{:S(2)}, u32[]{:S(2)}) async-start(bf16[32,32,128]{2,1,0:T(8,128)(2,1)} %get-tuple-element.51), calls=%async_computation.14 | async-start | bytes 524288 | tf_op jit(solution)/shard_map/all_to_all | solution.py:31
  277.4 14.3 %collective-permute-start.1 = (bf16[12,32,128]{2,1,0:T(8,128)(2,1)S(1)}, bf16[12,32,128]{2,1,0:T(8,128)(2,1)S(1)}, u32[]{:S(2)}, u32[]{:S(2)}) collective-permute-start(bf16[12,32,128]{2,1,0:T(8,128)(2,1)S(1)} %pad_maximum_fusion.3), channel_id=1, source_target_pairs={{0,0},{1,32},{2,64},{3,96},{4,128},{5,160},{6,192},{7,224},{8,8},{... | collective-permute-start | bytes 294920 | tf_op jit(solution)/shard_map/ppermute | solution.py:369
  291.8 0.6 copy-start.12
  298.3 22.4 %copy-start = (bf16[32,32,128]{2,1,0:T(8,128)(2,1)}, bf16[32,32,128]{2,1,0:T(8,128)(2,1)S(1)}, u32[]{:S(2)}) copy-start(bf16[32,32,128]{2,1,0:T(8,128)(2,1)S(1)} %all-to-all-done.14) | copy-start | bytes 786436
  314.5 16.8 %collective-permute-start.2 = (f32[3,32,128]{2,1,0:T(8,128)S(1)}, f32[3,32,128]{2,1,0:T(8,128)S(1)}, u32[]{:S(2)}, u32[]{:S(2)}) collective-permute-start(f32[3,32,128]{2,1,0:T(8,128)S(1)} %convert_reduce_fusion.1), channel_id=1, source_target_pairs={{0,0},{1,32},{2,64},{3,96},{4,128},{5,160},{6,192},{7,224},{8,8},{... | collective-permute-start | bytes 147464 | tf_op jit(solution)/shard_map/ppermute | solution.py:359
  323.2 15.7 %all-to-all-start.15 = ((bf16[32,32,128]{2,1,0:T(8,128)(2,1)}), bf16[32,32,128]{2,1,0:T(8,128)(2,1)S(1)}, u32[]{:S(2)}, u32[]{:S(2)}) async-start(bf16[32,32,128]{2,1,0:T(8,128)(2,1)} %get-tuple-element.54), calls=%async_computation.15 | async-start | bytes 524288 | tf_op jit(solution)/shard_map/all_to_all | solution.py:31
  338.9 0.7 copy-start.2
  342.2 12.8 %all-to-all-start.17 = ((bf16[32,32,128]{2,1,0:T(8,128)(2,1)}), bf16[32,32,128]{2,1,0:T(8,128)(2,1)S(1)}, u32[]{:S(2)}, u32[]{:S(2)}) async-start(bf16[32,32,128]{2,1,0:T(8,128)(2,1)} %get-tuple-element.56), calls=%async_computation.17 | async-start | bytes 524288 | tf_op jit(solution)/shard_map/all_to_all | solution.py:31
  354.9 0.7 copy-start.4
  358.2 12.8 %all-to-all-start.18 = ((bf16[32,32,128]{2,1,0:T(8,128)(2,1)}), bf16[32,32,128]{2,1,0:T(8,128)(2,1)S(1)}, u32[]{:S(2)}, u32[]{:S(2)}) async-start(bf16[32,32,128]{2,1,0:T(8,128)(2,1)} %get-tuple-element.57), calls=%async_computation.18 | async-start | bytes 524288 | tf_op jit(solution)/shard_map/all_to_all | solution.py:31
  370.9 0.7 copy-start.8
  371.6 3.3 copy-start.18
  371.6 3.3 copy-start.17
  371.6 3.4 copy-start.16
  371.6 3.4 copy-start.15
  371.6 3.4 copy-start.14
  371.7 3.4 copy-start.13
Sparse Core Ops, SparseCore 0:
  16.9 119.5 all-gather.9
  138.3 60.1 all-gather.11
  200.3 65.6 all-gather.13
  267.7 60.7 all-gather.7

commit v6 on v3

--- a/solution.py
+++ b/solution.py
@@ -18,7 +18,11 @@
 HIGHEST = lax.Precision.HIGHEST
 COL = ("grp", "sub")
 ALL = ("row", "grp", "sub")
-CHUNKS = ((6, 5, 4, 3), (2, 1), (0,))
+CHUNKS = (
+    ((6, 7, 8), (5, 6, 8), (4, 5, 8), (3, 4, 8)),
+    ((2, 3, 8), (1, 2, 8), (0, 6, 8)),
+    ((0, 1, 6),),
+)
 
 
 def exchange(pieces, axis):
@@ -48,13 +52,66 @@
             out_ref[...] = (y_ref[...] if s == 0 else out_ref[...]) - got
 
 
-def near_kernel(x_ref, g_ref, rest_ref, inverse_ref, out_ref, low_ref):
-    got = times_column(x_ref, g_ref, range(x_ref.shape[1]))
-    solved = jnp.dot(
-        rest_ref[...] - got, inverse_ref[...], precision=HIGHEST, preferred_element_type=F32
-    )
-    out_ref[...] = solved
-    low_ref[...] = jnp.broadcast_to(solved.astype(BF16)[None], low_ref.shape)
+def near_kernel(count, steps, *refs):
+    x_refs, g_refs = refs[:count], refs[count : 2 * count]
+    rest_ref, inverse_ref, out_ref, low_ref, acc_ref = refs[2 * count :]
+    step = x_refs[0].shape[1] // steps
+    for s in range(steps):
+
+        @pl.when(pl.program_id(0) == s)
+        def _():
+            rows = range(s * step, (s + 1) * step)
+            got = sum(times_column(x, g, rows) for x, g in zip(x_refs, g_refs))
+            rest = (rest_ref[...] if s == 0 else acc_ref[...]) - got
+            if s < steps - 1:
+                acc_ref[...] = rest
+            else:
+                solved = jnp.dot(
+                    rest, inverse_ref[...], precision=HIGHEST, preferred_element_type=F32
+                )
+                out_ref[...] = solved
+                low_ref[...] = jnp.broadcast_to(solved.astype(BF16)[None], low_ref.shape)
+
+
+def pack_kernel(chunk, flags_ref, factor_ref, out_ref, sems):
+    copies, at = [], 0
+    for n, (j, a, b) in enumerate(chunk):
+        size = (b - a) * PER_ROW
+        copies.append(
+            pltpu.make_async_copy(
+                factor_ref.at[pl.ds(a * PER_ROW, size), j], out_ref.at[pl.ds(at, size)], sems.at[n]
+            )
+        )
+        copies[-1].start()
+        at += size
+    at = 0
+    for copy, (j, a, b) in zip(copies, chunk):
+        copy.wait()
+        for i in range((b - a) * PER_ROW):
+            block = out_ref[at]
+            out_ref[at] = jnp.where(flags_ref[a * PER_ROW + i, j] != 0, block, 0).astype(BF16)
+            at += 1
+
+
+def pack(chunk, factor, flags):
+    count = sum(b - a for _, a, b in chunk) * PER_ROW
+    shape = (count,) + factor.shape[2:]
+    return pl.pallas_call(
+        functools.partial(pack_kernel, chunk),
+        in_specs=[
+            pl.BlockSpec(memory_space=pltpu.SMEM),
+            pl.BlockSpec(memory_space=pl.ANY),
+        ],
+        out_specs=pl.BlockSpec(memory_space=pltpu.VMEM),
+        out_shape=jax.ShapeDtypeStruct(shape, factor.dtype),
+        scratch_shapes=[pltpu.SemaphoreType.DMA((len(chunk),))],
+        cost_estimate=pl.CostEstimate(
+            flops=count * shape[1] * shape[2],
+            bytes_accessed=4 * count * shape[1] * shape[2],
+            transcendentals=0,
+        ),
+        name="pack",
+    )(flags, factor)
 
 
 def whole(shape):
@@ -85,29 +142,28 @@
     )(y, *xs, *([packed] * len(xs)))
 
 
-def near_solve(x, packed, first, rest, inverse, n_col):
-    n_row, part, block = x.shape[1:]
+def near_solve(xs, packed, firsts, rest, inverse, n_col):
+    n_row, part, block = xs[0].shape[1:]
+    steps = 1 if len(xs) == 1 else FAR_STEPS
     return pl.pallas_call(
-        near_kernel,
-        grid=(1,),
-        in_specs=[
-            whole(x.shape),
-            column_spec(n_row, first, block),
-            whole(rest.shape),
-            whole(inverse.shape),
-        ],
+        functools.partial(near_kernel, len(xs), steps),
+        grid=(steps,),
+        in_specs=[whole(x.shape) for x in xs]
+        + [column_spec(n_row // steps, f, block) for f in firsts]
+        + [whole(rest.shape), whole(inverse.shape)],
         out_specs=[whole((part, block)), whole((n_col, part, block))],
         out_shape=[
             jax.ShapeDtypeStruct((part, block), F32),
             jax.ShapeDtypeStruct((n_col, part, block), BF16),
         ],
+        scratch_shapes=[pltpu.VMEM((part, block), F32)],
         cost_estimate=pl.CostEstimate(
-            flops=2 * n_row * PER_ROW * part * block * block,
-            bytes_accessed=2 * n_row * PER_ROW * block * block,
+            flops=2 * len(xs) * n_row * PER_ROW * part * block * block,
+            bytes_accessed=2 * len(xs) * n_row * PER_ROW * block * block,
             transcendentals=0,
         ),
         name="near_solve",
-    )(x, packed, rest, inverse)
+    )(*xs, *([packed] * len(xs)), rest, inverse)
 
 
 def per_device(factor, pattern, loads, block_inverse):
@@ -135,31 +191,29 @@
     solved = [forward_solve(0, loads_t[0])]
     low = [solved[0].astype(BF16)]
 
-    flags = pattern[:, 0, :, 0].astype(BF16)
+    columns = []
+    for j in range(NATIVE + 1):
+        rows = slice((j + 1) * PER_ROW, LEVELS * PER_ROW)
+        columns.append(factor[rows, 0, j, 0] * pattern[rows, 0, j, 0].astype(BF16)[:, None, None])
+
+    flags = pattern[:, 0, :, 0]
     flags_after, low[0] = lax.optimization_barrier((flags, low[0]))
-
-    def column(j, flags):
-        rows = slice((j + 1) * PER_ROW, LEVELS * PER_ROW)
-        return factor[rows, 0, j, 0] * flags[rows, j][:, None, None]
-
-    columns = [column(j, flags) for j in range(LEVELS - 1)]
-    gathered, where = [None] * LEVELS, [None] * LEVELS
-    for chunk in CHUNKS:
-        use = flags if chunk is CHUNKS[0] else flags_after
-        packed = jnp.concatenate([column(j, use) for j in chunk], axis=0)
+    place = {}
+    for number, chunk in enumerate(CHUNKS):
+        packed = pack(chunk, factor[:, 0, :, 0], flags_after if number else flags)
         packed = lax.all_gather(packed, "row", axis=0)
         at = 0
-        for j in chunk:
-            size = columns[j].shape[0]
-            gathered[j], where[j] = packed, at // PER_ROW
-            at += size
+        for j, a, b in chunk:
+            for t in range(a, b):
+                place[t, j] = packed, at
+                at += 1
 
     def local(t, m):
         return columns[m][(t - m - 1) * PER_ROW : (t - m) * PER_ROW]
 
     def split(t, m):
-        at = (where[m] + t - m - 1) * PER_ROW
-        return gathered[m][:, at : at + PER_ROW]
+        packed, at = place[t, m]
+        return packed[:, at * PER_ROW : (at + 1) * PER_ROW]
 
     def local_sums(t, count):
         return sum(
@@ -210,16 +264,26 @@
     wide = jnp.broadcast_to(out[LEVELS - 1].astype(BF16)[None], (n_col, part, block))
     later = []
     for j in reversed(range(LEVELS - 1)):
-        rest = solved[j]
-        if later:
+        rest, packed = solved[j], place[j + 1, j][0]
+        joined = [(t, x) for t, x in later if j == 0 and place[t, j][0] is packed]
+        far = later[: len(later) - len(joined)]
+        if far:
             rest = far_rest(
                 rest,
-                [x for _, x in later],
-                gathered[j],
-                [where[j] + t - j - 1 for t, _ in later],
+                [x for _, x in far],
+                place[far[0][0], j][0],
+                [place[t, j][1] for t, _ in far],
             )
         near = exchange(wide, COL).reshape(PER_ROW, n_row, part, block)
-        out[j], wide = near_solve(near, gathered[j], where[j], rest, inverse[j], n_col)
+        joined.append((j + 1, near))
+        out[j], wide = near_solve(
+            [x for _, x in joined],
+            packed,
+            [place[t, j][1] for t, _ in joined],
+            rest,
+            inverse[j],
+            n_col,
+        )
         later.append((j + 1, near))
 
     both = spread(jnp.stack(out).astype(BF16), "row", n_row)

time: 383 us -> 379 us (0.990)
  other arithmetic: 14.9 us -> 2.71 us
  Pallas kernels: 37.8 us -> 48 us
    pallas_call x7 -> x10, Pallas kernels: 17.6 us -> 29.7 us  [the longest x7 19.6 us: near_solve(): pl.pallas_call(functools.partial(near_kernel, len(xs), steps), grid=(step...]
    mul x8 -> x1, other arithmetic: 10.3 us -> 1.31 us  [per_device(): factor[rows, 0, j, 0] * pattern[rows, 0, j, 0].astype(BF16)[:, None, None]]
  transfers between devices with their start and end apart: 20 -> 20, of which waited for: 16 -> 16; matrix products, arithmetic and copies ran while one was open for 17% -> 15% of each run, Pallas kernels for 9% -> 11%
where the time goes in v6:
time: 379 us; the launch traced here: 376 us
  waiting for transfers between devices  96.5 us (25%)
  starting transfers between devices  93.7 us (25%)
  blocking collectives  57.5 us (15%)
  Pallas kernels  48 us (13%)
  matrix products  43.3 us (11%)
  local copies, waits for them, and re-layouts  20.4 us (5%)
  between operations  13.7 us (4%)
    all_to_all x16, starting transfers between devices, exchange(): return lax.all_to_all(pieces, axis, 0, 0, tiled=True)  90.4 us
    all_to_all x16, waiting for transfers between devices, exchange(): return lax.all_to_all(pieces, axis, 0, 0, tiled=True)  68.1 us
    all_to_all x3, blocking collectives, exchange(): return lax.all_to_all(pieces, axis, 0, 0, tiled=True)  57.5 us
    all_gather x3, waiting for transfers between devices, per_device(): packed = lax.all_gather(packed, 'row', axis=0)  23.8 us
    dot_general x18, matrix products, local_sums(): jnp.einsum('sq,apq->asp', low[m], local(t, m), preferred_element_type=F32)  21.8 us
    pallas_call x7, Pallas kernels, near_solve(): pl.pallas_call(functools.partial(near_kernel, len(xs), steps), grid=(step...  19.6 us
    pallas_call x6, Pallas kernels, far_rest(): pl.pallas_call(functools.partial(far_kernel, len(xs)), grid=(FAR_STEPS,),...  18.3 us
    dot_general x10, matrix products, per_device(): jnp.einsum('sq,rapq->arsp', low[m], split(t, m), preferred_element_type=F32)  16.9 us
  transfers between devices with their start and end apart: 20, of which 16 were waited for; matrix products, arithmetic and copies ran while one was open for 15% of the time, Pallas kernels for 11%

profile of v6, /device:TPU:2, one launch (start us, length us, event | category | flops | bytes accessed | tf_op | source)
XLA Modules:
  0.0 375.7 jit_solution(93920589674739031)
XLA Ops:
  8.0 3.5 pack.3
  12.9 3.7 pack.4
  19.1 7.6 %all-to-all-start = ((bf16[32,32,128]{2,1,0:T(8,128)(2,1)}), bf16[32,32,128]{2,1,0:T(8,128)(2,1)S(1)}, u32[]{:S(2)}, u32[]{:S(2)}) async-start(bf16[32,32,128]{2,1,0:T(8,128)(2,1)} %bitcast.12), calls=%async_computation | async-start | bytes 524288 | tf_op jit(solution)/shard_map/all_to_all | solution.py:29
  26.8 3.0 pack.5
  35.9 8.5 %all-to-all-start.1 = ((bf16[8,32,128]{2,1,0:T(8,128)(2,1)}), bf16[8,32,128]{2,1,0:T(8,128)(2,1)}, u32[]{:S(2)}, u32[]{:S(2)}) async-start(bf16[8,32,128]{2,1,0:T(8,128)(2,1)} %broadcast_in_dim.8), calls=%async_computation.1 | async-start | bytes 131072 | tf_op jit(solution)/shard_map/all_to_all | solution.py:29
  44.5 9.2 %all-to-all-done.1 = bf16[8,32,128]{2,1,0:T(8,128)(2,1)} async-done(((bf16[8,32,128]{2,1,0:T(8,128)(2,1)}), bf16[8,32,128]{2,1,0:T(8,128)(2,1)}, u32[]{:S(2)}, u32[]{:S(2)}) %all-to-all-start.1) | async-done | bytes 65568 | tf_op jit(solution)/shard_map/all_to_all | solution.py:29
  53.7 4.8 %all-to-all-start.2 = ((bf16[8,32,128]{2,1,0:T(8,128)(2,1)}), bf16[8,32,128]{2,1,0:T(8,128)(2,1)S(1)}, u32[]{:S(2)}, u32[]{:S(2)}) async-start(bf16[8,32,128]{2,1,0:T(8,128)(2,1)} %all-to-all-done.1), calls=%async_computation.2 | async-start | bytes 131072 | tf_op jit(solution)/shard_map/all_to_all | solution.py:29
  58.6 4.1 %all-to-all-done.2 = bf16[8,32,128]{2,1,0:T(8,128)(2,1)S(1)} async-done(((bf16[8,32,128]{2,1,0:T(8,128)(2,1)}), bf16[8,32,128]{2,1,0:T(8,128)(2,1)S(1)}, u32[]{:S(2)}, u32[]{:S(2)}) %all-to-all-start.2) | async-done | bytes 65568 | tf_op jit(solution)/shard_map/all_to_all | solution.py:29
  67.0 6.5 %all-to-all-start.3 = ((bf16[32,32,128]{2,1,0:T(8,128)(2,1)}), bf16[32,32,128]{2,1,0:T(8,128)(2,1)S(1)}, u32[]{:S(2)}, u32[]{:S(2)}) async-start(bf16[32,32,128]{2,1,0:T(8,128)(2,1)} %bitcast.20), calls=%async_computation.3 | async-start | bytes 524288 | tf_op jit(solution)/shard_map/all_to_all | solution.py:29
  76.4 4.9 %all-to-all-done.3 = bf16[32,32,128]{2,1,0:T(8,128)(2,1)S(1)} async-done(((bf16[32,32,128]{2,1,0:T(8,128)(2,1)}), bf16[32,32,128]{2,1,0:T(8,128)(2,1)S(1)}, u32[]{:S(2)}, u32[]{:S(2)}) %all-to-all-start.3) | async-done | bytes 262176 | tf_op jit(solution)/shard_map/all_to_all | solution.py:29
  81.9 4.0 %all-to-all-start.4 = ((bf16[8,32,128]{2,1,0:T(8,128)(2,1)}), bf16[8,32,128]{2,1,0:T(8,128)(2,1)}, u32[]{:S(2)}, u32[]{:S(2)}) async-start(bf16[8,32,128]{2,1,0:T(8,128)(2,1)} %broadcast_in_dim.9), calls=%async_computation.4 | async-start | bytes 131072 | tf_op jit(solution)/shard_map/all_to_all | solution.py:29
  85.9 2.2 convolution_add_fusion.9
  88.1 7.2 %all-to-all-done.4 = bf16[8,32,128]{2,1,0:T(8,128)(2,1)} async-done(((bf16[8,32,128]{2,1,0:T(8,128)(2,1)}), bf16[8,32,128]{2,1,0:T(8,128)(2,1)}, u32[]{:S(2)}, u32[]{:S(2)}) %all-to-all-start.4) | async-done | bytes 65568 | tf_op jit(solution)/shard_map/all_to_all | solution.py:29
  95.3 4.6 %all-to-all-start.5 = ((bf16[8,32,128]{2,1,0:T(8,128)(2,1)}), bf16[8,32,128]{2,1,0:T(8,128)(2,1)S(1)}, u32[]{:S(2)}, u32[]{:S(2)}) async-start(bf16[8,32,128]{2,1,0:T(8,128)(2,1)} %all-to-all-done.4), calls=%async_computation.5 | async-start | bytes 131072 | tf_op jit(solution)/shard_map/all_to_all | solution.py:29
  99.9 2.2 convolution_add_fusion.7
  102.1 2.0 all-to-all-done.5
  112.8 23.4 %all_to_all.95 = bf16[32,5,32,128]{3,2,1,0:T(8,128)(2,1)S(1)} all-to-all(bf16[32,5,32,128]{3,2,1,0:T(8,128)(2,1)S(1)} %copy.39), channel_id=1, replica_groups=mesh['row'=8,'grp'=4,'sub'=8] {'grp','sub'}, dimensions={0} | all-to-all | bytes 2621440 | tf_op jit(solution)/shard_map/all_to_all | solution.py:29
  136.4 3.2 collective-permute-start
  139.6 4.5 %collective-permute-done = bf16[5,32,128]{2,1,0:T(8,128)(2,1)S(1)} collective-permute-done((bf16[5,32,128]{2,1,0:T(8,128)(2,1)S(1)}, bf16[5,32,128]{2,1,0:T(8,128)(2,1)S(1)}, u32[]{:S(2)}, u32[]{:S(2)}) %collective-permute-start) | collective-permute-done | bytes 40992 | tf_op jit(solution)/shard_map/ppermute | solution.py:243
  144.9 1.7 fusion.16
  147.3 9.4 %all-to-all-start.7 = ((bf16[32,32,128]{2,1,0:T(8,128)(2,1)}), bf16[32,32,128]{2,1,0:T(8,128)(2,1)S(1)}, u32[]{:S(2)}, u32[]{:S(2)}) async-start(bf16[32,32,128]{2,1,0:T(8,128)(2,1)} %bitcast.43), calls=%async_computation.7 | async-start | bytes 524288 | tf_op jit(solution)/shard_map/all_to_all | solution.py:29
  156.7 1.7 fusion.96
  158.4 1.7 fusion.93
  160.1 1.7 fusion.91
  161.8 2.6 all-to-all-done.7
  164.7 1.7 fusion.19
  167.1 5.0 %all-to-all-start.8 = ((bf16[32,32,128]{2,1,0:T(8,128)(2,1)}), bf16[32,32,128]{2,1,0:T(8,128)(2,1)S(1)}, u32[]{:S(2)}, u32[]{:S(2)}) async-start(bf16[32,32,128]{2,1,0:T(8,128)(2,1)} %bitcast.51), calls=%async_computation.8 | async-start | bytes 524288 | tf_op jit(solution)/shard_map/all_to_all | solution.py:29
  172.1 1.7 convolution_add_fusion.5
  173.8 1.7 convolution_add_fusion.2
  175.5 4.4 %all-to-all-done.8 = bf16[32,32,128]{2,1,0:T(8,128)(2,1)S(1)} async-done(((bf16[32,32,128]{2,1,0:T(8,128)(2,1)}), bf16[32,32,128]{2,1,0:T(8,128)(2,1)S(1)}, u32[]{:S(2)}, u32[]{:S(2)}) %all-to-all-start.8) | async-done | bytes 262176 | tf_op jit(solution)/shard_map/all_to_all | solution.py:29
  180.2 1.7 fusion.18
  182.6 5.0 %all-to-all-start.9 = ((bf16[32,32,128]{2,1,0:T(8,128)(2,1)}), bf16[32,32,128]{2,1,0:T(8,128)(2,1)S(1)}, u32[]{:S(2)}, u32[]{:S(2)}) async-start(bf16[32,32,128]{2,1,0:T(8,128)(2,1)} %bitcast.59), calls=%async_computation.9 | async-start | bytes 524288 | tf_op jit(solution)/shard_map/all_to_all | solution.py:29
  187.6 1.7 convolution_add_fusion.3
  189.3 6.1 %all-to-all-done.9 = bf16[32,32,128]{2,1,0:T(8,128)(2,1)S(1)} async-done(((bf16[32,32,128]{2,1,0:T(8,128)(2,1)}), bf16[32,32,128]{2,1,0:T(8,128)(2,1)S(1)}, u32[]{:S(2)}, u32[]{:S(2)}) %all-to-all-start.9) | async-done | bytes 262176 | tf_op jit(solution)/shard_map/all_to_all | solution.py:29
  195.7 1.7 fusion.17
  197.4 12.5 %all_to_all.96 = bf16[32,32,128]{2,1,0:T(8,128)(2,1)S(1)} all-to-all(bf16[32,32,128]{2,1,0:T(8,128)(2,1)S(1)} %bitcast.354), channel_id=1, replica_groups=mesh['row'=8,'grp'=4,'sub'=8] {'grp','sub'}, dimensions={0} | all-to-all | bytes 524288 | tf_op jit(solution)/shard_map/all_to_all | solution.py:29
  211.1 5.0 %all-to-all-start.11 = ((bf16[32,32,128]{2,1,0:T(8,128)(2,1)}), bf16[32,32,128]{2,1,0:T(8,128)(2,1)S(1)}, u32[]{:S(2)}, u32[]{:S(2)}) async-start(bf16[32,32,128]{2,1,0:T(8,128)(2,1)} %broadcast_in_dim.10), calls=%async_computation.11 | async-start | bytes 524288 | tf_op jit(solution)/shard_map/all_to_all | solution.py:29
  216.9 7.0 %all-to-all-done.11 = bf16[32,32,128]{2,1,0:T(8,128)(2,1)S(1)} async-done(((bf16[32,32,128]{2,1,0:T(8,128)(2,1)}), bf16[32,32,128]{2,1,0:T(8,128)(2,1)S(1)}, u32[]{:S(2)}, u32[]{:S(2)}) %all-to-all-start.11) | async-done | bytes 262176 | tf_op jit(solution)/shard_map/all_to_all | solution.py:29
  224.6 2.5 near_solve.7
  227.1 5.0 %all-to-all-start.12 = ((bf16[32,32,128]{2,1,0:T(8,128)(2,1)}), bf16[32,32,128]{2,1,0:T(8,128)(2,1)S(1)}, u32[]{:S(2)}, u32[]{:S(2)}) async-start(bf16[32,32,128]{2,1,0:T(8,128)(2,1)} %get-tuple-element.21), calls=%async_computation.12 | async-start | bytes 524288 | tf_op jit(solution)/shard_map/all_to_all | solution.py:29
  232.1 2.2 far_rest.6.refs_2_
  234.3 5.6 %all-to-all-done.12 = bf16[32,32,128]{2,1,0:T(8,128)(2,1)S(1)} async-done(((bf16[32,32,128]{2,1,0:T(8,128)(2,1)}), bf16[32,32,128]{2,1,0:T(8,128)(2,1)S(1)}, u32[]{:S(2)}, u32[]{:S(2)}) %all-to-all-start.12) | async-done | bytes 262176 | tf_op jit(solution)/shard_map/all_to_all | solution.py:29
  240.6 2.5 near_solve.8
  243.1 5.0 %all-to-all-start.13 = ((bf16[32,32,128]{2,1,0:T(8,128)(2,1)}), bf16[32,32,128]{2,1,0:T(8,128)(2,1)S(1)}, u32[]{:S(2)}, u32[]{:S(2)}) async-start(bf16[32,32,128]{2,1,0:T(8,128)(2,1)} %get-tuple-element.22), calls=%async_computation.13 | async-start | bytes 524288 | tf_op jit(solution)/shard_map/all_to_all | solution.py:29
  248.1 2.7 far_rest.7.refs_2_
  250.8 5.1 %all-to-all-done.13 = bf16[32,32,128]{2,1,0:T(8,128)(2,1)S(1)} async-done(((bf16[32,32,128]{2,1,0:T(8,128)(2,1)}), bf16[32,32,128]{2,1,0:T(8,128)(2,1)S(1)}, u32[]{:S(2)}, u32[]{:S(2)}) %all-to-all-start.13) | async-done | bytes 262176 | tf_op jit(solution)/shard_map/all_to_all | solution.py:29
  256.6 2.5 near_solve.9
  259.1 5.0 %all-to-all-start.14 = ((bf16[32,32,128]{2,1,0:T(8,128)(2,1)}), bf16[32,32,128]{2,1,0:T(8,128)(2,1)S(1)}, u32[]{:S(2)}, u32[]{:S(2)}) async-start(bf16[32,32,128]{2,1,0:T(8,128)(2,1)} %get-tuple-element.23), calls=%async_computation.14 | async-start | bytes 524288 | tf_op jit(solution)/shard_map/all_to_all | solution.py:29
  264.1 3.1 far_rest.8.refs_2_
  267.2 4.7 %all-to-all-done.14 = bf16[32,32,128]{2,1,0:T(8,128)(2,1)S(1)} async-done(((bf16[32,32,128]{2,1,0:T(8,128)(2,1)}), bf16[32,32,128]{2,1,0:T(8,128)(2,1)S(1)}, u32[]{:S(2)}, u32[]{:S(2)}) %all-to-all-start.14) | async-done | bytes 262176 | tf_op jit(solution)/shard_map/all_to_all | solution.py:29
  272.6 2.5 near_solve.10
  275.1 5.0 %all-to-all-start.15 = ((bf16[32,32,128]{2,1,0:T(8,128)(2,1)}), bf16[32,32,128]{2,1,0:T(8,128)(2,1)S(1)}, u32[]{:S(2)}, u32[]{:S(2)}) async-start(bf16[32,32,128]{2,1,0:T(8,128)(2,1)} %get-tuple-element.24), calls=%async_computation.15 | async-start | bytes 524288 | tf_op jit(solution)/shard_map/all_to_all | solution.py:29
  281.5 3.6 far_rest.9.refs_2_
  285.1 2.9 all-to-all-done.15
  288.6 2.5 near_solve.11
  291.1 5.1 %all-to-all-start.16 = ((bf16[32,32,128]{2,1,0:T(8,128)(2,1)}), bf16[32,32,128]{2,1,0:T(8,128)(2,1)S(1)}, u32[]{:S(2)}, u32[]{:S(2)}) async-start(bf16[32,32,128]{2,1,0:T(8,128)(2,1)} %get-tuple-element.26), calls=%async_computation.16 | async-start | bytes 524288 | tf_op jit(solution)/shard_map/all_to_all | solution.py:29
  297.5 4.1 %far_rest.10.refs_2_ = f32[32,128]{1,0:T(8,128)} custom-call(f32[32,128]{1,0:T(8,128)} %constant_dynamic-slice_fusion.1.refs_0_, bf16[4,8,32,128]{3,2,1,0:T(8,128)(2,1)} %bitcast.321, bf16[4,8,32,128]{3,2,1,0:T(8,128)(2,1)} %bitcast.327, bf16[4,8,32,128]{3,2,1,0:T(8,128)(2,1)} %bitcast.332, bf16[4,8,32,128]{3,2,1,0:T(8,128)(2,1)} %bitcast.336, ...), custom_call_target="tpu_custom_call" | custom-call | flops 167772160 | bytes 5242880 | tf_op jit(solution)/shard_map/far_rest/pallas_call | solution.py:128
  301.6 2.3 all-to-all-done.16
  304.6 2.5 near_solve.12
  307.1 5.1 %all-to-all-start.17 = ((bf16[32,32,128]{2,1,0:T(8,128)(2,1)}), bf16[32,32,128]{2,1,0:T(8,128)(2,1)S(1)}, u32[]{:S(2)}, u32[]{:S(2)}) async-start(bf16[32,32,128]{2,1,0:T(8,128)(2,1)} %get-tuple-element.27), calls=%async_computation.17 | async-start | bytes 524288 | tf_op jit(solution)/shard_map/all_to_all | solution.py:29
  313.6 2.6 far_rest.11.refs_10_
  316.2 23.8 %all-gather.11.cloned.1.call-done = bf16[160,128,128]{2,1,0:T(8,128)(2,1)} async-done(((bf16[20,128,128]{2,1,0:T(8,128)(2,1)}), bf16[160,128,128]{2,1,0:T(8,128)(2,1)}) %all-gather.11.cloned.1.call-update) | async-done | bytes 5242896 | tf_op jit(solution)/shard_map/all_gather | solution.py:204
  340.8 4.4 %near_solve.13 = (f32[32,128]{1,0:T(8,128)}, bf16[32,32,128]{2,1,0:T(8,128)(2,1)}) custom-call(bf16[4,8,32,128]{3,2,1,0:T(8,128)(2,1)} %bitcast.333, bf16[4,8,32,128]{3,2,1,0:T(8,128)(2,1)} %bitcast.337, bf16[4,8,32,128]{3,2,1,0:T(8,128)(2,1)} %bitcast.340, bf16[4,8,32,128]{3,2,1,0:T(8,128)(2,1)} %bitcast.347, bf16[4,8,32,128]{3,2,1,0:T(8,128)(2,1)} %bitcast.348, ...), custom_call_target="tpu_custom_call" | custom-call | flops 167772160 | bytes 5242880 | tf_op jit(solution)/shard_map/near_solve/pallas_call | solution.py:148
  346.2 21.6 %all_to_all.97 = bf16[8,8,32,128]{3,2,1,0:T(8,128)(2,1)S(1)} all-to-all(bf16[8,8,32,128]{3,2,1,0:T(8,128)(2,1)S(1)} %broadcast_in_dim.11), channel_id=1, replica_groups=mesh['row'=8,'grp'=4,'sub'=8] {'row'}, dimensions={0} | all-to-all | bytes 1048576 | tf_op jit(solution)/shard_map/all_to_all | solution.py:29
  (124 shorter events, 45.2 us)
Async XLA Ops:
  6.5 5.1 %copy-start.8 = (f32[8,1,128,256]{3,2,1,0:T(8,128)S(1)}, f32[8,1,128,256]{3,2,1,0:T(8,128)}, u32[]{:S(2)}) copy-start(f32[8,1,128,256]{3,2,1,0:T(8,128)} %param.6) | copy-start | bytes 3145732
  6.5 5.4 %copy-start.6 = (f32[8,1,128,128]{3,2,1,0:T(8,128)S(1)}, f32[8,1,128,128]{3,2,1,0:T(8,128)}, u32[]{:S(2)}) copy-start(f32[8,1,128,128]{3,2,1,0:T(8,128)} %param.7) | copy-start | bytes 1572868
  6.5 138.4 %all-gather.7.cloned.1.call-start = ((), (), s32[]{:S(2)}) async-start(), calls=%async_computation.19 | async-start | bytes 11796480 | tf_op jit(solution)/shard_map/all_gather | solution.py:204
  11.5 5.1 %copy-start.12 = (s32[32,1,8,1]{0,3,2,1:T(1,128)S(1)}, s32[32,1,8,1]{0,3,2,1:T(1,128)}, u32[]{:S(2)}) copy-start(s32[32,1,8,1]{0,3,2,1:T(1,128)} %param.5) | copy-start | bytes 3076
  11.5 269.9 %all-gather.9.cloned.1.call-start = ((), (), s32[]{:S(2)}) async-start(), calls=%async_computation.20 | async-start | bytes 15335424 | tf_op jit(solution)/shard_map/all_gather | solution.py:204
  19.1 16.1 %all-to-all-start = ((bf16[32,32,128]{2,1,0:T(8,128)(2,1)}), bf16[32,32,128]{2,1,0:T(8,128)(2,1)S(1)}, u32[]{:S(2)}, u32[]{:S(2)}) async-start(bf16[32,32,128]{2,1,0:T(8,128)(2,1)} %bitcast.12), calls=%async_computation | async-start | bytes 524288 | tf_op jit(solution)/shard_map/all_to_all | solution.py:29
  26.7 313.3 %all-gather.11.cloned.1.call-start = ((), (), s32[]{:S(2)}) async-start(), calls=%async_computation.21 | async-start | bytes 5898240 | tf_op jit(solution)/shard_map/all_gather | solution.py:204
  35.9 17.8 %all-to-all-start.1 = ((bf16[8,32,128]{2,1,0:T(8,128)(2,1)}), bf16[8,32,128]{2,1,0:T(8,128)(2,1)}, u32[]{:S(2)}, u32[]{:S(2)}) async-start(bf16[8,32,128]{2,1,0:T(8,128)(2,1)} %broadcast_in_dim.8), calls=%async_computation.1 | async-start | bytes 131072 | tf_op jit(solution)/shard_map/all_to_all | solution.py:29
  53.7 9.0 %all-to-all-start.2 = ((bf16[8,32,128]{2,1,0:T(8,128)(2,1)}), bf16[8,32,128]{2,1,0:T(8,128)(2,1)S(1)}, u32[]{:S(2)}, u32[]{:S(2)}) async-start(bf16[8,32,128]{2,1,0:T(8,128)(2,1)} %all-to-all-done.1), calls=%async_computation.2 | async-start | bytes 131072 | tf_op jit(solution)/shard_map/all_to_all | solution.py:29
  67.0 14.2 %all-to-all-start.3 = ((bf16[32,32,128]{2,1,0:T(8,128)(2,1)}), bf16[32,32,128]{2,1,0:T(8,128)(2,1)S(1)}, u32[]{:S(2)}, u32[]{:S(2)}) async-start(bf16[32,32,128]{2,1,0:T(8,128)(2,1)} %bitcast.20), calls=%async_computation.3 | async-start | bytes 524288 | tf_op jit(solution)/shard_map/all_to_all | solution.py:29
  81.9 13.4 %all-to-all-start.4 = ((bf16[8,32,128]{2,1,0:T(8,128)(2,1)}), bf16[8,32,128]{2,1,0:T(8,128)(2,1)}, u32[]{:S(2)}, u32[]{:S(2)}) async-start(bf16[8,32,128]{2,1,0:T(8,128)(2,1)} %broadcast_in_dim.9), calls=%async_computation.4 | async-start | bytes 131072 | tf_op jit(solution)/shard_map/all_to_all | solution.py:29
  95.3 8.8 %all-to-all-start.5 = ((bf16[8,32,128]{2,1,0:T(8,128)(2,1)}), bf16[8,32,128]{2,1,0:T(8,128)(2,1)S(1)}, u32[]{:S(2)}, u32[]{:S(2)}) async-start(bf16[8,32,128]{2,1,0:T(8,128)(2,1)} %all-to-all-done.4), calls=%async_computation.5 | async-start | bytes 131072 | tf_op jit(solution)/shard_map/all_to_all | solution.py:29
  136.4 7.7 %collective-permute-start = (bf16[5,32,128]{2,1,0:T(8,128)(2,1)S(1)}, bf16[5,32,128]{2,1,0:T(8,128)(2,1)S(1)}, u32[]{:S(2)}, u32[]{:S(2)}) collective-permute-start(bf16[5,32,128]{2,1,0:T(8,128)(2,1)S(1)} %reduce_sum.82), channel_id=1, source_target_pairs={{0,0},{1,32},{2,64},{3,96},{4,128},{5,160},{6,192},{7,224},{8,8},{... | collective-permute-start | bytes 122888 | tf_op jit(solution)/shard_map/ppermute | solution.py:243
  147.3 17.1 %all-to-all-start.7 = ((bf16[32,32,128]{2,1,0:T(8,128)(2,1)}), bf16[32,32,128]{2,1,0:T(8,128)(2,1)S(1)}, u32[]{:S(2)}, u32[]{:S(2)}) async-start(bf16[32,32,128]{2,1,0:T(8,128)(2,1)} %bitcast.43), calls=%async_computation.7 | async-start | bytes 524288 | tf_op jit(solution)/shard_map/all_to_all | solution.py:29
  164.7 32.7 %copy-start.9 = (f32[32,128]{1,0:T(8,128)}, f32[32,128]{1,0:T(8,128)S(1)}, u32[]{:S(2)}) copy-start(f32[32,128]{1,0:T(8,128)S(1)} %fusion.68.refs_0_) | copy-start | bytes 49156
  167.1 12.8 %all-to-all-start.8 = ((bf16[32,32,128]{2,1,0:T(8,128)(2,1)}), bf16[32,32,128]{2,1,0:T(8,128)(2,1)S(1)}, u32[]{:S(2)}, u32[]{:S(2)}) async-start(bf16[32,32,128]{2,1,0:T(8,128)(2,1)} %bitcast.51), calls=%async_computation.8 | async-start | bytes 524288 | tf_op jit(solution)/shard_map/all_to_all | solution.py:29
  180.1 47.0 %copy-start.10 = (f32[32,128]{1,0:T(8,128)}, f32[32,128]{1,0:T(8,128)S(1)}, u32[]{:S(2)}) copy-start(f32[32,128]{1,0:T(8,128)S(1)} %fusion.64.refs_0_) | copy-start | bytes 49156
  182.6 12.8 %all-to-all-start.9 = ((bf16[32,32,128]{2,1,0:T(8,128)(2,1)}), bf16[32,32,128]{2,1,0:T(8,128)(2,1)S(1)}, u32[]{:S(2)}, u32[]{:S(2)}) async-start(bf16[32,32,128]{2,1,0:T(8,128)(2,1)} %bitcast.59), calls=%async_computation.9 | async-start | bytes 524288 | tf_op jit(solution)/shard_map/all_to_all | solution.py:29
  195.7 28.2 %copy-start.11 = (f32[32,128]{1,0:T(8,128)}, f32[32,128]{1,0:T(8,128)S(1)}, u32[]{:S(2)}) copy-start(f32[32,128]{1,0:T(8,128)S(1)} %fusion.60.refs_2_) | copy-start | bytes 49156
  211.1 12.8 %all-to-all-start.11 = ((bf16[32,32,128]{2,1,0:T(8,128)(2,1)}), bf16[32,32,128]{2,1,0:T(8,128)(2,1)S(1)}, u32[]{:S(2)}, u32[]{:S(2)}) async-start(bf16[32,32,128]{2,1,0:T(8,128)(2,1)} %broadcast_in_dim.10), calls=%async_computation.11 | async-start | bytes 524288 | tf_op jit(solution)/shard_map/all_to_all | solution.py:29
  223.9 0.7 copy-start
  227.1 12.8 %all-to-all-start.12 = ((bf16[32,32,128]{2,1,0:T(8,128)(2,1)}), bf16[32,32,128]{2,1,0:T(8,128)(2,1)S(1)}, u32[]{:S(2)}, u32[]{:S(2)}) async-start(bf16[32,32,128]{2,1,0:T(8,128)(2,1)} %get-tuple-element.21), calls=%async_computation.12 | async-start | bytes 524288 | tf_op jit(solution)/shard_map/all_to_all | solution.py:29
  239.9 0.7 copy-start.1
  243.1 12.8 %all-to-all-start.13 = ((bf16[32,32,128]{2,1,0:T(8,128)(2,1)}), bf16[32,32,128]{2,1,0:T(8,128)(2,1)S(1)}, u32[]{:S(2)}, u32[]{:S(2)}) async-start(bf16[32,32,128]{2,1,0:T(8,128)(2,1)} %get-tuple-element.22), calls=%async_computation.13 | async-start | bytes 524288 | tf_op jit(solution)/shard_map/all_to_all | solution.py:29
  255.9 0.7 copy-start.2
  259.1 12.8 %all-to-all-start.14 = ((bf16[32,32,128]{2,1,0:T(8,128)(2,1)}), bf16[32,32,128]{2,1,0:T(8,128)(2,1)S(1)}, u32[]{:S(2)}, u32[]{:S(2)}) async-start(bf16[32,32,128]{2,1,0:T(8,128)(2,1)} %get-tuple-element.23), calls=%async_computation.14 | async-start | bytes 524288 | tf_op jit(solution)/shard_map/all_to_all | solution.py:29
  271.9 0.7 copy-start.3
  275.1 12.8 %all-to-all-start.15 = ((bf16[32,32,128]{2,1,0:T(8,128)(2,1)}), bf16[32,32,128]{2,1,0:T(8,128)(2,1)S(1)}, u32[]{:S(2)}, u32[]{:S(2)}) async-start(bf16[32,32,128]{2,1,0:T(8,128)(2,1)} %get-tuple-element.24), calls=%async_computation.15 | async-start | bytes 524288 | tf_op jit(solution)/shard_map/all_to_all | solution.py:29
  287.9 0.7 copy-start.4
  291.1 12.8 %all-to-all-start.16 = ((bf16[32,32,128]{2,1,0:T(8,128)(2,1)}), bf16[32,32,128]{2,1,0:T(8,128)(2,1)S(1)}, u32[]{:S(2)}, u32[]{:S(2)}) async-start(bf16[32,32,128]{2,1,0:T(8,128)(2,1)} %get-tuple-element.26), calls=%async_computation.16 | async-start | bytes 524288 | tf_op jit(solution)/shard_map/all_to_all | solution.py:29
  303.9 0.7 copy-start.5
  307.1 32.9 %all-to-all-start.17 = ((bf16[32,32,128]{2,1,0:T(8,128)(2,1)}), bf16[32,32,128]{2,1,0:T(8,128)(2,1)S(1)}, u32[]{:S(2)}, u32[]{:S(2)}) async-start(bf16[32,32,128]{2,1,0:T(8,128)(2,1)} %get-tuple-element.27), calls=%async_computation.17 | async-start | bytes 524288 | tf_op jit(solution)/shard_map/all_to_all | solution.py:29
  340.1 0.7 copy-start.7
  340.8 5.2 %copy-start.18 = (f32[32,128]{1,0:T(8,128)S(1)}, f32[32,128]{1,0:T(8,128)}, u32[]{:S(2)}) copy-start(f32[32,128]{1,0:T(8,128)} %get-tuple-element.29) | copy-start | bytes 49156
  340.8 5.2 %copy-start.17 = (f32[32,128]{1,0:T(8,128)S(1)}, f32[32,128]{1,0:T(8,128)}, u32[]{:S(2)}) copy-start(f32[32,128]{1,0:T(8,128)} %get-tuple-element.30) | copy-start | bytes 49156
  340.8 5.2 %copy-start.16 = (f32[32,128]{1,0:T(8,128)S(1)}, f32[32,128]{1,0:T(8,128)}, u32[]{:S(2)}) copy-start(f32[32,128]{1,0:T(8,128)} %get-tuple-element.31) | copy-start | bytes 49156
  340.8 5.2 %copy-start.15 = (f32[32,128]{1,0:T(8,128)S(1)}, f32[32,128]{1,0:T(8,128)}, u32[]{:S(2)}) copy-start(f32[32,128]{1,0:T(8,128)} %get-tuple-element.32) | copy-start | bytes 49156
  340.8 5.2 %copy-start.14 = (f32[32,128]{1,0:T(8,128)S(1)}, f32[32,128]{1,0:T(8,128)}, u32[]{:S(2)}) copy-start(f32[32,128]{1,0:T(8,128)} %get-tuple-element.33) | copy-start | bytes 49156
  340.8 5.3 %copy-start.13 = (f32[32,128]{1,0:T(8,128)S(1)}, f32[32,128]{1,0:T(8,128)}, u32[]{:S(2)}) copy-start(f32[32,128]{1,0:T(8,128)} %get-tuple-element.34) | copy-start | bytes 49156
Sparse Core Ops, SparseCore 0:
  11.7 119.5 all-gather.6
  133.0 141.8 all-gather.8
  276.8 63.2 all-gather.10

commit v7 on v6

--- a/solution.py
+++ b/solution.py
@@ -11,6 +11,7 @@
 LEVELS = 8
 NATIVE = 2
 FAR_STEPS = 2
+OUT_SPLIT = 3
 PER_ROW = 4
 SUB = 8
 BF16 = jnp.bfloat16
@@ -285,8 +286,12 @@
             n_col,
         )
         later.append((j + 1, near))
-
-    both = spread(jnp.stack(out).astype(BF16), "row", n_row)
+        if j == OUT_SPLIT:
+            upper = spread(jnp.stack(out[j:]).astype(BF16), "row", n_row)
+            upper, wide = lax.optimization_barrier((upper, wide))
+
+    lower = spread(jnp.stack(out[:OUT_SPLIT]).astype(BF16), "row", n_row)
+    both = jnp.concatenate([lower, upper], axis=1)
     return jnp.transpose(both, (1, 3, 0, 2)).reshape(LEVELS, 1, block, scen).astype(F32)
 
 

time: 379 us -> 372 us (0.982)
  blocking collectives: 57.5 us -> 43.5 us
  starting transfers between devices: 93.7 us -> 98.9 us
    all_to_all x16 -> x17, waiting for transfers between devices: 68.1 us -> 83.7 us  [exchange(): return lax.all_to_all(pieces, axis, 0, 0, tiled=True)]
    all_gather x3, waiting for transfers between devices: 23.8 us -> 8.49 us  [per_device(): packed = lax.all_gather(packed, 'row', axis=0)]
    all_to_all x3, blocking collectives: 57.5 us -> 43.5 us  [exchange(): return lax.all_to_all(pieces, axis, 0, 0, tiled=True)]
    all_to_all x16 -> x17, starting transfers between devices: 90.4 us -> 94.9 us  [exchange(): return lax.all_to_all(pieces, axis, 0, 0, tiled=True)]
  transfers between devices with their start and end apart: 20 -> 21, of which waited for: 16 -> 18; matrix products, arithmetic and copies ran while one was open for 15% -> 16% of each run, Pallas kernels for 11% -> 11%
where the time goes in v7:
time: 372 us; the launch traced here: 368 us
  starting transfers between devices  98.9 us (27%)
  waiting for transfers between devices  95.9 us (26%)
  Pallas kernels  48 us (13%)
  matrix products  43.5 us (12%)
  blocking collectives  43.5 us (12%)
  local copies, waits for them, and re-layouts  21.5 us (6%)
  between operations  13.7 us (4%)
    all_to_all x17, starting transfers between devices, exchange(): return lax.all_to_all(pieces, axis, 0, 0, tiled=True)  94.9 us
    all_to_all x17, waiting for transfers between devices, exchange(): return lax.all_to_all(pieces, axis, 0, 0, tiled=True)  83.7 us
    all_to_all x3, blocking collectives, exchange(): return lax.all_to_all(pieces, axis, 0, 0, tiled=True)  43.5 us
    dot_general x18, matrix products, local_sums(): jnp.einsum('sq,apq->asp', low[m], local(t, m), preferred_element_type=F32)  21.9 us
    pallas_call x7, Pallas kernels, near_solve(): pl.pallas_call(functools.partial(near_kernel, len(xs), steps), grid=(step...  19.5 us
    pallas_call x6, Pallas kernels, far_rest(): pl.pallas_call(functools.partial(far_kernel, len(xs)), grid=(FAR_STEPS,),...  18.3 us
    dot_general x10, matrix products, per_device(): jnp.einsum('sq,rapq->arsp', low[m], split(t, m), preferred_element_type=F32)  17.1 us
    pallas_call x3, Pallas kernels, pack(): pl.pallas_call(functools.partial(pack_kernel, chunk), in_specs=[pl.BlockS...  10.2 us
  transfers between devices with their start and end apart: 21, of which 18 were waited for; matrix products, arithmetic and copies ran while one was open for 16% of the time, Pallas kernels for 11%

profile of v7, /device:TPU:2, one launch (start us, length us, event | category | flops | bytes accessed | tf_op | source)
XLA Modules:
  0.0 368.4 jit_solution(11753134927093922219)
XLA Ops:
  8.0 3.5 pack.3
  12.9 3.7 %pack.4 = bf16[52,128,128]{2,1,0:T(8,128)(2,1)} custom-call(s32[32,8]{1,0:T(8,128)} %bitcast.356, bf16[32,8,128,128]{3,2,1,0:T(8,128)(2,1)} %bitcast.314), custom_call_target="tpu_custom_call" | custom-call | flops 851968 | bytes 3407872 | tf_op jit(solution)/shard_map/pack/pallas_call | solution.py:100
  19.1 7.6 %all-to-all-start = ((bf16[32,32,128]{2,1,0:T(8,128)(2,1)}), bf16[32,32,128]{2,1,0:T(8,128)(2,1)S(1)}, u32[]{:S(2)}, u32[]{:S(2)}) async-start(bf16[32,32,128]{2,1,0:T(8,128)(2,1)} %bitcast.12), calls=%async_computation | async-start | bytes 524288 | tf_op jit(solution)/shard_map/all_to_all | solution.py:30
  32.2 2.2 all-to-all-done
  35.1 8.5 %all-to-all-start.1 = ((bf16[8,32,128]{2,1,0:T(8,128)(2,1)}), bf16[8,32,128]{2,1,0:T(8,128)(2,1)}, u32[]{:S(2)}, u32[]{:S(2)}) async-start(bf16[8,32,128]{2,1,0:T(8,128)(2,1)} %broadcast_in_dim.10), calls=%async_computation.1 | async-start | bytes 131072 | tf_op jit(solution)/shard_map/all_to_all | solution.py:30
  43.6 9.3 %all-to-all-done.1 = bf16[8,32,128]{2,1,0:T(8,128)(2,1)} async-done(((bf16[8,32,128]{2,1,0:T(8,128)(2,1)}), bf16[8,32,128]{2,1,0:T(8,128)(2,1)}, u32[]{:S(2)}, u32[]{:S(2)}) %all-to-all-start.1) | async-done | bytes 65568 | tf_op jit(solution)/shard_map/all_to_all | solution.py:30
  53.0 4.6 %all-to-all-start.2 = ((bf16[8,32,128]{2,1,0:T(8,128)(2,1)}), bf16[8,32,128]{2,1,0:T(8,128)(2,1)S(1)}, u32[]{:S(2)}, u32[]{:S(2)}) async-start(bf16[8,32,128]{2,1,0:T(8,128)(2,1)} %all-to-all-done.1), calls=%async_computation.2 | async-start | bytes 131072 | tf_op jit(solution)/shard_map/all_to_all | solution.py:30
  57.7 4.1 %all-to-all-done.2 = bf16[8,32,128]{2,1,0:T(8,128)(2,1)S(1)} async-done(((bf16[8,32,128]{2,1,0:T(8,128)(2,1)}), bf16[8,32,128]{2,1,0:T(8,128)(2,1)S(1)}, u32[]{:S(2)}, u32[]{:S(2)}) %all-to-all-start.2) | async-done | bytes 65568 | tf_op jit(solution)/shard_map/all_to_all | solution.py:30
  64.8 5.0 %all-to-all-start.3 = ((bf16[32,32,128]{2,1,0:T(8,128)(2,1)}), bf16[32,32,128]{2,1,0:T(8,128)(2,1)S(1)}, u32[]{:S(2)}, u32[]{:S(2)}) async-start(bf16[32,32,128]{2,1,0:T(8,128)(2,1)} %bitcast.20), calls=%async_computation.3 | async-start | bytes 524288 | tf_op jit(solution)/shard_map/all_to_all | solution.py:30
  74.0 3.6 all-to-all-done.3
  78.3 4.0 %all-to-all-start.4 = ((bf16[8,32,128]{2,1,0:T(8,128)(2,1)}), bf16[8,32,128]{2,1,0:T(8,128)(2,1)}, u32[]{:S(2)}, u32[]{:S(2)}) async-start(bf16[8,32,128]{2,1,0:T(8,128)(2,1)} %broadcast_in_dim.11), calls=%async_computation.4 | async-start | bytes 131072 | tf_op jit(solution)/shard_map/all_to_all | solution.py:30
  82.2 2.2 convolution_add_fusion.9
  84.4 7.2 %all-to-all-done.4 = bf16[8,32,128]{2,1,0:T(8,128)(2,1)} async-done(((bf16[8,32,128]{2,1,0:T(8,128)(2,1)}), bf16[8,32,128]{2,1,0:T(8,128)(2,1)}, u32[]{:S(2)}, u32[]{:S(2)}) %all-to-all-start.4) | async-done | bytes 65568 | tf_op jit(solution)/shard_map/all_to_all | solution.py:30
  91.7 4.6 %all-to-all-start.5 = ((bf16[8,32,128]{2,1,0:T(8,128)(2,1)}), bf16[8,32,128]{2,1,0:T(8,128)(2,1)S(1)}, u32[]{:S(2)}, u32[]{:S(2)}) async-start(bf16[8,32,128]{2,1,0:T(8,128)(2,1)} %all-to-all-done.4), calls=%async_computation.5 | async-start | bytes 131072 | tf_op jit(solution)/shard_map/all_to_all | solution.py:30
  96.3 2.2 convolution_add_fusion.7
  98.5 1.9 all-to-all-done.5
  110.2 5.0 %all-to-all-start.6 = ((bf16[32,5,32,128]{3,2,1,0:T(8,128)(2,1)}), bf16[32,5,32,128]{3,2,1,0:T(8,128)(2,1)S(1)}, u32[]{:S(2)}, u32[]{:S(2)}) async-start(bf16[32,5,32,128]{3,2,1,0:T(8,128)(2,1)} %copy.40), calls=%async_computation.6 | async-start | bytes 2621440 | tf_op jit(solution)/shard_map/all_to_all | solution.py:30
  115.3 3.0 pack.5
  118.3 15.9 %all-to-all-done.6 = bf16[32,5,32,128]{3,2,1,0:T(8,128)(2,1)S(1)} async-done(((bf16[32,5,32,128]{3,2,1,0:T(8,128)(2,1)}), bf16[32,5,32,128]{3,2,1,0:T(8,128)(2,1)S(1)}, u32[]{:S(2)}, u32[]{:S(2)}) %all-to-all-start.6) | async-done | bytes 1310752 | tf_op jit(solution)/shard_map/all_to_all | solution.py:30
  134.5 3.9 %collective-permute-start = (bf16[5,32,128]{2,1,0:T(8,128)(2,1)S(1)}, bf16[5,32,128]{2,1,0:T(8,128)(2,1)S(1)}, u32[]{:S(2)}, u32[]{:S(2)}) collective-permute-start(bf16[5,32,128]{2,1,0:T(8,128)(2,1)S(1)} %reduce_sum.82), channel_id=1, source_target_pairs={{0,0},{1,32},{2,64},{3,96},{4,128},{5,160},{6,192},{7,224},{8,8},{... | collective-permute-start | bytes 122888 | tf_op jit(solution)/shard_map/ppermute | solution.py:244
  138.5 3.7 %collective-permute-done = bf16[5,32,128]{2,1,0:T(8,128)(2,1)S(1)} collective-permute-done((bf16[5,32,128]{2,1,0:T(8,128)(2,1)S(1)}, bf16[5,32,128]{2,1,0:T(8,128)(2,1)S(1)}, u32[]{:S(2)}, u32[]{:S(2)}) %collective-permute-start) | collective-permute-done | bytes 40992 | tf_op jit(solution)/shard_map/ppermute | solution.py:244
  143.0 1.8 fusion.16
  145.5 9.1 %all-to-all-start.7 = ((bf16[32,32,128]{2,1,0:T(8,128)(2,1)}), bf16[32,32,128]{2,1,0:T(8,128)(2,1)S(1)}, u32[]{:S(2)}, u32[]{:S(2)}) async-start(bf16[32,32,128]{2,1,0:T(8,128)(2,1)} %bitcast.43), calls=%async_computation.7 | async-start | bytes 524288 | tf_op jit(solution)/shard_map/all_to_all | solution.py:30
  156.3 1.7 fusion.93
  158.0 1.7 fusion.91
  159.8 2.6 all-to-all-done.7
  162.6 1.7 fusion.19
  165.1 5.0 %all-to-all-start.8 = ((bf16[32,32,128]{2,1,0:T(8,128)(2,1)}), bf16[32,32,128]{2,1,0:T(8,128)(2,1)S(1)}, u32[]{:S(2)}, u32[]{:S(2)}) async-start(bf16[32,32,128]{2,1,0:T(8,128)(2,1)} %bitcast.51), calls=%async_computation.8 | async-start | bytes 524288 | tf_op jit(solution)/shard_map/all_to_all | solution.py:30
  170.1 1.7 convolution_add_fusion.5
  171.8 1.7 convolution_add_fusion.2
  173.5 4.4 %all-to-all-done.8 = bf16[32,32,128]{2,1,0:T(8,128)(2,1)S(1)} async-done(((bf16[32,32,128]{2,1,0:T(8,128)(2,1)}), bf16[32,32,128]{2,1,0:T(8,128)(2,1)S(1)}, u32[]{:S(2)}, u32[]{:S(2)}) %all-to-all-start.8) | async-done | bytes 262176 | tf_op jit(solution)/shard_map/all_to_all | solution.py:30
  180.6 5.2 %all-to-all-start.9 = ((bf16[32,32,128]{2,1,0:T(8,128)(2,1)}), bf16[32,32,128]{2,1,0:T(8,128)(2,1)S(1)}, u32[]{:S(2)}, u32[]{:S(2)}) async-start(bf16[32,32,128]{2,1,0:T(8,128)(2,1)} %bitcast.59), calls=%async_computation.9 | async-start | bytes 524288 | tf_op jit(solution)/shard_map/all_to_all | solution.py:30
  185.7 1.7 convolution_add_fusion.3
  187.4 6.1 %all-to-all-done.9 = bf16[32,32,128]{2,1,0:T(8,128)(2,1)S(1)} async-done(((bf16[32,32,128]{2,1,0:T(8,128)(2,1)}), bf16[32,32,128]{2,1,0:T(8,128)(2,1)S(1)}, u32[]{:S(2)}, u32[]{:S(2)}) %all-to-all-start.9) | async-done | bytes 262176 | tf_op jit(solution)/shard_map/all_to_all | solution.py:30
  193.8 1.7 fusion.17
  195.6 12.4 %all_to_all.100 = bf16[32,32,128]{2,1,0:T(8,128)(2,1)S(1)} all-to-all(bf16[32,32,128]{2,1,0:T(8,128)(2,1)S(1)} %bitcast.354), channel_id=1, replica_groups=mesh['row'=8,'grp'=4,'sub'=8] {'grp','sub'}, dimensions={0} | all-to-all | bytes 524288 | tf_op jit(solution)/shard_map/all_to_all | solution.py:30
  209.2 5.0 %all-to-all-start.11 = ((bf16[32,32,128]{2,1,0:T(8,128)(2,1)}), bf16[32,32,128]{2,1,0:T(8,128)(2,1)S(1)}, u32[]{:S(2)}, u32[]{:S(2)}) async-start(bf16[32,32,128]{2,1,0:T(8,128)(2,1)} %broadcast_in_dim.12), calls=%async_computation.11 | async-start | bytes 524288 | tf_op jit(solution)/shard_map/all_to_all | solution.py:30
  215.0 7.0 %all-to-all-done.11 = bf16[32,32,128]{2,1,0:T(8,128)(2,1)S(1)} async-done(((bf16[32,32,128]{2,1,0:T(8,128)(2,1)}), bf16[32,32,128]{2,1,0:T(8,128)(2,1)S(1)}, u32[]{:S(2)}, u32[]{:S(2)}) %all-to-all-start.11) | async-done | bytes 262176 | tf_op jit(solution)/shard_map/all_to_all | solution.py:30
  222.7 2.5 near_solve.7
  225.2 5.0 %all-to-all-start.12 = ((bf16[32,32,128]{2,1,0:T(8,128)(2,1)}), bf16[32,32,128]{2,1,0:T(8,128)(2,1)S(1)}, u32[]{:S(2)}, u32[]{:S(2)}) async-start(bf16[32,32,128]{2,1,0:T(8,128)(2,1)} %get-tuple-element.23), calls=%async_computation.12 | async-start | bytes 524288 | tf_op jit(solution)/shard_map/all_to_all | solution.py:30
  230.2 2.2 far_rest.6.refs_2_
  232.4 5.6 %all-to-all-done.12 = bf16[32,32,128]{2,1,0:T(8,128)(2,1)S(1)} async-done(((bf16[32,32,128]{2,1,0:T(8,128)(2,1)}), bf16[32,32,128]{2,1,0:T(8,128)(2,1)S(1)}, u32[]{:S(2)}, u32[]{:S(2)}) %all-to-all-start.12) | async-done | bytes 262176 | tf_op jit(solution)/shard_map/all_to_all | solution.py:30
  238.7 2.5 near_solve.8
  241.3 5.0 %all-to-all-start.13 = ((bf16[32,32,128]{2,1,0:T(8,128)(2,1)}), bf16[32,32,128]{2,1,0:T(8,128)(2,1)S(1)}, u32[]{:S(2)}, u32[]{:S(2)}) async-start(bf16[32,32,128]{2,1,0:T(8,128)(2,1)} %get-tuple-element.24), calls=%async_computation.13 | async-start | bytes 524288 | tf_op jit(solution)/shard_map/all_to_all | solution.py:30
  246.2 2.6 far_rest.7.refs_2_
  248.9 5.2 %all-to-all-done.13 = bf16[32,32,128]{2,1,0:T(8,128)(2,1)S(1)} async-done(((bf16[32,32,128]{2,1,0:T(8,128)(2,1)}), bf16[32,32,128]{2,1,0:T(8,128)(2,1)S(1)}, u32[]{:S(2)}, u32[]{:S(2)}) %all-to-all-start.13) | async-done | bytes 262176 | tf_op jit(solution)/shard_map/all_to_all | solution.py:30
  254.8 2.5 near_solve.9
  257.3 5.0 %all-to-all-start.14 = ((bf16[32,32,128]{2,1,0:T(8,128)(2,1)}), bf16[32,32,128]{2,1,0:T(8,128)(2,1)S(1)}, u32[]{:S(2)}, u32[]{:S(2)}) async-start(bf16[32,32,128]{2,1,0:T(8,128)(2,1)} %get-tuple-element.25), calls=%async_computation.14 | async-start | bytes 524288 | tf_op jit(solution)/shard_map/all_to_all | solution.py:30
  262.3 3.1 far_rest.8.refs_2_
  265.4 4.7 %all-to-all-done.14 = bf16[32,32,128]{2,1,0:T(8,128)(2,1)S(1)} async-done(((bf16[32,32,128]{2,1,0:T(8,128)(2,1)}), bf16[32,32,128]{2,1,0:T(8,128)(2,1)S(1)}, u32[]{:S(2)}, u32[]{:S(2)}) %all-to-all-start.14) | async-done | bytes 262176 | tf_op jit(solution)/shard_map/all_to_all | solution.py:30
  270.8 2.5 near_solve.10
  274.1 16.6 %all_to_all.101 = bf16[8,5,32,128]{3,2,1,0:T(8,128)(2,1)S(1)} all-to-all(bf16[8,5,32,128]{3,2,1,0:T(8,128)(2,1)S(1)} %broadcast_in_dim.13), channel_id=1, replica_groups=mesh['row'=8,'grp'=4,'sub'=8] {'row'}, dimensions={0} | all-to-all | bytes 655360 | tf_op jit(solution)/shard_map/all_to_all | solution.py:30
  290.7 4.8 %all-to-all-start.16 = ((bf16[32,32,128]{2,1,0:T(8,128)(2,1)}), bf16[32,32,128]{2,1,0:T(8,128)(2,1)S(1)}, u32[]{:S(2)}, u32[]{:S(2)}) async-start(bf16[32,32,128]{2,1,0:T(8,128)(2,1)} %get-tuple-element.31), calls=%async_computation.16 | async-start | bytes 524288 | tf_op jit(solution)/shard_map/all_to_all | solution.py:30
  296.9 3.6 far_rest.9.refs_2_
  300.5 2.8 all-to-all-done.16
  304.0 2.5 near_solve.11
  306.5 5.0 %all-to-all-start.17 = ((bf16[32,32,128]{2,1,0:T(8,128)(2,1)}), bf16[32,32,128]{2,1,0:T(8,128)(2,1)S(1)}, u32[]{:S(2)}, u32[]{:S(2)}) async-start(bf16[32,32,128]{2,1,0:T(8,128)(2,1)} %get-tuple-element.33), calls=%async_computation.17 | async-start | bytes 524288 | tf_op jit(solution)/shard_map/all_to_all | solution.py:30
  314.2 4.1 %far_rest.10.refs_2_ = f32[32,128]{1,0:T(8,128)} custom-call(f32[32,128]{1,0:T(8,128)} %constant_dynamic-slice_fusion.1.refs_0_, bf16[4,8,32,128]{3,2,1,0:T(8,128)(2,1)} %bitcast.321, bf16[4,8,32,128]{3,2,1,0:T(8,128)(2,1)} %bitcast.327, bf16[4,8,32,128]{3,2,1,0:T(8,128)(2,1)} %bitcast.332, bf16[4,8,32,128]{3,2,1,0:T(8,128)(2,1)} %bitcast.336, ...), custom_call_target="tpu_custom_call" | custom-call | flops 167772160 | bytes 5242880 | tf_op jit(solution)/shard_map/far_rest/pallas_call | solution.py:129
  320.0 2.5 near_solve.12
  322.5 6.5 %all-to-all-start.18 = ((bf16[32,32,128]{2,1,0:T(8,128)(2,1)}), bf16[32,32,128]{2,1,0:T(8,128)(2,1)S(1)}, u32[]{:S(2)}, u32[]{:S(2)}) async-start(bf16[32,32,128]{2,1,0:T(8,128)(2,1)} %get-tuple-element.34), calls=%async_computation.18 | async-start | bytes 524288 | tf_op jit(solution)/shard_map/all_to_all | solution.py:30
  329.0 2.6 far_rest.11.refs_10_
  331.7 8.5 %all-gather.11.cloned.1.call-done = bf16[160,128,128]{2,1,0:T(8,128)(2,1)} async-done(((bf16[20,128,128]{2,1,0:T(8,128)(2,1)}), bf16[160,128,128]{2,1,0:T(8,128)(2,1)}) %all-gather.11.cloned.1.call-update) | async-done | bytes 5242896 | tf_op jit(solution)/shard_map/all_gather | solution.py:205
  340.9 4.4 %near_solve.13 = (f32[32,128]{1,0:T(8,128)}, bf16[32,32,128]{2,1,0:T(8,128)(2,1)}) custom-call(bf16[4,8,32,128]{3,2,1,0:T(8,128)(2,1)} %bitcast.333, bf16[4,8,32,128]{3,2,1,0:T(8,128)(2,1)} %bitcast.337, bf16[4,8,32,128]{3,2,1,0:T(8,128)(2,1)} %bitcast.340, bf16[4,8,32,128]{3,2,1,0:T(8,128)(2,1)} %bitcast.347, bf16[4,8,32,128]{3,2,1,0:T(8,128)(2,1)} %bitcast.348, ...), custom_call_target="tpu_custom_call" | custom-call | flops 167772160 | bytes 5242880 | tf_op jit(solution)/shard_map/near_solve/pallas_call | solution.py:149
  346.0 14.5 %all_to_all.102 = bf16[8,3,32,128]{3,2,1,0:T(8,128)(2,1)S(1)} all-to-all(bf16[8,3,32,128]{3,2,1,0:T(8,128)(2,1)S(1)} %broadcast_in_dim.14), channel_id=1, replica_groups=mesh['row'=8,'grp'=4,'sub'=8] {'row'}, dimensions={0} | all-to-all | bytes 393216 | tf_op jit(solution)/shard_map/all_to_all | solution.py:30
  (126 shorter events, 51.5 us)
Async XLA Ops:
  6.5 5.1 %copy-start.8 = (f32[8,1,128,256]{3,2,1,0:T(8,128)S(1)}, f32[8,1,128,256]{3,2,1,0:T(8,128)}, u32[]{:S(2)}) copy-start(f32[8,1,128,256]{3,2,1,0:T(8,128)} %param.6) | copy-start | bytes 3145732
  6.5 5.4 %copy-start.6 = (f32[8,1,128,128]{3,2,1,0:T(8,128)S(1)}, f32[8,1,128,128]{3,2,1,0:T(8,128)}, u32[]{:S(2)}) copy-start(f32[8,1,128,128]{3,2,1,0:T(8,128)} %param.7) | copy-start | bytes 1572868
  6.5 136.5 %all-gather.7.cloned.1.call-start = ((), (), s32[]{:S(2)}) async-start(), calls=%async_computation.20 | async-start | bytes 11796480 | tf_op jit(solution)/shard_map/all_gather | solution.py:205
  11.5 5.1 %copy-start.12 = (s32[32,1,8,1]{0,3,2,1:T(1,128)S(1)}, s32[32,1,8,1]{0,3,2,1:T(1,128)}, u32[]{:S(2)}) copy-start(s32[32,1,8,1]{0,3,2,1:T(1,128)} %param.5) | copy-start | bytes 3076
  11.5 285.3 %all-gather.9.cloned.1.call-start = ((), (), s32[]{:S(2)}) async-start(), calls=%async_computation.21 | async-start | bytes 15335424 | tf_op jit(solution)/shard_map/all_gather | solution.py:205
  19.1 15.3 %all-to-all-start = ((bf16[32,32,128]{2,1,0:T(8,128)(2,1)}), bf16[32,32,128]{2,1,0:T(8,128)(2,1)S(1)}, u32[]{:S(2)}, u32[]{:S(2)}) async-start(bf16[32,32,128]{2,1,0:T(8,128)(2,1)} %bitcast.12), calls=%async_computation | async-start | bytes 524288 | tf_op jit(solution)/shard_map/all_to_all | solution.py:30
  35.1 17.9 %all-to-all-start.1 = ((bf16[8,32,128]{2,1,0:T(8,128)(2,1)}), bf16[8,32,128]{2,1,0:T(8,128)(2,1)}, u32[]{:S(2)}, u32[]{:S(2)}) async-start(bf16[8,32,128]{2,1,0:T(8,128)(2,1)} %broadcast_in_dim.10), calls=%async_computation.1 | async-start | bytes 131072 | tf_op jit(solution)/shard_map/all_to_all | solution.py:30
  53.0 8.8 %all-to-all-start.2 = ((bf16[8,32,128]{2,1,0:T(8,128)(2,1)}), bf16[8,32,128]{2,1,0:T(8,128)(2,1)S(1)}, u32[]{:S(2)}, u32[]{:S(2)}) async-start(bf16[8,32,128]{2,1,0:T(8,128)(2,1)} %all-to-all-done.1), calls=%async_computation.2 | async-start | bytes 131072 | tf_op jit(solution)/shard_map/all_to_all | solution.py:30
  64.8 12.8 %all-to-all-start.3 = ((bf16[32,32,128]{2,1,0:T(8,128)(2,1)}), bf16[32,32,128]{2,1,0:T(8,128)(2,1)S(1)}, u32[]{:S(2)}, u32[]{:S(2)}) async-start(bf16[32,32,128]{2,1,0:T(8,128)(2,1)} %bitcast.20), calls=%async_computation.3 | async-start | bytes 524288 | tf_op jit(solution)/shard_map/all_to_all | solution.py:30
  78.3 13.4 %all-to-all-start.4 = ((bf16[8,32,128]{2,1,0:T(8,128)(2,1)}), bf16[8,32,128]{2,1,0:T(8,128)(2,1)}, u32[]{:S(2)}, u32[]{:S(2)}) async-start(bf16[8,32,128]{2,1,0:T(8,128)(2,1)} %broadcast_in_dim.11), calls=%async_computation.4 | async-start | bytes 131072 | tf_op jit(solution)/shard_map/all_to_all | solution.py:30
  91.7 8.8 %all-to-all-start.5 = ((bf16[8,32,128]{2,1,0:T(8,128)(2,1)}), bf16[8,32,128]{2,1,0:T(8,128)(2,1)S(1)}, u32[]{:S(2)}, u32[]{:S(2)}) async-start(bf16[8,32,128]{2,1,0:T(8,128)(2,1)} %all-to-all-done.4), calls=%async_computation.5 | async-start | bytes 131072 | tf_op jit(solution)/shard_map/all_to_all | solution.py:30
  110.2 24.1 %all-to-all-start.6 = ((bf16[32,5,32,128]{3,2,1,0:T(8,128)(2,1)}), bf16[32,5,32,128]{3,2,1,0:T(8,128)(2,1)S(1)}, u32[]{:S(2)}, u32[]{:S(2)}) async-start(bf16[32,5,32,128]{3,2,1,0:T(8,128)(2,1)} %copy.40), calls=%async_computation.6 | async-start | bytes 2621440 | tf_op jit(solution)/shard_map/all_to_all | solution.py:30
  115.3 224.9 %all-gather.11.cloned.1.call-start = ((), (), s32[]{:S(2)}) async-start(), calls=%async_computation.22 | async-start | bytes 5898240 | tf_op jit(solution)/shard_map/all_gather | solution.py:205
  134.5 7.7 %collective-permute-start = (bf16[5,32,128]{2,1,0:T(8,128)(2,1)S(1)}, bf16[5,32,128]{2,1,0:T(8,128)(2,1)S(1)}, u32[]{:S(2)}, u32[]{:S(2)}) collective-permute-start(bf16[5,32,128]{2,1,0:T(8,128)(2,1)S(1)} %reduce_sum.82), channel_id=1, source_target_pairs={{0,0},{1,32},{2,64},{3,96},{4,128},{5,160},{6,192},{7,224},{8,8},{... | collective-permute-start | bytes 122888 | tf_op jit(solution)/shard_map/ppermute | solution.py:244
  145.5 16.8 %all-to-all-start.7 = ((bf16[32,32,128]{2,1,0:T(8,128)(2,1)}), bf16[32,32,128]{2,1,0:T(8,128)(2,1)S(1)}, u32[]{:S(2)}, u32[]{:S(2)}) async-start(bf16[32,32,128]{2,1,0:T(8,128)(2,1)} %bitcast.43), calls=%async_computation.7 | async-start | bytes 524288 | tf_op jit(solution)/shard_map/all_to_all | solution.py:30
  162.6 33.0 %copy-start.9 = (f32[32,128]{1,0:T(8,128)}, f32[32,128]{1,0:T(8,128)S(1)}, u32[]{:S(2)}) copy-start(f32[32,128]{1,0:T(8,128)S(1)} %fusion.68.refs_0_) | copy-start | bytes 49156
  165.1 12.8 %all-to-all-start.8 = ((bf16[32,32,128]{2,1,0:T(8,128)(2,1)}), bf16[32,32,128]{2,1,0:T(8,128)(2,1)S(1)}, u32[]{:S(2)}, u32[]{:S(2)}) async-start(bf16[32,32,128]{2,1,0:T(8,128)(2,1)} %bitcast.51), calls=%async_computation.8 | async-start | bytes 524288 | tf_op jit(solution)/shard_map/all_to_all | solution.py:30
  178.1 47.1 %copy-start.10 = (f32[32,128]{1,0:T(8,128)}, f32[32,128]{1,0:T(8,128)S(1)}, u32[]{:S(2)}) copy-start(f32[32,128]{1,0:T(8,128)S(1)} %fusion.64.refs_0_) | copy-start | bytes 49156
  180.6 13.0 %all-to-all-start.9 = ((bf16[32,32,128]{2,1,0:T(8,128)(2,1)}), bf16[32,32,128]{2,1,0:T(8,128)(2,1)S(1)}, u32[]{:S(2)}, u32[]{:S(2)}) async-start(bf16[32,32,128]{2,1,0:T(8,128)(2,1)} %bitcast.59), calls=%async_computation.9 | async-start | bytes 524288 | tf_op jit(solution)/shard_map/all_to_all | solution.py:30
  193.8 28.2 %copy-start.11 = (f32[32,128]{1,0:T(8,128)}, f32[32,128]{1,0:T(8,128)S(1)}, u32[]{:S(2)}) copy-start(f32[32,128]{1,0:T(8,128)S(1)} %fusion.60.refs_2_) | copy-start | bytes 49156
  209.2 12.8 %all-to-all-start.11 = ((bf16[32,32,128]{2,1,0:T(8,128)(2,1)}), bf16[32,32,128]{2,1,0:T(8,128)(2,1)S(1)}, u32[]{:S(2)}, u32[]{:S(2)}) async-start(bf16[32,32,128]{2,1,0:T(8,128)(2,1)} %broadcast_in_dim.12), calls=%async_computation.11 | async-start | bytes 524288 | tf_op jit(solution)/shard_map/all_to_all | solution.py:30
  222.0 0.7 copy-start
  225.2 12.8 %all-to-all-start.12 = ((bf16[32,32,128]{2,1,0:T(8,128)(2,1)}), bf16[32,32,128]{2,1,0:T(8,128)(2,1)S(1)}, u32[]{:S(2)}, u32[]{:S(2)}) async-start(bf16[32,32,128]{2,1,0:T(8,128)(2,1)} %get-tuple-element.23), calls=%async_computation.12 | async-start | bytes 524288 | tf_op jit(solution)/shard_map/all_to_all | solution.py:30
  238.0 0.7 copy-start.1
  241.3 12.8 %all-to-all-start.13 = ((bf16[32,32,128]{2,1,0:T(8,128)(2,1)}), bf16[32,32,128]{2,1,0:T(8,128)(2,1)S(1)}, u32[]{:S(2)}, u32[]{:S(2)}) async-start(bf16[32,32,128]{2,1,0:T(8,128)(2,1)} %get-tuple-element.24), calls=%async_computation.13 | async-start | bytes 524288 | tf_op jit(solution)/shard_map/all_to_all | solution.py:30
  254.0 0.7 copy-start.2
  257.3 12.8 %all-to-all-start.14 = ((bf16[32,32,128]{2,1,0:T(8,128)(2,1)}), bf16[32,32,128]{2,1,0:T(8,128)(2,1)S(1)}, u32[]{:S(2)}, u32[]{:S(2)}) async-start(bf16[32,32,128]{2,1,0:T(8,128)(2,1)} %get-tuple-element.25), calls=%async_computation.14 | async-start | bytes 524288 | tf_op jit(solution)/shard_map/all_to_all | solution.py:30
  265.4 8.6 %copy-start.16 = (f32[32,128]{1,0:T(8,128)S(1)}, f32[32,128]{1,0:T(8,128)}, u32[]{:S(2)}) copy-start(f32[32,128]{1,0:T(8,128)} %get-tuple-element.27) | copy-start | bytes 49156
  265.4 8.6 %copy-start.14 = (f32[32,128]{1,0:T(8,128)S(1)}, f32[32,128]{1,0:T(8,128)}, u32[]{:S(2)}) copy-start(f32[32,128]{1,0:T(8,128)} %get-tuple-element.28) | copy-start | bytes 49156
  265.4 8.7 %copy-start.13 = (f32[32,128]{1,0:T(8,128)S(1)}, f32[32,128]{1,0:T(8,128)}, u32[]{:S(2)}) copy-start(f32[32,128]{1,0:T(8,128)} %get-tuple-element.29) | copy-start | bytes 49156
  270.1 0.7 copy-start.3
  290.7 12.6 %all-to-all-start.16 = ((bf16[32,32,128]{2,1,0:T(8,128)(2,1)}), bf16[32,32,128]{2,1,0:T(8,128)(2,1)S(1)}, u32[]{:S(2)}, u32[]{:S(2)}) async-start(bf16[32,32,128]{2,1,0:T(8,128)(2,1)} %get-tuple-element.31), calls=%async_computation.16 | async-start | bytes 524288 | tf_op jit(solution)/shard_map/all_to_all | solution.py:30
  303.3 0.7 copy-start.4
  306.5 12.8 %all-to-all-start.17 = ((bf16[32,32,128]{2,1,0:T(8,128)(2,1)}), bf16[32,32,128]{2,1,0:T(8,128)(2,1)S(1)}, u32[]{:S(2)}, u32[]{:S(2)}) async-start(bf16[32,32,128]{2,1,0:T(8,128)(2,1)} %get-tuple-element.33), calls=%async_computation.17 | async-start | bytes 524288 | tf_op jit(solution)/shard_map/all_to_all | solution.py:30
  318.3 10.7 %copy-start.15 = (f32[32,128]{1,0:T(8,128)S(1)}, f32[32,128]{1,0:T(8,128)}, u32[]{:S(2)}) copy-start(f32[32,128]{1,0:T(8,128)} %get-tuple-element.37) | copy-start | bytes 49156
  319.3 0.7 copy-start.5
  322.5 17.7 %all-to-all-start.18 = ((bf16[32,32,128]{2,1,0:T(8,128)(2,1)}), bf16[32,32,128]{2,1,0:T(8,128)(2,1)S(1)}, u32[]{:S(2)}, u32[]{:S(2)}) async-start(bf16[32,32,128]{2,1,0:T(8,128)(2,1)} %get-tuple-element.34), calls=%async_computation.18 | async-start | bytes 524288 | tf_op jit(solution)/shard_map/all_to_all | solution.py:30
  329.0 2.6 copy-start.17
  340.2 0.7 copy-start.7
Sparse Core Ops, SparseCore 0:
  11.7 119.5 all-gather.6
  133.0 141.8 all-gather.8
  276.8 63.3 all-gather.10

commit v8 on v7

--- a/solution.py
+++ b/solution.py
@@ -90,7 +90,7 @@
         copy.wait()
         for i in range((b - a) * PER_ROW):
             block = out_ref[at]
-            out_ref[at] = jnp.where(flags_ref[a * PER_ROW + i, j] != 0, block, 0).astype(BF16)
+            out_ref[at] = jnp.where(flags_ref[j, a * PER_ROW + i] != 0, block, 0).astype(BF16)
             at += 1
 
 
@@ -115,8 +115,12 @@
     )(flags, factor)
 
 
+def near_memory(x):
+    return pltpu.with_memory_space_constraint(x, pltpu.VMEM)
+
+
 def whole(shape):
-    return pl.BlockSpec(shape, lambda s: (0,) * len(shape))
+    return pl.BlockSpec(memory_space=pltpu.VMEM)
 
 
 def column_spec(rows, first, block):
@@ -133,14 +137,14 @@
         + [whole(x.shape) for x in xs]
         + [column_spec(step, f, block) for f in firsts],
         out_specs=whole((part, block)),
-        out_shape=jax.ShapeDtypeStruct((part, block), F32),
+        out_shape=pltpu.VMEM((part, block), F32),
         cost_estimate=pl.CostEstimate(
             flops=2 * len(xs) * n_row * PER_ROW * part * block * block,
             bytes_accessed=2 * len(xs) * n_row * PER_ROW * block * block,
             transcendentals=0,
         ),
         name="far_rest",
-    )(y, *xs, *([packed] * len(xs)))
+    )(near_memory(y), *map(near_memory, xs), *([packed] * len(xs)))
 
 
 def near_solve(xs, packed, firsts, rest, inverse, n_col):
@@ -154,8 +158,8 @@
         + [whole(rest.shape), whole(inverse.shape)],
         out_specs=[whole((part, block)), whole((n_col, part, block))],
         out_shape=[
-            jax.ShapeDtypeStruct((part, block), F32),
-            jax.ShapeDtypeStruct((n_col, part, block), BF16),
+            pltpu.VMEM((part, block), F32),
+            pltpu.VMEM((n_col, part, block), BF16),
         ],
         scratch_shapes=[pltpu.VMEM((part, block), F32)],
         cost_estimate=pl.CostEstimate(
@@ -164,7 +168,7 @@
             transcendentals=0,
         ),
         name="near_solve",
-    )(*xs, *([packed] * len(xs)), rest, inverse)
+    )(*map(near_memory, xs), *([packed] * len(xs)), near_memory(rest), near_memory(inverse))
 
 
 def per_device(factor, pattern, loads, block_inverse):
@@ -197,7 +201,7 @@
         rows = slice((j + 1) * PER_ROW, LEVELS * PER_ROW)
         columns.append(factor[rows, 0, j, 0] * pattern[rows, 0, j, 0].astype(BF16)[:, None, None])
 
-    flags = pattern[:, 0, :, 0]
+    flags = pattern[:, 0, :, 0].T
     flags_after, low[0] = lax.optimization_barrier((flags, low[0]))
     place = {}
     for number, chunk in enumerate(CHUNKS):
@@ -275,6 +279,9 @@
                 place[far[0][0], j][0],
                 [place[t, j][1] for t, _ in far],
             )
+        if j == OUT_SPLIT - 1:
+            upper, rest = lax.optimization_barrier((jnp.stack(out[j + 1 :]).astype(BF16), rest))
+            upper, wide = lax.optimization_barrier((spread(upper, "row", n_row), wide))
         near = exchange(wide, COL).reshape(PER_ROW, n_row, part, block)
         joined.append((j + 1, near))
         out[j], wide = near_solve(
@@ -286,9 +293,6 @@
             n_col,
         )
         later.append((j + 1, near))
-        if j == OUT_SPLIT:
-            upper = spread(jnp.stack(out[j:]).astype(BF16), "row", n_row)
-            upper, wide = lax.optimization_barrier((upper, wide))
 
     lower = spread(jnp.stack(out[:OUT_SPLIT]).astype(BF16), "row", n_row)
     both = jnp.concatenate([lower, upper], axis=1)

time: 372 us -> 370 us (level)
  blocking collectives: 43.5 us -> 60.5 us
  local copies, waits for them, and re-layouts: 21.5 us -> 12.4 us
  Pallas kernels: 48 us -> 40.7 us
  waiting for transfers between devices: 95.9 us -> 102 us
  starting transfers between devices: 98.9 us -> 93.5 us
    all_to_all x3 -> x4, blocking collectives: 43.5 us -> 60.5 us  [exchange(): return lax.all_to_all(pieces, axis, 0, 0, tiled=True)]
    unnamed x42 -> x11, local copies, waits for them, and re-layouts: 6.99 us -> 0.47 us
    all_to_all x17 -> x16, starting transfers between devices: 94.9 us -> 89.5 us  [exchange(): return lax.all_to_all(pieces, axis, 0, 0, tiled=True)]
    pallas_call x6, Pallas kernels: 18.3 us -> 13.2 us  [far_rest(): pl.pallas_call(functools.partial(far_kernel, len(xs)), grid=(FAR_STEPS,),...]
    all_gather x3, waiting for transfers between devices: 8.49 us -> 13.5 us  [per_device(): packed = lax.all_gather(packed, 'row', axis=0)]
    all_to_all x17 -> x16, waiting for transfers between devices: 83.7 us -> 84.6 us  [exchange(): return lax.all_to_all(pieces, axis, 0, 0, tiled=True)]
  transfers between devices with their start and end apart: 21 -> 20, of which waited for: 18 -> 19; matrix products, arithmetic and copies ran while one was open for 16% -> 15% of each run, Pallas kernels for 11% -> 9%
where the time goes in v8:
time: 370 us; the launch traced here: 368 us
  waiting for transfers between devices  102 us (28%)
  starting transfers between devices  93.5 us (25%)
  blocking collectives  60.5 us (16%)
  matrix products  42.9 us (12%)
  Pallas kernels  40.7 us (11%)
  between operations  13.7 us (4%)
  local copies, waits for them, and re-layouts  12.4 us (3%)
    all_to_all x16, starting transfers between devices, exchange(): return lax.all_to_all(pieces, axis, 0, 0, tiled=True)  89.5 us
    all_to_all x16, waiting for transfers between devices, exchange(): return lax.all_to_all(pieces, axis, 0, 0, tiled=True)  84.6 us
    all_to_all x4, blocking collectives, exchange(): return lax.all_to_all(pieces, axis, 0, 0, tiled=True)  60.5 us
    dot_general x18, matrix products, local_sums(): jnp.einsum('sq,apq->asp', low[m], local(t, m), preferred_element_type=F32)  21.9 us
    pallas_call x7, Pallas kernels, near_solve(): pl.pallas_call(functools.partial(near_kernel, len(xs), steps), grid=(step...  17.8 us
    dot_general x10, matrix products, per_device(): jnp.einsum('sq,rapq->arsp', low[m], split(t, m), preferred_element_type=F32)  17.1 us
    all_gather x3, waiting for transfers between devices, per_device(): packed = lax.all_gather(packed, 'row', axis=0)  13.5 us
    pallas_call x6, Pallas kernels, far_rest(): pl.pallas_call(functools.partial(far_kernel, len(xs)), grid=(FAR_STEPS,),...  13.2 us
  transfers between devices with their start and end apart: 20, of which 19 were waited for; matrix products, arithmetic and copies ran while one was open for 15% of the time, Pallas kernels for 9%

profile of v8, /device:TPU:2, one launch (start us, length us, event | category | flops | bytes accessed | tf_op | source)
XLA Modules:
  0.0 367.6 jit_solution(14325894025606013922)
XLA Ops:
  6.5 3.4 pack.3
  11.3 3.5 pack.4
  17.4 7.6 %all-to-all-start = ((bf16[32,32,128]{2,1,0:T(8,128)(2,1)}), bf16[32,32,128]{2,1,0:T(8,128)(2,1)S(1)}, u32[]{:S(2)}, u32[]{:S(2)}) async-start(bf16[32,32,128]{2,1,0:T(8,128)(2,1)} %bitcast.13), calls=%async_computation | async-start | bytes 524288 | tf_op jit(solution)/shard_map/all_to_all | solution.py:30
  30.4 2.3 all-to-all-done
  33.4 8.5 %all-to-all-start.1 = ((bf16[8,32,128]{2,1,0:T(8,128)(2,1)}), bf16[8,32,128]{2,1,0:T(8,128)(2,1)}, u32[]{:S(2)}, u32[]{:S(2)}) async-start(bf16[8,32,128]{2,1,0:T(8,128)(2,1)} %broadcast_in_dim.10), calls=%async_computation.1 | async-start | bytes 131072 | tf_op jit(solution)/shard_map/all_to_all | solution.py:30
  41.9 9.3 %all-to-all-done.1 = bf16[8,32,128]{2,1,0:T(8,128)(2,1)} async-done(((bf16[8,32,128]{2,1,0:T(8,128)(2,1)}), bf16[8,32,128]{2,1,0:T(8,128)(2,1)}, u32[]{:S(2)}, u32[]{:S(2)}) %all-to-all-start.1) | async-done | bytes 65568 | tf_op jit(solution)/shard_map/all_to_all | solution.py:30
  51.3 4.6 %all-to-all-start.2 = ((bf16[8,32,128]{2,1,0:T(8,128)(2,1)}), bf16[8,32,128]{2,1,0:T(8,128)(2,1)S(1)}, u32[]{:S(2)}, u32[]{:S(2)}) async-start(bf16[8,32,128]{2,1,0:T(8,128)(2,1)} %all-to-all-done.1), calls=%async_computation.2 | async-start | bytes 131072 | tf_op jit(solution)/shard_map/all_to_all | solution.py:30
  56.0 4.1 %all-to-all-done.2 = bf16[8,32,128]{2,1,0:T(8,128)(2,1)S(1)} async-done(((bf16[8,32,128]{2,1,0:T(8,128)(2,1)}), bf16[8,32,128]{2,1,0:T(8,128)(2,1)S(1)}, u32[]{:S(2)}, u32[]{:S(2)}) %all-to-all-start.2) | async-done | bytes 65568 | tf_op jit(solution)/shard_map/all_to_all | solution.py:30
  63.1 5.0 %all-to-all-start.3 = ((bf16[32,32,128]{2,1,0:T(8,128)(2,1)}), bf16[32,32,128]{2,1,0:T(8,128)(2,1)S(1)}, u32[]{:S(2)}, u32[]{:S(2)}) async-start(bf16[32,32,128]{2,1,0:T(8,128)(2,1)} %bitcast.21), calls=%async_computation.3 | async-start | bytes 524288 | tf_op jit(solution)/shard_map/all_to_all | solution.py:30
  72.3 3.6 all-to-all-done.3
  76.5 4.0 %all-to-all-start.4 = ((bf16[8,32,128]{2,1,0:T(8,128)(2,1)}), bf16[8,32,128]{2,1,0:T(8,128)(2,1)}, u32[]{:S(2)}, u32[]{:S(2)}) async-start(bf16[8,32,128]{2,1,0:T(8,128)(2,1)} %broadcast_in_dim.11), calls=%async_computation.4 | async-start | bytes 131072 | tf_op jit(solution)/shard_map/all_to_all | solution.py:30
  80.5 2.2 convolution_add_fusion.9
  82.7 7.2 %all-to-all-done.4 = bf16[8,32,128]{2,1,0:T(8,128)(2,1)} async-done(((bf16[8,32,128]{2,1,0:T(8,128)(2,1)}), bf16[8,32,128]{2,1,0:T(8,128)(2,1)}, u32[]{:S(2)}, u32[]{:S(2)}) %all-to-all-start.4) | async-done | bytes 65568 | tf_op jit(solution)/shard_map/all_to_all | solution.py:30
  89.9 4.6 %all-to-all-start.5 = ((bf16[8,32,128]{2,1,0:T(8,128)(2,1)}), bf16[8,32,128]{2,1,0:T(8,128)(2,1)S(1)}, u32[]{:S(2)}, u32[]{:S(2)}) async-start(bf16[8,32,128]{2,1,0:T(8,128)(2,1)} %all-to-all-done.4), calls=%async_computation.5 | async-start | bytes 131072 | tf_op jit(solution)/shard_map/all_to_all | solution.py:30
  94.6 2.3 convolution_add_fusion.7
  96.8 1.9 all-to-all-done.5
  108.5 5.1 %all-to-all-start.6 = ((bf16[32,5,32,128]{3,2,1,0:T(8,128)(2,1)}), bf16[32,5,32,128]{3,2,1,0:T(8,128)(2,1)S(1)}, u32[]{:S(2)}, u32[]{:S(2)}) async-start(bf16[32,5,32,128]{3,2,1,0:T(8,128)(2,1)} %copy.37), calls=%async_computation.6 | async-start | bytes 2621440 | tf_op jit(solution)/shard_map/all_to_all | solution.py:30
  113.6 2.8 pack.5
  116.4 16.1 %all-to-all-done.6 = bf16[32,5,32,128]{3,2,1,0:T(8,128)(2,1)S(1)} async-done(((bf16[32,5,32,128]{3,2,1,0:T(8,128)(2,1)}), bf16[32,5,32,128]{3,2,1,0:T(8,128)(2,1)S(1)}, u32[]{:S(2)}, u32[]{:S(2)}) %all-to-all-start.6) | async-done | bytes 1310752 | tf_op jit(solution)/shard_map/all_to_all | solution.py:30
  132.8 3.9 %collective-permute-start = (bf16[5,32,128]{2,1,0:T(8,128)(2,1)S(1)}, bf16[5,32,128]{2,1,0:T(8,128)(2,1)S(1)}, u32[]{:S(2)}, u32[]{:S(2)}) collective-permute-start(bf16[5,32,128]{2,1,0:T(8,128)(2,1)S(1)} %reduce_sum.82), channel_id=1, source_target_pairs={{0,0},{1,32},{2,64},{3,96},{4,128},{5,160},{6,192},{7,224},{8,8},{... | collective-permute-start | bytes 122888 | tf_op jit(solution)/shard_map/ppermute | solution.py:248
  136.7 3.7 %collective-permute-done = bf16[5,32,128]{2,1,0:T(8,128)(2,1)S(1)} collective-permute-done((bf16[5,32,128]{2,1,0:T(8,128)(2,1)S(1)}, bf16[5,32,128]{2,1,0:T(8,128)(2,1)S(1)}, u32[]{:S(2)}, u32[]{:S(2)}) %collective-permute-start) | collective-permute-done | bytes 40992 | tf_op jit(solution)/shard_map/ppermute | solution.py:248
  140.7 1.8 fusion.16
  143.2 9.2 %all-to-all-start.7 = ((bf16[32,32,128]{2,1,0:T(8,128)(2,1)}), bf16[32,32,128]{2,1,0:T(8,128)(2,1)S(1)}, u32[]{:S(2)}, u32[]{:S(2)}) async-start(bf16[32,32,128]{2,1,0:T(8,128)(2,1)} %bitcast.45), calls=%async_computation.7 | async-start | bytes 524288 | tf_op jit(solution)/shard_map/all_to_all | solution.py:30
  154.1 1.7 fusion.93
  155.8 1.7 fusion.91
  157.5 2.6 all-to-all-done.7
  160.4 1.7 fusion.19
  162.8 5.0 %all-to-all-start.8 = ((bf16[32,32,128]{2,1,0:T(8,128)(2,1)}), bf16[32,32,128]{2,1,0:T(8,128)(2,1)S(1)}, u32[]{:S(2)}, u32[]{:S(2)}) async-start(bf16[32,32,128]{2,1,0:T(8,128)(2,1)} %bitcast.53), calls=%async_computation.8 | async-start | bytes 524288 | tf_op jit(solution)/shard_map/all_to_all | solution.py:30
  167.8 1.7 convolution_add_fusion.5
  169.5 1.7 convolution_add_fusion.2
  171.2 4.4 %all-to-all-done.8 = bf16[32,32,128]{2,1,0:T(8,128)(2,1)S(1)} async-done(((bf16[32,32,128]{2,1,0:T(8,128)(2,1)}), bf16[32,32,128]{2,1,0:T(8,128)(2,1)S(1)}, u32[]{:S(2)}, u32[]{:S(2)}) %all-to-all-start.8) | async-done | bytes 262176 | tf_op jit(solution)/shard_map/all_to_all | solution.py:30
  175.8 1.7 fusion.18
  178.3 5.0 %all-to-all-start.9 = ((bf16[32,32,128]{2,1,0:T(8,128)(2,1)}), bf16[32,32,128]{2,1,0:T(8,128)(2,1)S(1)}, u32[]{:S(2)}, u32[]{:S(2)}) async-start(bf16[32,32,128]{2,1,0:T(8,128)(2,1)} %bitcast.61), calls=%async_computation.9 | async-start | bytes 524288 | tf_op jit(solution)/shard_map/all_to_all | solution.py:30
  183.3 1.7 convolution_add_fusion.3
  185.0 6.1 %all-to-all-done.9 = bf16[32,32,128]{2,1,0:T(8,128)(2,1)S(1)} async-done(((bf16[32,32,128]{2,1,0:T(8,128)(2,1)}), bf16[32,32,128]{2,1,0:T(8,128)(2,1)S(1)}, u32[]{:S(2)}, u32[]{:S(2)}) %all-to-all-start.9) | async-done | bytes 262176 | tf_op jit(solution)/shard_map/all_to_all | solution.py:30
  191.3 1.7 fusion.17
  193.1 12.4 %all_to_all.100 = bf16[32,32,128]{2,1,0:T(8,128)(2,1)S(1)} all-to-all(bf16[32,32,128]{2,1,0:T(8,128)(2,1)S(1)} %bitcast.356), channel_id=1, replica_groups=mesh['row'=8,'grp'=4,'sub'=8] {'grp','sub'}, dimensions={0} | all-to-all | bytes 524288 | tf_op jit(solution)/shard_map/all_to_all | solution.py:30
  206.7 5.0 %all-to-all-start.11 = ((bf16[32,32,128]{2,1,0:T(8,128)(2,1)}), bf16[32,32,128]{2,1,0:T(8,128)(2,1)S(1)}, u32[]{:S(2)}, u32[]{:S(2)}) async-start(bf16[32,32,128]{2,1,0:T(8,128)(2,1)} %broadcast_in_dim.12), calls=%async_computation.11 | async-start | bytes 524288 | tf_op jit(solution)/shard_map/all_to_all | solution.py:30
  211.7 7.8 %all-to-all-done.11 = bf16[32,32,128]{2,1,0:T(8,128)(2,1)S(1)} async-done(((bf16[32,32,128]{2,1,0:T(8,128)(2,1)}), bf16[32,32,128]{2,1,0:T(8,128)(2,1)S(1)}, u32[]{:S(2)}, u32[]{:S(2)}) %all-to-all-start.11) | async-done | bytes 262176 | tf_op jit(solution)/shard_map/all_to_all | solution.py:30
  219.5 2.4 near_solve.7
  221.9 5.0 %all-to-all-start.12 = ((bf16[32,32,128]{2,1,0:T(8,128)(2,1)}), bf16[32,32,128]{2,1,0:T(8,128)(2,1)S(1)}, u32[]{:S(2)}, u32[]{:S(2)}) async-start(bf16[32,32,128]{2,1,0:T(8,128)(2,1)} %get-tuple-element.25), calls=%async_computation.12 | async-start | bytes 524288 | tf_op jit(solution)/shard_map/all_to_all | solution.py:30
  228.4 6.3 %all-to-all-done.12 = bf16[32,32,128]{2,1,0:T(8,128)(2,1)S(1)} async-done(((bf16[32,32,128]{2,1,0:T(8,128)(2,1)}), bf16[32,32,128]{2,1,0:T(8,128)(2,1)S(1)}, u32[]{:S(2)}, u32[]{:S(2)}) %all-to-all-start.12) | async-done | bytes 262176 | tf_op jit(solution)/shard_map/all_to_all | solution.py:30
  234.7 2.4 near_solve.8
  237.1 5.0 %all-to-all-start.13 = ((bf16[32,32,128]{2,1,0:T(8,128)(2,1)}), bf16[32,32,128]{2,1,0:T(8,128)(2,1)S(1)}, u32[]{:S(2)}, u32[]{:S(2)}) async-start(bf16[32,32,128]{2,1,0:T(8,128)(2,1)} %get-tuple-element.26), calls=%async_computation.13 | async-start | bytes 524288 | tf_op jit(solution)/shard_map/all_to_all | solution.py:30
  242.1 1.9 far_rest.7.refs_2_
  244.0 5.9 %all-to-all-done.13 = bf16[32,32,128]{2,1,0:T(8,128)(2,1)S(1)} async-done(((bf16[32,32,128]{2,1,0:T(8,128)(2,1)}), bf16[32,32,128]{2,1,0:T(8,128)(2,1)S(1)}, u32[]{:S(2)}, u32[]{:S(2)}) %all-to-all-start.13) | async-done | bytes 262176 | tf_op jit(solution)/shard_map/all_to_all | solution.py:30
  249.9 2.4 near_solve.9
  252.3 5.0 %all-to-all-start.14 = ((bf16[32,32,128]{2,1,0:T(8,128)(2,1)}), bf16[32,32,128]{2,1,0:T(8,128)(2,1)S(1)}, u32[]{:S(2)}, u32[]{:S(2)}) async-start(bf16[32,32,128]{2,1,0:T(8,128)(2,1)} %get-tuple-element.27), calls=%async_computation.14 | async-start | bytes 524288 | tf_op jit(solution)/shard_map/all_to_all | solution.py:30
  258.1 2.2 far_rest.8.refs_2_
  260.3 4.8 %all-to-all-done.14 = bf16[32,32,128]{2,1,0:T(8,128)(2,1)S(1)} async-done(((bf16[32,32,128]{2,1,0:T(8,128)(2,1)}), bf16[32,32,128]{2,1,0:T(8,128)(2,1)S(1)}, u32[]{:S(2)}, u32[]{:S(2)}) %all-to-all-start.14) | async-done | bytes 262176 | tf_op jit(solution)/shard_map/all_to_all | solution.py:30
  265.1 1.7 near_solve.10
  266.9 6.5 %all-gather.9.cloned.1.call-done = bf16[416,128,128]{2,1,0:T(8,128)(2,1)} async-done(((bf16[52,128,128]{2,1,0:T(8,128)(2,1)}), bf16[416,128,128]{2,1,0:T(8,128)(2,1)}) %all-gather.9.cloned.1.call-update) | async-done | bytes 13631504 | tf_op jit(solution)/shard_map/all_gather | solution.py:209
  273.4 2.6 far_rest.9.refs_2_
  276.1 18.9 %all_to_all.101 = bf16[8,5,32,128]{3,2,1,0:T(8,128)(2,1)S(1)} all-to-all(bf16[8,5,32,128]{3,2,1,0:T(8,128)(2,1)S(1)} %broadcast_in_dim.13), channel_id=1, replica_groups=mesh['row'=8,'grp'=4,'sub'=8] {'row'}, dimensions={0} | all-to-all | bytes 655360 | tf_op jit(solution)/shard_map/all_to_all | solution.py:30
  295.0 14.9 %all_to_all.102 = bf16[32,32,128]{2,1,0:T(8,128)(2,1)S(1)} all-to-all(bf16[32,32,128]{2,1,0:T(8,128)(2,1)S(1)} %get-tuple-element.35), channel_id=1, replica_groups=mesh['row'=8,'grp'=4,'sub'=8] {'grp','sub'}, dimensions={0} | all-to-all | bytes 524288 | tf_op jit(solution)/shard_map/all_to_all | solution.py:30
  309.9 2.4 near_solve.11
  312.3 5.0 %all-to-all-start.17 = ((bf16[32,32,128]{2,1,0:T(8,128)(2,1)}), bf16[32,32,128]{2,1,0:T(8,128)(2,1)S(1)}, u32[]{:S(2)}, u32[]{:S(2)}) async-start(bf16[32,32,128]{2,1,0:T(8,128)(2,1)} %get-tuple-element.37), calls=%async_computation.17 | async-start | bytes 524288 | tf_op jit(solution)/shard_map/all_to_all | solution.py:30
  318.8 1.8 far_rest.11.refs_10_
  320.6 3.1 far_rest.10.refs_2_
  325.1 2.4 near_solve.12
  327.6 6.1 %all-to-all-start.18 = ((bf16[32,32,128]{2,1,0:T(8,128)(2,1)}), bf16[32,32,128]{2,1,0:T(8,128)(2,1)S(1)}, u32[]{:S(2)}, u32[]{:S(2)}) async-start(bf16[32,32,128]{2,1,0:T(8,128)(2,1)} %get-tuple-element.38), calls=%async_computation.18 | async-start | bytes 524288 | tf_op jit(solution)/shard_map/all_to_all | solution.py:30
  333.7 6.9 %all-gather.11.cloned.1.call-done = bf16[160,128,128]{2,1,0:T(8,128)(2,1)} async-done(((bf16[20,128,128]{2,1,0:T(8,128)(2,1)}), bf16[160,128,128]{2,1,0:T(8,128)(2,1)}) %all-gather.11.cloned.1.call-update) | async-done | bytes 5242896 | tf_op jit(solution)/shard_map/all_gather | solution.py:209
  341.4 3.9 %near_solve.13 = (f32[32,128]{1,0:T(8,128)S(1)}, bf16[32,32,128]{2,1,0:T(8,128)(2,1)}) custom-call(bf16[4,8,32,128]{3,2,1,0:T(8,128)(2,1)S(1)} %bitcast.294, bf16[4,8,32,128]{3,2,1,0:T(8,128)(2,1)S(1)} %bitcast.298, bf16[4,8,32,128]{3,2,1,0:T(8,128)(2,1)S(1)} %bitcast.301, bf16[4,8,32,128]{3,2,1,0:T(8,128)(2,1)S(1)} %bitcast.303, ...), custom_call_target="tpu_custom_call" | custom-call | flops 167772160 | bytes 5242880 | tf_op jit(solution)/shard_map/near_solve/pallas_call | solution.py:153
  345.3 14.3 %all_to_all.103 = bf16[8,3,32,128]{3,2,1,0:T(8,128)(2,1)S(1)} all-to-all(bf16[8,3,32,128]{3,2,1,0:T(8,128)(2,1)S(1)} %broadcast_in_dim.14), channel_id=1, replica_groups=mesh['row'=8,'grp'=4,'sub'=8] {'row'}, dimensions={0} | all-to-all | bytes 393216 | tf_op jit(solution)/shard_map/all_to_all | solution.py:30
  (94 shorter events, 41.3 us)
Async XLA Ops:
  6.5 3.5 copy-start.1
  6.5 3.9 %copy-start = (f32[8,1,128,128]{3,2,1,0:T(8,128)S(1)}, f32[8,1,128,128]{3,2,1,0:T(8,128)}, u32[]{:S(2)}) copy-start(f32[8,1,128,128]{3,2,1,0:T(8,128)} %param.7) | copy-start | bytes 1572868
  6.5 134.2 %all-gather.7.cloned.1.call-start = ((), (), s32[]{:S(2)}) async-start(), calls=%async_computation.20 | async-start | bytes 11796480 | tf_op jit(solution)/shard_map/all_gather | solution.py:209
  10.0 4.9 %copy-start.2 = (s32[32,1,8,1]{0,3,2,1:T(1,128)S(1)}, s32[32,1,8,1]{0,3,2,1:T(1,128)}, u32[]{:S(2)}) copy-start(s32[32,1,8,1]{0,3,2,1:T(1,128)} %param.5) | copy-start | bytes 3076
  10.0 263.4 %all-gather.9.cloned.1.call-start = ((), (), s32[]{:S(2)}) async-start(), calls=%async_computation.21 | async-start | bytes 15335424 | tf_op jit(solution)/shard_map/all_gather | solution.py:209
  17.4 15.3 %all-to-all-start = ((bf16[32,32,128]{2,1,0:T(8,128)(2,1)}), bf16[32,32,128]{2,1,0:T(8,128)(2,1)S(1)}, u32[]{:S(2)}, u32[]{:S(2)}) async-start(bf16[32,32,128]{2,1,0:T(8,128)(2,1)} %bitcast.13), calls=%async_computation | async-start | bytes 524288 | tf_op jit(solution)/shard_map/all_to_all | solution.py:30
  33.4 17.9 %all-to-all-start.1 = ((bf16[8,32,128]{2,1,0:T(8,128)(2,1)}), bf16[8,32,128]{2,1,0:T(8,128)(2,1)}, u32[]{:S(2)}, u32[]{:S(2)}) async-start(bf16[8,32,128]{2,1,0:T(8,128)(2,1)} %broadcast_in_dim.10), calls=%async_computation.1 | async-start | bytes 131072 | tf_op jit(solution)/shard_map/all_to_all | solution.py:30
  51.3 8.8 %all-to-all-start.2 = ((bf16[8,32,128]{2,1,0:T(8,128)(2,1)}), bf16[8,32,128]{2,1,0:T(8,128)(2,1)S(1)}, u32[]{:S(2)}, u32[]{:S(2)}) async-start(bf16[8,32,128]{2,1,0:T(8,128)(2,1)} %all-to-all-done.1), calls=%async_computation.2 | async-start | bytes 131072 | tf_op jit(solution)/shard_map/all_to_all | solution.py:30
  63.1 12.8 %all-to-all-start.3 = ((bf16[32,32,128]{2,1,0:T(8,128)(2,1)}), bf16[32,32,128]{2,1,0:T(8,128)(2,1)S(1)}, u32[]{:S(2)}, u32[]{:S(2)}) async-start(bf16[32,32,128]{2,1,0:T(8,128)(2,1)} %bitcast.21), calls=%async_computation.3 | async-start | bytes 524288 | tf_op jit(solution)/shard_map/all_to_all | solution.py:30
  76.5 13.4 %all-to-all-start.4 = ((bf16[8,32,128]{2,1,0:T(8,128)(2,1)}), bf16[8,32,128]{2,1,0:T(8,128)(2,1)}, u32[]{:S(2)}, u32[]{:S(2)}) async-start(bf16[8,32,128]{2,1,0:T(8,128)(2,1)} %broadcast_in_dim.11), calls=%async_computation.4 | async-start | bytes 131072 | tf_op jit(solution)/shard_map/all_to_all | solution.py:30
  89.9 8.8 %all-to-all-start.5 = ((bf16[8,32,128]{2,1,0:T(8,128)(2,1)}), bf16[8,32,128]{2,1,0:T(8,128)(2,1)S(1)}, u32[]{:S(2)}, u32[]{:S(2)}) async-start(bf16[8,32,128]{2,1,0:T(8,128)(2,1)} %all-to-all-done.4), calls=%async_computation.5 | async-start | bytes 131072 | tf_op jit(solution)/shard_map/all_to_all | solution.py:30
  108.5 24.1 %all-to-all-start.6 = ((bf16[32,5,32,128]{3,2,1,0:T(8,128)(2,1)}), bf16[32,5,32,128]{3,2,1,0:T(8,128)(2,1)S(1)}, u32[]{:S(2)}, u32[]{:S(2)}) async-start(bf16[32,5,32,128]{3,2,1,0:T(8,128)(2,1)} %copy.37), calls=%async_computation.6 | async-start | bytes 2621440 | tf_op jit(solution)/shard_map/all_to_all | solution.py:30
  113.6 227.1 %all-gather.11.cloned.1.call-start = ((), (), s32[]{:S(2)}) async-start(), calls=%async_computation.22 | async-start | bytes 5898240 | tf_op jit(solution)/shard_map/all_gather | solution.py:209
  132.8 7.7 %collective-permute-start = (bf16[5,32,128]{2,1,0:T(8,128)(2,1)S(1)}, bf16[5,32,128]{2,1,0:T(8,128)(2,1)S(1)}, u32[]{:S(2)}, u32[]{:S(2)}) collective-permute-start(bf16[5,32,128]{2,1,0:T(8,128)(2,1)S(1)} %reduce_sum.82), channel_id=1, source_target_pairs={{0,0},{1,32},{2,64},{3,96},{4,128},{5,160},{6,192},{7,224},{8,8},{... | collective-permute-start | bytes 122888 | tf_op jit(solution)/shard_map/ppermute | solution.py:248
  143.2 16.9 %all-to-all-start.7 = ((bf16[32,32,128]{2,1,0:T(8,128)(2,1)}), bf16[32,32,128]{2,1,0:T(8,128)(2,1)S(1)}, u32[]{:S(2)}, u32[]{:S(2)}) async-start(bf16[32,32,128]{2,1,0:T(8,128)(2,1)} %bitcast.45), calls=%async_computation.7 | async-start | bytes 524288 | tf_op jit(solution)/shard_map/all_to_all | solution.py:30
  162.8 12.8 %all-to-all-start.8 = ((bf16[32,32,128]{2,1,0:T(8,128)(2,1)}), bf16[32,32,128]{2,1,0:T(8,128)(2,1)S(1)}, u32[]{:S(2)}, u32[]{:S(2)}) async-start(bf16[32,32,128]{2,1,0:T(8,128)(2,1)} %bitcast.53), calls=%async_computation.8 | async-start | bytes 524288 | tf_op jit(solution)/shard_map/all_to_all | solution.py:30
  178.3 12.8 %all-to-all-start.9 = ((bf16[32,32,128]{2,1,0:T(8,128)(2,1)}), bf16[32,32,128]{2,1,0:T(8,128)(2,1)S(1)}, u32[]{:S(2)}, u32[]{:S(2)}) async-start(bf16[32,32,128]{2,1,0:T(8,128)(2,1)} %bitcast.61), calls=%async_computation.9 | async-start | bytes 524288 | tf_op jit(solution)/shard_map/all_to_all | solution.py:30
  206.7 12.8 %all-to-all-start.11 = ((bf16[32,32,128]{2,1,0:T(8,128)(2,1)}), bf16[32,32,128]{2,1,0:T(8,128)(2,1)S(1)}, u32[]{:S(2)}, u32[]{:S(2)}) async-start(bf16[32,32,128]{2,1,0:T(8,128)(2,1)} %broadcast_in_dim.12), calls=%async_computation.11 | async-start | bytes 524288 | tf_op jit(solution)/shard_map/all_to_all | solution.py:30
  221.9 12.8 %all-to-all-start.12 = ((bf16[32,32,128]{2,1,0:T(8,128)(2,1)}), bf16[32,32,128]{2,1,0:T(8,128)(2,1)S(1)}, u32[]{:S(2)}, u32[]{:S(2)}) async-start(bf16[32,32,128]{2,1,0:T(8,128)(2,1)} %get-tuple-element.25), calls=%async_computation.12 | async-start | bytes 524288 | tf_op jit(solution)/shard_map/all_to_all | solution.py:30
  237.1 12.8 %all-to-all-start.13 = ((bf16[32,32,128]{2,1,0:T(8,128)(2,1)}), bf16[32,32,128]{2,1,0:T(8,128)(2,1)S(1)}, u32[]{:S(2)}, u32[]{:S(2)}) async-start(bf16[32,32,128]{2,1,0:T(8,128)(2,1)} %get-tuple-element.26), calls=%async_computation.13 | async-start | bytes 524288 | tf_op jit(solution)/shard_map/all_to_all | solution.py:30
  252.3 12.8 %all-to-all-start.14 = ((bf16[32,32,128]{2,1,0:T(8,128)(2,1)}), bf16[32,32,128]{2,1,0:T(8,128)(2,1)S(1)}, u32[]{:S(2)}, u32[]{:S(2)}) async-start(bf16[32,32,128]{2,1,0:T(8,128)(2,1)} %get-tuple-element.27), calls=%async_computation.14 | async-start | bytes 524288 | tf_op jit(solution)/shard_map/all_to_all | solution.py:30
  312.3 12.8 %all-to-all-start.17 = ((bf16[32,32,128]{2,1,0:T(8,128)(2,1)}), bf16[32,32,128]{2,1,0:T(8,128)(2,1)S(1)}, u32[]{:S(2)}, u32[]{:S(2)}) async-start(bf16[32,32,128]{2,1,0:T(8,128)(2,1)} %get-tuple-element.37), calls=%async_computation.17 | async-start | bytes 524288 | tf_op jit(solution)/shard_map/all_to_all | solution.py:30
  327.6 13.8 %all-to-all-start.18 = ((bf16[32,32,128]{2,1,0:T(8,128)(2,1)}), bf16[32,32,128]{2,1,0:T(8,128)(2,1)S(1)}, u32[]{:S(2)}, u32[]{:S(2)}) async-start(bf16[32,32,128]{2,1,0:T(8,128)(2,1)} %get-tuple-element.38), calls=%async_computation.18 | async-start | bytes 524288 | tf_op jit(solution)/shard_map/all_to_all | solution.py:30
Sparse Core Ops, SparseCore 0:
  10.1 119.5 all-gather.6
  131.5 141.8 all-gather.8
  275.2 65.3 all-gather.10

commit v9 on v8

--- a/solution.py
+++ b/solution.py
@@ -74,24 +74,29 @@
                 low_ref[...] = jnp.broadcast_to(solved.astype(BF16)[None], low_ref.shape)
 
 
-def pack_kernel(chunk, flags_ref, factor_ref, out_ref, sems):
-    copies, at = [], 0
+def pack_kernel(chunk, flags_ref, factor_ref, out_ref, held_ref, in_sems, out_sems):
+    ins, outs, at = [], [], 0
     for n, (j, a, b) in enumerate(chunk):
         size = (b - a) * PER_ROW
-        copies.append(
+        held = held_ref.at[pl.ds(at, size)]
+        ins.append(
             pltpu.make_async_copy(
-                factor_ref.at[pl.ds(a * PER_ROW, size), j], out_ref.at[pl.ds(at, size)], sems.at[n]
+                factor_ref.at[pl.ds(a * PER_ROW, size), j], held, in_sems.at[n]
             )
         )
-        copies[-1].start()
+        outs.append(pltpu.make_async_copy(held, out_ref.at[pl.ds(at, size)], out_sems.at[n]))
+        ins[-1].start()
         at += size
     at = 0
-    for copy, (j, a, b) in zip(copies, chunk):
-        copy.wait()
+    for n, (j, a, b) in enumerate(chunk):
+        ins[n].wait()
         for i in range((b - a) * PER_ROW):
-            block = out_ref[at]
-            out_ref[at] = jnp.where(flags_ref[j, a * PER_ROW + i] != 0, block, 0).astype(BF16)
+            block = held_ref[at]
+            held_ref[at] = jnp.where(flags_ref[j, a * PER_ROW + i] != 0, block, 0).astype(BF16)
             at += 1
+        outs[n].start()
+    for out in outs:
+        out.wait()
 
 
 def pack(chunk, factor, flags):
@@ -103,9 +108,13 @@
             pl.BlockSpec(memory_space=pltpu.SMEM),
             pl.BlockSpec(memory_space=pl.ANY),
         ],
-        out_specs=pl.BlockSpec(memory_space=pltpu.VMEM),
+        out_specs=pl.BlockSpec(memory_space=pl.ANY),
         out_shape=jax.ShapeDtypeStruct(shape, factor.dtype),
-        scratch_shapes=[pltpu.SemaphoreType.DMA((len(chunk),))],
+        scratch_shapes=[
+            pltpu.VMEM(shape, factor.dtype),
+            pltpu.SemaphoreType.DMA((len(chunk),)),
+            pltpu.SemaphoreType.DMA((len(chunk),)),
+        ],
         cost_estimate=pl.CostEstimate(
             flops=count * shape[1] * shape[2],
             bytes_accessed=4 * count * shape[1] * shape[2],
@@ -149,7 +158,7 @@
 
 def near_solve(xs, packed, firsts, rest, inverse, n_col):
     n_row, part, block = xs[0].shape[1:]
-    steps = 1 if len(xs) == 1 else FAR_STEPS
+    steps = 1 if len(xs) == 1 else 2 * FAR_STEPS
     return pl.pallas_call(
         functools.partial(near_kernel, len(xs), steps),
         grid=(steps,),

time: 370 us -> 371 us (level)
  no operation moved by 1% of the time
where the time goes in v9:
time: 371 us; the launch traced here: 368 us
  waiting for transfers between devices  102 us (27%)
  starting transfers between devices  93.8 us (25%)
  blocking collectives  60.5 us (16%)
  matrix products  42.9 us (12%)
  Pallas kernels  40.9 us (11%)
  between operations  13.7 us (4%)
  local copies, waits for them, and re-layouts  12.4 us (3%)
    all_to_all x16, starting transfers between devices, exchange(): return lax.all_to_all(pieces, axis, 0, 0, tiled=True)  89.8 us
    all_to_all x16, waiting for transfers between devices, exchange(): return lax.all_to_all(pieces, axis, 0, 0, tiled=True)  84.6 us
    all_to_all x4, blocking collectives, exchange(): return lax.all_to_all(pieces, axis, 0, 0, tiled=True)  60.5 us
    dot_general x18, matrix products, local_sums(): jnp.einsum('sq,apq->asp', low[m], local(t, m), preferred_element_type=F32)  21.9 us
    pallas_call x7, Pallas kernels, near_solve(): pl.pallas_call(functools.partial(near_kernel, len(xs), steps), grid=(step...  18.5 us
    dot_general x10, matrix products, per_device(): jnp.einsum('sq,rapq->arsp', low[m], split(t, m), preferred_element_type=F32)  17.1 us
    all_gather x3, waiting for transfers between devices, per_device(): packed = lax.all_gather(packed, 'row', axis=0)  13.4 us
    pallas_call x6, Pallas kernels, far_rest(): pl.pallas_call(functools.partial(far_kernel, len(xs)), grid=(FAR_STEPS,),...  13.2 us
  transfers between devices with their start and end apart: 20, of which 19 were waited for; matrix products, arithmetic and copies ran while one was open for 15% of the time, Pallas kernels for 9%

profile of v9, /device:TPU:2, one launch (start us, length us, event | category | flops | bytes accessed | tf_op | source)
XLA Modules:
  0.0 368.0 jit_solution(3640525300408780658)
XLA Ops:
  6.5 3.1 pack.3
  11.1 3.3 pack.4
  16.9 7.6 %all-to-all-start = ((bf16[32,32,128]{2,1,0:T(8,128)(2,1)}), bf16[32,32,128]{2,1,0:T(8,128)(2,1)S(1)}, u32[]{:S(2)}, u32[]{:S(2)}) async-start(bf16[32,32,128]{2,1,0:T(8,128)(2,1)} %bitcast.13), calls=%async_computation | async-start | bytes 524288 | tf_op jit(solution)/shard_map/all_to_all | solution.py:30
  29.9 2.2 all-to-all-done
  32.9 8.5 %all-to-all-start.1 = ((bf16[8,32,128]{2,1,0:T(8,128)(2,1)}), bf16[8,32,128]{2,1,0:T(8,128)(2,1)}, u32[]{:S(2)}, u32[]{:S(2)}) async-start(bf16[8,32,128]{2,1,0:T(8,128)(2,1)} %broadcast_in_dim.10), calls=%async_computation.1 | async-start | bytes 131072 | tf_op jit(solution)/shard_map/all_to_all | solution.py:30
  41.4 9.3 %all-to-all-done.1 = bf16[8,32,128]{2,1,0:T(8,128)(2,1)} async-done(((bf16[8,32,128]{2,1,0:T(8,128)(2,1)}), bf16[8,32,128]{2,1,0:T(8,128)(2,1)}, u32[]{:S(2)}, u32[]{:S(2)}) %all-to-all-start.1) | async-done | bytes 65568 | tf_op jit(solution)/shard_map/all_to_all | solution.py:30
  50.7 4.6 %all-to-all-start.2 = ((bf16[8,32,128]{2,1,0:T(8,128)(2,1)}), bf16[8,32,128]{2,1,0:T(8,128)(2,1)S(1)}, u32[]{:S(2)}, u32[]{:S(2)}) async-start(bf16[8,32,128]{2,1,0:T(8,128)(2,1)} %all-to-all-done.1), calls=%async_computation.2 | async-start | bytes 131072 | tf_op jit(solution)/shard_map/all_to_all | solution.py:30
  55.5 4.1 %all-to-all-done.2 = bf16[8,32,128]{2,1,0:T(8,128)(2,1)S(1)} async-done(((bf16[8,32,128]{2,1,0:T(8,128)(2,1)}), bf16[8,32,128]{2,1,0:T(8,128)(2,1)S(1)}, u32[]{:S(2)}, u32[]{:S(2)}) %all-to-all-start.2) | async-done | bytes 65568 | tf_op jit(solution)/shard_map/all_to_all | solution.py:30
  62.5 5.0 %all-to-all-start.3 = ((bf16[32,32,128]{2,1,0:T(8,128)(2,1)}), bf16[32,32,128]{2,1,0:T(8,128)(2,1)S(1)}, u32[]{:S(2)}, u32[]{:S(2)}) async-start(bf16[32,32,128]{2,1,0:T(8,128)(2,1)} %bitcast.21), calls=%async_computation.3 | async-start | bytes 524288 | tf_op jit(solution)/shard_map/all_to_all | solution.py:30
  71.8 3.6 all-to-all-done.3
  76.0 4.0 %all-to-all-start.4 = ((bf16[8,32,128]{2,1,0:T(8,128)(2,1)}), bf16[8,32,128]{2,1,0:T(8,128)(2,1)}, u32[]{:S(2)}, u32[]{:S(2)}) async-start(bf16[8,32,128]{2,1,0:T(8,128)(2,1)} %broadcast_in_dim.11), calls=%async_computation.4 | async-start | bytes 131072 | tf_op jit(solution)/shard_map/all_to_all | solution.py:30
  80.0 2.2 convolution_add_fusion.9
  82.2 7.2 %all-to-all-done.4 = bf16[8,32,128]{2,1,0:T(8,128)(2,1)} async-done(((bf16[8,32,128]{2,1,0:T(8,128)(2,1)}), bf16[8,32,128]{2,1,0:T(8,128)(2,1)}, u32[]{:S(2)}, u32[]{:S(2)}) %all-to-all-start.4) | async-done | bytes 65568 | tf_op jit(solution)/shard_map/all_to_all | solution.py:30
  89.4 4.6 %all-to-all-start.5 = ((bf16[8,32,128]{2,1,0:T(8,128)(2,1)}), bf16[8,32,128]{2,1,0:T(8,128)(2,1)S(1)}, u32[]{:S(2)}, u32[]{:S(2)}) async-start(bf16[8,32,128]{2,1,0:T(8,128)(2,1)} %all-to-all-done.4), calls=%async_computation.5 | async-start | bytes 131072 | tf_op jit(solution)/shard_map/all_to_all | solution.py:30
  94.0 2.2 convolution_add_fusion.7
  96.3 1.9 all-to-all-done.5
  108.0 5.1 %all-to-all-start.6 = ((bf16[32,5,32,128]{3,2,1,0:T(8,128)(2,1)}), bf16[32,5,32,128]{3,2,1,0:T(8,128)(2,1)S(1)}, u32[]{:S(2)}, u32[]{:S(2)}) async-start(bf16[32,5,32,128]{3,2,1,0:T(8,128)(2,1)} %copy.37), calls=%async_computation.6 | async-start | bytes 2621440 | tf_op jit(solution)/shard_map/all_to_all | solution.py:30
  113.1 2.8 pack.5
  115.9 16.1 %all-to-all-done.6 = bf16[32,5,32,128]{3,2,1,0:T(8,128)(2,1)S(1)} async-done(((bf16[32,5,32,128]{3,2,1,0:T(8,128)(2,1)}), bf16[32,5,32,128]{3,2,1,0:T(8,128)(2,1)S(1)}, u32[]{:S(2)}, u32[]{:S(2)}) %all-to-all-start.6) | async-done | bytes 1310752 | tf_op jit(solution)/shard_map/all_to_all | solution.py:30
  132.3 3.9 %collective-permute-start = (bf16[5,32,128]{2,1,0:T(8,128)(2,1)S(1)}, bf16[5,32,128]{2,1,0:T(8,128)(2,1)S(1)}, u32[]{:S(2)}, u32[]{:S(2)}) collective-permute-start(bf16[5,32,128]{2,1,0:T(8,128)(2,1)S(1)} %reduce_sum.82), channel_id=1, source_target_pairs={{0,0},{1,32},{2,64},{3,96},{4,128},{5,160},{6,192},{7,224},{8,8},{... | collective-permute-start | bytes 122888 | tf_op jit(solution)/shard_map/ppermute | solution.py:257
  136.2 3.7 %collective-permute-done = bf16[5,32,128]{2,1,0:T(8,128)(2,1)S(1)} collective-permute-done((bf16[5,32,128]{2,1,0:T(8,128)(2,1)S(1)}, bf16[5,32,128]{2,1,0:T(8,128)(2,1)S(1)}, u32[]{:S(2)}, u32[]{:S(2)}) %collective-permute-start) | collective-permute-done | bytes 40992 | tf_op jit(solution)/shard_map/ppermute | solution.py:257
  140.2 1.7 fusion.16
  142.7 9.3 %all-to-all-start.7 = ((bf16[32,32,128]{2,1,0:T(8,128)(2,1)}), bf16[32,32,128]{2,1,0:T(8,128)(2,1)S(1)}, u32[]{:S(2)}, u32[]{:S(2)}) async-start(bf16[32,32,128]{2,1,0:T(8,128)(2,1)} %bitcast.45), calls=%async_computation.7 | async-start | bytes 524288 | tf_op jit(solution)/shard_map/all_to_all | solution.py:30
  152.0 1.7 fusion.96
  155.3 1.7 fusion.91
  157.0 2.6 all-to-all-done.7
  159.9 1.7 fusion.19
  162.4 5.0 %all-to-all-start.8 = ((bf16[32,32,128]{2,1,0:T(8,128)(2,1)}), bf16[32,32,128]{2,1,0:T(8,128)(2,1)S(1)}, u32[]{:S(2)}, u32[]{:S(2)}) async-start(bf16[32,32,128]{2,1,0:T(8,128)(2,1)} %bitcast.53), calls=%async_computation.8 | async-start | bytes 524288 | tf_op jit(solution)/shard_map/all_to_all | solution.py:30
  167.4 1.7 convolution_add_fusion.5
  169.0 1.7 convolution_add_fusion.2
  170.7 4.4 %all-to-all-done.8 = bf16[32,32,128]{2,1,0:T(8,128)(2,1)S(1)} async-done(((bf16[32,32,128]{2,1,0:T(8,128)(2,1)}), bf16[32,32,128]{2,1,0:T(8,128)(2,1)S(1)}, u32[]{:S(2)}, u32[]{:S(2)}) %all-to-all-start.8) | async-done | bytes 262176 | tf_op jit(solution)/shard_map/all_to_all | solution.py:30
  175.4 1.7 fusion.18
  177.8 5.2 %all-to-all-start.9 = ((bf16[32,32,128]{2,1,0:T(8,128)(2,1)}), bf16[32,32,128]{2,1,0:T(8,128)(2,1)S(1)}, u32[]{:S(2)}, u32[]{:S(2)}) async-start(bf16[32,32,128]{2,1,0:T(8,128)(2,1)} %bitcast.61), calls=%async_computation.9 | async-start | bytes 524288 | tf_op jit(solution)/shard_map/all_to_all | solution.py:30
  183.0 1.7 convolution_add_fusion.3
  184.7 6.1 %all-to-all-done.9 = bf16[32,32,128]{2,1,0:T(8,128)(2,1)S(1)} async-done(((bf16[32,32,128]{2,1,0:T(8,128)(2,1)}), bf16[32,32,128]{2,1,0:T(8,128)(2,1)S(1)}, u32[]{:S(2)}, u32[]{:S(2)}) %all-to-all-start.9) | async-done | bytes 262176 | tf_op jit(solution)/shard_map/all_to_all | solution.py:30
  191.0 1.7 fusion.17
  192.8 12.4 %all_to_all.100 = bf16[32,32,128]{2,1,0:T(8,128)(2,1)S(1)} all-to-all(bf16[32,32,128]{2,1,0:T(8,128)(2,1)S(1)} %bitcast.356), channel_id=1, replica_groups=mesh['row'=8,'grp'=4,'sub'=8] {'grp','sub'}, dimensions={0} | all-to-all | bytes 524288 | tf_op jit(solution)/shard_map/all_to_all | solution.py:30
  206.4 5.0 %all-to-all-start.11 = ((bf16[32,32,128]{2,1,0:T(8,128)(2,1)}), bf16[32,32,128]{2,1,0:T(8,128)(2,1)S(1)}, u32[]{:S(2)}, u32[]{:S(2)}) async-start(bf16[32,32,128]{2,1,0:T(8,128)(2,1)} %broadcast_in_dim.12), calls=%async_computation.11 | async-start | bytes 524288 | tf_op jit(solution)/shard_map/all_to_all | solution.py:30
  211.5 7.8 %all-to-all-done.11 = bf16[32,32,128]{2,1,0:T(8,128)(2,1)S(1)} async-done(((bf16[32,32,128]{2,1,0:T(8,128)(2,1)}), bf16[32,32,128]{2,1,0:T(8,128)(2,1)S(1)}, u32[]{:S(2)}, u32[]{:S(2)}) %all-to-all-start.11) | async-done | bytes 262176 | tf_op jit(solution)/shard_map/all_to_all | solution.py:30
  219.2 2.4 near_solve.7
  221.7 5.0 %all-to-all-start.12 = ((bf16[32,32,128]{2,1,0:T(8,128)(2,1)}), bf16[32,32,128]{2,1,0:T(8,128)(2,1)S(1)}, u32[]{:S(2)}, u32[]{:S(2)}) async-start(bf16[32,32,128]{2,1,0:T(8,128)(2,1)} %get-tuple-element.25), calls=%async_computation.12 | async-start | bytes 524288 | tf_op jit(solution)/shard_map/all_to_all | solution.py:30
  228.2 6.3 %all-to-all-done.12 = bf16[32,32,128]{2,1,0:T(8,128)(2,1)S(1)} async-done(((bf16[32,32,128]{2,1,0:T(8,128)(2,1)}), bf16[32,32,128]{2,1,0:T(8,128)(2,1)S(1)}, u32[]{:S(2)}, u32[]{:S(2)}) %all-to-all-start.12) | async-done | bytes 262176 | tf_op jit(solution)/shard_map/all_to_all | solution.py:30
  234.4 2.4 near_solve.8
  236.9 5.0 %all-to-all-start.13 = ((bf16[32,32,128]{2,1,0:T(8,128)(2,1)}), bf16[32,32,128]{2,1,0:T(8,128)(2,1)S(1)}, u32[]{:S(2)}, u32[]{:S(2)}) async-start(bf16[32,32,128]{2,1,0:T(8,128)(2,1)} %get-tuple-element.26), calls=%async_computation.13 | async-start | bytes 524288 | tf_op jit(solution)/shard_map/all_to_all | solution.py:30
  241.9 1.9 far_rest.7.refs_2_
  243.8 5.9 %all-to-all-done.13 = bf16[32,32,128]{2,1,0:T(8,128)(2,1)S(1)} async-done(((bf16[32,32,128]{2,1,0:T(8,128)(2,1)}), bf16[32,32,128]{2,1,0:T(8,128)(2,1)S(1)}, u32[]{:S(2)}, u32[]{:S(2)}) %all-to-all-start.13) | async-done | bytes 262176 | tf_op jit(solution)/shard_map/all_to_all | solution.py:30
  249.6 2.4 near_solve.9
  252.1 5.0 %all-to-all-start.14 = ((bf16[32,32,128]{2,1,0:T(8,128)(2,1)}), bf16[32,32,128]{2,1,0:T(8,128)(2,1)S(1)}, u32[]{:S(2)}, u32[]{:S(2)}) async-start(bf16[32,32,128]{2,1,0:T(8,128)(2,1)} %get-tuple-element.27), calls=%async_computation.14 | async-start | bytes 524288 | tf_op jit(solution)/shard_map/all_to_all | solution.py:30
  257.8 2.2 far_rest.8.refs_2_
  260.0 4.8 %all-to-all-done.14 = bf16[32,32,128]{2,1,0:T(8,128)(2,1)S(1)} async-done(((bf16[32,32,128]{2,1,0:T(8,128)(2,1)}), bf16[32,32,128]{2,1,0:T(8,128)(2,1)S(1)}, u32[]{:S(2)}, u32[]{:S(2)}) %all-to-all-start.14) | async-done | bytes 262176 | tf_op jit(solution)/shard_map/all_to_all | solution.py:30
  264.9 1.7 near_solve.10
  266.7 6.5 %all-gather.9.cloned.1.call-done = bf16[416,128,128]{2,1,0:T(8,128)(2,1)} async-done(((bf16[52,128,128]{2,1,0:T(8,128)(2,1)}), bf16[416,128,128]{2,1,0:T(8,128)(2,1)}) %all-gather.9.cloned.1.call-update) | async-done | bytes 13631504 | tf_op jit(solution)/shard_map/all_gather | solution.py:218
  273.2 2.6 far_rest.9.refs_2_
  275.9 18.9 %all_to_all.101 = bf16[8,5,32,128]{3,2,1,0:T(8,128)(2,1)S(1)} all-to-all(bf16[8,5,32,128]{3,2,1,0:T(8,128)(2,1)S(1)} %broadcast_in_dim.13), channel_id=1, replica_groups=mesh['row'=8,'grp'=4,'sub'=8] {'row'}, dimensions={0} | all-to-all | bytes 655360 | tf_op jit(solution)/shard_map/all_to_all | solution.py:30
  294.8 14.9 %all_to_all.102 = bf16[32,32,128]{2,1,0:T(8,128)(2,1)S(1)} all-to-all(bf16[32,32,128]{2,1,0:T(8,128)(2,1)S(1)} %get-tuple-element.35), channel_id=1, replica_groups=mesh['row'=8,'grp'=4,'sub'=8] {'grp','sub'}, dimensions={0} | all-to-all | bytes 524288 | tf_op jit(solution)/shard_map/all_to_all | solution.py:30
  309.7 2.4 near_solve.11
  312.1 5.0 %all-to-all-start.17 = ((bf16[32,32,128]{2,1,0:T(8,128)(2,1)}), bf16[32,32,128]{2,1,0:T(8,128)(2,1)S(1)}, u32[]{:S(2)}, u32[]{:S(2)}) async-start(bf16[32,32,128]{2,1,0:T(8,128)(2,1)} %get-tuple-element.37), calls=%async_computation.17 | async-start | bytes 524288 | tf_op jit(solution)/shard_map/all_to_all | solution.py:30
  318.5 1.8 far_rest.11.refs_10_
  320.4 3.1 far_rest.10.refs_2_
  324.9 2.4 near_solve.12
  327.3 6.1 %all-to-all-start.18 = ((bf16[32,32,128]{2,1,0:T(8,128)(2,1)}), bf16[32,32,128]{2,1,0:T(8,128)(2,1)S(1)}, u32[]{:S(2)}, u32[]{:S(2)}) async-start(bf16[32,32,128]{2,1,0:T(8,128)(2,1)} %get-tuple-element.38), calls=%async_computation.18 | async-start | bytes 524288 | tf_op jit(solution)/shard_map/all_to_all | solution.py:30
  333.4 6.9 %all-gather.11.cloned.1.call-done = bf16[160,128,128]{2,1,0:T(8,128)(2,1)} async-done(((bf16[20,128,128]{2,1,0:T(8,128)(2,1)}), bf16[160,128,128]{2,1,0:T(8,128)(2,1)}) %all-gather.11.cloned.1.call-update) | async-done | bytes 5242896 | tf_op jit(solution)/shard_map/all_gather | solution.py:218
  341.1 4.6 %near_solve.13 = (f32[32,128]{1,0:T(8,128)S(1)}, bf16[32,32,128]{2,1,0:T(8,128)(2,1)}) custom-call(bf16[4,8,32,128]{3,2,1,0:T(8,128)(2,1)S(1)} %bitcast.294, bf16[4,8,32,128]{3,2,1,0:T(8,128)(2,1)S(1)} %bitcast.298, bf16[4,8,32,128]{3,2,1,0:T(8,128)(2,1)S(1)} %bitcast.301, bf16[4,8,32,128]{3,2,1,0:T(8,128)(2,1)S(1)} %bitcast.303, ...), custom_call_target="tpu_custom_call" | custom-call | flops 167772160 | bytes 5242880 | tf_op jit(solution)/shard_map/near_solve/pallas_call | solution.py:162
  345.8 14.3 %all_to_all.103 = bf16[8,3,32,128]{3,2,1,0:T(8,128)(2,1)S(1)} all-to-all(bf16[8,3,32,128]{3,2,1,0:T(8,128)(2,1)S(1)} %broadcast_in_dim.14), channel_id=1, replica_groups=mesh['row'=8,'grp'=4,'sub'=8] {'row'}, dimensions={0} | all-to-all | bytes 393216 | tf_op jit(solution)/shard_map/all_to_all | solution.py:30
  (94 shorter events, 41.3 us)
Async XLA Ops:
  6.5 3.3 copy-start.1
  6.5 3.6 copy-start
  6.5 133.7 %all-gather.7.cloned.1.call-start = ((), (), s32[]{:S(2)}) async-start(), calls=%async_computation.20 | async-start | bytes 11796480 | tf_op jit(solution)/shard_map/all_gather | solution.py:218
  9.7 4.7 %copy-start.2 = (s32[32,1,8,1]{0,3,2,1:T(1,128)S(1)}, s32[32,1,8,1]{0,3,2,1:T(1,128)}, u32[]{:S(2)}) copy-start(s32[32,1,8,1]{0,3,2,1:T(1,128)} %param.5) | copy-start | bytes 3076
  9.7 263.5 %all-gather.9.cloned.1.call-start = ((), (), s32[]{:S(2)}) async-start(), calls=%async_computation.21 | async-start | bytes 15335424 | tf_op jit(solution)/shard_map/all_gather | solution.py:218
  16.9 15.3 %all-to-all-start = ((bf16[32,32,128]{2,1,0:T(8,128)(2,1)}), bf16[32,32,128]{2,1,0:T(8,128)(2,1)S(1)}, u32[]{:S(2)}, u32[]{:S(2)}) async-start(bf16[32,32,128]{2,1,0:T(8,128)(2,1)} %bitcast.13), calls=%async_computation | async-start | bytes 524288 | tf_op jit(solution)/shard_map/all_to_all | solution.py:30
  32.9 17.9 %all-to-all-start.1 = ((bf16[8,32,128]{2,1,0:T(8,128)(2,1)}), bf16[8,32,128]{2,1,0:T(8,128)(2,1)}, u32[]{:S(2)}, u32[]{:S(2)}) async-start(bf16[8,32,128]{2,1,0:T(8,128)(2,1)} %broadcast_in_dim.10), calls=%async_computation.1 | async-start | bytes 131072 | tf_op jit(solution)/shard_map/all_to_all | solution.py:30
  50.7 8.8 %all-to-all-start.2 = ((bf16[8,32,128]{2,1,0:T(8,128)(2,1)}), bf16[8,32,128]{2,1,0:T(8,128)(2,1)S(1)}, u32[]{:S(2)}, u32[]{:S(2)}) async-start(bf16[8,32,128]{2,1,0:T(8,128)(2,1)} %all-to-all-done.1), calls=%async_computation.2 | async-start | bytes 131072 | tf_op jit(solution)/shard_map/all_to_all | solution.py:30
  62.5 12.8 %all-to-all-start.3 = ((bf16[32,32,128]{2,1,0:T(8,128)(2,1)}), bf16[32,32,128]{2,1,0:T(8,128)(2,1)S(1)}, u32[]{:S(2)}, u32[]{:S(2)}) async-start(bf16[32,32,128]{2,1,0:T(8,128)(2,1)} %bitcast.21), calls=%async_computation.3 | async-start | bytes 524288 | tf_op jit(solution)/shard_map/all_to_all | solution.py:30
  76.0 13.4 %all-to-all-start.4 = ((bf16[8,32,128]{2,1,0:T(8,128)(2,1)}), bf16[8,32,128]{2,1,0:T(8,128)(2,1)}, u32[]{:S(2)}, u32[]{:S(2)}) async-start(bf16[8,32,128]{2,1,0:T(8,128)(2,1)} %broadcast_in_dim.11), calls=%async_computation.4 | async-start | bytes 131072 | tf_op jit(solution)/shard_map/all_to_all | solution.py:30
  89.4 8.8 %all-to-all-start.5 = ((bf16[8,32,128]{2,1,0:T(8,128)(2,1)}), bf16[8,32,128]{2,1,0:T(8,128)(2,1)S(1)}, u32[]{:S(2)}, u32[]{:S(2)}) async-start(bf16[8,32,128]{2,1,0:T(8,128)(2,1)} %all-to-all-done.4), calls=%async_computation.5 | async-start | bytes 131072 | tf_op jit(solution)/shard_map/all_to_all | solution.py:30
  108.0 24.1 %all-to-all-start.6 = ((bf16[32,5,32,128]{3,2,1,0:T(8,128)(2,1)}), bf16[32,5,32,128]{3,2,1,0:T(8,128)(2,1)S(1)}, u32[]{:S(2)}, u32[]{:S(2)}) async-start(bf16[32,5,32,128]{3,2,1,0:T(8,128)(2,1)} %copy.37), calls=%async_computation.6 | async-start | bytes 2621440 | tf_op jit(solution)/shard_map/all_to_all | solution.py:30
  113.0 227.3 %all-gather.11.cloned.1.call-start = ((), (), s32[]{:S(2)}) async-start(), calls=%async_computation.22 | async-start | bytes 5898240 | tf_op jit(solution)/shard_map/all_gather | solution.py:218
  132.3 7.7 %collective-permute-start = (bf16[5,32,128]{2,1,0:T(8,128)(2,1)S(1)}, bf16[5,32,128]{2,1,0:T(8,128)(2,1)S(1)}, u32[]{:S(2)}, u32[]{:S(2)}) collective-permute-start(bf16[5,32,128]{2,1,0:T(8,128)(2,1)S(1)} %reduce_sum.82), channel_id=1, source_target_pairs={{0,0},{1,32},{2,64},{3,96},{4,128},{5,160},{6,192},{7,224},{8,8},{... | collective-permute-start | bytes 122888 | tf_op jit(solution)/shard_map/ppermute | solution.py:257
  142.7 17.0 %all-to-all-start.7 = ((bf16[32,32,128]{2,1,0:T(8,128)(2,1)}), bf16[32,32,128]{2,1,0:T(8,128)(2,1)S(1)}, u32[]{:S(2)}, u32[]{:S(2)}) async-start(bf16[32,32,128]{2,1,0:T(8,128)(2,1)} %bitcast.45), calls=%async_computation.7 | async-start | bytes 524288 | tf_op jit(solution)/shard_map/all_to_all | solution.py:30
  162.4 12.8 %all-to-all-start.8 = ((bf16[32,32,128]{2,1,0:T(8,128)(2,1)}), bf16[32,32,128]{2,1,0:T(8,128)(2,1)S(1)}, u32[]{:S(2)}, u32[]{:S(2)}) async-start(bf16[32,32,128]{2,1,0:T(8,128)(2,1)} %bitcast.53), calls=%async_computation.8 | async-start | bytes 524288 | tf_op jit(solution)/shard_map/all_to_all | solution.py:30
  177.8 13.0 %all-to-all-start.9 = ((bf16[32,32,128]{2,1,0:T(8,128)(2,1)}), bf16[32,32,128]{2,1,0:T(8,128)(2,1)S(1)}, u32[]{:S(2)}, u32[]{:S(2)}) async-start(bf16[32,32,128]{2,1,0:T(8,128)(2,1)} %bitcast.61), calls=%async_computation.9 | async-start | bytes 524288 | tf_op jit(solution)/shard_map/all_to_all | solution.py:30
  206.4 12.8 %all-to-all-start.11 = ((bf16[32,32,128]{2,1,0:T(8,128)(2,1)}), bf16[32,32,128]{2,1,0:T(8,128)(2,1)S(1)}, u32[]{:S(2)}, u32[]{:S(2)}) async-start(bf16[32,32,128]{2,1,0:T(8,128)(2,1)} %broadcast_in_dim.12), calls=%async_computation.11 | async-start | bytes 524288 | tf_op jit(solution)/shard_map/all_to_all | solution.py:30
  221.7 12.8 %all-to-all-start.12 = ((bf16[32,32,128]{2,1,0:T(8,128)(2,1)}), bf16[32,32,128]{2,1,0:T(8,128)(2,1)S(1)}, u32[]{:S(2)}, u32[]{:S(2)}) async-start(bf16[32,32,128]{2,1,0:T(8,128)(2,1)} %get-tuple-element.25), calls=%async_computation.12 | async-start | bytes 524288 | tf_op jit(solution)/shard_map/all_to_all | solution.py:30
  236.9 12.8 %all-to-all-start.13 = ((bf16[32,32,128]{2,1,0:T(8,128)(2,1)}), bf16[32,32,128]{2,1,0:T(8,128)(2,1)S(1)}, u32[]{:S(2)}, u32[]{:S(2)}) async-start(bf16[32,32,128]{2,1,0:T(8,128)(2,1)} %get-tuple-element.26), calls=%async_computation.13 | async-start | bytes 524288 | tf_op jit(solution)/shard_map/all_to_all | solution.py:30
  252.1 12.8 %all-to-all-start.14 = ((bf16[32,32,128]{2,1,0:T(8,128)(2,1)}), bf16[32,32,128]{2,1,0:T(8,128)(2,1)S(1)}, u32[]{:S(2)}, u32[]{:S(2)}) async-start(bf16[32,32,128]{2,1,0:T(8,128)(2,1)} %get-tuple-element.27), calls=%async_computation.14 | async-start | bytes 524288 | tf_op jit(solution)/shard_map/all_to_all | solution.py:30
  312.1 12.8 %all-to-all-start.17 = ((bf16[32,32,128]{2,1,0:T(8,128)(2,1)}), bf16[32,32,128]{2,1,0:T(8,128)(2,1)S(1)}, u32[]{:S(2)}, u32[]{:S(2)}) async-start(bf16[32,32,128]{2,1,0:T(8,128)(2,1)} %get-tuple-element.37), calls=%async_computation.17 | async-start | bytes 524288 | tf_op jit(solution)/shard_map/all_to_all | solution.py:30
  327.3 13.8 %all-to-all-start.18 = ((bf16[32,32,128]{2,1,0:T(8,128)(2,1)}), bf16[32,32,128]{2,1,0:T(8,128)(2,1)S(1)}, u32[]{:S(2)}, u32[]{:S(2)}) async-start(bf16[32,32,128]{2,1,0:T(8,128)(2,1)} %get-tuple-element.38), calls=%async_computation.18 | async-start | bytes 524288 | tf_op jit(solution)/shard_map/all_to_all | solution.py:30
Sparse Core Ops, SparseCore 0:
  9.9 119.5 all-gather.6
  131.2 141.9 all-gather.8
  275.0 65.3 all-gather.10

commit v10 on v8

--- a/solution.py
+++ b/solution.py
@@ -21,8 +21,8 @@
 ALL = ("row", "grp", "sub")
 CHUNKS = (
     ((6, 7, 8), (5, 6, 8), (4, 5, 8), (3, 4, 8)),
-    ((2, 3, 8), (1, 2, 8), (0, 6, 8)),
-    ((0, 1, 6),),
+    ((2, 3, 8), (1, 2, 8), (0, 7, 8)),
+    ((0, 1, 7),),
 )
 
 
@@ -280,8 +280,8 @@
                 [place[t, j][1] for t, _ in far],
             )
         if j == OUT_SPLIT - 1:
-            upper, rest = lax.optimization_barrier((jnp.stack(out[j + 1 :]).astype(BF16), rest))
-            upper, wide = lax.optimization_barrier((spread(upper, "row", n_row), wide))
+            upper = spread(jnp.stack(out[j + 1 :]).astype(BF16), "row", n_row)
+            upper, wide = lax.optimization_barrier((upper, wide))
         near = exchange(wide, COL).reshape(PER_ROW, n_row, part, block)
         joined.append((j + 1, near))
         out[j], wide = near_solve(

time: 370 us -> 372 us (level)
  blocking collectives: 60.5 us -> 69.1 us
  waiting for transfers between devices: 102 us -> 95.1 us
    all_to_all x16, waiting for transfers between devices: 84.6 us -> 72.2 us  [exchange(): return lax.all_to_all(pieces, axis, 0, 0, tiled=True)]
    all_to_all x4, blocking collectives: 60.5 us -> 69.1 us  [exchange(): return lax.all_to_all(pieces, axis, 0, 0, tiled=True)]
    all_gather x3, waiting for transfers between devices: 13.5 us -> 18.4 us  [per_device(): packed = lax.all_gather(packed, 'row', axis=0)]
  transfers between devices with their start and end apart: 20 -> 20, of which waited for: 19 -> 16; matrix products, arithmetic and copies ran while one was open for 15% -> 15% of each run, Pallas kernels for 9% -> 9%
where the time goes in v10:
time: 372 us; the launch traced here: 369 us
  waiting for transfers between devices  95.1 us (26%)
  starting transfers between devices  93.3 us (25%)
  blocking collectives  69.1 us (19%)
  matrix products  42.8 us (12%)
  Pallas kernels  41.7 us (11%)
  between operations  13.7 us (4%)
  local copies, waits for them, and re-layouts  11.4 us (3%)
    all_to_all x16, starting transfers between devices, exchange(): return lax.all_to_all(pieces, axis, 0, 0, tiled=True)  90.1 us
    all_to_all x16, waiting for transfers between devices, exchange(): return lax.all_to_all(pieces, axis, 0, 0, tiled=True)  72.2 us
    all_to_all x4, blocking collectives, exchange(): return lax.all_to_all(pieces, axis, 0, 0, tiled=True)  69.1 us
    dot_general x18, matrix products, local_sums(): jnp.einsum('sq,apq->asp', low[m], local(t, m), preferred_element_type=F32)  21.7 us
    pallas_call x7, Pallas kernels, near_solve(): pl.pallas_call(functools.partial(near_kernel, len(xs), steps), grid=(step...  19 us
    all_gather x3, waiting for transfers between devices, per_device(): packed = lax.all_gather(packed, 'row', axis=0)  18.4 us
    dot_general x10, matrix products, per_device(): jnp.einsum('sq,rapq->arsp', low[m], split(t, m), preferred_element_type=F32)  17.1 us
    pallas_call x6, Pallas kernels, far_rest(): pl.pallas_call(functools.partial(far_kernel, len(xs)), grid=(FAR_STEPS,),...  12.9 us
  transfers between devices with their start and end apart: 20, of which 16 were waited for; matrix products, arithmetic and copies ran while one was open for 15% of the time, Pallas kernels for 9%

profile of v10, /device:TPU:2, one launch (start us, length us, event | category | flops | bytes accessed | tf_op | source)
XLA Modules:
  0.0 369.0 jit_solution(5328352907093643860)
XLA Ops:
  6.5 3.4 pack.3
  11.3 3.4 pack.4
  17.3 7.6 %all-to-all-start = ((bf16[32,32,128]{2,1,0:T(8,128)(2,1)}), bf16[32,32,128]{2,1,0:T(8,128)(2,1)S(1)}, u32[]{:S(2)}, u32[]{:S(2)}) async-start(bf16[32,32,128]{2,1,0:T(8,128)(2,1)} %bitcast.13), calls=%async_computation | async-start | bytes 524288 | tf_op jit(solution)/shard_map/all_to_all | solution.py:30
  24.9 2.9 pack.5
  34.0 8.5 %all-to-all-start.1 = ((bf16[8,32,128]{2,1,0:T(8,128)(2,1)}), bf16[8,32,128]{2,1,0:T(8,128)(2,1)}, u32[]{:S(2)}, u32[]{:S(2)}) async-start(bf16[8,32,128]{2,1,0:T(8,128)(2,1)} %broadcast_in_dim.10), calls=%async_computation.1 | async-start | bytes 131072 | tf_op jit(solution)/shard_map/all_to_all | solution.py:30
  42.5 9.2 %all-to-all-done.1 = bf16[8,32,128]{2,1,0:T(8,128)(2,1)} async-done(((bf16[8,32,128]{2,1,0:T(8,128)(2,1)}), bf16[8,32,128]{2,1,0:T(8,128)(2,1)}, u32[]{:S(2)}, u32[]{:S(2)}) %all-to-all-start.1) | async-done | bytes 65568 | tf_op jit(solution)/shard_map/all_to_all | solution.py:30
  51.7 4.8 %all-to-all-start.2 = ((bf16[8,32,128]{2,1,0:T(8,128)(2,1)}), bf16[8,32,128]{2,1,0:T(8,128)(2,1)S(1)}, u32[]{:S(2)}, u32[]{:S(2)}) async-start(bf16[8,32,128]{2,1,0:T(8,128)(2,1)} %all-to-all-done.1), calls=%async_computation.2 | async-start | bytes 131072 | tf_op jit(solution)/shard_map/all_to_all | solution.py:30
  56.6 4.1 %all-to-all-done.2 = bf16[8,32,128]{2,1,0:T(8,128)(2,1)S(1)} async-done(((bf16[8,32,128]{2,1,0:T(8,128)(2,1)}), bf16[8,32,128]{2,1,0:T(8,128)(2,1)S(1)}, u32[]{:S(2)}, u32[]{:S(2)}) %all-to-all-start.2) | async-done | bytes 65568 | tf_op jit(solution)/shard_map/all_to_all | solution.py:30
  63.7 6.5 %all-to-all-start.3 = ((bf16[32,32,128]{2,1,0:T(8,128)(2,1)}), bf16[32,32,128]{2,1,0:T(8,128)(2,1)S(1)}, u32[]{:S(2)}, u32[]{:S(2)}) async-start(bf16[32,32,128]{2,1,0:T(8,128)(2,1)} %bitcast.21), calls=%async_computation.3 | async-start | bytes 524288 | tf_op jit(solution)/shard_map/all_to_all | solution.py:30
  74.4 3.4 all-to-all-done.3
  78.5 4.0 %all-to-all-start.4 = ((bf16[8,32,128]{2,1,0:T(8,128)(2,1)}), bf16[8,32,128]{2,1,0:T(8,128)(2,1)}, u32[]{:S(2)}, u32[]{:S(2)}) async-start(bf16[8,32,128]{2,1,0:T(8,128)(2,1)} %broadcast_in_dim.11), calls=%async_computation.4 | async-start | bytes 131072 | tf_op jit(solution)/shard_map/all_to_all | solution.py:30
  82.5 2.2 convolution_add_fusion.9
  84.7 7.2 %all-to-all-done.4 = bf16[8,32,128]{2,1,0:T(8,128)(2,1)} async-done(((bf16[8,32,128]{2,1,0:T(8,128)(2,1)}), bf16[8,32,128]{2,1,0:T(8,128)(2,1)}, u32[]{:S(2)}, u32[]{:S(2)}) %all-to-all-start.4) | async-done | bytes 65568 | tf_op jit(solution)/shard_map/all_to_all | solution.py:30
  91.9 4.6 %all-to-all-start.5 = ((bf16[8,32,128]{2,1,0:T(8,128)(2,1)}), bf16[8,32,128]{2,1,0:T(8,128)(2,1)S(1)}, u32[]{:S(2)}, u32[]{:S(2)}) async-start(bf16[8,32,128]{2,1,0:T(8,128)(2,1)} %all-to-all-done.4), calls=%async_computation.5 | async-start | bytes 131072 | tf_op jit(solution)/shard_map/all_to_all | solution.py:30
  96.5 2.2 convolution_add_fusion.7
  98.7 2.0 all-to-all-done.5
  109.4 23.4 %all_to_all.100 = bf16[32,5,32,128]{3,2,1,0:T(8,128)(2,1)S(1)} all-to-all(bf16[32,5,32,128]{3,2,1,0:T(8,128)(2,1)S(1)} %copy.37), channel_id=1, replica_groups=mesh['row'=8,'grp'=4,'sub'=8] {'grp','sub'}, dimensions={0} | all-to-all | bytes 2621440 | tf_op jit(solution)/shard_map/all_to_all | solution.py:30
  133.0 3.2 collective-permute-start
  136.2 4.4 %collective-permute-done = bf16[5,32,128]{2,1,0:T(8,128)(2,1)S(1)} collective-permute-done((bf16[5,32,128]{2,1,0:T(8,128)(2,1)S(1)}, bf16[5,32,128]{2,1,0:T(8,128)(2,1)S(1)}, u32[]{:S(2)}, u32[]{:S(2)}) %collective-permute-start) | collective-permute-done | bytes 40992 | tf_op jit(solution)/shard_map/ppermute | solution.py:248
  140.9 1.8 fusion.16
  143.5 9.3 %all-to-all-start.7 = ((bf16[32,32,128]{2,1,0:T(8,128)(2,1)}), bf16[32,32,128]{2,1,0:T(8,128)(2,1)S(1)}, u32[]{:S(2)}, u32[]{:S(2)}) async-start(bf16[32,32,128]{2,1,0:T(8,128)(2,1)} %bitcast.45), calls=%async_computation.7 | async-start | bytes 524288 | tf_op jit(solution)/shard_map/all_to_all | solution.py:30
  152.8 1.7 fusion.91
  154.5 1.7 fusion.93
  156.2 1.7 fusion.96
  157.9 2.6 all-to-all-done.7
  160.7 1.7 fusion.19
  163.2 5.0 %all-to-all-start.8 = ((bf16[32,32,128]{2,1,0:T(8,128)(2,1)}), bf16[32,32,128]{2,1,0:T(8,128)(2,1)S(1)}, u32[]{:S(2)}, u32[]{:S(2)}) async-start(bf16[32,32,128]{2,1,0:T(8,128)(2,1)} %bitcast.53), calls=%async_computation.8 | async-start | bytes 524288 | tf_op jit(solution)/shard_map/all_to_all | solution.py:30
  168.2 1.7 convolution_add_fusion.2
  169.9 1.7 convolution_add_fusion.5
  171.6 4.4 %all-to-all-done.8 = bf16[32,32,128]{2,1,0:T(8,128)(2,1)S(1)} async-done(((bf16[32,32,128]{2,1,0:T(8,128)(2,1)}), bf16[32,32,128]{2,1,0:T(8,128)(2,1)S(1)}, u32[]{:S(2)}, u32[]{:S(2)}) %all-to-all-start.8) | async-done | bytes 262176 | tf_op jit(solution)/shard_map/all_to_all | solution.py:30
  176.2 1.7 fusion.18
  178.7 5.0 %all-to-all-start.9 = ((bf16[32,32,128]{2,1,0:T(8,128)(2,1)}), bf16[32,32,128]{2,1,0:T(8,128)(2,1)S(1)}, u32[]{:S(2)}, u32[]{:S(2)}) async-start(bf16[32,32,128]{2,1,0:T(8,128)(2,1)} %bitcast.61), calls=%async_computation.9 | async-start | bytes 524288 | tf_op jit(solution)/shard_map/all_to_all | solution.py:30
  183.7 1.7 convolution_add_fusion.3
  185.4 6.1 %all-to-all-done.9 = bf16[32,32,128]{2,1,0:T(8,128)(2,1)S(1)} async-done(((bf16[32,32,128]{2,1,0:T(8,128)(2,1)}), bf16[32,32,128]{2,1,0:T(8,128)(2,1)S(1)}, u32[]{:S(2)}, u32[]{:S(2)}) %all-to-all-start.9) | async-done | bytes 262176 | tf_op jit(solution)/shard_map/all_to_all | solution.py:30
  191.7 1.7 fusion.17
  193.5 12.5 %all_to_all.101 = bf16[32,32,128]{2,1,0:T(8,128)(2,1)S(1)} all-to-all(bf16[32,32,128]{2,1,0:T(8,128)(2,1)S(1)} %bitcast.356), channel_id=1, replica_groups=mesh['row'=8,'grp'=4,'sub'=8] {'grp','sub'}, dimensions={0} | all-to-all | bytes 524288 | tf_op jit(solution)/shard_map/all_to_all | solution.py:30
  207.2 5.0 %all-to-all-start.11 = ((bf16[32,32,128]{2,1,0:T(8,128)(2,1)}), bf16[32,32,128]{2,1,0:T(8,128)(2,1)S(1)}, u32[]{:S(2)}, u32[]{:S(2)}) async-start(bf16[32,32,128]{2,1,0:T(8,128)(2,1)} %broadcast_in_dim.12), calls=%async_computation.11 | async-start | bytes 524288 | tf_op jit(solution)/shard_map/all_to_all | solution.py:30
  212.2 7.8 %all-to-all-done.11 = bf16[32,32,128]{2,1,0:T(8,128)(2,1)S(1)} async-done(((bf16[32,32,128]{2,1,0:T(8,128)(2,1)}), bf16[32,32,128]{2,1,0:T(8,128)(2,1)S(1)}, u32[]{:S(2)}, u32[]{:S(2)}) %all-to-all-start.11) | async-done | bytes 262176 | tf_op jit(solution)/shard_map/all_to_all | solution.py:30
  219.9 2.4 near_solve.7
  222.4 5.0 %all-to-all-start.12 = ((bf16[32,32,128]{2,1,0:T(8,128)(2,1)}), bf16[32,32,128]{2,1,0:T(8,128)(2,1)S(1)}, u32[]{:S(2)}, u32[]{:S(2)}) async-start(bf16[32,32,128]{2,1,0:T(8,128)(2,1)} %get-tuple-element.23), calls=%async_computation.12 | async-start | bytes 524288 | tf_op jit(solution)/shard_map/all_to_all | solution.py:30
  227.4 1.5 far_rest.6.refs_2_
  228.9 6.3 %all-to-all-done.12 = bf16[32,32,128]{2,1,0:T(8,128)(2,1)S(1)} async-done(((bf16[32,32,128]{2,1,0:T(8,128)(2,1)}), bf16[32,32,128]{2,1,0:T(8,128)(2,1)S(1)}, u32[]{:S(2)}, u32[]{:S(2)}) %all-to-all-start.12) | async-done | bytes 262176 | tf_op jit(solution)/shard_map/all_to_all | solution.py:30
  235.2 2.5 near_solve.8
  237.6 5.0 %all-to-all-start.13 = ((bf16[32,32,128]{2,1,0:T(8,128)(2,1)}), bf16[32,32,128]{2,1,0:T(8,128)(2,1)S(1)}, u32[]{:S(2)}, u32[]{:S(2)}) async-start(bf16[32,32,128]{2,1,0:T(8,128)(2,1)} %get-tuple-element.24), calls=%async_computation.13 | async-start | bytes 524288 | tf_op jit(solution)/shard_map/all_to_all | solution.py:30
  242.6 1.9 far_rest.7.refs_2_
  244.5 5.9 %all-to-all-done.13 = bf16[32,32,128]{2,1,0:T(8,128)(2,1)S(1)} async-done(((bf16[32,32,128]{2,1,0:T(8,128)(2,1)}), bf16[32,32,128]{2,1,0:T(8,128)(2,1)S(1)}, u32[]{:S(2)}, u32[]{:S(2)}) %all-to-all-start.13) | async-done | bytes 262176 | tf_op jit(solution)/shard_map/all_to_all | solution.py:30
  250.4 2.4 near_solve.9
  252.8 5.0 %all-to-all-start.14 = ((bf16[32,32,128]{2,1,0:T(8,128)(2,1)}), bf16[32,32,128]{2,1,0:T(8,128)(2,1)S(1)}, u32[]{:S(2)}, u32[]{:S(2)}) async-start(bf16[32,32,128]{2,1,0:T(8,128)(2,1)} %get-tuple-element.25), calls=%async_computation.14 | async-start | bytes 524288 | tf_op jit(solution)/shard_map/all_to_all | solution.py:30
  257.8 2.2 far_rest.8.refs_2_
  260.1 5.5 %all-to-all-done.14 = bf16[32,32,128]{2,1,0:T(8,128)(2,1)S(1)} async-done(((bf16[32,32,128]{2,1,0:T(8,128)(2,1)}), bf16[32,32,128]{2,1,0:T(8,128)(2,1)S(1)}, u32[]{:S(2)}, u32[]{:S(2)}) %all-to-all-start.14) | async-done | bytes 262176 | tf_op jit(solution)/shard_map/all_to_all | solution.py:30
  265.6 2.4 near_solve.10
  268.2 18.1 %all_to_all.102 = bf16[8,5,32,128]{3,2,1,0:T(8,128)(2,1)S(1)} all-to-all(bf16[8,5,32,128]{3,2,1,0:T(8,128)(2,1)S(1)} %broadcast_in_dim.13), channel_id=1, replica_groups=mesh['row'=8,'grp'=4,'sub'=8] {'row'}, dimensions={0} | all-to-all | bytes 655360 | tf_op jit(solution)/shard_map/all_to_all | solution.py:30
  286.3 5.0 %all-to-all-start.16 = ((bf16[32,32,128]{2,1,0:T(8,128)(2,1)}), bf16[32,32,128]{2,1,0:T(8,128)(2,1)S(1)}, u32[]{:S(2)}, u32[]{:S(2)}) async-start(bf16[32,32,128]{2,1,0:T(8,128)(2,1)} %get-tuple-element.31), calls=%async_computation.16 | async-start | bytes 524288 | tf_op jit(solution)/shard_map/all_to_all | solution.py:30
  292.0 2.7 far_rest.9.refs_2_
  294.7 4.4 %all-to-all-done.16 = bf16[32,32,128]{2,1,0:T(8,128)(2,1)S(1)} async-done(((bf16[32,32,128]{2,1,0:T(8,128)(2,1)}), bf16[32,32,128]{2,1,0:T(8,128)(2,1)S(1)}, u32[]{:S(2)}, u32[]{:S(2)}) %all-to-all-start.16) | async-done | bytes 262176 | tf_op jit(solution)/shard_map/all_to_all | solution.py:30
  299.1 2.4 near_solve.11
  301.5 5.0 %all-to-all-start.17 = ((bf16[32,32,128]{2,1,0:T(8,128)(2,1)}), bf16[32,32,128]{2,1,0:T(8,128)(2,1)S(1)}, u32[]{:S(2)}, u32[]{:S(2)}) async-start(bf16[32,32,128]{2,1,0:T(8,128)(2,1)} %get-tuple-element.33), calls=%async_computation.17 | async-start | bytes 524288 | tf_op jit(solution)/shard_map/all_to_all | solution.py:30
  308.0 3.1 far_rest.10.refs_2_
  311.1 3.3 all-to-all-done.17
  314.3 2.5 near_solve.12
  316.8 5.0 %all-to-all-start.18 = ((bf16[32,32,128]{2,1,0:T(8,128)(2,1)}), bf16[32,32,128]{2,1,0:T(8,128)(2,1)S(1)}, u32[]{:S(2)}, u32[]{:S(2)}) async-start(bf16[32,32,128]{2,1,0:T(8,128)(2,1)} %get-tuple-element.34), calls=%async_computation.18 | async-start | bytes 524288 | tf_op jit(solution)/shard_map/all_to_all | solution.py:30
  323.3 18.3 %all-gather.11.cloned.1.call-done = bf16[192,128,128]{2,1,0:T(8,128)(2,1)} async-done(((bf16[24,128,128]{2,1,0:T(8,128)(2,1)}), bf16[192,128,128]{2,1,0:T(8,128)(2,1)}) %all-gather.11.cloned.1.call-update) | async-done | bytes 6291472 | tf_op jit(solution)/shard_map/all_gather | solution.py:209
  341.7 4.3 %near_solve.13 = (f32[32,128]{1,0:T(8,128)S(1)}, bf16[32,32,128]{2,1,0:T(8,128)(2,1)}) custom-call(bf16[4,8,32,128]{3,2,1,0:T(8,128)(2,1)S(1)} %bitcast.289, bf16[4,8,32,128]{3,2,1,0:T(8,128)(2,1)S(1)} %bitcast.294, bf16[4,8,32,128]{3,2,1,0:T(8,128)(2,1)S(1)} %bitcast.298, bf16[4,8,32,128]{3,2,1,0:T(8,128)(2,1)S(1)} %bitcast.301, ...), custom_call_target="tpu_custom_call" | custom-call | flops 201326592 | bytes 6291456 | tf_op jit(solution)/shard_map/near_solve/pallas_call | solution.py:153
  346.0 15.0 %all_to_all.103 = bf16[8,3,32,128]{3,2,1,0:T(8,128)(2,1)S(1)} all-to-all(bf16[8,3,32,128]{3,2,1,0:T(8,128)(2,1)S(1)} %broadcast_in_dim.14), channel_id=1, replica_groups=mesh['row'=8,'grp'=4,'sub'=8] {'row'}, dimensions={0} | all-to-all | bytes 393216 | tf_op jit(solution)/shard_map/all_to_all | solution.py:30
  (94 shorter events, 36.3 us)
Async XLA Ops:
  6.5 3.5 copy-start.1
  6.5 3.8 %copy-start = (f32[8,1,128,128]{3,2,1,0:T(8,128)S(1)}, f32[8,1,128,128]{3,2,1,0:T(8,128)}, u32[]{:S(2)}) copy-start(f32[8,1,128,128]{3,2,1,0:T(8,128)} %param.7) | copy-start | bytes 1572868
  6.5 134.4 %all-gather.7.cloned.1.call-start = ((), (), s32[]{:S(2)}) async-start(), calls=%async_computation.20 | async-start | bytes 11796480 | tf_op jit(solution)/shard_map/all_gather | solution.py:209
  9.9 4.8 %copy-start.2 = (s32[32,1,8,1]{0,3,2,1:T(1,128)S(1)}, s32[32,1,8,1]{0,3,2,1:T(1,128)}, u32[]{:S(2)}) copy-start(s32[32,1,8,1]{0,3,2,1:T(1,128)} %param.5) | copy-start | bytes 3076
  10.0 282.0 %all-gather.9.cloned.1.call-start = ((), (), s32[]{:S(2)}) async-start(), calls=%async_computation.21 | async-start | bytes 14155776 | tf_op jit(solution)/shard_map/all_gather | solution.py:209
  17.3 16.0 %all-to-all-start = ((bf16[32,32,128]{2,1,0:T(8,128)(2,1)}), bf16[32,32,128]{2,1,0:T(8,128)(2,1)S(1)}, u32[]{:S(2)}, u32[]{:S(2)}) async-start(bf16[32,32,128]{2,1,0:T(8,128)(2,1)} %bitcast.13), calls=%async_computation | async-start | bytes 524288 | tf_op jit(solution)/shard_map/all_to_all | solution.py:30
  24.9 316.8 %all-gather.11.cloned.1.call-start = ((), (), s32[]{:S(2)}) async-start(), calls=%async_computation.22 | async-start | bytes 7077888 | tf_op jit(solution)/shard_map/all_gather | solution.py:209
  34.0 17.8 %all-to-all-start.1 = ((bf16[8,32,128]{2,1,0:T(8,128)(2,1)}), bf16[8,32,128]{2,1,0:T(8,128)(2,1)}, u32[]{:S(2)}, u32[]{:S(2)}) async-start(bf16[8,32,128]{2,1,0:T(8,128)(2,1)} %broadcast_in_dim.10), calls=%async_computation.1 | async-start | bytes 131072 | tf_op jit(solution)/shard_map/all_to_all | solution.py:30
  51.7 9.0 %all-to-all-start.2 = ((bf16[8,32,128]{2,1,0:T(8,128)(2,1)}), bf16[8,32,128]{2,1,0:T(8,128)(2,1)S(1)}, u32[]{:S(2)}, u32[]{:S(2)}) async-start(bf16[8,32,128]{2,1,0:T(8,128)(2,1)} %all-to-all-done.1), calls=%async_computation.2 | async-start | bytes 131072 | tf_op jit(solution)/shard_map/all_to_all | solution.py:30
  63.7 14.2 %all-to-all-start.3 = ((bf16[32,32,128]{2,1,0:T(8,128)(2,1)}), bf16[32,32,128]{2,1,0:T(8,128)(2,1)S(1)}, u32[]{:S(2)}, u32[]{:S(2)}) async-start(bf16[32,32,128]{2,1,0:T(8,128)(2,1)} %bitcast.21), calls=%async_computation.3 | async-start | bytes 524288 | tf_op jit(solution)/shard_map/all_to_all | solution.py:30
  78.5 13.4 %all-to-all-start.4 = ((bf16[8,32,128]{2,1,0:T(8,128)(2,1)}), bf16[8,32,128]{2,1,0:T(8,128)(2,1)}, u32[]{:S(2)}, u32[]{:S(2)}) async-start(bf16[8,32,128]{2,1,0:T(8,128)(2,1)} %broadcast_in_dim.11), calls=%async_computation.4 | async-start | bytes 131072 | tf_op jit(solution)/shard_map/all_to_all | solution.py:30
  91.9 8.8 %all-to-all-start.5 = ((bf16[8,32,128]{2,1,0:T(8,128)(2,1)}), bf16[8,32,128]{2,1,0:T(8,128)(2,1)S(1)}, u32[]{:S(2)}, u32[]{:S(2)}) async-start(bf16[8,32,128]{2,1,0:T(8,128)(2,1)} %all-to-all-done.4), calls=%async_computation.5 | async-start | bytes 131072 | tf_op jit(solution)/shard_map/all_to_all | solution.py:30
  133.0 7.7 %collective-permute-start = (bf16[5,32,128]{2,1,0:T(8,128)(2,1)S(1)}, bf16[5,32,128]{2,1,0:T(8,128)(2,1)S(1)}, u32[]{:S(2)}, u32[]{:S(2)}) collective-permute-start(bf16[5,32,128]{2,1,0:T(8,128)(2,1)S(1)} %reduce_sum.82), channel_id=1, source_target_pairs={{0,0},{1,32},{2,64},{3,96},{4,128},{5,160},{6,192},{7,224},{8,8},{... | collective-permute-start | bytes 122888 | tf_op jit(solution)/shard_map/ppermute | solution.py:248
  143.5 17.0 %all-to-all-start.7 = ((bf16[32,32,128]{2,1,0:T(8,128)(2,1)}), bf16[32,32,128]{2,1,0:T(8,128)(2,1)S(1)}, u32[]{:S(2)}, u32[]{:S(2)}) async-start(bf16[32,32,128]{2,1,0:T(8,128)(2,1)} %bitcast.45), calls=%async_computation.7 | async-start | bytes 524288 | tf_op jit(solution)/shard_map/all_to_all | solution.py:30
  163.2 12.8 %all-to-all-start.8 = ((bf16[32,32,128]{2,1,0:T(8,128)(2,1)}), bf16[32,32,128]{2,1,0:T(8,128)(2,1)S(1)}, u32[]{:S(2)}, u32[]{:S(2)}) async-start(bf16[32,32,128]{2,1,0:T(8,128)(2,1)} %bitcast.53), calls=%async_computation.8 | async-start | bytes 524288 | tf_op jit(solution)/shard_map/all_to_all | solution.py:30
  178.7 12.8 %all-to-all-start.9 = ((bf16[32,32,128]{2,1,0:T(8,128)(2,1)}), bf16[32,32,128]{2,1,0:T(8,128)(2,1)S(1)}, u32[]{:S(2)}, u32[]{:S(2)}) async-start(bf16[32,32,128]{2,1,0:T(8,128)(2,1)} %bitcast.61), calls=%async_computation.9 | async-start | bytes 524288 | tf_op jit(solution)/shard_map/all_to_all | solution.py:30
  207.2 12.8 %all-to-all-start.11 = ((bf16[32,32,128]{2,1,0:T(8,128)(2,1)}), bf16[32,32,128]{2,1,0:T(8,128)(2,1)S(1)}, u32[]{:S(2)}, u32[]{:S(2)}) async-start(bf16[32,32,128]{2,1,0:T(8,128)(2,1)} %broadcast_in_dim.12), calls=%async_computation.11 | async-start | bytes 524288 | tf_op jit(solution)/shard_map/all_to_all | solution.py:30
  222.4 12.8 %all-to-all-start.12 = ((bf16[32,32,128]{2,1,0:T(8,128)(2,1)}), bf16[32,32,128]{2,1,0:T(8,128)(2,1)S(1)}, u32[]{:S(2)}, u32[]{:S(2)}) async-start(bf16[32,32,128]{2,1,0:T(8,128)(2,1)} %get-tuple-element.23), calls=%async_computation.12 | async-start | bytes 524288 | tf_op jit(solution)/shard_map/all_to_all | solution.py:30
  237.6 12.8 %all-to-all-start.13 = ((bf16[32,32,128]{2,1,0:T(8,128)(2,1)}), bf16[32,32,128]{2,1,0:T(8,128)(2,1)S(1)}, u32[]{:S(2)}, u32[]{:S(2)}) async-start(bf16[32,32,128]{2,1,0:T(8,128)(2,1)} %get-tuple-element.24), calls=%async_computation.13 | async-start | bytes 524288 | tf_op jit(solution)/shard_map/all_to_all | solution.py:30
  252.8 12.8 %all-to-all-start.14 = ((bf16[32,32,128]{2,1,0:T(8,128)(2,1)}), bf16[32,32,128]{2,1,0:T(8,128)(2,1)S(1)}, u32[]{:S(2)}, u32[]{:S(2)}) async-start(bf16[32,32,128]{2,1,0:T(8,128)(2,1)} %get-tuple-element.25), calls=%async_computation.14 | async-start | bytes 524288 | tf_op jit(solution)/shard_map/all_to_all | solution.py:30
  286.3 12.8 %all-to-all-start.16 = ((bf16[32,32,128]{2,1,0:T(8,128)(2,1)}), bf16[32,32,128]{2,1,0:T(8,128)(2,1)S(1)}, u32[]{:S(2)}, u32[]{:S(2)}) async-start(bf16[32,32,128]{2,1,0:T(8,128)(2,1)} %get-tuple-element.31), calls=%async_computation.16 | async-start | bytes 524288 | tf_op jit(solution)/shard_map/all_to_all | solution.py:30
  301.5 12.8 %all-to-all-start.17 = ((bf16[32,32,128]{2,1,0:T(8,128)(2,1)}), bf16[32,32,128]{2,1,0:T(8,128)(2,1)S(1)}, u32[]{:S(2)}, u32[]{:S(2)}) async-start(bf16[32,32,128]{2,1,0:T(8,128)(2,1)} %get-tuple-element.33), calls=%async_computation.17 | async-start | bytes 524288 | tf_op jit(solution)/shard_map/all_to_all | solution.py:30
  316.8 24.9 %all-to-all-start.18 = ((bf16[32,32,128]{2,1,0:T(8,128)(2,1)}), bf16[32,32,128]{2,1,0:T(8,128)(2,1)S(1)}, u32[]{:S(2)}, u32[]{:S(2)}) async-start(bf16[32,32,128]{2,1,0:T(8,128)(2,1)} %get-tuple-element.34), calls=%async_computation.18 | async-start | bytes 524288 | tf_op jit(solution)/shard_map/all_to_all | solution.py:30
Sparse Core Ops, SparseCore 0:
  10.1 119.5 all-gather.6
  131.5 132.0 all-gather.8
  265.4 76.2 all-gather.10
